TPU v7x, 768 devices: a whole 4x8x12 slice. The times are simulated.
768 devices in a mesh: gx: 32 (over y, x_lo, core), gy: 24 (over x_hi, z).
Axes of the slice: x: 4 (x_hi: 2, x_lo: 2; x = x_hi * 2 + x_lo), y: 8, z: 12, core: 2. Of those that a mesh axis runs over, the one named last changes fastest.
Arguments:
- u_flow: bfloat16 [16, 4608, 3072], P(None, 'gx', 'gy'), may hold values from -6 to 6
- v_flow: bfloat16 [16, 4608, 3072], P(None, 'gx', 'gy'), may hold values from -6 to 6
- sea_mask: int32 [4608, 3072], P('gx', 'gy'), may hold values 0 or 1
- bottom_level: int32 [4608, 3072], P('gx', 'gy'), may hold values from 1 to 16
- mode_project: bfloat16 [16, 2], replicated, may hold values from -1.5 to 1.5
- mode_shape: float32 [16, 2], replicated, may hold values from -4 to 4
- forward_x: bfloat16 [4608, 4608], P('gx'), may hold values from -0.09375 to 0.09375
- forward_y: bfloat16 [3072, 3072], P('gy'), may hold values from -0.109375 to 0.109375
- inverse_x: bfloat16 [4608, 4608], P('gx'), may hold values from -0.09375 to 0.09375
- inverse_y: bfloat16 [3072, 3072], P('gy'), may hold values from -0.109375 to 0.109375
- eigen_x: float32 [4608], P('gx'), may hold values from 0.5 to 4
- eigen_y: float32 [3072], P('gy'), may hold values from 0.5 to 4
- mode_shift: float32 [2], replicated, may hold values from 0.5 to 2
Outputs:
- u_correct: bfloat16 [16, 4608, 3072], P(None, 'gx', 'gy')
- v_correct: bfloat16 [16, 4608, 3072], P(None, 'gx', 'gy')
- pressure: float32 [2, 4608, 3072], P(None, 'gx', 'gy')
Inputs may be any that keep to these rules, and one draw needn't show every extreme that they name: `sea_mask`: land and sea flags.
All inputs are finite; a program needn't handle non-finite values. No bound on the sum of `sea_mask` on one device may be relied on, other than what follows from the above.
Results may differ from a plain program's by a relative error of at most 0.014.
Values may be sent and summed in bfloat16 or wider, within the bound.
No kernel may reach another device: no remote copies, remote signals or barrier semaphores. Data moves between devices by JAX's collectives and lax.ppermute only.
A program may use at most 32 MiB of HBM per device.

v0:
```python
import jax
import jax.numpy as jnp
from jax import lax
from jax.sharding import PartitionSpec as P


def extended(block, sides, width, periodic):
    for axis, dim in sides:
        count = lax.axis_size(axis)
        forward = [(i, i + 1) for i in range(count - 1)]
        if periodic:
            forward.append((count - 1, 0))
        backward = [(target, source) for source, target in forward]
        low = lax.ppermute(
            lax.slice_in_dim(block, block.shape[dim] - width, None, axis=dim), axis, forward
        )
        high = lax.ppermute(lax.slice_in_dim(block, 0, width, axis=dim), axis, backward)
        block = jnp.concatenate([low, block, high], axis=dim)
    return block


def centre_x(field):
    padded = extended(field.astype(jnp.bfloat16), (("gx", 1),), 1, True).astype(field.dtype)
    return 0.5 * (padded[:, 2:, :] - padded[:, :-2, :])


def centre_y(field):
    padded = extended(field.astype(jnp.bfloat16), (("gy", 2),), 1, False).astype(field.dtype)
    return 0.5 * (padded[:, :, 2:] - padded[:, :, :-2])


def fold_x(data, table):
    return jnp.einsum(
        "kn,mnj->mkj",
        table,
        lax.all_gather(data, "gx", axis=1, tiled=True),
        preferred_element_type=jnp.float32,
    )


def transform_x(data, table):
    return jnp.concatenate(
        [fold_x(data[mode : mode + 1], table) for mode in range(data.shape[0])], 0
    )


def transform_y(data, table):
    return jnp.einsum(
        "min,kn->mik",
        lax.all_gather(data, "gy", axis=2, tiled=True),
        table,
        preferred_element_type=jnp.float32,
    )


def body(
    u_flow,
    v_flow,
    sea_mask,
    bottom_level,
    mode_project,
    mode_shape,
    forward_x,
    forward_y,
    inverse_x,
    inverse_y,
    eigen_x,
    eigen_y,
    mode_shift,
):
    level_ids = lax.broadcasted_iota(jnp.int32, u_flow.shape, 0)
    wet_int = sea_mask[None] * (level_ids < bottom_level[None]).astype(jnp.int32)
    wet = wet_int.astype(jnp.bfloat16)
    flux_u = jnp.einsum(
        "lm,lij->mij", mode_project, u_flow * wet, preferred_element_type=jnp.float32
    )
    flux_v = jnp.einsum(
        "lm,lij->mij", mode_project, v_flow * wet, preferred_element_type=jnp.float32
    )
    flux_u = flux_u.astype(jnp.bfloat16).astype(jnp.float32)
    flux_v = flux_v.astype(jnp.bfloat16).astype(jnp.float32)
    mask_f = sea_mask.astype(jnp.float32)
    divergence = (mask_f[None] * (centre_x(flux_u) + centre_y(flux_v))).astype(jnp.bfloat16)
    spec_x = transform_x(divergence, forward_x).astype(jnp.bfloat16)
    spec_xy = transform_y(spec_x, forward_y)
    denom = eigen_x[None, :, None] + eigen_y[None, None, :] + mode_shift[:, None, None]
    scaled = (spec_xy / denom).astype(jnp.bfloat16)
    back_y = transform_y(scaled, inverse_y).astype(jnp.bfloat16)
    pressure = transform_x(back_y, inverse_x)
    grad_x = centre_x(pressure)
    grad_y = centre_y(pressure)
    wet_f = wet_int.astype(jnp.float32)
    shape_zero = mode_shape[:, 0][:, None, None]
    shape_one = mode_shape[:, 1][:, None, None]
    u_correct = (-wet_f * (shape_zero * grad_x[0][None] + shape_one * grad_x[1][None])).astype(
        jnp.bfloat16
    )
    v_correct = (-wet_f * (shape_zero * grad_y[0][None] + shape_one * grad_y[1][None])).astype(
        jnp.bfloat16
    )
    return (u_correct, v_correct, pressure)


def solution(mesh):
    return jax.shard_map(
        body,
        mesh=mesh,
        in_specs=(
            P(None, "gx", "gy"),
            P(None, "gx", "gy"),
            P("gx", "gy"),
            P("gx", "gy"),
            P(),
            P(),
            P("gx", None),
            P("gy", None),
            P("gx", None),
            P("gy", None),
            P("gx"),
            P("gy"),
            P(),
        ),
        out_specs=(P(None, "gx", "gy"), P(None, "gx", "gy"), P(None, "gx", "gy")),
        check_vma=False,
    )
```

profile of v0, /device:TPU:1, one launch (start us, length us, event | category | flops | bytes accessed | tf_op | source)
XLA Modules:
  0.0 585.9 jit_solution(5707059856952653183)
XLA Ops:
  7.2 0.0 all-gather.9.cloned.1.call-start
  7.2 1.7 fusion.37
  9.0 0.2 fusion.14
  9.2 4.5 collective-permute-start
  13.7 9.8 %collective-permute-start.1 = (bf16[2,1,128]{2,0,1:T(2,128)(2,1)S(1)}, bf16[2,1,128]{2,0,1:T(2,128)(2,1)S(1)}, u32[]{:S(2)}, u32[]{:S(2)}) collective-permute-start(bf16[2,1,128]{2,0,1:T(2,128)(2,1)S(1)} %get-tuple-element.22), channel_id=1, source_target_pairs={{24,0},{48,24},{72,48},{96,72},{120,96},{144,120},{168,144},{192,1... | collective-permute-start | bytes 1544 | tf_op jit(solution)/shard_map/ppermute | solution.py:17
  23.6 0.2 fusion.15
  23.8 0.1 fusion.53
  23.9 1.3 collective-permute-start.2
  25.2 1.3 collective-permute-start.3
  26.6 0.1 maximum_convert_fusion.3
  26.7 3.6 collective-permute-done.3
  30.3 0.4 maximum_convert_fusion
  30.7 0.2 fusion.44
  31.0 0.1 fusion.51
  31.1 0.6 copy.23
  31.7 0.0 all-gather.7.cloned.1.call-start
  31.8 0.6 copy.22
  32.4 0.1 all-gather.7.cloned.1.call-update
  32.5 0.0 all-gather.11.cloned.1.call-start
  32.5 74.4 %all-gather.9.cloned.1.call-done = bf16[1,4608,128]{2,1,0:T(8,128)(2,1)} async-done(((bf16[1,144,128]{2,1,0:T(8,128)(2,1)}), bf16[1,4608,128]{2,1,0:T(8,128)(2,1)}) %all-gather.9.cloned.1.call-update) | async-done | bytes 1179664 | tf_op jit(solution)/shard_map/all_gather | solution.py:36
  106.9 1.8 fusion.28
  108.7 70.5 %all-gather.7.cloned.1.call-done = bf16[1,4608,128]{2,1,0:T(8,128)(2,1)} async-done(((bf16[1,144,128]{2,1,0:T(8,128)(2,1)}), bf16[1,4608,128]{2,1,0:T(8,128)(2,1)}) %all-gather.7.cloned.1.call-update) | async-done | bytes 1179664 | tf_op jit(solution)/shard_map/all_gather | solution.py:36
  179.2 1.8 fusion.31
  181.0 0.6 pad_maximum_fusion.1
  181.7 0.0 all-gather.13.cloned.1.call-start
  181.8 0.1 broadcast_add_fusion
  181.9 115.1 %all-gather.11.cloned.1.call-done = bf16[2,144,3072]{2,1,0:T(8,128)(2,1)} async-done(((bf16[2,144,128]{2,1,0:T(8,128)(2,1)}), bf16[2,144,3072]{2,1,0:T(8,128)(2,1)}) %all-gather.11.cloned.1.call-update) | async-done | bytes 1769488 | tf_op jit(solution)/shard_map/all_gather | solution.py:50
  297.0 2.7 fusion.13
  299.8 0.0 all-gather.15.cloned.1.call-start
  299.8 116.0 %all-gather.13.cloned.1.call-done = bf16[2,144,3072]{2,1,0:T(8,128)(2,1)} async-done(((bf16[2,144,128]{2,1,0:T(8,128)(2,1)}), bf16[2,144,3072]{2,1,0:T(8,128)(2,1)}) %all-gather.13.cloned.1.call-update) | async-done | bytes 1769488 | tf_op jit(solution)/shard_map/all_gather | solution.py:50
  415.9 2.1 convolution_convert_fusion.2
  418.0 0.6 fusion.50
  418.6 0.0 all-gather.17.cloned.1.call-start
  418.7 0.5 all-gather.17.cloned.1.call-update
  419.2 70.1 %all-gather.15.cloned.1.call-done = bf16[1,4608,128]{2,1,0:T(8,128)(2,1)} async-done(((bf16[1,144,128]{2,1,0:T(8,128)(2,1)}), bf16[1,4608,128]{2,1,0:T(8,128)(2,1)}) %all-gather.15.cloned.1.call-update) | async-done | bytes 1179664 | tf_op jit(solution)/shard_map/all_gather | solution.py:36
  489.3 1.8 fusion.16
  491.1 70.4 %all-gather.17.cloned.1.call-done = bf16[1,4608,128]{2,1,0:T(8,128)(2,1)} async-done(((bf16[1,144,128]{2,1,0:T(8,128)(2,1)}), bf16[1,4608,128]{2,1,0:T(8,128)(2,1)}) %all-gather.17.cloned.1.call-update) | async-done | bytes 1179664 | tf_op jit(solution)/shard_map/all_gather | solution.py:36
  561.5 1.8 fusion.19
  563.3 0.7 fusion.47
  564.0 2.7 collective-permute-start.4
  566.7 1.9 collective-permute-start.5
  568.6 0.1 fusion.48
  568.7 3.4 collective-permute-start.6
  572.1 1.3 collective-permute-start.7
  573.5 3.7 collective-permute-done.7
  577.2 0.1 maximum_convert_fusion.1
  577.4 0.1 fusion.40
  577.5 1.6 fusion.4
  (39 shorter events, 0.2 us)
Async XLA Ops:
  7.2 99.7 %copy-start = (bf16[144,4608]{1,0:T(8,128)(2,1)S(1)}, bf16[144,4608]{1,0:T(8,128)(2,1)}, u32[]{:S(2)}) copy-start(bf16[144,4608]{1,0:T(8,128)(2,1)} %param.19) | copy-start | bytes 3981316
  7.2 1.8 copy-start.9
  7.2 99.7 %all-gather.9.cloned.1.call-start = ((), (), s32[]{:S(2)}) async-start(), calls=%async_computation.1 | async-start | bytes 1216512 | tf_op jit(solution)/shard_map/all_gather | solution.py:36
  8.9 17.6 %copy-start.3 = (s32[144,128]{1,0:T(8,128)S(1)}, s32[144,128]{1,0:T(8,128)}, u32[]{:S(2)}) copy-start(s32[144,128]{1,0:T(8,128)} %param.15) | copy-start | bytes 221188
  9.2 17.4 %collective-permute-start = (bf16[2,1,128]{2,0,1:T(2,128)(2,1)S(1)}, bf16[2,1,128]{2,0,1:T(2,128)(2,1)S(1)}, u32[]{:S(2)}, u32[]{:S(2)}) collective-permute-start(bf16[2,1,128]{2,0,1:T(2,128)(2,1)S(1)} %get-tuple-element.21), channel_id=1, source_target_pairs={{0,24},{24,48},{48,72},{72,96},{96,120},{120,144},{144,168},{168,1... | collective-permute-start | bytes 1544 | tf_op jit(solution)/shard_map/ppermute | solution.py:14
  13.7 12.9 %collective-permute-start.1 = (bf16[2,1,128]{2,0,1:T(2,128)(2,1)S(1)}, bf16[2,1,128]{2,0,1:T(2,128)(2,1)S(1)}, u32[]{:S(2)}, u32[]{:S(2)}) collective-permute-start(bf16[2,1,128]{2,0,1:T(2,128)(2,1)S(1)} %get-tuple-element.22), channel_id=1, source_target_pairs={{24,0},{48,24},{72,48},{96,72},{120,96},{144,120},{168,144},{192,1... | collective-permute-start | bytes 1544 | tf_op jit(solution)/shard_map/ppermute | solution.py:17
  23.9 2.8 collective-permute-start.2
  25.2 5.1 collective-permute-start.3
  31.7 147.5 %all-gather.7.cloned.1.call-start = ((), (), s32[]{:S(2)}) async-start(), calls=%async_computation | async-start | bytes 1216512 | tf_op jit(solution)/shard_map/all_gather | solution.py:36
  32.5 264.5 %all-gather.11.cloned.1.call-start = ((), (), s32[]{:S(2)}) async-start(), calls=%async_computation.2 | async-start | bytes 1843200 | tf_op jit(solution)/shard_map/all_gather | solution.py:50
  108.7 73.1 %copy-start.5 = (f32[144]{0:T(256)S(1)}, f32[144]{0:T(256)}, u32[]{:S(2)}) copy-start(f32[144]{0:T(256)} %param.23) | copy-start | bytes 1732
  108.7 73.1 %copy-start.7 = (f32[128]{0:T(128)S(1)}, f32[128]{0:T(128)}, u32[]{:S(2)}) copy-start(f32[128]{0:T(128)} %param.24) | copy-start | bytes 1540
  108.7 188.3 %copy-start.8 = (bf16[128,3072]{1,0:T(8,128)(2,1)S(1)}, bf16[128,3072]{1,0:T(8,128)(2,1)}, u32[]{:S(2)}) copy-start(bf16[128,3072]{1,0:T(8,128)(2,1)} %param.20) | copy-start | bytes 2359300
  108.7 188.3 %copy-start.10 = (f32[2]{0:T(128)S(1)}, f32[2]{0:T(128)}, u32[]{:S(2)}) copy-start(f32[2]{0:T(128)} %param.25) | copy-start | bytes 28
  181.7 234.2 %all-gather.13.cloned.1.call-start = ((), (), s32[]{:S(2)}) async-start(), calls=%async_computation.3 | async-start | bytes 1843200 | tf_op jit(solution)/shard_map/all_gather | solution.py:50
  181.8 234.0 %copy-start.2 = (bf16[128,3072]{1,0:T(8,128)(2,1)S(1)}, bf16[128,3072]{1,0:T(8,128)(2,1)}, u32[]{:S(2)}) copy-start(bf16[128,3072]{1,0:T(8,128)(2,1)} %param.22) | copy-start | bytes 2359300
  299.8 119.4 %copy-start.6 = (f32[16,2]{0,1:T(2,128)S(1)}, f32[16,2]{0,1:T(2,128)}, u32[]{:S(2)}) copy-start(f32[16,2]{0,1:T(2,128)} %param.18) | copy-start | bytes 388
  299.8 189.6 %copy-start.1 = (bf16[144,4608]{1,0:T(8,128)(2,1)S(1)}, bf16[144,4608]{1,0:T(8,128)(2,1)}, u32[]{:S(2)}) copy-start(bf16[144,4608]{1,0:T(8,128)(2,1)} %param.21) | copy-start | bytes 3981316
  299.8 189.5 %all-gather.15.cloned.1.call-start = ((), (), s32[]{:S(2)}) async-start(), calls=%async_computation.4 | async-start | bytes 1216512 | tf_op jit(solution)/shard_map/all_gather | solution.py:36
  418.6 142.9 %all-gather.17.cloned.1.call-start = ((), (), s32[]{:S(2)}) async-start(), calls=%async_computation.5 | async-start | bytes 1216512 | tf_op jit(solution)/shard_map/all_gather | solution.py:36
  564.0 9.4 %collective-permute-start.4 = (bf16[2,1,128]{2,1,0:T(2,128)(2,1)S(1)}, bf16[2,1,128]{2,1,0:T(2,128)(2,1)S(1)}, u32[]{:S(2)}, u32[]{:S(2)}) collective-permute-start(bf16[2,1,128]{2,1,0:T(2,128)(2,1)S(1)} %get-tuple-element.15), channel_id=1, source_target_pairs={{0,24},{24,48},{48,72},{72,96},{96,120},{120,144},{144,168},{168,1... | collective-permute-start | bytes 1544 | tf_op jit(solution)/shard_map/ppermute | solution.py:14
  566.7 6.8 %collective-permute-start.5 = (bf16[2,1,128]{2,1,0:T(2,128)(2,1)S(1)}, bf16[2,1,128]{2,1,0:T(2,128)(2,1)S(1)}, u32[]{:S(2)}, u32[]{:S(2)}) collective-permute-start(bf16[2,1,128]{2,1,0:T(2,128)(2,1)S(1)} %get-tuple-element.16), channel_id=1, source_target_pairs={{24,0},{48,24},{72,48},{96,72},{120,96},{144,120},{168,144},{192,1... | collective-permute-start | bytes 1544 | tf_op jit(solution)/shard_map/ppermute | solution.py:17
  568.7 8.8 %copy-start.4 = (s32[144,128]{1,0:T(8,128)S(1)}, s32[144,128]{1,0:T(8,128)}, u32[]{:S(2)}) copy-start(s32[144,128]{1,0:T(8,128)} %param.16) | copy-start | bytes 221188
  568.7 4.8 collective-permute-start.6
  572.1 5.1 collective-permute-start.7
Sparse Core Ops, SparseCore 0:
  31.9 74.9 all-gather.8
  109.9 69.2 all-gather.6
  183.4 113.5 all-gather.10
  301.0 114.8 all-gather.12
  418.7 70.5 all-gather.14
  492.2 69.2 all-gather.16
where the time goes:
time: 591 us; the launch traced here: 586 us
  waiting for transfers between devices  525 us (89%)
  starting transfers between devices  26.5 us (4%)
  between operations  14.5 us (2%)
  matrix products  12.3 us (2%)
    all_gather x4, waiting for transfers between devices, fold_x(): lax.all_gather(data, 'gx', axis=1, tiled=True)  285 us
    all_gather x2, waiting for transfers between devices, transform_y(): lax.all_gather(data, 'gy', axis=2, tiled=True)  231 us
    ppermute x4, starting transfers between devices, extended(): lax.ppermute(lax.slice_in_dim(block, 0, width, axis=dim), axis, backward)  14.3 us
    ppermute x4, starting transfers between devices, extended(): lax.ppermute(lax.slice_in_dim(block, block.shape[dim] - width, None, axis...  11.9 us
  transfers between devices with their start and end apart: 14, of which 8 were waited for; matrix products, arithmetic and copies ran while one was open for 1% of the time, Pallas kernels for 0%

commit v1 on v0

v1 whole, which is shorter than its diff:
```python
import jax
import jax.numpy as jnp
from jax import lax
from jax.sharding import Mesh
from jax.sharding import PartitionSpec as P

SUB = (("y", 8), ("xl", 2), ("c", 2), ("xh", 2), ("zh", 3), ("zl", 4))
GX = ("y", "xl", "c")
GY = ("xh", "zh", "zl")
QUAD = ("xl", "c")
BF = jnp.bfloat16
F32 = jnp.float32


def gather(block, axes, count):
    return lax.all_to_all(jnp.broadcast_to(block[None], (count,) + block.shape), axes, 0, 0)


def scatter_sum(parts, axes):
    return jnp.sum(lax.all_to_all(parts, axes, 0, 0).astype(F32), axis=0)


def edges(block, axes, dim, count, periodic):
    forward = [(i, i + 1) for i in range(count - 1)]
    if periodic:
        forward.append((count - 1, 0))
    backward = [(target, source) for source, target in forward]
    low = lax.ppermute(lax.slice_in_dim(block, block.shape[dim] - 1, None, axis=dim), axes, forward)
    high = lax.ppermute(lax.slice_in_dim(block, 0, 1, axis=dim), axes, backward)
    return low, high


def centre_x(field):
    low, high = edges(field.astype(BF), GX, 1, 32, True)
    padded = jnp.concatenate([low.astype(F32), field, high.astype(F32)], axis=1)
    return 0.5 * (padded[:, 2:, :] - padded[:, :-2, :])


def centre_y(field):
    low, high = edges(field.astype(BF), GY, 2, 24, False)
    padded = jnp.concatenate([low.astype(F32), field, high.astype(F32)], axis=2)
    return 0.5 * (padded[:, :, 2:] - padded[:, :, :-2])


def quad_tables(fx, ix):
    me = lax.axis_index("xl") * 2 + lax.axis_index("c")
    both = jnp.stack([fx, ix]).reshape(2, 144, 8, 4, 144)
    both = jnp.moveaxis(both, 3, 0).reshape(4, 2, 144, 1152)
    pieces = [lax.dynamic_index_in_dim(both, me, 0, False)]
    for step in (1, 2, 3):
        send = lax.dynamic_index_in_dim(both, me ^ step, 0, False)
        pieces.append(lax.ppermute(send, QUAD, [(i, i ^ step) for i in range(4)]))
    held = jnp.stack(pieces)
    ordered = jnp.stack([lax.dynamic_index_in_dim(held, me ^ i, 0, False) for i in range(4)])
    return ordered[:, 0].reshape(576, 1152), ordered[:, 1].reshape(576, 1152)


def ring_tables(fy, iy):
    me = lax.axis_index("zh")
    both = jnp.stack([fy, iy]).reshape(2, 128, 2, 3, 512)
    both = jnp.moveaxis(both, 3, 0).reshape(3, 2, 128, 1024)
    pieces = [lax.dynamic_index_in_dim(both, me, 0, False)]
    for step in (1, 2):
        send = lax.dynamic_index_in_dim(both, (me + step) % 3, 0, False)
        pieces.append(lax.ppermute(send, "zh", [(i, (i + step) % 3) for i in range(3)]))
    held = jnp.stack(pieces)
    ordered = jnp.stack([lax.dynamic_index_in_dim(held, (me + 3 - i) % 3, 0, False) for i in range(3)])
    return ordered[:, 0], ordered[:, 1]


def transform_x(block, table):
    held = gather(block, "y", 8).reshape(1152, 256)
    parts = jnp.dot(table, held, preferred_element_type=F32).astype(BF)
    return scatter_sum(parts.reshape(4, 144, 256), QUAD)


def transform_y(block, table):
    held = gather(block, ("xh", "zl"), 8)
    parts = jnp.einsum("bkj,tqbj->tkq", held, table.reshape(3, 128, 8, 128), preferred_element_type=F32)
    return scatter_sum(parts.astype(BF), "zh")


def to_x(block):
    return jnp.concatenate([block[:144], block[144:]], axis=1)


def to_y(block):
    return jnp.concatenate([block[:, :128], block[:, 128:]], axis=0)


def body(
    u_flow,
    v_flow,
    sea_mask,
    bottom_level,
    mode_project,
    mode_shape,
    forward_x,
    forward_y,
    inverse_x,
    inverse_y,
    eigen_x,
    eigen_y,
    mode_shift,
):
    level_ids = lax.broadcasted_iota(jnp.int32, u_flow.shape, 0)
    wet_int = sea_mask[None] * (level_ids < bottom_level[None]).astype(jnp.int32)
    wet = wet_int.astype(BF)
    flux_u = jnp.einsum("lm,lij->mij", mode_project, u_flow * wet, preferred_element_type=F32)
    flux_v = jnp.einsum("lm,lij->mij", mode_project, v_flow * wet, preferred_element_type=F32)
    flux_u = flux_u.astype(BF).astype(F32)
    flux_v = flux_v.astype(BF).astype(F32)
    mask_f = sea_mask.astype(F32)
    divergence = (mask_f[None] * (centre_x(flux_u) + centre_y(flux_v))).astype(BF)
    table_fx, table_ix = quad_tables(forward_x, inverse_x)
    table_fy, table_iy = ring_tables(forward_y, inverse_y)
    spec_x = transform_x(to_x(divergence.reshape(288, 128)), table_fx).astype(BF)
    spec_xy = transform_y(to_y(spec_x), table_fy).reshape(2, 144, 128)
    denom = eigen_x[None, :, None] + eigen_y[None, None, :] + mode_shift[:, None, None]
    scaled = (spec_xy / denom).astype(BF)
    back_y = transform_y(scaled.reshape(288, 128), table_iy).astype(BF)
    pressure = to_y(transform_x(to_x(back_y), table_ix)).reshape(2, 144, 128)
    grad_x = centre_x(pressure)
    grad_y = centre_y(pressure)
    wet_f = wet_int.astype(F32)
    shape_zero = mode_shape[:, 0][:, None, None]
    shape_one = mode_shape[:, 1][:, None, None]
    u_correct = (-wet_f * (shape_zero * grad_x[0][None] + shape_one * grad_x[1][None])).astype(BF)
    v_correct = (-wet_f * (shape_zero * grad_y[0][None] + shape_one * grad_y[1][None])).astype(BF)
    return (u_correct, v_correct, pressure)


def solution(mesh):
    sub = Mesh(mesh.devices.reshape([n for _, n in SUB]), [name for name, _ in SUB])
    return jax.shard_map(
        body,
        mesh=sub,
        in_specs=(
            P(None, GX, GY),
            P(None, GX, GY),
            P(GX, GY),
            P(GX, GY),
            P(),
            P(),
            P(GX, None),
            P(GY, None),
            P(GX, None),
            P(GY, None),
            P(GX),
            P(GY),
            P(),
        ),
        out_specs=(P(None, GX, GY), P(None, GX, GY), P(None, GX, GY)),
        check_vma=False,
    )
```

time: 591 us -> 275 us (0.47)
  the two profiles are of different devices: /device:TPU:1 before, /device:TPU:63 now
where the time goes in v1:
time: 275 us; the launch traced here: 274 us
  blocking collectives  92.7 us (34%)
  starting transfers between devices  81.9 us (30%)
  waiting for transfers between devices  58.6 us (21%)
  local copies, waits for them, and re-layouts  28 us (10%)
  other arithmetic  7.46 us (3%)
  matrix products  4.24 us (2%)
    all_to_all x2, blocking collectives, gather(): lax.all_to_all(jnp.broadcast_to(block[None], (count,) + block.shape), axe...  55.1 us
    all_to_all x3, blocking collectives, scatter_sum(): return jnp.sum(lax.all_to_all(parts, axes, 0, 0).astype(F32), axis=0)  37.7 us
    ppermute x4, starting transfers between devices, edges(): high = lax.ppermute(lax.slice_in_dim(block, 0, 1, axis=dim), axes, backward)  27.2 us
    all_to_all x2, waiting for transfers between devices, gather(): lax.all_to_all(jnp.broadcast_to(block[None], (count,) + block.shape), axe...  25.5 us
    ppermute x2, waiting for transfers between devices, ring_tables(): lax.ppermute(send, 'zh', [(i, (i + step) % 3) for i in range(3)])  16.5 us
    ppermute x4, starting transfers between devices, edges(): lax.ppermute(lax.slice_in_dim(block, block.shape[dim] - 1, None, axis=dim...  14.4 us
    ppermute x2, starting transfers between devices, ring_tables(): lax.ppermute(send, 'zh', [(i, (i + step) % 3) for i in range(3)])  12.5 us
    another operation x4, local copies, waits for them, and re-layouts, quad_tables(): both = jnp.stack([fx, ix]).reshape(2, 144, 8, 4, 144)  12 us
  transfers between devices with their start and end apart: 16, of which 8 were waited for; matrix products, arithmetic and copies ran while one was open for 3% of the time, Pallas kernels for 0%

profile of v1, /device:TPU:63, one launch (start us, length us, event | category | flops | bytes accessed | tf_op | source)
XLA Modules:
  0.0 274.3 jit_solution(15597302402622395762)
XLA Ops:
  0.7 5.0 %stack.55 = bf16[1,144,8,4,144]{4,3,2,1,0:T(4,128)(2,1)S(1)} reshape(bf16[144,4608]{1,0:T(8,128)(2,1)} %param.21) | data formatting | bytes 2654208 | tf_op jit(solution)/shard_map/stack | solution.py:47
  5.7 1.7 copy.36
  7.4 5.0 %stack.54 = bf16[1,144,8,4,144]{4,3,2,1,0:T(4,128)(2,1)S(1)} reshape(bf16[144,4608]{1,0:T(8,128)(2,1)} %param.19) | data formatting | bytes 2654208 | tf_op jit(solution)/shard_map/stack | solution.py:47
  12.7 1.3 copy-done.1
  14.1 3.0 %maximum_bitcast_fusion = bf16[4,2,144,8,144]{4,3,2,1,0:T(8,128)(2,1)} fusion(bf16[1,144,8,4,144]{4,2,1,0,3:T(8,128)(2,1)S(1)} %copy-done.1, bf16[1,144,8,4,144]{4,2,1,0,3:T(8,128)(2,1)S(1)} %copy.35), kind=kLoop, calls=%fused_computation | loop fusion | flops 1327104 | bytes 5308416 | tf_op jit(solution)/shard_map/transpose | solution.py:48
  17.1 6.9 %reshape.100 = bf16[4,2,144,1152]{3,2,1,0:T(8,128)(2,1)S(1)} reshape(bf16[4,2,144,8,144]{4,3,2,1,0:T(8,128)(2,1)} %maximum_bitcast_fusion) | data formatting | bytes 5308416 | tf_op jit(solution)/shard_map/reshape | solution.py:48
  24.1 1.3 constant_dynamic-slice_fusion.8
  25.5 3.0 %collective-permute-start.2 = (bf16[2,144,1152]{2,1,0:T(8,128)(2,1)}, bf16[2,144,1152]{2,1,0:T(8,128)(2,1)S(1)}, u32[]{:S(2)}, u32[]{:S(2)}) collective-permute-start(bf16[2,144,1152]{2,1,0:T(8,128)(2,1)} %get-tuple-element.10), channel_id=1, source_target_pairs={{0,72},{24,48},{48,24},{72,0},{1,73},{25,49},{49,25},{73,1},{2,74}... | collective-permute-start | bytes 1990664 | tf_op jit(solution)/shard_map/ppermute | solution.py:52
  29.2 4.0 %collective-permute-start.8 = (bf16[2,144,1]{2,0,1:T(2,128)(2,1)S(1)}, bf16[2,144,1]{2,0,1:T(2,128)(2,1)S(1)}, u32[]{:S(2)}, u32[]{:S(2)}) collective-permute-start(bf16[2,144,1]{2,0,1:T(2,128)(2,1)S(1)} %get-tuple-element.46), channel_id=1, source_target_pairs={{0,1},{1,2},{2,3},{3,4},{4,5},{5,6},{6,7},{7,8},{8,9},{9,10},{10,1... | collective-permute-start | bytes 1736 | tf_op jit(solution)/shard_map/ppermute | solution.py:28
  33.2 12.8 %collective-permute-start.7 = (bf16[2,144,1]{2,0,1:T(2,128)(2,1)S(1)}, bf16[2,144,1]{2,0,1:T(2,128)(2,1)S(1)}, u32[]{:S(2)}, u32[]{:S(2)}) collective-permute-start(bf16[2,144,1]{2,0,1:T(2,128)(2,1)S(1)} %get-tuple-element.45), channel_id=1, source_target_pairs={{1,0},{2,1},{3,2},{4,3},{5,4},{6,5},{7,6},{8,7},{9,8},{10,9},{11,1... | collective-permute-start | bytes 1736 | tf_op jit(solution)/shard_map/ppermute | solution.py:29
  46.3 1.9 collective-permute-start.6
  48.2 2.4 collective-permute-start.5
  50.6 2.9 %collective-permute-start.1 = (bf16[2,144,1152]{2,1,0:T(8,128)(2,1)}, bf16[2,144,1152]{2,1,0:T(8,128)(2,1)S(1)}, u32[]{:S(2)}, u32[]{:S(2)}) collective-permute-start(bf16[2,144,1152]{2,1,0:T(8,128)(2,1)} %get-tuple-element.11), channel_id=1, source_target_pairs={{0,48},{24,72},{48,0},{72,24},{1,49},{25,73},{49,1},{73,25},{2,50}... | collective-permute-start | bytes 1990664 | tf_op jit(solution)/shard_map/ppermute | solution.py:52
  53.6 1.6 collective-permute-done.5
  55.1 2.5 collective-permute-start
  57.8 0.5 fusion.27
  58.4 0.9 broadcast_in_dim.8
  59.3 7.5 %all-to-all-start = ((bf16[8,144,256]{2,1,0:T(8,128)(2,1)}), bf16[8,144,256]{2,1,0:T(8,128)(2,1)S(1)}, u32[]{:S(2)}, u32[]{:S(2)}) async-start(bf16[8,144,256]{2,1,0:T(8,128)(2,1)} %broadcast_in_dim.8), calls=%async_computation | async-start | bytes 1179648 | tf_op jit(solution)/shard_map/all_to_all | solution.py:16
  66.8 0.9 collective-permute-done.1
  67.7 0.4 pad_maximum_fusion
  68.4 0.4 pad_maximum_fusion.1
  69.0 9.9 %all-to-all-done = bf16[8,144,256]{2,1,0:T(8,128)(2,1)S(1)} async-done(((bf16[8,144,256]{2,1,0:T(8,128)(2,1)}), bf16[8,144,256]{2,1,0:T(8,128)(2,1)S(1)}, u32[]{:S(2)}, u32[]{:S(2)}) %all-to-all-start) | async-done | bytes 589856 | tf_op jit(solution)/shard_map/all_to_all | solution.py:16
  78.9 0.6 convolution_convert_fusion.1
  79.5 10.7 %all_to_all.40 = bf16[4,144,256]{2,1,0:T(8,128)(2,1)S(1)} all-to-all(bf16[4,144,256]{2,1,0:T(8,128)(2,1)S(1)} %bitcast.115), channel_id=1, replica_groups=mesh['y'=8,'xl'=2,'c'=2,'xh'=2,'zh'=3,'zl'=4] {'xl','c'}, dimensions={0} | all-to-all | bytes 589824 | tf_op jit(solution)/shard_map/all_to_all | solution.py:20
  90.2 0.9 broadcast_in_dim.9
  91.1 4.2 %all-to-all-start.2 = ((bf16[8,288,128]{2,1,0:T(8,128)(2,1)}), bf16[8,288,128]{2,1,0:T(8,128)(2,1)}, u32[]{:S(2)}, u32[]{:S(2)}) async-start(bf16[8,288,128]{2,1,0:T(8,128)(2,1)} %broadcast_in_dim.9), calls=%async_computation.2 | async-start | bytes 1179648 | tf_op jit(solution)/shard_map/all_to_all | solution.py:16
  95.8 1.5 copy.37
  97.6 1.1 constant_dynamic-slice_fusion.3
  98.7 10.4 %collective-permute-start.4 = (bf16[2,128,1024]{1,2,0:T(8,128)(2,1)}, bf16[2,128,1024]{1,2,0:T(8,128)(2,1)S(1)}, u32[]{:S(2)}, u32[]{:S(2)}) collective-permute-start(bf16[2,128,1024]{1,2,0:T(8,128)(2,1)} %get-tuple-element.19), channel_id=1, source_target_pairs={{0,8},{4,0},{8,4},{1,9},{5,1},{9,5},{2,10},{6,2},{10,6},{3,11},{7,... | collective-permute-start | bytes 1572872 | tf_op jit(solution)/shard_map/ppermute | solution.py:65
  109.0 2.1 collective-permute-start.3
  111.2 15.7 %collective-permute-done.4 = bf16[2,128,1024]{1,2,0:T(8,128)(2,1)S(1)} collective-permute-done((bf16[2,128,1024]{1,2,0:T(8,128)(2,1)}, bf16[2,128,1024]{1,2,0:T(8,128)(2,1)S(1)}, u32[]{:S(2)}, u32[]{:S(2)}) %collective-permute-start.4) | collective-permute-done | bytes 524320 | tf_op jit(solution)/shard_map/ppermute | solution.py:65
  126.8 0.9 collective-permute-done.3
  128.3 15.6 %all-to-all-done.2 = bf16[8,288,128]{2,1,0:T(8,128)(2,1)} async-done(((bf16[8,288,128]{2,1,0:T(8,128)(2,1)}), bf16[8,288,128]{2,1,0:T(8,128)(2,1)}, u32[]{:S(2)}, u32[]{:S(2)}) %all-to-all-start.2) | async-done | bytes 589856 | tf_op jit(solution)/shard_map/all_to_all | solution.py:16
  143.9 2.2 fusion.8
  146.2 7.7 %all-to-all-start.3 = ((bf16[3,288,128]{2,1,0:T(8,128)(2,1)}), bf16[3,288,128]{2,1,0:T(8,128)(2,1)S(1)}, u32[]{:S(2)}, u32[]{:S(2)}) async-start(bf16[3,288,128]{2,1,0:T(8,128)(2,1)} %fusion.8), calls=%async_computation.3 | async-start | bytes 442368 | tf_op jit(solution)/shard_map/all_to_all | solution.py:20
  154.2 9.0 %all-to-all-done.3 = bf16[3,288,128]{2,1,0:T(8,128)(2,1)S(1)} async-done(((bf16[3,288,128]{2,1,0:T(8,128)(2,1)}), bf16[3,288,128]{2,1,0:T(8,128)(2,1)S(1)}, u32[]{:S(2)}, u32[]{:S(2)}) %all-to-all-start.3) | async-done | bytes 221216 | tf_op jit(solution)/shard_map/all_to_all | solution.py:20
  163.4 38.2 %all_to_all.41 = bf16[8,288,128]{2,1,0:T(8,128)(2,1)S(1)} all-to-all(bf16[8,288,128]{2,1,0:T(8,128)(2,1)S(1)} %broadcast_in_dim.10), channel_id=1, replica_groups=mesh['y'=8,'xl'=2,'c'=2,'xh'=2,'zh'=3,'zl'=4] {'xh','zl'}, dimensions={0} | all-to-all | bytes 1179648 | tf_op jit(solution)/shard_map/all_to_all | solution.py:16
  201.6 0.5 fusion.7
  202.1 11.4 %all_to_all.42 = bf16[3,288,128]{2,1,0:T(8,128)(2,1)S(1)} all-to-all(bf16[3,288,128]{2,1,0:T(8,128)(2,1)S(1)} %fusion.7), channel_id=1, replica_groups=mesh['y'=8,'xl'=2,'c'=2,'xh'=2,'zh'=3,'zl'=4] {'zh'}, dimensions={0} | all-to-all | bytes 442368 | tf_op jit(solution)/shard_map/all_to_all | solution.py:20
  213.6 16.9 %all_to_all.43 = bf16[8,144,256]{2,1,0:T(8,128)(2,1)S(1)} all-to-all(bf16[8,144,256]{2,1,0:T(8,128)(2,1)S(1)} %broadcast_in_dim.11), channel_id=1, replica_groups=mesh['y'=8,'xl'=2,'c'=2,'xh'=2,'zh'=3,'zl'=4] {'y'}, dimensions={0} | all-to-all | bytes 1179648 | tf_op jit(solution)/shard_map/all_to_all | solution.py:16
  230.5 0.5 convolution_convert_fusion
  231.1 15.6 %all_to_all.44 = bf16[4,144,256]{2,1,0:T(8,128)(2,1)S(1)} all-to-all(bf16[4,144,256]{2,1,0:T(8,128)(2,1)S(1)} %bitcast.116), channel_id=1, replica_groups=mesh['y'=8,'xl'=2,'c'=2,'xh'=2,'zh'=3,'zl'=4] {'xl','c'}, dimensions={0} | all-to-all | bytes 589824 | tf_op jit(solution)/shard_map/all_to_all | solution.py:20
  246.8 2.1 collective-permute-start.12
  248.9 10.1 %collective-permute-start.11 = (bf16[2,144,1]{2,1,0:T(8,128)(2,1)S(1)}, bf16[2,144,1]{2,1,0:T(8,128)(2,1)S(1)}, u32[]{:S(2)}, u32[]{:S(2)}) collective-permute-start(bf16[2,144,1]{2,1,0:T(8,128)(2,1)S(1)} %get-tuple-element.33), channel_id=1, source_target_pairs={{1,0},{2,1},{3,2},{4,3},{5,4},{6,5},{7,6},{8,7},{9,8},{10,9},{11,1... | collective-permute-start | bytes 1736 | tf_op jit(solution)/shard_map/ppermute | solution.py:29
  259.0 6.4 %collective-permute-start.10 = (bf16[2,1,128]{2,1,0:T(2,128)(2,1)S(1)}, bf16[2,1,128]{2,1,0:T(2,128)(2,1)S(1)}, u32[]{:S(2)}, u32[]{:S(2)}) collective-permute-start(bf16[2,1,128]{2,1,0:T(2,128)(2,1)S(1)} %get-tuple-element.36), channel_id=1, source_target_pairs={{0,24},{24,48},{48,72},{72,96},{96,120},{120,144},{144,168},{168,1... | collective-permute-start | bytes 1544 | tf_op jit(solution)/shard_map/ppermute | solution.py:28
  265.4 1.9 collective-permute-start.9
  267.4 5.0 %collective-permute-done.9 = bf16[2,1,128]{2,1,0:T(2,128)(2,1)S(1)} collective-permute-done((bf16[2,1,128]{2,1,0:T(2,128)(2,1)S(1)}, bf16[2,1,128]{2,1,0:T(2,128)(2,1)S(1)}, u32[]{:S(2)}, u32[]{:S(2)}) %collective-permute-start.9) | collective-permute-done | bytes 544 | tf_op jit(solution)/shard_map/ppermute | solution.py:29
  272.7 1.6 fusion.6
  (83 shorter events, 4.2 us)
Async XLA Ops:
  0.6 28.2 %copy-start = (bf16[16,2]{0,1:T(2,128)(2,1)S(1)}, bf16[16,2]{0,1:T(2,128)(2,1)}, u32[]{:S(2)}) copy-start(bf16[16,2]{0,1:T(2,128)(2,1)} %param.17) | copy-start | bytes 196
  12.4 1.7 copy-start.1
  24.1 4.4 %copy-start.4 = (s32[144,128]{1,0:T(8,128)S(1)}, s32[144,128]{1,0:T(8,128)}, u32[]{:S(2)}) copy-start(s32[144,128]{1,0:T(8,128)} %param.15) | copy-start | bytes 221188
  24.1 4.4 %copy-start.5 = (bf16[16,144,128]{2,1,0:T(8,128)(2,1)S(1)}, bf16[16,144,128]{2,1,0:T(8,128)(2,1)}, u32[]{:S(2)}) copy-start(bf16[16,144,128]{2,1,0:T(8,128)(2,1)} %param.13) | copy-start | bytes 1769476
  24.1 4.4 %copy-start.6 = (bf16[16,144,128]{2,1,0:T(8,128)(2,1)S(1)}, bf16[16,144,128]{2,1,0:T(8,128)(2,1)}, u32[]{:S(2)}) copy-start(bf16[16,144,128]{2,1,0:T(8,128)(2,1)} %param.14) | copy-start | bytes 1769476
  24.1 4.4 %copy-start.7 = (s32[144,128]{1,0:T(8,128)S(1)}, s32[144,128]{1,0:T(8,128)}, u32[]{:S(2)}) copy-start(s32[144,128]{1,0:T(8,128)} %param.16) | copy-start | bytes 221188
  25.5 41.4 %collective-permute-start.2 = (bf16[2,144,1152]{2,1,0:T(8,128)(2,1)}, bf16[2,144,1152]{2,1,0:T(8,128)(2,1)S(1)}, u32[]{:S(2)}, u32[]{:S(2)}) collective-permute-start(bf16[2,144,1152]{2,1,0:T(8,128)(2,1)} %get-tuple-element.10), channel_id=1, source_target_pairs={{0,72},{24,48},{48,24},{72,0},{1,73},{25,49},{49,25},{73,1},{2,74}... | collective-permute-start | bytes 1990664 | tf_op jit(solution)/shard_map/ppermute | solution.py:52
  29.2 28.4 %collective-permute-start.8 = (bf16[2,144,1]{2,0,1:T(2,128)(2,1)S(1)}, bf16[2,144,1]{2,0,1:T(2,128)(2,1)S(1)}, u32[]{:S(2)}, u32[]{:S(2)}) collective-permute-start(bf16[2,144,1]{2,0,1:T(2,128)(2,1)S(1)} %get-tuple-element.46), channel_id=1, source_target_pairs={{0,1},{1,2},{2,3},{3,4},{4,5},{5,6},{6,7},{7,8},{8,9},{9,10},{10,1... | collective-permute-start | bytes 1736 | tf_op jit(solution)/shard_map/ppermute | solution.py:28
  33.2 24.5 %collective-permute-start.7 = (bf16[2,144,1]{2,0,1:T(2,128)(2,1)S(1)}, bf16[2,144,1]{2,0,1:T(2,128)(2,1)S(1)}, u32[]{:S(2)}, u32[]{:S(2)}) collective-permute-start(bf16[2,144,1]{2,0,1:T(2,128)(2,1)S(1)} %get-tuple-element.45), channel_id=1, source_target_pairs={{1,0},{2,1},{3,2},{4,3},{5,4},{6,5},{7,6},{8,7},{9,8},{10,9},{11,1... | collective-permute-start | bytes 1736 | tf_op jit(solution)/shard_map/ppermute | solution.py:29
  46.3 4.4 %collective-permute-start.6 = (bf16[2,1,128]{2,0,1:T(2,128)(2,1)S(1)}, bf16[2,1,128]{2,0,1:T(2,128)(2,1)S(1)}, u32[]{:S(2)}, u32[]{:S(2)}) collective-permute-start(bf16[2,1,128]{2,0,1:T(2,128)(2,1)S(1)} %get-tuple-element.44), channel_id=1, source_target_pairs={{0,24},{24,48},{48,72},{72,96},{96,120},{120,144},{144,168},{168,1... | collective-permute-start | bytes 1544 | tf_op jit(solution)/shard_map/ppermute | solution.py:28
  48.2 7.0 %collective-permute-start.5 = (bf16[2,1,128]{2,0,1:T(2,128)(2,1)S(1)}, bf16[2,1,128]{2,0,1:T(2,128)(2,1)S(1)}, u32[]{:S(2)}, u32[]{:S(2)}) collective-permute-start(bf16[2,1,128]{2,0,1:T(2,128)(2,1)S(1)} %get-tuple-element.43), channel_id=1, source_target_pairs={{24,0},{48,24},{72,48},{96,72},{120,96},{144,120},{168,144},{192,1... | collective-permute-start | bytes 1544 | tf_op jit(solution)/shard_map/ppermute | solution.py:29
  50.6 17.1 %collective-permute-start.1 = (bf16[2,144,1152]{2,1,0:T(8,128)(2,1)}, bf16[2,144,1152]{2,1,0:T(8,128)(2,1)S(1)}, u32[]{:S(2)}, u32[]{:S(2)}) collective-permute-start(bf16[2,144,1152]{2,1,0:T(8,128)(2,1)} %get-tuple-element.11), channel_id=1, source_target_pairs={{0,48},{24,72},{48,0},{72,24},{1,49},{25,73},{49,1},{73,25},{2,50}... | collective-permute-start | bytes 1990664 | tf_op jit(solution)/shard_map/ppermute | solution.py:52
  55.1 12.6 %collective-permute-start = (bf16[2,144,1152]{2,1,0:T(8,128)(2,1)}, bf16[2,144,1152]{2,1,0:T(8,128)(2,1)S(1)}, u32[]{:S(2)}, u32[]{:S(2)}) collective-permute-start(bf16[2,144,1152]{2,1,0:T(8,128)(2,1)} %get-tuple-element.12), channel_id=1, source_target_pairs={{0,24},{24,0},{48,72},{72,48},{1,25},{25,1},{49,73},{73,49},{2,26}... | collective-permute-start | bytes 1990664 | tf_op jit(solution)/shard_map/ppermute | solution.py:52
  59.3 19.6 %all-to-all-start = ((bf16[8,144,256]{2,1,0:T(8,128)(2,1)}), bf16[8,144,256]{2,1,0:T(8,128)(2,1)S(1)}, u32[]{:S(2)}, u32[]{:S(2)}) async-start(bf16[8,144,256]{2,1,0:T(8,128)(2,1)} %broadcast_in_dim.8), calls=%async_computation | async-start | bytes 1179648 | tf_op jit(solution)/shard_map/all_to_all | solution.py:16
  79.5 15.9 %copy-start.3 = (bf16[128,3072]{1,0:T(8,128)(2,1)S(1)}, bf16[128,3072]{1,0:T(8,128)(2,1)}, u32[]{:S(2)}) copy-start(bf16[128,3072]{1,0:T(8,128)(2,1)} %param.22) | copy-start | bytes 2359300
  91.1 52.8 %all-to-all-start.2 = ((bf16[8,288,128]{2,1,0:T(8,128)(2,1)}), bf16[8,288,128]{2,1,0:T(8,128)(2,1)}, u32[]{:S(2)}, u32[]{:S(2)}) async-start(bf16[8,288,128]{2,1,0:T(8,128)(2,1)} %broadcast_in_dim.9), calls=%async_computation.2 | async-start | bytes 1179648 | tf_op jit(solution)/shard_map/all_to_all | solution.py:16
  98.7 28.2 %collective-permute-start.4 = (bf16[2,128,1024]{1,2,0:T(8,128)(2,1)}, bf16[2,128,1024]{1,2,0:T(8,128)(2,1)S(1)}, u32[]{:S(2)}, u32[]{:S(2)}) collective-permute-start(bf16[2,128,1024]{1,2,0:T(8,128)(2,1)} %get-tuple-element.19), channel_id=1, source_target_pairs={{0,8},{4,0},{8,4},{1,9},{5,1},{9,5},{2,10},{6,2},{10,6},{3,11},{7,... | collective-permute-start | bytes 1572872 | tf_op jit(solution)/shard_map/ppermute | solution.py:65
  109.0 18.7 %collective-permute-start.3 = (bf16[2,128,1024]{1,2,0:T(8,128)(2,1)}, bf16[2,128,1024]{1,2,0:T(8,128)(2,1)S(1)}, u32[]{:S(2)}, u32[]{:S(2)}) collective-permute-start(bf16[2,128,1024]{1,2,0:T(8,128)(2,1)} %get-tuple-element.20), channel_id=1, source_target_pairs={{0,4},{4,8},{8,0},{1,5},{5,9},{9,1},{2,6},{6,10},{10,2},{3,7},{7,1... | collective-permute-start | bytes 1572872 | tf_op jit(solution)/shard_map/ppermute | solution.py:65
  128.3 25.6 %copy-start.12 = (f32[2]{0:T(128)S(1)}, f32[2]{0:T(128)}, u32[]{:S(2)}) copy-start(f32[2]{0:T(128)} %param.25) | copy-start | bytes 28
  128.3 25.8 %copy-start.9 = (f32[144]{0:T(256)S(1)}, f32[144]{0:T(256)}, u32[]{:S(2)}) copy-start(f32[144]{0:T(256)} %param.23) | copy-start | bytes 1732
  128.3 25.7 %copy-start.11 = (f32[128]{0:T(128)S(1)}, f32[128]{0:T(128)}, u32[]{:S(2)}) copy-start(f32[128]{0:T(128)} %param.24) | copy-start | bytes 1540
  146.2 17.0 %all-to-all-start.3 = ((bf16[3,288,128]{2,1,0:T(8,128)(2,1)}), bf16[3,288,128]{2,1,0:T(8,128)(2,1)S(1)}, u32[]{:S(2)}, u32[]{:S(2)}) async-start(bf16[3,288,128]{2,1,0:T(8,128)(2,1)} %fusion.8), calls=%async_computation.3 | async-start | bytes 442368 | tf_op jit(solution)/shard_map/all_to_all | solution.py:20
  231.0 36.3 %copy-start.10 = (f32[16,2]{0,1:T(2,128)S(1)}, f32[16,2]{0,1:T(2,128)}, u32[]{:S(2)}) copy-start(f32[16,2]{0,1:T(2,128)} %param.18) | copy-start | bytes 388
  246.6 26.1 %copy-start.8 = (s32[144,128]{1,0:T(8,128)S(1)}, s32[144,128]{1,0:T(8,128)}, u32[]{:S(2)}) copy-start(s32[144,128]{1,0:T(8,128)} %param.16) | copy-start | bytes 221188
  246.7 27.6 %copy-start.2 = (f32[288,128]{1,0:T(8,128)}, f32[288,128]{1,0:T(8,128)S(1)}, u32[]{:S(2)}) copy-start(f32[288,128]{1,0:T(8,128)S(1)} %pad_maximum_fusion.12) | copy-start | bytes 442372
  246.8 25.6 %collective-permute-start.12 = (bf16[2,144,1]{2,1,0:T(8,128)(2,1)S(1)}, bf16[2,144,1]{2,1,0:T(8,128)(2,1)S(1)}, u32[]{:S(2)}, u32[]{:S(2)}) collective-permute-start(bf16[2,144,1]{2,1,0:T(8,128)(2,1)S(1)} %get-tuple-element.34), channel_id=1, source_target_pairs={{0,1},{1,2},{2,3},{3,4},{4,5},{5,6},{6,7},{7,8},{8,9},{9,10},{10,1... | collective-permute-start | bytes 1736 | tf_op jit(solution)/shard_map/ppermute | solution.py:28
  248.9 23.5 %collective-permute-start.11 = (bf16[2,144,1]{2,1,0:T(8,128)(2,1)S(1)}, bf16[2,144,1]{2,1,0:T(8,128)(2,1)S(1)}, u32[]{:S(2)}, u32[]{:S(2)}) collective-permute-start(bf16[2,144,1]{2,1,0:T(8,128)(2,1)S(1)} %get-tuple-element.33), channel_id=1, source_target_pairs={{1,0},{2,1},{3,2},{4,3},{5,4},{6,5},{7,6},{8,7},{9,8},{10,9},{11,1... | collective-permute-start | bytes 1736 | tf_op jit(solution)/shard_map/ppermute | solution.py:29
  259.0 8.3 %collective-permute-start.10 = (bf16[2,1,128]{2,1,0:T(2,128)(2,1)S(1)}, bf16[2,1,128]{2,1,0:T(2,128)(2,1)S(1)}, u32[]{:S(2)}, u32[]{:S(2)}) collective-permute-start(bf16[2,1,128]{2,1,0:T(2,128)(2,1)S(1)} %get-tuple-element.36), channel_id=1, source_target_pairs={{0,24},{24,48},{48,72},{72,96},{96,120},{120,144},{144,168},{168,1... | collective-permute-start | bytes 1544 | tf_op jit(solution)/shard_map/ppermute | solution.py:28
  265.4 7.0 %collective-permute-start.9 = (bf16[2,1,128]{2,1,0:T(2,128)(2,1)S(1)}, bf16[2,1,128]{2,1,0:T(2,128)(2,1)S(1)}, u32[]{:S(2)}, u32[]{:S(2)}) collective-permute-start(bf16[2,1,128]{2,1,0:T(2,128)(2,1)S(1)} %get-tuple-element.35), channel_id=1, source_target_pairs={{24,0},{48,24},{72,48},{96,72},{120,96},{144,120},{168,144},{192,1... | collective-permute-start | bytes 1544 | tf_op jit(solution)/shard_map/ppermute | solution.py:29

commit v2 on v1

--- a/solution.py
+++ b/solution.py
@@ -1,10 +1,14 @@
+import functools
+
 import jax
 import jax.numpy as jnp
 from jax import lax
+from jax.experimental import pallas as pl
+from jax.experimental.pallas import tpu as pltpu
 from jax.sharding import Mesh
 from jax.sharding import PartitionSpec as P
 
-SUB = (("y", 8), ("xl", 2), ("c", 2), ("xh", 2), ("zh", 3), ("zl", 4))
+SUB = (("y", 8), ("xl", 2), ("c", 2), ("xh", 2), ("zh", 4), ("zl", 3))
 GX = ("y", "xl", "c")
 GY = ("xh", "zh", "zl")
 QUAD = ("xl", "c")
@@ -42,42 +46,107 @@
     return 0.5 * (padded[:, :, 2:] - padded[:, :, :-2])
 
 
-def quad_tables(fx, ix):
-    me = lax.axis_index("xl") * 2 + lax.axis_index("c")
-    both = jnp.stack([fx, ix]).reshape(2, 144, 8, 4, 144)
-    both = jnp.moveaxis(both, 3, 0).reshape(4, 2, 144, 1152)
-    pieces = [lax.dynamic_index_in_dim(both, me, 0, False)]
-    for step in (1, 2, 3):
-        send = lax.dynamic_index_in_dim(both, me ^ step, 0, False)
-        pieces.append(lax.ppermute(send, QUAD, [(i, i ^ step) for i in range(4)]))
-    held = jnp.stack(pieces)
-    ordered = jnp.stack([lax.dynamic_index_in_dim(held, me ^ i, 0, False) for i in range(4)])
-    return ordered[:, 0].reshape(576, 1152), ordered[:, 1].reshape(576, 1152)
-
-
-def ring_tables(fy, iy):
-    me = lax.axis_index("zh")
-    both = jnp.stack([fy, iy]).reshape(2, 128, 2, 3, 512)
-    both = jnp.moveaxis(both, 3, 0).reshape(3, 2, 128, 1024)
-    pieces = [lax.dynamic_index_in_dim(both, me, 0, False)]
-    for step in (1, 2):
-        send = lax.dynamic_index_in_dim(both, (me + step) % 3, 0, False)
-        pieces.append(lax.ppermute(send, "zh", [(i, (i + step) % 3) for i in range(3)]))
-    held = jnp.stack(pieces)
-    ordered = jnp.stack([lax.dynamic_index_in_dim(held, (me + 3 - i) % 3, 0, False) for i in range(3)])
-    return ordered[:, 0], ordered[:, 1]
-
-
-def transform_x(block, table):
-    held = gather(block, "y", 8).reshape(1152, 256)
-    parts = jnp.dot(table, held, preferred_element_type=F32).astype(BF)
-    return scatter_sum(parts.reshape(4, 144, 256), QUAD)
-
-
-def transform_y(block, table):
-    held = gather(block, ("xh", "zl"), 8)
-    parts = jnp.einsum("bkj,tqbj->tkq", held, table.reshape(3, 128, 8, 128), preferred_element_type=F32)
-    return scatter_sum(parts.astype(BF), "zh")
+def call(kernel, out_shape, operands, scratch=(), flops=0):
+    smem, vmem = pl.BlockSpec(memory_space=pltpu.SMEM), pl.BlockSpec(memory_space=pltpu.VMEM)
+    outs = out_shape if isinstance(out_shape, list) else [out_shape]
+    moved = sum(x.size * x.dtype.itemsize for x in list(operands[1:]) + outs)
+    return pl.pallas_call(
+        kernel,
+        out_shape=out_shape,
+        in_specs=[smem] + [vmem] * (len(operands) - 1),
+        out_specs=[vmem] * len(outs) if isinstance(out_shape, list) else vmem,
+        scratch_shapes=list(scratch),
+        cost_estimate=pl.CostEstimate(flops=flops, bytes_accessed=moved, transcendentals=0),
+        compiler_params=pltpu.CompilerParams(vmem_limit_bytes=24 << 20),
+    )(*operands)
+
+
+def window(place, half):
+    return 9 * (place // 2) + 4 * (place % 2) + half
+
+
+def quad_cut_kernel(me_ref, rows_ref, *out_refs):
+    me = me_ref[0]
+    for step, out_ref in enumerate(out_refs):
+        other = lax.bitwise_xor(me, step)
+        for y in range(8):
+            start = pl.multiple_of((window(y, 0) + other) * 128, 128)
+            out_ref[:, y * 256 : (y + 1) * 256] = rows_ref[:, pl.ds(start, 256)]
+
+
+def quad_cut(me, rows):
+    return call(quad_cut_kernel, [jax.ShapeDtypeStruct((144, 2048), BF)] * 4, (me, rows))
+
+
+def quad_send(piece, step):
+    return lax.ppermute(piece, QUAD, [(i, i ^ step) for i in range(4)])
+
+
+def ring_cut_kernel(me_ref, first_ref, second_ref, *out_refs):
+    me = me_ref[0]
+    for step, out_ref in enumerate(out_refs):
+        other = lax.rem(me + step, 3)
+        for g in range(8):
+            start = pl.multiple_of((3 * g + other) * 128, 128)
+            out_ref[:128, g * 128 : (g + 1) * 128] = first_ref[:, pl.ds(start, 128)]
+            out_ref[128:, g * 128 : (g + 1) * 128] = second_ref[:, pl.ds(start, 128)]
+
+
+def ring_tables(me, first, second):
+    pieces = call(ring_cut_kernel, [jax.ShapeDtypeStruct((256, 1024), BF)] * 3, (me, first, second))
+    moved = [
+        lax.ppermute(pieces[step], "zl", [(i, (i + step) % 3) for i in range(3)]) for step in (1, 2)
+    ]
+    return [pieces[0]] + moved
+
+
+def x_kernel(me_ref, held_ref, t0, t1, t2, t3, out_ref, placed):
+    me = me_ref[0]
+    placed[...] = jnp.zeros_like(placed)
+    for y in range(8):
+        start = pl.multiple_of(256 * y + 64 * (y % 2) + 16 * me, 16)
+        placed[pl.ds(start, 144), :] = held_ref[y]
+    for step, table in enumerate((t0, t1, t2, t3)):
+        part = jnp.dot(table[...], placed[...], preferred_element_type=F32)
+        out_ref[lax.bitwise_xor(me, step)] = part.astype(BF)
+
+
+def transform_x(me, block, table):
+    held = gather(block, "y", 8)
+    parts = call(
+        x_kernel,
+        jax.ShapeDtypeStruct((4, 144, 256), BF),
+        (me, held, *table),
+        [pltpu.VMEM((2048, 256), BF)],
+        flops=2 * 576 * 2048 * 256,
+    )
+    return scatter_sum(parts, QUAD)
+
+
+def y_kernel(offset, me_ref, held_ref, t0, t1, t2, out_ref, placed):
+    me = me_ref[0]
+    for g in range(8):
+        placed[:, g * 128 : (g + 1) * 128] = held_ref[g]
+    for step, table in enumerate((t0, t1, t2)):
+        part = lax.dot_general(
+            placed[...],
+            table[offset : offset + 128, :],
+            (((1,), (1,)), ((), ())),
+            preferred_element_type=F32,
+        )
+        out_ref[lax.rem(me + 3 - step, 3)] = part.astype(BF)
+
+
+def transform_y(me, block, table, offset):
+    held = gather(block, ("xh", "zh"), 8)
+    parts = call(
+        functools.partial(y_kernel, offset),
+        jax.ShapeDtypeStruct((3, 288, 128), BF),
+        (me, held, *table),
+        [pltpu.VMEM((288, 1024), BF)],
+        flops=2 * 288 * 1024 * 384,
+    )
+    return scatter_sum(parts, "zl")
 
 
 def to_x(block):
@@ -112,14 +181,22 @@
     flux_v = flux_v.astype(BF).astype(F32)
     mask_f = sea_mask.astype(F32)
     divergence = (mask_f[None] * (centre_x(flux_u) + centre_y(flux_v))).astype(BF)
-    table_fx, table_ix = quad_tables(forward_x, inverse_x)
-    table_fy, table_iy = ring_tables(forward_y, inverse_y)
-    spec_x = transform_x(to_x(divergence.reshape(288, 128)), table_fx).astype(BF)
-    spec_xy = transform_y(to_y(spec_x), table_fy).reshape(2, 144, 128)
+    quad_me = (lax.axis_index("xl") * 2 + lax.axis_index("c")).astype(jnp.int32).reshape(1)
+    ring_me = lax.axis_index("zl").astype(jnp.int32).reshape(1)
+    cut_fx = quad_cut(quad_me, forward_x)
+    divergence, fx_two = lax.optimization_barrier((divergence, quad_send(cut_fx[2], 2)))
+    table_fx = (cut_fx[0], quad_send(cut_fx[1], 1), fx_two, quad_send(cut_fx[3], 3))
+    table_y = ring_tables(ring_me, forward_y, inverse_y)
+    spec_x = transform_x(quad_me, to_x(divergence.reshape(288, 128)), table_fx).astype(BF)
+    spec_x, table_y = lax.optimization_barrier((spec_x, table_y))
+    spec_xy = transform_y(ring_me, to_y(spec_x), table_y, 0).reshape(2, 144, 128)
     denom = eigen_x[None, :, None] + eigen_y[None, None, :] + mode_shift[:, None, None]
     scaled = (spec_xy / denom).astype(BF)
-    back_y = transform_y(scaled.reshape(288, 128), table_iy).astype(BF)
-    pressure = to_y(transform_x(to_x(back_y), table_ix)).reshape(2, 144, 128)
+    back_y = transform_y(ring_me, scaled.reshape(288, 128), table_y, 128).astype(BF)
+    cut_ix = quad_cut(quad_me, inverse_x)
+    back_y, ix_two = lax.optimization_barrier((back_y, quad_send(cut_ix[2], 2)))
+    table_ix = (cut_ix[0], quad_send(cut_ix[1], 1), ix_two, quad_send(cut_ix[3], 3))
+    pressure = to_y(transform_x(quad_me, to_x(back_y), table_ix)).reshape(2, 144, 128)
     grad_x = centre_x(pressure)
     grad_y = centre_y(pressure)
     wet_f = wet_int.astype(F32)

time: 275 us -> 225 us (0.82)
  the two profiles are of different devices: /device:TPU:63 before, /device:TPU:1 now
where the time goes in v2:
time: 225 us; the launch traced here: 222 us
  blocking collectives  80.4 us (36%)
  starting transfers between devices  76.8 us (34%)
  waiting for transfers between devices  41.4 us (18%)
  Pallas kernels  7.9 us (4%)
  local copies, waits for them, and re-layouts  6.72 us (3%)
  other arithmetic  6.25 us (3%)
    all_to_all x1, blocking collectives, gather(): lax.all_to_all(jnp.broadcast_to(block[None], (count,) + block.shape), axe...  40.5 us
    all_to_all x3, blocking collectives, scatter_sum(): return jnp.sum(lax.all_to_all(parts, axes, 0, 0).astype(F32), axis=0)  39.9 us
    ppermute x6, waiting for transfers between devices, quad_send(): return lax.ppermute(piece, QUAD, [(i, i ^ step) for i in range(4)])  22.3 us
    ppermute x6, starting transfers between devices, quad_send(): return lax.ppermute(piece, QUAD, [(i, i ^ step) for i in range(4)])  18.9 us
    ppermute x4, starting transfers between devices, edges(): high = lax.ppermute(lax.slice_in_dim(block, 0, 1, axis=dim), axes, backward)  15.9 us
    ppermute x4, starting transfers between devices, edges(): lax.ppermute(lax.slice_in_dim(block, block.shape[dim] - 1, None, axis=dim...  15.5 us
    all_to_all x3, starting transfers between devices, gather(): lax.all_to_all(jnp.broadcast_to(block[None], (count,) + block.shape), axe...  14.5 us
    pallas_call x7, Pallas kernels, call(): pl.pallas_call(kernel, out_shape=out_shape, in_specs=[smem] + [vmem] * (l...  7.9 us
  transfers between devices with their start and end apart: 20, of which 7 were waited for; matrix products, arithmetic and copies ran while one was open for 1% of the time, Pallas kernels for 3%

profile of v2, /device:TPU:1, one launch (start us, length us, event | category | flops | bytes accessed | tf_op | source)
XLA Modules:
  0.0 222.3 jit_solution(17525518936846165302)
XLA Ops:
  0.7 2.5 %fusion.8 = (bf16[16,144,128]{2,1,0:T(8,128)(2,1)}, bf16[16,144,128]{2,1,0:T(8,128)(2,1)S(1)}) fusion(bf16[16,144,128]{2,1,0:T(8,128)(2,1)} %param.13, s32[144,128]{1,0:T(8,128)} %param.15, s32[144,128]{1,0:T(8,128)} %param.16, bf16[16,144,128]{2,1,0:T(8,128)(2,1)} %param.14), kind=kLoop, calls=%fused_computation.13 | loop fusion | flops 2949120 | bytes 2506752 | tf_op jit(solution)/shard_map/mul | solution.py:178
  3.4 0.8 fusion.31
  4.2 1.3 collective-permute-start.2
  5.5 5.5 %collective-permute-start.3 = (bf16[2,144,1]{2,0,1:T(2,128)(2,1)}, bf16[2,144,1]{2,0,1:T(2,128)(2,1)S(1)}, u32[]{:S(2)}, u32[]{:S(2)}) collective-permute-start(bf16[2,144,1]{2,0,1:T(2,128)(2,1)} %get-tuple-element.66), channel_id=1, source_target_pairs={{0,1},{1,2},{2,3},{3,4},{4,5},{5,6},{6,7},{7,8},{8,9},{9,10},{10,1... | collective-permute-start | bytes 1736 | tf_op jit(solution)/shard_map/ppermute | solution.py:32
  11.3 3.1 %collective-permute-start.4 = (bf16[144,2048]{1,0:T(8,128)(2,1)S(1)}, bf16[144,2048]{1,0:T(8,128)(2,1)S(1)}, u32[]{:S(2)}, u32[]{:S(2)}) collective-permute-start(bf16[144,2048]{1,0:T(8,128)(2,1)S(1)} %get-tuple-element.22), channel_id=1, source_target_pairs={{0,48},{24,72},{48,0},{72,24},{1,49},{25,73},{49,1},{73,25},{2,50}... | collective-permute-start | bytes 1769480 | tf_op jit(solution)/shard_map/ppermute | solution.py:82
  14.4 1.3 fusion.33
  15.7 10.3 %collective-permute-start = (bf16[2,1,128]{2,0,1:T(2,128)(2,1)S(1)}, bf16[2,1,128]{2,0,1:T(2,128)(2,1)S(1)}, u32[]{:S(2)}, u32[]{:S(2)}) collective-permute-start(bf16[2,1,128]{2,0,1:T(2,128)(2,1)S(1)} %get-tuple-element.63), channel_id=1, source_target_pairs={{24,0},{48,24},{72,48},{96,72},{120,96},{144,120},{168,144},{192,1... | collective-permute-start | bytes 1544 | tf_op jit(solution)/shard_map/ppermute | solution.py:33
  26.1 3.5 %collective-permute-start.1 = (bf16[2,1,128]{2,0,1:T(2,128)(2,1)S(1)}, bf16[2,1,128]{2,0,1:T(2,128)(2,1)S(1)}, u32[]{:S(2)}, u32[]{:S(2)}) collective-permute-start(bf16[2,1,128]{2,0,1:T(2,128)(2,1)S(1)} %get-tuple-element.64), channel_id=1, source_target_pairs={{0,24},{24,48},{48,72},{72,96},{96,120},{120,144},{144,168},{168,1... | collective-permute-start | bytes 1544 | tf_op jit(solution)/shard_map/ppermute | solution.py:32
  29.6 4.2 %collective-permute-done = bf16[2,1,128]{2,0,1:T(2,128)(2,1)S(1)} collective-permute-done((bf16[2,1,128]{2,0,1:T(2,128)(2,1)S(1)}, bf16[2,1,128]{2,0,1:T(2,128)(2,1)S(1)}, u32[]{:S(2)}, u32[]{:S(2)}) %collective-permute-start) | collective-permute-done | bytes 544 | tf_op jit(solution)/shard_map/ppermute | solution.py:33
  33.9 0.9 convert_element_type.94
  35.6 0.9 broadcast_in_dim.8
  36.5 3.5 %all-to-all-start = ((bf16[8,144,256]{2,1,0:T(8,128)(2,1)}), bf16[8,144,256]{2,1,0:T(8,128)(2,1)S(1)}, u32[]{:S(2)}, u32[]{:S(2)}) async-start(bf16[8,144,256]{2,1,0:T(8,128)(2,1)} %broadcast_in_dim.8), calls=%async_computation | async-start | bytes 1179648 | tf_op jit(solution)/shard_map/all_to_all | solution.py:20
  40.0 1.9 collective-permute-start.5
  42.0 1.9 collective-permute-start.6
  43.9 1.3 shard_map.150
  45.2 2.2 collective-permute-start.7
  47.4 4.0 %collective-permute-start.8 = (bf16[256,1024]{1,0:T(8,128)(2,1)}, bf16[256,1024]{1,0:T(8,128)(2,1)S(1)}, u32[]{:S(2)}, u32[]{:S(2)}) collective-permute-start(bf16[256,1024]{1,0:T(8,128)(2,1)} %get-tuple-element.30), channel_id=1, source_target_pairs={{0,2},{1,0},{2,1},{3,5},{4,3},{5,4},{6,8},{7,6},{8,7},{9,11},{10,9... | collective-permute-start | bytes 1572872 | tf_op jit(solution)/shard_map/ppermute | solution.py:98
  51.4 8.4 %collective-permute-done.6.t3 = bf16[144,2048]{1,0:T(8,128)(2,1)} collective-permute-done((bf16[144,2048]{1,0:T(8,128)(2,1)}, bf16[144,2048]{1,0:T(8,128)(2,1)}, u32[]{:S(2)}, u32[]{:S(2)}) %collective-permute-start.6) | collective-permute-done | bytes 589856 | tf_op jit(solution)/shard_map/ppermute | solution.py:82
  59.8 1.1 copy-done.6
  60.9 2.1 shard_map.149
  63.0 8.6 %all_to_all.40 = bf16[4,144,256]{2,1,0:T(8,128)(2,1)S(1)} all-to-all(bf16[4,144,256]{2,1,0:T(8,128)(2,1)S(1)} %shard_map.149), channel_id=1, replica_groups=mesh['y'=8,'xl'=2,'c'=2,'xh'=2,'zh'=4,'zl'=3] {'xl','c'}, dimensions={0} | all-to-all | bytes 589824 | tf_op jit(solution)/shard_map/all_to_all | solution.py:24
  71.7 1.6 collective-permute-done.8.t2
  73.4 40.5 %all_to_all.41.held_ref = bf16[8,288,128]{2,1,0:T(8,128)(2,1)S(1)} all-to-all(bf16[8,288,128]{2,1,0:T(8,128)(2,1)S(1)} %broadcast_in_dim.9), channel_id=1, replica_groups=mesh['y'=8,'xl'=2,'c'=2,'xh'=2,'zh'=4,'zl'=3] {'xh','zh'}, dimensions={0} | all-to-all | bytes 1179648 | tf_op jit(solution)/shard_map/all_to_all | solution.py:20
  113.9 1.4 shard_map.151
  115.2 5.8 %all-to-all-start.3 = ((bf16[3,288,128]{2,1,0:T(8,128)(2,1)}), bf16[3,288,128]{2,1,0:T(8,128)(2,1)S(1)}, u32[]{:S(2)}, u32[]{:S(2)}) async-start(bf16[3,288,128]{2,1,0:T(8,128)(2,1)} %shard_map.151), calls=%async_computation.3 | async-start | bytes 442368 | tf_op jit(solution)/shard_map/all_to_all | solution.py:24
  121.3 4.0 %all-to-all-done.3 = bf16[3,288,128]{2,1,0:T(8,128)(2,1)S(1)} async-done(((bf16[3,288,128]{2,1,0:T(8,128)(2,1)}), bf16[3,288,128]{2,1,0:T(8,128)(2,1)S(1)}, u32[]{:S(2)}, u32[]{:S(2)}) %all-to-all-start.3) | async-done | bytes 221216 | tf_op jit(solution)/shard_map/all_to_all | solution.py:24
  125.5 0.9 broadcast_in_dim.10
  126.4 4.8 %all-to-all-start.4 = ((bf16[8,288,128]{2,1,0:T(8,128)(2,1)}), bf16[8,288,128]{2,1,0:T(8,128)(2,1)S(1)}, u32[]{:S(2)}, u32[]{:S(2)}) async-start(bf16[8,288,128]{2,1,0:T(8,128)(2,1)} %broadcast_in_dim.10), calls=%async_computation.4 | async-start | bytes 1179648 | tf_op jit(solution)/shard_map/all_to_all | solution.py:20
  131.2 1.3 shard_map.153
  132.5 0.8 copy-done.7
  133.3 0.8 copy-done.11
  134.1 3.5 %collective-permute-start.9 = (bf16[144,2048]{1,0:T(8,128)(2,1)}, bf16[144,2048]{1,0:T(8,128)(2,1)S(1)}, u32[]{:S(2)}, u32[]{:S(2)}) collective-permute-start(bf16[144,2048]{1,0:T(8,128)(2,1)} %get-tuple-element.35), channel_id=1, source_target_pairs={{0,48},{24,72},{48,0},{72,24},{1,49},{25,73},{49,1},{73,25},{2,50}... | collective-permute-start | bytes 1769480 | tf_op jit(solution)/shard_map/ppermute | solution.py:82
  137.6 7.2 %all-to-all-done.4.held_ref = bf16[8,288,128]{2,1,0:T(8,128)(2,1)S(1)} async-done(((bf16[8,288,128]{2,1,0:T(8,128)(2,1)}), bf16[8,288,128]{2,1,0:T(8,128)(2,1)S(1)}, u32[]{:S(2)}, u32[]{:S(2)}) %all-to-all-start.4) | async-done | bytes 589856 | tf_op jit(solution)/shard_map/all_to_all | solution.py:20
  144.9 0.7 shard_map.152
  145.5 22.7 %all_to_all.42 = bf16[3,288,128]{2,1,0:T(8,128)(2,1)S(1)} all-to-all(bf16[3,288,128]{2,1,0:T(8,128)(2,1)S(1)} %shard_map.152), channel_id=1, replica_groups=mesh['y'=8,'xl'=2,'c'=2,'xh'=2,'zh'=4,'zl'=3] {'zl'}, dimensions={0} | all-to-all | bytes 442368 | tf_op jit(solution)/shard_map/all_to_all | solution.py:24
  168.3 0.9 broadcast_in_dim.11
  169.1 6.2 %all-to-all-start.6 = ((bf16[8,144,256]{2,1,0:T(8,128)(2,1)}), bf16[8,144,256]{2,1,0:T(8,128)(2,1)S(1)}, u32[]{:S(2)}, u32[]{:S(2)}) async-start(bf16[8,144,256]{2,1,0:T(8,128)(2,1)} %broadcast_in_dim.11), calls=%async_computation.6 | async-start | bytes 1179648 | tf_op jit(solution)/shard_map/all_to_all | solution.py:20
  175.3 5.1 %collective-permute-start.10 = (bf16[144,2048]{1,0:T(8,128)(2,1)}, bf16[144,2048]{1,0:T(8,128)(2,1)S(1)}, u32[]{:S(2)}, u32[]{:S(2)}) collective-permute-start(bf16[144,2048]{1,0:T(8,128)(2,1)} %get-tuple-element.38), channel_id=1, source_target_pairs={{0,24},{24,0},{48,72},{72,48},{1,25},{25,1},{49,73},{73,49},{2,26}... | collective-permute-start | bytes 1769480 | tf_op jit(solution)/shard_map/ppermute | solution.py:82
  180.4 3.4 %collective-permute-start.11 = (bf16[144,2048]{1,0:T(8,128)(2,1)}, bf16[144,2048]{1,0:T(8,128)(2,1)S(1)}, u32[]{:S(2)}, u32[]{:S(2)}) collective-permute-start(bf16[144,2048]{1,0:T(8,128)(2,1)} %copy-done.11), channel_id=1, source_target_pairs={{0,72},{24,48},{48,24},{72,0},{1,73},{25,49},{49,25},{73,1},{2,74}... | collective-permute-start | bytes 1769480 | tf_op jit(solution)/shard_map/ppermute | solution.py:82
  183.8 13.9 %collective-permute-done.11.t3 = bf16[144,2048]{1,0:T(8,128)(2,1)S(1)} collective-permute-done((bf16[144,2048]{1,0:T(8,128)(2,1)}, bf16[144,2048]{1,0:T(8,128)(2,1)S(1)}, u32[]{:S(2)}, u32[]{:S(2)}) %collective-permute-start.11) | collective-permute-done | bytes 589856 | tf_op jit(solution)/shard_map/ppermute | solution.py:82
  197.7 0.9 shard_map.154
  198.6 8.6 %all_to_all.43 = bf16[4,144,256]{2,1,0:T(8,128)(2,1)S(1)} all-to-all(bf16[4,144,256]{2,1,0:T(8,128)(2,1)S(1)} %shard_map.154), channel_id=1, replica_groups=mesh['y'=8,'xl'=2,'c'=2,'xh'=2,'zh'=4,'zl'=3] {'xl','c'}, dimensions={0} | all-to-all | bytes 589824 | tf_op jit(solution)/shard_map/all_to_all | solution.py:24
  207.5 1.3 collective-permute-start.14
  208.8 4.0 %collective-permute-start.15 = (bf16[2,144,1]{2,1,0:T(8,128)(2,1)S(1)}, bf16[2,144,1]{2,1,0:T(8,128)(2,1)S(1)}, u32[]{:S(2)}, u32[]{:S(2)}) collective-permute-start(bf16[2,144,1]{2,1,0:T(8,128)(2,1)S(1)} %get-tuple-element.54), channel_id=1, source_target_pairs={{0,1},{1,2},{2,3},{3,4},{4,5},{5,6},{6,7},{7,8},{8,9},{9,10},{10,1... | collective-permute-start | bytes 1736 | tf_op jit(solution)/shard_map/ppermute | solution.py:32
  212.8 3.0 %collective-permute-start.12 = (bf16[2,1,128]{2,1,0:T(2,128)(2,1)S(1)}, bf16[2,1,128]{2,1,0:T(2,128)(2,1)S(1)}, u32[]{:S(2)}, u32[]{:S(2)}) collective-permute-start(bf16[2,1,128]{2,1,0:T(2,128)(2,1)S(1)} %get-tuple-element.55), channel_id=1, source_target_pairs={{24,0},{48,24},{72,48},{96,72},{120,96},{144,120},{168,144},{192,1... | collective-permute-start | bytes 1544 | tf_op jit(solution)/shard_map/ppermute | solution.py:33
  215.9 2.5 %collective-permute-start.13 = (bf16[2,1,128]{2,1,0:T(2,128)(2,1)S(1)}, bf16[2,1,128]{2,1,0:T(2,128)(2,1)S(1)}, u32[]{:S(2)}, u32[]{:S(2)}) collective-permute-start(bf16[2,1,128]{2,1,0:T(2,128)(2,1)S(1)} %get-tuple-element.56), channel_id=1, source_target_pairs={{0,24},{24,48},{48,72},{72,96},{96,120},{120,144},{144,168},{168,1... | collective-permute-start | bytes 1544 | tf_op jit(solution)/shard_map/ppermute | solution.py:32
  218.4 2.0 collective-permute-done.13
  220.7 1.6 fusion.4
  (87 shorter events, 2.3 us)
Async XLA Ops:
  0.6 2.6 %copy-start = (bf16[16,2]{0,1:T(2,128)(2,1)S(1)}, bf16[16,2]{0,1:T(2,128)(2,1)}, u32[]{:S(2)}) copy-start(bf16[16,2]{0,1:T(2,128)(2,1)} %param.17) | copy-start | bytes 196
  0.6 10.4 %copy-start.1 = (bf16[144,4608]{1,0:T(8,128)(2,1)S(1)}, bf16[144,4608]{1,0:T(8,128)(2,1)}, u32[]{:S(2)}) copy-start(bf16[144,4608]{1,0:T(8,128)(2,1)} %rows_ref.2) | copy-start | bytes 3981316
  3.4 26.2 %copy-start.13 = (s32[144,128]{1,0:T(8,128)S(1)}, s32[144,128]{1,0:T(8,128)}, u32[]{:S(2)}) copy-start(s32[144,128]{1,0:T(8,128)} %param.15) | copy-start | bytes 221188
  4.2 29.6 %collective-permute-start.2 = (bf16[2,144,1]{2,0,1:T(2,128)(2,1)}, bf16[2,144,1]{2,0,1:T(2,128)(2,1)}, u32[]{:S(2)}, u32[]{:S(2)}) collective-permute-start(bf16[2,144,1]{2,0,1:T(2,128)(2,1)} %get-tuple-element.65), channel_id=1, source_target_pairs={{1,0},{2,1},{3,2},{4,3},{5,4},{6,5},{7,6},{8,7},{9,8},{10,9},{11,1... | collective-permute-start | bytes 1736 | tf_op jit(solution)/shard_map/ppermute | solution.py:33
  5.5 29.3 %collective-permute-start.3 = (bf16[2,144,1]{2,0,1:T(2,128)(2,1)}, bf16[2,144,1]{2,0,1:T(2,128)(2,1)S(1)}, u32[]{:S(2)}, u32[]{:S(2)}) collective-permute-start(bf16[2,144,1]{2,0,1:T(2,128)(2,1)} %get-tuple-element.66), channel_id=1, source_target_pairs={{0,1},{1,2},{2,3},{3,4},{4,5},{5,6},{6,7},{7,8},{8,9},{9,10},{10,1... | collective-permute-start | bytes 1736 | tf_op jit(solution)/shard_map/ppermute | solution.py:32
  11.3 24.2 %copy-start.9 = (bf16[144,2048]{1,0:T(8,128)(2,1)}, bf16[144,2048]{1,0:T(8,128)(2,1)S(1)}, u32[]{:S(2)}) copy-start(bf16[144,2048]{1,0:T(8,128)(2,1)S(1)} %get-tuple-element.27) | copy-start | bytes 1769476
  11.3 24.2 %copy-start.10 = (bf16[144,2048]{1,0:T(8,128)(2,1)}, bf16[144,2048]{1,0:T(8,128)(2,1)S(1)}, u32[]{:S(2)}) copy-start(bf16[144,2048]{1,0:T(8,128)(2,1)S(1)} %get-tuple-element.25) | copy-start | bytes 1769476
  11.3 24.1 %collective-permute-start.4 = (bf16[144,2048]{1,0:T(8,128)(2,1)S(1)}, bf16[144,2048]{1,0:T(8,128)(2,1)S(1)}, u32[]{:S(2)}, u32[]{:S(2)}) collective-permute-start(bf16[144,2048]{1,0:T(8,128)(2,1)S(1)} %get-tuple-element.22), channel_id=1, source_target_pairs={{0,48},{24,72},{48,0},{72,24},{1,49},{25,73},{49,1},{73,25},{2,50}... | collective-permute-start | bytes 1769480 | tf_op jit(solution)/shard_map/ppermute | solution.py:82
  15.7 18.1 %collective-permute-start = (bf16[2,1,128]{2,0,1:T(2,128)(2,1)S(1)}, bf16[2,1,128]{2,0,1:T(2,128)(2,1)S(1)}, u32[]{:S(2)}, u32[]{:S(2)}) collective-permute-start(bf16[2,1,128]{2,0,1:T(2,128)(2,1)S(1)} %get-tuple-element.63), channel_id=1, source_target_pairs={{24,0},{48,24},{72,48},{96,72},{120,96},{144,120},{168,144},{192,1... | collective-permute-start | bytes 1544 | tf_op jit(solution)/shard_map/ppermute | solution.py:33
  26.1 7.8 %collective-permute-start.1 = (bf16[2,1,128]{2,0,1:T(2,128)(2,1)S(1)}, bf16[2,1,128]{2,0,1:T(2,128)(2,1)S(1)}, u32[]{:S(2)}, u32[]{:S(2)}) collective-permute-start(bf16[2,1,128]{2,0,1:T(2,128)(2,1)S(1)} %get-tuple-element.64), channel_id=1, source_target_pairs={{0,24},{24,48},{48,72},{72,96},{96,120},{120,144},{144,168},{168,1... | collective-permute-start | bytes 1544 | tf_op jit(solution)/shard_map/ppermute | solution.py:32
  35.5 1.0 copy-start.5
  35.6 8.3 %copy-start.3 = (bf16[128,3072]{1,0:T(8,128)(2,1)S(1)}, bf16[128,3072]{1,0:T(8,128)(2,1)}, u32[]{:S(2)}) copy-start(bf16[128,3072]{1,0:T(8,128)(2,1)} %first_ref.1) | copy-start | bytes 2359300
  35.6 8.3 %copy-start.4 = (bf16[128,3072]{1,0:T(8,128)(2,1)S(1)}, bf16[128,3072]{1,0:T(8,128)(2,1)}, u32[]{:S(2)}) copy-start(bf16[128,3072]{1,0:T(8,128)(2,1)} %second_ref.1) | copy-start | bytes 2359300
  36.5 23.3 %all-to-all-start = ((bf16[8,144,256]{2,1,0:T(8,128)(2,1)}), bf16[8,144,256]{2,1,0:T(8,128)(2,1)S(1)}, u32[]{:S(2)}, u32[]{:S(2)}) async-start(bf16[8,144,256]{2,1,0:T(8,128)(2,1)} %broadcast_in_dim.8), calls=%async_computation | async-start | bytes 1179648 | tf_op jit(solution)/shard_map/all_to_all | solution.py:20
  40.0 11.3 %collective-permute-start.5 = (bf16[144,2048]{1,0:T(8,128)(2,1)}, bf16[144,2048]{1,0:T(8,128)(2,1)}, u32[]{:S(2)}, u32[]{:S(2)}) collective-permute-start(bf16[144,2048]{1,0:T(8,128)(2,1)} %copy-done.10), channel_id=1, source_target_pairs={{0,24},{24,0},{48,72},{72,48},{1,25},{25,1},{49,73},{73,49},{2,26}... | collective-permute-start | bytes 1769480 | tf_op jit(solution)/shard_map/ppermute | solution.py:82
  42.0 17.8 %collective-permute-start.6 = (bf16[144,2048]{1,0:T(8,128)(2,1)}, bf16[144,2048]{1,0:T(8,128)(2,1)}, u32[]{:S(2)}, u32[]{:S(2)}) collective-permute-start(bf16[144,2048]{1,0:T(8,128)(2,1)} %copy-done.9), channel_id=1, source_target_pairs={{0,72},{24,48},{48,24},{72,0},{1,73},{25,49},{49,25},{73,1},{2,74}... | collective-permute-start | bytes 1769480 | tf_op jit(solution)/shard_map/ppermute | solution.py:82
  45.2 26.5 %collective-permute-start.7 = (bf16[256,1024]{1,0:T(8,128)(2,1)}, bf16[256,1024]{1,0:T(8,128)(2,1)S(1)}, u32[]{:S(2)}, u32[]{:S(2)}) collective-permute-start(bf16[256,1024]{1,0:T(8,128)(2,1)} %get-tuple-element.29), channel_id=1, source_target_pairs={{0,1},{1,2},{2,0},{3,4},{4,5},{5,3},{6,7},{7,8},{8,6},{9,10},{10,1... | collective-permute-start | bytes 1572872 | tf_op jit(solution)/shard_map/ppermute | solution.py:98
  47.4 25.9 %collective-permute-start.8 = (bf16[256,1024]{1,0:T(8,128)(2,1)}, bf16[256,1024]{1,0:T(8,128)(2,1)S(1)}, u32[]{:S(2)}, u32[]{:S(2)}) collective-permute-start(bf16[256,1024]{1,0:T(8,128)(2,1)} %get-tuple-element.30), channel_id=1, source_target_pairs={{0,2},{1,0},{2,1},{3,5},{4,3},{5,4},{6,8},{7,6},{8,7},{9,11},{10,9... | collective-permute-start | bytes 1572872 | tf_op jit(solution)/shard_map/ppermute | solution.py:98
  59.8 1.1 copy-start.6
  113.9 7.2 %copy-start.19 = (f32[2]{0:T(128)S(1)}, f32[2]{0:T(128)}, u32[]{:S(2)}) copy-start(f32[2]{0:T(128)} %param.25) | copy-start | bytes 28
  113.9 7.3 %copy-start.16 = (f32[144]{0:T(256)S(1)}, f32[144]{0:T(256)}, u32[]{:S(2)}) copy-start(f32[144]{0:T(256)} %param.23) | copy-start | bytes 1732
  113.9 7.3 %copy-start.18 = (f32[128]{0:T(128)S(1)}, f32[128]{0:T(128)}, u32[]{:S(2)}) copy-start(f32[128]{0:T(128)} %param.24) | copy-start | bytes 1540
  115.2 10.1 %all-to-all-start.3 = ((bf16[3,288,128]{2,1,0:T(8,128)(2,1)}), bf16[3,288,128]{2,1,0:T(8,128)(2,1)S(1)}, u32[]{:S(2)}, u32[]{:S(2)}) async-start(bf16[3,288,128]{2,1,0:T(8,128)(2,1)} %shard_map.151), calls=%async_computation.3 | async-start | bytes 442368 | tf_op jit(solution)/shard_map/all_to_all | solution.py:24
  121.3 9.9 %copy-start.2 = (bf16[144,4608]{1,0:T(8,128)(2,1)S(1)}, bf16[144,4608]{1,0:T(8,128)(2,1)}, u32[]{:S(2)}) copy-start(bf16[144,4608]{1,0:T(8,128)(2,1)} %rows_ref.3) | copy-start | bytes 3981316
  126.4 18.4 %all-to-all-start.4 = ((bf16[8,288,128]{2,1,0:T(8,128)(2,1)}), bf16[8,288,128]{2,1,0:T(8,128)(2,1)S(1)}, u32[]{:S(2)}, u32[]{:S(2)}) async-start(bf16[8,288,128]{2,1,0:T(8,128)(2,1)} %broadcast_in_dim.10), calls=%async_computation.4 | async-start | bytes 1179648 | tf_op jit(solution)/shard_map/all_to_all | solution.py:20
  132.5 0.8 copy-start.7
  133.3 0.8 copy-start.11
  134.1 34.1 %collective-permute-start.9 = (bf16[144,2048]{1,0:T(8,128)(2,1)}, bf16[144,2048]{1,0:T(8,128)(2,1)S(1)}, u32[]{:S(2)}, u32[]{:S(2)}) collective-permute-start(bf16[144,2048]{1,0:T(8,128)(2,1)} %get-tuple-element.35), channel_id=1, source_target_pairs={{0,48},{24,72},{48,0},{72,24},{1,49},{25,73},{49,1},{73,25},{2,50}... | collective-permute-start | bytes 1769480 | tf_op jit(solution)/shard_map/ppermute | solution.py:82
  168.2 29.5 %copy-start.8 = (bf16[144,2048]{1,0:T(8,128)(2,1)S(1)}, bf16[144,2048]{1,0:T(8,128)(2,1)}, u32[]{:S(2)}) copy-start(bf16[144,2048]{1,0:T(8,128)(2,1)} %copy-done.7) | copy-start | bytes 1769476
  169.1 28.5 %all-to-all-start.6 = ((bf16[8,144,256]{2,1,0:T(8,128)(2,1)}), bf16[8,144,256]{2,1,0:T(8,128)(2,1)S(1)}, u32[]{:S(2)}, u32[]{:S(2)}) async-start(bf16[8,144,256]{2,1,0:T(8,128)(2,1)} %broadcast_in_dim.11), calls=%async_computation.6 | async-start | bytes 1179648 | tf_op jit(solution)/shard_map/all_to_all | solution.py:20
  175.3 8.5 %collective-permute-start.10 = (bf16[144,2048]{1,0:T(8,128)(2,1)}, bf16[144,2048]{1,0:T(8,128)(2,1)S(1)}, u32[]{:S(2)}, u32[]{:S(2)}) collective-permute-start(bf16[144,2048]{1,0:T(8,128)(2,1)} %get-tuple-element.38), channel_id=1, source_target_pairs={{0,24},{24,0},{48,72},{72,48},{1,25},{25,1},{49,73},{73,49},{2,26}... | collective-permute-start | bytes 1769480 | tf_op jit(solution)/shard_map/ppermute | solution.py:82
  180.4 17.3 %collective-permute-start.11 = (bf16[144,2048]{1,0:T(8,128)(2,1)}, bf16[144,2048]{1,0:T(8,128)(2,1)S(1)}, u32[]{:S(2)}, u32[]{:S(2)}) collective-permute-start(bf16[144,2048]{1,0:T(8,128)(2,1)} %copy-done.11), channel_id=1, source_target_pairs={{0,72},{24,48},{48,24},{72,0},{1,73},{25,49},{49,25},{73,1},{2,74}... | collective-permute-start | bytes 1769480 | tf_op jit(solution)/shard_map/ppermute | solution.py:82
  198.6 19.8 %copy-start.17 = (f32[16,2]{0,1:T(2,128)S(1)}, f32[16,2]{0,1:T(2,128)}, u32[]{:S(2)}) copy-start(f32[16,2]{0,1:T(2,128)} %param.18) | copy-start | bytes 388
  207.3 14.9 %copy-start.12 = (f32[288,128]{1,0:T(8,128)}, f32[288,128]{1,0:T(8,128)S(1)}, u32[]{:S(2)}) copy-start(f32[288,128]{1,0:T(8,128)S(1)} %pad_maximum_fusion.8) | copy-start | bytes 442372
  207.4 13.3 %copy-start.14 = (s32[144,128]{1,0:T(8,128)S(1)}, s32[144,128]{1,0:T(8,128)}, u32[]{:S(2)}) copy-start(s32[144,128]{1,0:T(8,128)} %param.15) | copy-start | bytes 221188
  207.4 13.3 %copy-start.15 = (s32[144,128]{1,0:T(8,128)S(1)}, s32[144,128]{1,0:T(8,128)}, u32[]{:S(2)}) copy-start(s32[144,128]{1,0:T(8,128)} %param.16) | copy-start | bytes 221188
  207.5 12.9 %collective-permute-start.14 = (bf16[2,144,1]{2,1,0:T(8,128)(2,1)S(1)}, bf16[2,144,1]{2,1,0:T(8,128)(2,1)S(1)}, u32[]{:S(2)}, u32[]{:S(2)}) collective-permute-start(bf16[2,144,1]{2,1,0:T(8,128)(2,1)S(1)} %get-tuple-element.53), channel_id=1, source_target_pairs={{1,0},{2,1},{3,2},{4,3},{5,4},{6,5},{7,6},{8,7},{9,8},{10,9},{11,1... | collective-permute-start | bytes 1736 | tf_op jit(solution)/shard_map/ppermute | solution.py:33
  208.8 11.6 %collective-permute-start.15 = (bf16[2,144,1]{2,1,0:T(8,128)(2,1)S(1)}, bf16[2,144,1]{2,1,0:T(8,128)(2,1)S(1)}, u32[]{:S(2)}, u32[]{:S(2)}) collective-permute-start(bf16[2,144,1]{2,1,0:T(8,128)(2,1)S(1)} %get-tuple-element.54), channel_id=1, source_target_pairs={{0,1},{1,2},{2,3},{3,4},{4,5},{5,6},{6,7},{7,8},{8,9},{9,10},{10,1... | collective-permute-start | bytes 1736 | tf_op jit(solution)/shard_map/ppermute | solution.py:32
  212.8 5.6 %collective-permute-start.12 = (bf16[2,1,128]{2,1,0:T(2,128)(2,1)S(1)}, bf16[2,1,128]{2,1,0:T(2,128)(2,1)S(1)}, u32[]{:S(2)}, u32[]{:S(2)}) collective-permute-start(bf16[2,1,128]{2,1,0:T(2,128)(2,1)S(1)} %get-tuple-element.55), channel_id=1, source_target_pairs={{24,0},{48,24},{72,48},{96,72},{120,96},{144,120},{168,144},{192,1... | collective-permute-start | bytes 1544 | tf_op jit(solution)/shard_map/ppermute | solution.py:33
  215.9 4.6 %collective-permute-start.13 = (bf16[2,1,128]{2,1,0:T(2,128)(2,1)S(1)}, bf16[2,1,128]{2,1,0:T(2,128)(2,1)S(1)}, u32[]{:S(2)}, u32[]{:S(2)}) collective-permute-start(bf16[2,1,128]{2,1,0:T(2,128)(2,1)S(1)} %get-tuple-element.56), channel_id=1, source_target_pairs={{0,24},{24,48},{48,72},{72,96},{96,120},{120,144},{144,168},{168,1... | collective-permute-start | bytes 1544 | tf_op jit(solution)/shard_map/ppermute | solution.py:32

commit v3 on v2

--- a/solution.py
+++ b/solution.py
@@ -57,7 +57,7 @@
         out_specs=[vmem] * len(outs) if isinstance(out_shape, list) else vmem,
         scratch_shapes=list(scratch),
         cost_estimate=pl.CostEstimate(flops=flops, bytes_accessed=moved, transcendentals=0),
-        compiler_params=pltpu.CompilerParams(vmem_limit_bytes=24 << 20),
+        compiler_params=pltpu.CompilerParams(vmem_limit_bytes=12 << 20),
     )(*operands)
 
 
@@ -65,17 +65,19 @@
     return 9 * (place // 2) + 4 * (place % 2) + half
 
 
-def quad_cut_kernel(me_ref, rows_ref, *out_refs):
-    me = me_ref[0]
-    for step, out_ref in enumerate(out_refs):
+def quad_cut_kernel(me_ref, rows_ref, own_ref, core_ref, chip_ref):
+    me = me_ref[0]
+    places = ((own_ref, 0), (core_ref, 0), (chip_ref, 0), (chip_ref, 144))
+    for step, (out_ref, row) in enumerate(places):
         other = lax.bitwise_xor(me, step)
         for y in range(8):
             start = pl.multiple_of((window(y, 0) + other) * 128, 128)
-            out_ref[:, y * 256 : (y + 1) * 256] = rows_ref[:, pl.ds(start, 256)]
+            out_ref[row : row + 144, y * 256 : (y + 1) * 256] = rows_ref[:, pl.ds(start, 256)]
 
 
 def quad_cut(me, rows):
-    return call(quad_cut_kernel, [jax.ShapeDtypeStruct((144, 2048), BF)] * 4, (me, rows))
+    shapes = [jax.ShapeDtypeStruct((count, 2048), BF) for count in (144, 144, 288)]
+    return call(quad_cut_kernel, shapes, (me, rows))
 
 
 def quad_send(piece, step):
@@ -107,7 +109,7 @@
         start = pl.multiple_of(256 * y + 64 * (y % 2) + 16 * me, 16)
         placed[pl.ds(start, 144), :] = held_ref[y]
     for step, table in enumerate((t0, t1, t2, t3)):
-        part = jnp.dot(table[...], placed[...], preferred_element_type=F32)
+        part = jnp.dot(table[:144, :], placed[...], preferred_element_type=F32)
         out_ref[lax.bitwise_xor(me, step)] = part.astype(BF)
 
 
@@ -184,18 +186,21 @@
     quad_me = (lax.axis_index("xl") * 2 + lax.axis_index("c")).astype(jnp.int32).reshape(1)
     ring_me = lax.axis_index("zl").astype(jnp.int32).reshape(1)
     cut_fx = quad_cut(quad_me, forward_x)
-    divergence, fx_two = lax.optimization_barrier((divergence, quad_send(cut_fx[2], 2)))
-    table_fx = (cut_fx[0], quad_send(cut_fx[1], 1), fx_two, quad_send(cut_fx[3], 3))
+    divergence, fx_chip = lax.optimization_barrier((divergence, quad_send(cut_fx[2], 2)))
+    table_fx = (cut_fx[0], quad_send(cut_fx[1], 1), fx_chip, quad_send(fx_chip[144:], 1))
     table_y = ring_tables(ring_me, forward_y, inverse_y)
     spec_x = transform_x(quad_me, to_x(divergence.reshape(288, 128)), table_fx).astype(BF)
     spec_x, table_y = lax.optimization_barrier((spec_x, table_y))
     spec_xy = transform_y(ring_me, to_y(spec_x), table_y, 0).reshape(2, 144, 128)
+    cut_ix = quad_cut(quad_me, inverse_x)
+    spec_xy, ix_chip = lax.optimization_barrier((spec_xy, quad_send(cut_ix[2], 2)))
     denom = eigen_x[None, :, None] + eigen_y[None, None, :] + mode_shift[:, None, None]
     scaled = (spec_xy / denom).astype(BF)
     back_y = transform_y(ring_me, scaled.reshape(288, 128), table_y, 128).astype(BF)
-    cut_ix = quad_cut(quad_me, inverse_x)
-    back_y, ix_two = lax.optimization_barrier((back_y, quad_send(cut_ix[2], 2)))
-    table_ix = (cut_ix[0], quad_send(cut_ix[1], 1), ix_two, quad_send(cut_ix[3], 3))
+    back_y, ix_one, ix_three = lax.optimization_barrier(
+        (back_y, quad_send(cut_ix[1], 1), quad_send(ix_chip[144:], 1))
+    )
+    table_ix = (cut_ix[0], ix_one, ix_chip, ix_three)
     pressure = to_y(transform_x(quad_me, to_x(back_y), table_ix)).reshape(2, 144, 128)
     grad_x = centre_x(pressure)
     grad_y = centre_y(pressure)

time: 225 us -> 235 us (1.044)
  blocking collectives: 80.4 us -> 61 us
  starting transfers between devices: 76.8 us -> 90 us
  waiting for transfers between devices: 41.4 us -> 52.8 us
  local copies, waits for them, and re-layouts: 6.72 us -> 13.7 us
  other arithmetic: 6.25 us -> 3.13 us
    all_to_all x3, waiting for transfers between devices: 7.25 us -> 27.8 us  [gather(): lax.all_to_all(jnp.broadcast_to(block[None], (count,) + block.shape), axe...]
    all_to_all x1, blocking collectives: 40.5 us -> 21.2 us  [gather(): lax.all_to_all(jnp.broadcast_to(block[None], (count,) + block.shape), axe...]
    ppermute x6, waiting for transfers between devices: 22.3 us -> 3.13 us  [quad_send(): return lax.ppermute(piece, QUAD, [(i, i ^ step) for i in range(4)])]
    all_to_all x3, starting transfers between devices: 14.5 us -> 32.9 us  [gather(): lax.all_to_all(jnp.broadcast_to(block[None], (count,) + block.shape), axe...]
    ppermute x4, starting transfers between devices: 15.9 us -> 6.46 us  [edges(): high = lax.ppermute(lax.slice_in_dim(block, 0, 1, axis=dim), axes, backward)]
    ppermute x4, waiting for transfers between devices: 4.23 us -> 12.3 us  [edges(): high = lax.ppermute(lax.slice_in_dim(block, 0, 1, axis=dim), axes, backward)]
    unnamed x41 -> x43, local copies, waits for them, and re-layouts: 2.82 us -> 8.85 us
    all_to_all x1, starting transfers between devices: 5.81 us -> 10.4 us  [scatter_sum(): return jnp.sum(lax.all_to_all(parts, axes, 0, 0).astype(F32), axis=0)]
  transfers between devices with their start and end apart: 20 -> 20, of which waited for: 7 -> 9; matrix products, arithmetic and copies ran while one was open for 1% -> 2% of each run, Pallas kernels for 3% -> 3%
where the time goes in v3:
time: 235 us; the launch traced here: 231 us
  starting transfers between devices  90 us (38%)
  blocking collectives  61 us (26%)
  waiting for transfers between devices  52.8 us (22%)
  local copies, waits for them, and re-layouts  13.7 us (6%)
  Pallas kernels  8.47 us (4%)
  other arithmetic  3.13 us (1%)
    all_to_all x3, blocking collectives, scatter_sum(): return jnp.sum(lax.all_to_all(parts, axes, 0, 0).astype(F32), axis=0)  39.8 us
    all_to_all x3, starting transfers between devices, gather(): lax.all_to_all(jnp.broadcast_to(block[None], (count,) + block.shape), axe...  32.9 us
    all_to_all x3, waiting for transfers between devices, gather(): lax.all_to_all(jnp.broadcast_to(block[None], (count,) + block.shape), axe...  27.8 us
    all_to_all x1, blocking collectives, gather(): lax.all_to_all(jnp.broadcast_to(block[None], (count,) + block.shape), axe...  21.2 us
    ppermute x4, starting transfers between devices, edges(): lax.ppermute(lax.slice_in_dim(block, block.shape[dim] - 1, None, axis=dim...  18.4 us
    ppermute x6, starting transfers between devices, quad_send(): return lax.ppermute(piece, QUAD, [(i, i ^ step) for i in range(4)])  15.7 us
    ppermute x4, waiting for transfers between devices, edges(): high = lax.ppermute(lax.slice_in_dim(block, 0, 1, axis=dim), axes, backward)  12.3 us
    all_to_all x1, starting transfers between devices, scatter_sum(): return jnp.sum(lax.all_to_all(parts, axes, 0, 0).astype(F32), axis=0)  10.4 us
  transfers between devices with their start and end apart: 20, of which 9 were waited for; matrix products, arithmetic and copies ran while one was open for 2% of the time, Pallas kernels for 3%

profile of v3, /device:TPU:1, one launch (start us, length us, event | category | flops | bytes accessed | tf_op | source)
XLA Modules:
  0.0 230.7 jit_solution(13950734012054177848)
XLA Ops:
  0.7 1.3 copy-done.1
  3.1 0.8 copy-done.10
  3.9 3.9 %collective-permute-start.4 = (bf16[288,2048]{1,0:T(8,128)(2,1)S(1)}, bf16[288,2048]{1,0:T(8,128)(2,1)S(1)}, u32[]{:S(2)}, u32[]{:S(2)}) collective-permute-start(bf16[288,2048]{1,0:T(8,128)(2,1)S(1)} %get-tuple-element.23), channel_id=1, source_target_pairs={{0,48},{24,72},{48,0},{72,24},{1,49},{25,73},{49,1},{73,25},{2,50}... | collective-permute-start | bytes 3538952 | tf_op jit(solution)/shard_map/ppermute | solution.py:84
  8.6 4.0 %collective-permute-start.3 = (bf16[2,144,1]{2,0,1:T(2,128)(2,1)S(1)}, bf16[2,144,1]{2,0,1:T(2,128)(2,1)S(1)}, u32[]{:S(2)}, u32[]{:S(2)}) collective-permute-start(bf16[2,144,1]{2,0,1:T(2,128)(2,1)S(1)} %get-tuple-element.68), channel_id=1, source_target_pairs={{0,1},{1,2},{2,3},{3,4},{4,5},{5,6},{6,7},{7,8},{8,9},{9,10},{10,1... | collective-permute-start | bytes 1736 | tf_op jit(solution)/shard_map/ppermute | solution.py:32
  12.6 1.3 collective-permute-start.2
  14.2 9.3 %collective-permute-start.1 = (bf16[2,1,128]{2,0,1:T(2,128)(2,1)S(1)}, bf16[2,1,128]{2,0,1:T(2,128)(2,1)S(1)}, u32[]{:S(2)}, u32[]{:S(2)}) collective-permute-start(bf16[2,1,128]{2,0,1:T(2,128)(2,1)S(1)} %get-tuple-element.66), channel_id=1, source_target_pairs={{0,24},{24,48},{48,72},{72,96},{96,120},{120,144},{144,168},{168,1... | collective-permute-start | bytes 1544 | tf_op jit(solution)/shard_map/ppermute | solution.py:32
  23.5 1.9 collective-permute-start
  25.4 1.1 collective-permute-done.1
  26.5 9.4 %collective-permute-done = bf16[2,1,128]{2,0,1:T(2,128)(2,1)S(1)} collective-permute-done((bf16[2,1,128]{2,0,1:T(2,128)(2,1)S(1)}, bf16[2,1,128]{2,0,1:T(2,128)(2,1)S(1)}, u32[]{:S(2)}, u32[]{:S(2)}) %collective-permute-start) | collective-permute-done | bytes 544 | tf_op jit(solution)/shard_map/ppermute | solution.py:33
  36.8 0.9 broadcast_in_dim.10
  37.6 7.2 %all-to-all-start = ((bf16[8,144,256]{2,1,0:T(8,128)(2,1)}), bf16[8,144,256]{2,1,0:T(8,128)(2,1)S(1)}, u32[]{:S(2)}, u32[]{:S(2)}) async-start(bf16[8,144,256]{2,1,0:T(8,128)(2,1)} %broadcast_in_dim.10), calls=%async_computation | async-start | bytes 1179648 | tf_op jit(solution)/shard_map/all_to_all | solution.py:20
  44.8 1.9 collective-permute-start.5
  46.7 0.9 slice.123
  47.6 2.4 %collective-permute-start.6 = (bf16[144,2048]{1,0:T(8,128)(2,1)}, bf16[144,2048]{1,0:T(8,128)(2,1)}, u32[]{:S(2)}, u32[]{:S(2)}) collective-permute-start(bf16[144,2048]{1,0:T(8,128)(2,1)} %slice.123), channel_id=1, source_target_pairs={{0,24},{24,0},{48,72},{72,48},{1,25},{25,1},{49,73},{73,49},{2,26}... | collective-permute-start | bytes 1769480 | tf_op jit(solution)/shard_map/ppermute | solution.py:84
  50.0 1.1 copy-done.5
  51.2 1.2 shard_map.150
  52.4 2.4 %collective-permute-start.7 = (bf16[256,1024]{1,0:T(8,128)(2,1)}, bf16[256,1024]{1,0:T(8,128)(2,1)S(1)}, u32[]{:S(2)}, u32[]{:S(2)}) collective-permute-start(bf16[256,1024]{1,0:T(8,128)(2,1)} %get-tuple-element.29), channel_id=1, source_target_pairs={{0,1},{1,2},{2,0},{3,4},{4,5},{5,3},{6,7},{7,8},{8,6},{9,10},{10,1... | collective-permute-start | bytes 1572872 | tf_op jit(solution)/shard_map/ppermute | solution.py:100
  54.8 3.8 %collective-permute-start.8 = (bf16[256,1024]{1,0:T(8,128)(2,1)}, bf16[256,1024]{1,0:T(8,128)(2,1)S(1)}, u32[]{:S(2)}, u32[]{:S(2)}) collective-permute-start(bf16[256,1024]{1,0:T(8,128)(2,1)} %get-tuple-element.30), channel_id=1, source_target_pairs={{0,2},{1,0},{2,1},{3,5},{4,3},{5,4},{6,8},{7,6},{8,7},{9,11},{10,9... | collective-permute-start | bytes 1572872 | tf_op jit(solution)/shard_map/ppermute | solution.py:100
  58.6 5.7 %all-to-all-done.held_ref = bf16[8,144,256]{2,1,0:T(8,128)(2,1)S(1)} async-done(((bf16[8,144,256]{2,1,0:T(8,128)(2,1)}), bf16[8,144,256]{2,1,0:T(8,128)(2,1)S(1)}, u32[]{:S(2)}, u32[]{:S(2)}) %all-to-all-start) | async-done | bytes 589856 | tf_op jit(solution)/shard_map/all_to_all | solution.py:20
  64.3 1.1 copy-done.7
  65.3 2.2 shard_map.149
  67.5 8.7 %all_to_all.40 = bf16[4,144,256]{2,1,0:T(8,128)(2,1)S(1)} all-to-all(bf16[4,144,256]{2,1,0:T(8,128)(2,1)S(1)} %shard_map.149), channel_id=1, replica_groups=mesh['y'=8,'xl'=2,'c'=2,'xh'=2,'zh'=4,'zl'=3] {'xl','c'}, dimensions={0} | all-to-all | bytes 589824 | tf_op jit(solution)/shard_map/all_to_all | solution.py:24
  76.3 4.3 %collective-permute-done.8.t2 = bf16[256,1024]{1,0:T(8,128)(2,1)S(1)} collective-permute-done((bf16[256,1024]{1,0:T(8,128)(2,1)}, bf16[256,1024]{1,0:T(8,128)(2,1)S(1)}, u32[]{:S(2)}, u32[]{:S(2)}) %collective-permute-start.8) | collective-permute-done | bytes 524320 | tf_op jit(solution)/shard_map/ppermute | solution.py:100
  80.6 0.9 broadcast_in_dim.11
  81.4 16.3 %all-to-all-start.2 = ((bf16[8,288,128]{2,1,0:T(8,128)(2,1)}), bf16[8,288,128]{2,1,0:T(8,128)(2,1)S(1)}, u32[]{:S(2)}, u32[]{:S(2)}) async-start(bf16[8,288,128]{2,1,0:T(8,128)(2,1)} %broadcast_in_dim.11), calls=%async_computation.2 | async-start | bytes 1179648 | tf_op jit(solution)/shard_map/all_to_all | solution.py:20
  97.7 1.3 copy-done.2
  99.1 1.3 shard_map.152
  102.0 2.0 collective-permute-start.9
  104.1 12.5 %all-to-all-done.2.held_ref = bf16[8,288,128]{2,1,0:T(8,128)(2,1)S(1)} async-done(((bf16[8,288,128]{2,1,0:T(8,128)(2,1)}), bf16[8,288,128]{2,1,0:T(8,128)(2,1)S(1)}, u32[]{:S(2)}, u32[]{:S(2)}) %all-to-all-start.2) | async-done | bytes 589856 | tf_op jit(solution)/shard_map/all_to_all | solution.py:20
  117.9 10.4 %all-to-all-start.3 = ((bf16[3,288,128]{2,1,0:T(8,128)(2,1)}), bf16[3,288,128]{2,1,0:T(8,128)(2,1)S(1)}, u32[]{:S(2)}, u32[]{:S(2)}) async-start(bf16[3,288,128]{2,1,0:T(8,128)(2,1)} %copy-done.3), calls=%async_computation.3 | async-start | bytes 442368 | tf_op jit(solution)/shard_map/all_to_all | solution.py:24
  128.4 4.2 %all-to-all-done.3 = bf16[3,288,128]{2,1,0:T(8,128)(2,1)S(1)} async-done(((bf16[3,288,128]{2,1,0:T(8,128)(2,1)}), bf16[3,288,128]{2,1,0:T(8,128)(2,1)S(1)}, u32[]{:S(2)}, u32[]{:S(2)}) %all-to-all-start.3) | async-done | bytes 221216 | tf_op jit(solution)/shard_map/all_to_all | solution.py:24
  132.6 3.1 %collective-permute-done.9.t2 = bf16[288,2048]{1,0:T(8,128)(2,1)S(1)} collective-permute-done((bf16[288,2048]{1,0:T(8,128)(2,1)}, bf16[288,2048]{1,0:T(8,128)(2,1)S(1)}, u32[]{:S(2)}, u32[]{:S(2)}) %collective-permute-start.9) | collective-permute-done | bytes 1179680 | tf_op jit(solution)/shard_map/ppermute | solution.py:84
  135.8 0.9 broadcast_in_dim.13
  136.7 9.4 %all-to-all-start.4 = ((bf16[8,288,128]{2,1,0:T(8,128)(2,1)}), bf16[8,288,128]{2,1,0:T(8,128)(2,1)S(1)}, u32[]{:S(2)}, u32[]{:S(2)}) async-start(bf16[8,288,128]{2,1,0:T(8,128)(2,1)} %broadcast_in_dim.13), calls=%async_computation.4 | async-start | bytes 1179648 | tf_op jit(solution)/shard_map/all_to_all | solution.py:20
  146.1 3.5 %collective-permute-start.10 = (bf16[144,2048]{1,0:T(8,128)(2,1)}, bf16[144,2048]{1,0:T(8,128)(2,1)}, u32[]{:S(2)}, u32[]{:S(2)}) collective-permute-start(bf16[144,2048]{1,0:T(8,128)(2,1)} %copy-done.11), channel_id=1, source_target_pairs={{0,24},{24,0},{48,72},{72,48},{1,25},{25,1},{49,73},{73,49},{2,26}... | collective-permute-start | bytes 1769480 | tf_op jit(solution)/shard_map/ppermute | solution.py:84
  149.7 0.9 slice.126
  150.5 1.9 collective-permute-start.11
  152.5 9.6 %all-to-all-done.4.held_ref = bf16[8,288,128]{2,1,0:T(8,128)(2,1)S(1)} async-done(((bf16[8,288,128]{2,1,0:T(8,128)(2,1)}), bf16[8,288,128]{2,1,0:T(8,128)(2,1)S(1)}, u32[]{:S(2)}, u32[]{:S(2)}) %all-to-all-start.4) | async-done | bytes 589856 | tf_op jit(solution)/shard_map/all_to_all | solution.py:20
  162.7 17.3 %all_to_all.41 = bf16[3,288,128]{2,1,0:T(8,128)(2,1)S(1)} all-to-all(bf16[3,288,128]{2,1,0:T(8,128)(2,1)S(1)} %shard_map.153), channel_id=1, replica_groups=mesh['y'=8,'xl'=2,'c'=2,'xh'=2,'zh'=4,'zl'=3] {'zl'}, dimensions={0} | all-to-all | bytes 442368 | tf_op jit(solution)/shard_map/all_to_all | solution.py:24
  180.1 21.2 %all_to_all.42.held_ref = bf16[8,144,256]{2,1,0:T(8,128)(2,1)S(1)} all-to-all(bf16[8,144,256]{2,1,0:T(8,128)(2,1)S(1)} %broadcast_in_dim.14), channel_id=1, replica_groups=mesh['y'=8,'xl'=2,'c'=2,'xh'=2,'zh'=4,'zl'=3] {'y'}, dimensions={0} | all-to-all | bytes 1179648 | tf_op jit(solution)/shard_map/all_to_all | solution.py:20
  201.4 2.2 shard_map.154
  203.5 13.8 %all_to_all.43 = bf16[4,144,256]{2,1,0:T(8,128)(2,1)S(1)} all-to-all(bf16[4,144,256]{2,1,0:T(8,128)(2,1)S(1)} %shard_map.154), channel_id=1, replica_groups=mesh['y'=8,'xl'=2,'c'=2,'xh'=2,'zh'=4,'zl'=3] {'xl','c'}, dimensions={0} | all-to-all | bytes 589824 | tf_op jit(solution)/shard_map/all_to_all | solution.py:24
  217.6 2.4 %collective-permute-start.15 = (bf16[2,144,1]{2,1,0:T(8,128)(2,1)S(1)}, bf16[2,144,1]{2,1,0:T(8,128)(2,1)S(1)}, u32[]{:S(2)}, u32[]{:S(2)}) collective-permute-start(bf16[2,144,1]{2,1,0:T(8,128)(2,1)S(1)} %get-tuple-element.56), channel_id=1, source_target_pairs={{0,1},{1,2},{2,3},{3,4},{4,5},{5,6},{6,7},{7,8},{8,9},{9,10},{10,1... | collective-permute-start | bytes 1736 | tf_op jit(solution)/shard_map/ppermute | solution.py:32
  220.0 1.3 collective-permute-start.14
  221.3 2.7 %collective-permute-start.13 = (bf16[2,1,128]{2,1,0:T(2,128)(2,1)S(1)}, bf16[2,1,128]{2,1,0:T(2,128)(2,1)S(1)}, u32[]{:S(2)}, u32[]{:S(2)}) collective-permute-start(bf16[2,1,128]{2,1,0:T(2,128)(2,1)S(1)} %get-tuple-element.58), channel_id=1, source_target_pairs={{0,24},{24,48},{48,72},{72,96},{96,120},{120,144},{144,168},{168,1... | collective-permute-start | bytes 1544 | tf_op jit(solution)/shard_map/ppermute | solution.py:32
  224.0 2.0 collective-permute-start.12
  226.0 2.9 %collective-permute-done.12 = bf16[2,1,128]{2,1,0:T(2,128)(2,1)S(1)} collective-permute-done((bf16[2,1,128]{2,1,0:T(2,128)(2,1)S(1)}, bf16[2,1,128]{2,1,0:T(2,128)(2,1)S(1)}, u32[]{:S(2)}, u32[]{:S(2)}) %collective-permute-start.12) | collective-permute-done | bytes 544 | tf_op jit(solution)/shard_map/ppermute | solution.py:33
  229.2 1.6 fusion.4
  (89 shorter events, 7.2 us)
Async XLA Ops:
  0.6 7.6 %copy-start = (bf16[16,2]{0,1:T(2,128)(2,1)S(1)}, bf16[16,2]{0,1:T(2,128)(2,1)}, u32[]{:S(2)}) copy-start(bf16[16,2]{0,1:T(2,128)(2,1)} %param.17) | copy-start | bytes 196
  0.7 1.3 copy-start.1
  2.0 5.9 %copy-start.13 = (s32[144,128]{1,0:T(8,128)S(1)}, s32[144,128]{1,0:T(8,128)}, u32[]{:S(2)}) copy-start(s32[144,128]{1,0:T(8,128)} %param.15) | copy-start | bytes 221188
  2.0 5.9 %copy-start.14 = (bf16[16,144,128]{2,1,0:T(8,128)(2,1)S(1)}, bf16[16,144,128]{2,1,0:T(8,128)(2,1)}, u32[]{:S(2)}) copy-start(bf16[16,144,128]{2,1,0:T(8,128)(2,1)} %param.13) | copy-start | bytes 1769476
  2.0 5.9 %copy-start.15 = (bf16[16,144,128]{2,1,0:T(8,128)(2,1)S(1)}, bf16[16,144,128]{2,1,0:T(8,128)(2,1)}, u32[]{:S(2)}) copy-start(bf16[16,144,128]{2,1,0:T(8,128)(2,1)} %param.14) | copy-start | bytes 1769476
  2.0 5.9 %copy-start.16 = (s32[144,128]{1,0:T(8,128)S(1)}, s32[144,128]{1,0:T(8,128)}, u32[]{:S(2)}) copy-start(s32[144,128]{1,0:T(8,128)} %param.16) | copy-start | bytes 221188
  2.3 0.8 copy-start.6
  3.1 0.8 copy-start.10
  3.9 32.7 %collective-permute-start.4 = (bf16[288,2048]{1,0:T(8,128)(2,1)S(1)}, bf16[288,2048]{1,0:T(8,128)(2,1)S(1)}, u32[]{:S(2)}, u32[]{:S(2)}) collective-permute-start(bf16[288,2048]{1,0:T(8,128)(2,1)S(1)} %get-tuple-element.23), channel_id=1, source_target_pairs={{0,48},{24,72},{48,0},{72,24},{1,49},{25,73},{49,1},{73,25},{2,50}... | collective-permute-start | bytes 3538952 | tf_op jit(solution)/shard_map/ppermute | solution.py:84
  8.6 27.3 %collective-permute-start.3 = (bf16[2,144,1]{2,0,1:T(2,128)(2,1)S(1)}, bf16[2,144,1]{2,0,1:T(2,128)(2,1)S(1)}, u32[]{:S(2)}, u32[]{:S(2)}) collective-permute-start(bf16[2,144,1]{2,0,1:T(2,128)(2,1)S(1)} %get-tuple-element.68), channel_id=1, source_target_pairs={{0,1},{1,2},{2,3},{3,4},{4,5},{5,6},{6,7},{7,8},{8,9},{9,10},{10,1... | collective-permute-start | bytes 1736 | tf_op jit(solution)/shard_map/ppermute | solution.py:32
  12.6 23.4 %collective-permute-start.2 = (bf16[2,144,1]{2,0,1:T(2,128)(2,1)S(1)}, bf16[2,144,1]{2,0,1:T(2,128)(2,1)S(1)}, u32[]{:S(2)}, u32[]{:S(2)}) collective-permute-start(bf16[2,144,1]{2,0,1:T(2,128)(2,1)S(1)} %get-tuple-element.67), channel_id=1, source_target_pairs={{1,0},{2,1},{3,2},{4,3},{5,4},{6,5},{7,6},{8,7},{9,8},{10,9},{11,1... | collective-permute-start | bytes 1736 | tf_op jit(solution)/shard_map/ppermute | solution.py:33
  14.2 12.4 %collective-permute-start.1 = (bf16[2,1,128]{2,0,1:T(2,128)(2,1)S(1)}, bf16[2,1,128]{2,0,1:T(2,128)(2,1)S(1)}, u32[]{:S(2)}, u32[]{:S(2)}) collective-permute-start(bf16[2,1,128]{2,0,1:T(2,128)(2,1)S(1)} %get-tuple-element.66), channel_id=1, source_target_pairs={{0,24},{24,48},{48,72},{72,96},{96,120},{120,144},{144,168},{168,1... | collective-permute-start | bytes 1544 | tf_op jit(solution)/shard_map/ppermute | solution.py:32
  23.5 12.5 %collective-permute-start = (bf16[2,1,128]{2,0,1:T(2,128)(2,1)S(1)}, bf16[2,1,128]{2,0,1:T(2,128)(2,1)S(1)}, u32[]{:S(2)}, u32[]{:S(2)}) collective-permute-start(bf16[2,1,128]{2,0,1:T(2,128)(2,1)S(1)} %get-tuple-element.65), channel_id=1, source_target_pairs={{24,0},{48,24},{72,48},{96,72},{120,96},{144,120},{168,144},{192,1... | collective-permute-start | bytes 1544 | tf_op jit(solution)/shard_map/ppermute | solution.py:33
  37.6 12.4 %copy-start.4 = (bf16[128,3072]{1,0:T(8,128)(2,1)S(1)}, bf16[128,3072]{1,0:T(8,128)(2,1)}, u32[]{:S(2)}) copy-start(bf16[128,3072]{1,0:T(8,128)(2,1)} %first_ref.1) | copy-start | bytes 2359300
  37.6 26.7 %all-to-all-start = ((bf16[8,144,256]{2,1,0:T(8,128)(2,1)}), bf16[8,144,256]{2,1,0:T(8,128)(2,1)S(1)}, u32[]{:S(2)}, u32[]{:S(2)}) async-start(bf16[8,144,256]{2,1,0:T(8,128)(2,1)} %broadcast_in_dim.10), calls=%async_computation | async-start | bytes 1179648 | tf_op jit(solution)/shard_map/all_to_all | solution.py:20
  44.8 13.8 %collective-permute-start.5 = (bf16[144,2048]{1,0:T(8,128)(2,1)}, bf16[144,2048]{1,0:T(8,128)(2,1)}, u32[]{:S(2)}, u32[]{:S(2)}) collective-permute-start(bf16[144,2048]{1,0:T(8,128)(2,1)} %copy-done.10), channel_id=1, source_target_pairs={{0,24},{24,0},{48,72},{72,48},{1,25},{25,1},{49,73},{73,49},{2,26}... | collective-permute-start | bytes 1769480 | tf_op jit(solution)/shard_map/ppermute | solution.py:84
  47.6 11.0 %collective-permute-start.6 = (bf16[144,2048]{1,0:T(8,128)(2,1)}, bf16[144,2048]{1,0:T(8,128)(2,1)}, u32[]{:S(2)}, u32[]{:S(2)}) collective-permute-start(bf16[144,2048]{1,0:T(8,128)(2,1)} %slice.123), channel_id=1, source_target_pairs={{0,24},{24,0},{48,72},{72,48},{1,25},{25,1},{49,73},{73,49},{2,26}... | collective-permute-start | bytes 1769480 | tf_op jit(solution)/shard_map/ppermute | solution.py:84
  50.0 1.1 copy-start.5
  52.4 23.9 %collective-permute-start.7 = (bf16[256,1024]{1,0:T(8,128)(2,1)}, bf16[256,1024]{1,0:T(8,128)(2,1)S(1)}, u32[]{:S(2)}, u32[]{:S(2)}) collective-permute-start(bf16[256,1024]{1,0:T(8,128)(2,1)} %get-tuple-element.29), channel_id=1, source_target_pairs={{0,1},{1,2},{2,0},{3,4},{4,5},{5,3},{6,7},{7,8},{8,6},{9,10},{10,1... | collective-permute-start | bytes 1572872 | tf_op jit(solution)/shard_map/ppermute | solution.py:100
  54.8 25.7 %collective-permute-start.8 = (bf16[256,1024]{1,0:T(8,128)(2,1)}, bf16[256,1024]{1,0:T(8,128)(2,1)S(1)}, u32[]{:S(2)}, u32[]{:S(2)}) collective-permute-start(bf16[256,1024]{1,0:T(8,128)(2,1)} %get-tuple-element.30), channel_id=1, source_target_pairs={{0,2},{1,0},{2,1},{3,5},{4,3},{5,4},{6,8},{7,6},{8,7},{9,11},{10,9... | collective-permute-start | bytes 1572872 | tf_op jit(solution)/shard_map/ppermute | solution.py:100
  64.3 1.1 copy-start.7
  81.4 35.1 %all-to-all-start.2 = ((bf16[8,288,128]{2,1,0:T(8,128)(2,1)}), bf16[8,288,128]{2,1,0:T(8,128)(2,1)S(1)}, u32[]{:S(2)}, u32[]{:S(2)}) async-start(bf16[8,288,128]{2,1,0:T(8,128)(2,1)} %broadcast_in_dim.11), calls=%async_computation.2 | async-start | bytes 1179648 | tf_op jit(solution)/shard_map/all_to_all | solution.py:20
  97.7 1.3 copy-start.2
  100.4 0.8 copy-start.8
  101.2 0.8 copy-start.11
  102.0 26.2 %copy-start.17 = (f32[144]{0:T(256)S(1)}, f32[144]{0:T(256)}, u32[]{:S(2)}) copy-start(f32[144]{0:T(256)} %param.23) | copy-start | bytes 1732
  102.0 26.2 %copy-start.19 = (f32[128]{0:T(128)S(1)}, f32[128]{0:T(128)}, u32[]{:S(2)}) copy-start(f32[128]{0:T(128)} %param.24) | copy-start | bytes 1540
  102.0 33.7 %copy-start.20 = (f32[2]{0:T(128)S(1)}, f32[2]{0:T(128)}, u32[]{:S(2)}) copy-start(f32[2]{0:T(128)} %param.25) | copy-start | bytes 28
  102.0 33.7 %collective-permute-start.9 = (bf16[288,2048]{1,0:T(8,128)(2,1)}, bf16[288,2048]{1,0:T(8,128)(2,1)S(1)}, u32[]{:S(2)}, u32[]{:S(2)}) collective-permute-start(bf16[288,2048]{1,0:T(8,128)(2,1)} %get-tuple-element.35), channel_id=1, source_target_pairs={{0,48},{24,72},{48,0},{72,24},{1,49},{25,73},{49,1},{73,25},{2,50}... | collective-permute-start | bytes 3538952 | tf_op jit(solution)/shard_map/ppermute | solution.py:84
  117.2 0.7 copy-start.3
  117.9 14.7 %all-to-all-start.3 = ((bf16[3,288,128]{2,1,0:T(8,128)(2,1)}), bf16[3,288,128]{2,1,0:T(8,128)(2,1)S(1)}, u32[]{:S(2)}, u32[]{:S(2)}) async-start(bf16[3,288,128]{2,1,0:T(8,128)(2,1)} %copy-done.3), calls=%async_computation.3 | async-start | bytes 442368 | tf_op jit(solution)/shard_map/all_to_all | solution.py:24
  136.7 25.3 %all-to-all-start.4 = ((bf16[8,288,128]{2,1,0:T(8,128)(2,1)}), bf16[8,288,128]{2,1,0:T(8,128)(2,1)S(1)}, u32[]{:S(2)}, u32[]{:S(2)}) async-start(bf16[8,288,128]{2,1,0:T(8,128)(2,1)} %broadcast_in_dim.13), calls=%async_computation.4 | async-start | bytes 1179648 | tf_op jit(solution)/shard_map/all_to_all | solution.py:20
  146.1 33.9 %collective-permute-start.10 = (bf16[144,2048]{1,0:T(8,128)(2,1)}, bf16[144,2048]{1,0:T(8,128)(2,1)}, u32[]{:S(2)}, u32[]{:S(2)}) collective-permute-start(bf16[144,2048]{1,0:T(8,128)(2,1)} %copy-done.11), channel_id=1, source_target_pairs={{0,24},{24,0},{48,72},{72,48},{1,25},{25,1},{49,73},{73,49},{2,26}... | collective-permute-start | bytes 1769480 | tf_op jit(solution)/shard_map/ppermute | solution.py:84
  150.5 29.5 %collective-permute-start.11 = (bf16[144,2048]{1,0:T(8,128)(2,1)}, bf16[144,2048]{1,0:T(8,128)(2,1)}, u32[]{:S(2)}, u32[]{:S(2)}) collective-permute-start(bf16[144,2048]{1,0:T(8,128)(2,1)} %slice.126), channel_id=1, source_target_pairs={{0,24},{24,0},{48,72},{72,48},{1,25},{25,1},{49,73},{73,49},{2,26}... | collective-permute-start | bytes 1769480 | tf_op jit(solution)/shard_map/ppermute | solution.py:84
  180.0 21.4 %copy-start.9 = (bf16[144,2048]{1,0:T(8,128)(2,1)S(1)}, bf16[144,2048]{1,0:T(8,128)(2,1)}, u32[]{:S(2)}) copy-start(bf16[144,2048]{1,0:T(8,128)(2,1)} %copy-done.8) | copy-start | bytes 1769476
  203.5 22.4 %copy-start.18 = (f32[16,2]{0,1:T(2,128)S(1)}, f32[16,2]{0,1:T(2,128)}, u32[]{:S(2)}) copy-start(f32[16,2]{0,1:T(2,128)} %param.18) | copy-start | bytes 388
  217.4 13.3 %copy-start.12 = (f32[288,128]{1,0:T(8,128)}, f32[288,128]{1,0:T(8,128)S(1)}, u32[]{:S(2)}) copy-start(f32[288,128]{1,0:T(8,128)S(1)} %pad_maximum_fusion.8) | copy-start | bytes 442372
  217.6 11.3 %collective-permute-start.15 = (bf16[2,144,1]{2,1,0:T(8,128)(2,1)S(1)}, bf16[2,144,1]{2,1,0:T(8,128)(2,1)S(1)}, u32[]{:S(2)}, u32[]{:S(2)}) collective-permute-start(bf16[2,144,1]{2,1,0:T(8,128)(2,1)S(1)} %get-tuple-element.56), channel_id=1, source_target_pairs={{0,1},{1,2},{2,3},{3,4},{4,5},{5,6},{6,7},{7,8},{8,9},{9,10},{10,1... | collective-permute-start | bytes 1736 | tf_op jit(solution)/shard_map/ppermute | solution.py:32
  220.0 8.9 %collective-permute-start.14 = (bf16[2,144,1]{2,1,0:T(8,128)(2,1)S(1)}, bf16[2,144,1]{2,1,0:T(8,128)(2,1)S(1)}, u32[]{:S(2)}, u32[]{:S(2)}) collective-permute-start(bf16[2,144,1]{2,1,0:T(8,128)(2,1)S(1)} %get-tuple-element.55), channel_id=1, source_target_pairs={{1,0},{2,1},{3,2},{4,3},{5,4},{6,5},{7,6},{8,7},{9,8},{10,9},{11,1... | collective-permute-start | bytes 1736 | tf_op jit(solution)/shard_map/ppermute | solution.py:33
  221.3 4.7 %collective-permute-start.13 = (bf16[2,1,128]{2,1,0:T(2,128)(2,1)S(1)}, bf16[2,1,128]{2,1,0:T(2,128)(2,1)S(1)}, u32[]{:S(2)}, u32[]{:S(2)}) collective-permute-start(bf16[2,1,128]{2,1,0:T(2,128)(2,1)S(1)} %get-tuple-element.58), channel_id=1, source_target_pairs={{0,24},{24,48},{48,72},{72,96},{96,120},{120,144},{144,168},{168,1... | collective-permute-start | bytes 1544 | tf_op jit(solution)/shard_map/ppermute | solution.py:32
  224.0 4.9 %collective-permute-start.12 = (bf16[2,1,128]{2,1,0:T(2,128)(2,1)S(1)}, bf16[2,1,128]{2,1,0:T(2,128)(2,1)S(1)}, u32[]{:S(2)}, u32[]{:S(2)}) collective-permute-start(bf16[2,1,128]{2,1,0:T(2,128)(2,1)S(1)} %get-tuple-element.57), channel_id=1, source_target_pairs={{24,0},{48,24},{72,48},{96,72},{120,96},{144,120},{168,144},{192,1... | collective-permute-start | bytes 1544 | tf_op jit(solution)/shard_map/ppermute | solution.py:33

commit v4 on v3

--- a/solution.py
+++ b/solution.py
@@ -149,6 +149,122 @@
         flops=2 * 288 * 1024 * 384,
     )
     return scatter_sum(parts, "zl")
+
+
+def nt_dot(left, right):
+    return lax.dot_general(left, right, (((1,), (1,)), ((), ())), preferred_element_type=F32)
+
+
+def x_back_kernel(me_ref, held_ref, t0, t1, t2, t3, lo_ref, hi_ref, out_ref, placed, side, last, first, sums):
+    me = me_ref[0]
+    placed[...] = jnp.zeros_like(placed)
+    sums[...] = jnp.zeros_like(sums)
+    for y in range(8):
+        shift = 64 * (y % 2) + 16 * me
+        placed[pl.ds(pl.multiple_of(256 * y + shift, 16), 144), :] = held_ref[y, :144, :]
+        turned = pltpu.roll(held_ref[y, 144:160, :].astype(F32), shift, 1)
+        side[:, 256 * y : 256 * (y + 1)] = turned.astype(BF)
+    last[0] = jnp.dot(lo_ref[...], placed[...], preferred_element_type=F32)[8:16]
+    first[5] = jnp.dot(hi_ref[...], placed[...], preferred_element_type=F32)[:8]
+    for step, table in enumerate((t0, t1, t2, t3)):
+        target = lax.bitwise_xor(me, step)
+        part = jnp.dot(table[:144, :], placed[...], preferred_element_type=F32)
+        out_ref[target, :144, :] = part.astype(BF)
+        last[target + 1] = part[136:144]
+        first[target + 1] = part[:8]
+        sums[target, :, :144] = nt_dot(side[...], table[:144, :])
+    row = lax.broadcasted_iota(jnp.int32, (16, 256), 0)
+    for target in range(4):
+        low = jnp.broadcast_to(last[target][7:8], (16, 256))
+        high = jnp.broadcast_to(first[target + 2][:1], (16, 256))
+        group = jnp.where(row == 2, low, jnp.where(row == 3, high, sums[target]))
+        out_ref[target, 144:160, :] = group.astype(BF)
+
+
+def transform_x_back(me, block, table, outer):
+    held = gather(block, "y", 8)
+    scratch = [
+        pltpu.VMEM((2048, 256), BF),
+        pltpu.VMEM((16, 2048), BF),
+        pltpu.VMEM((5, 8, 256), F32),
+        pltpu.VMEM((6, 8, 256), F32),
+        pltpu.VMEM((4, 16, 256), F32),
+    ]
+    parts = call(
+        x_back_kernel,
+        jax.ShapeDtypeStruct((4, 160, 256), BF),
+        (me, held, *table, *outer),
+        scratch,
+        flops=2 * 576 * 2048 * 256,
+    )
+    return scatter_sum(parts, QUAD)
+
+
+def y_back_kernel(me_ref, held_ref, t0, t1, t2, lo_ref, hi_ref, out_ref, placed, last, first):
+    me = me_ref[0]
+    placed[288:, :] = jnp.zeros((112, 1024), BF)
+    for g in range(8):
+        placed[:288, g * 128 : (g + 1) * 128] = held_ref[g]
+    last[0] = lo_ref[...]
+    first[4] = hi_ref[...]
+    for step, table in enumerate((t0, t1, t2)):
+        target = lax.rem(me + 3 - step, 3)
+        out_ref[target, :288, :] = nt_dot(placed[:288, :], table[128:, :]).astype(BF)
+        last[target + 1] = table[240:256, :]
+        first[target + 1] = table[128:144, :]
+    row = lax.broadcasted_iota(jnp.int32, (16, 128), 0)
+    lane = lax.broadcasted_iota(jnp.int32, (32, 128), 1)
+    for target in range(3):
+        rows = jnp.concatenate([last[target], first[target + 2]], axis=0)
+        for mode in range(2):
+            head = nt_dot(rows, placed[144 * mode : 144 * mode + 128, :])
+            rest = nt_dot(rows, placed[144 * mode + 128 : 144 * mode + 256, :])
+            rest = jnp.where(lane < 16, rest, 0.0)
+            group = jnp.zeros((16, 128), F32)
+            for at, value in ((0, head[15:16]), (1, head[16:17]), (8, rest[15:16]), (9, rest[16:17])):
+                group = jnp.where(row == at, jnp.broadcast_to(value, (16, 128)), group)
+            out_ref[target, 288 + 16 * mode : 304 + 16 * mode, :] = group.astype(BF)
+
+
+def transform_y_back(me, block, table, outer):
+    held = gather(block, ("xh", "zh"), 8)
+    scratch = [
+        pltpu.VMEM((400, 1024), BF),
+        pltpu.VMEM((4, 16, 1024), BF),
+        pltpu.VMEM((5, 16, 1024), BF),
+    ]
+    parts = call(
+        y_back_kernel,
+        jax.ShapeDtypeStruct((3, 320, 128), BF),
+        (me, held, *table, *outer),
+        scratch,
+        flops=2 * 288 * 1024 * 384,
+    )
+    return scatter_sum(parts, "zl")
+
+
+def ring_outer(me, table):
+    low = lax.dynamic_index_in_dim(jnp.stack([t[240:256] for t in table]), (me + 1) % 3, 0, False)
+    high = lax.dynamic_index_in_dim(jnp.stack([t[128:144] for t in table]), me, 0, False)
+    up = [(i, i + 1) for i in range(7)]
+    down = [(i + 1, i) for i in range(7)]
+    return lax.ppermute(low, ("xh", "zh"), up), lax.ppermute(high, ("xh", "zh"), down)
+
+
+def quad_outer(me, table):
+    low = lax.dynamic_index_in_dim(jnp.stack([t[128:144] for t in table]), me ^ 3, 0, False)
+    high = lax.dynamic_index_in_dim(jnp.stack([t[:16] for t in table]), me, 0, False)
+    up = [(i, (i + 1) % 8) for i in range(8)]
+    down = [((i + 1) % 8, i) for i in range(8)]
+    return lax.ppermute(low, "y", up), lax.ppermute(high, "y", down)
+
+
+def with_sides(back):
+    sides = [
+        jnp.concatenate([back[288 + 16 * m : 296 + 16 * m], back[296 + 16 * m : 304 + 16 * m]], axis=1)
+        for m in range(2)
+    ]
+    return jnp.concatenate([to_x(back[:288])] + sides, axis=0)
 
 
 def to_x(block):
@@ -196,14 +312,21 @@
     spec_xy, ix_chip = lax.optimization_barrier((spec_xy, quad_send(cut_ix[2], 2)))
     denom = eigen_x[None, :, None] + eigen_y[None, None, :] + mode_shift[:, None, None]
     scaled = (spec_xy / denom).astype(BF)
-    back_y = transform_y(ring_me, scaled.reshape(288, 128), table_y, 128).astype(BF)
+    outer_y = ring_outer(ring_me[0], table_y)
+    back_y = transform_y_back(ring_me, scaled.reshape(288, 128), table_y, outer_y).astype(BF)
     back_y, ix_one, ix_three = lax.optimization_barrier(
         (back_y, quad_send(cut_ix[1], 1), quad_send(ix_chip[144:], 1))
     )
     table_ix = (cut_ix[0], ix_one, ix_chip, ix_three)
-    pressure = to_y(transform_x(quad_me, to_x(back_y), table_ix)).reshape(2, 144, 128)
-    grad_x = centre_x(pressure)
-    grad_y = centre_y(pressure)
+    outer_x = quad_outer(quad_me[0], table_ix)
+    total = transform_x_back(quad_me, with_sides(back_y), table_ix, outer_x)
+    pressure = to_y(total[:144]).reshape(2, 144, 128)
+    low, high = total[146].reshape(2, 1, 128), total[147].reshape(2, 1, 128)
+    padded = jnp.concatenate([low, pressure, high], axis=1)
+    grad_x = 0.5 * (padded[:, 2:, :] - padded[:, :-2, :])
+    sides = jnp.stack([total[144:146, :144], total[152:154, :144]])
+    padded = jnp.concatenate([sides[:, 0, :, None], pressure, sides[:, 1, :, None]], axis=2)
+    grad_y = 0.5 * (padded[:, :, 2:] - padded[:, :, :-2])
     wet_f = wet_int.astype(F32)
     shape_zero = mode_shape[:, 0][:, None, None]
     shape_one = mode_shape[:, 1][:, None, None]

time: 235 us -> 229 us (0.974); the launches traced: 231 us -> 228 us
  blocking collectives: 61 us -> 8.71 us
  starting transfers between devices: 90 us -> 116 us
  waiting for transfers between devices: 52.8 us -> 69 us
  local copies, waits for them, and re-layouts: 13.7 us -> 18.4 us
  Pallas kernels: 8.47 us -> 10.9 us
    all_to_all x3 -> x1, blocking collectives: 39.8 us -> 8.71 us  [scatter_sum(): return jnp.sum(lax.all_to_all(parts, axes, 0, 0).astype(F32), axis=0)]
    all_to_all x1 -> x0, blocking collectives: 21.2 us -> none  [gather(): lax.all_to_all(jnp.broadcast_to(block[None], (count,) + block.shape), axe...]
    ppermute x0 -> x4, waiting for transfers between devices: none -> 17.3 us  [the longest x1 10.4 us: ring_outer(): lax.ppermute(high, ('xh', 'zh'), down)]
    all_to_all x1 -> x3, starting transfers between devices: 10.4 us -> 23.4 us  [scatter_sum(): return jnp.sum(lax.all_to_all(parts, axes, 0, 0).astype(F32), axis=0)]
    ppermute x0 -> x4, starting transfers between devices: none -> 13 us  [the longest x2 6.5 us: quad_outer(): return (lax.ppermute(low, 'y', up), lax.ppermute(high, 'y', down))]
    all_to_all x1 -> x3, waiting for transfers between devices: 4.23 us -> 13.6 us  [scatter_sum(): return jnp.sum(lax.all_to_all(parts, axes, 0, 0).astype(F32), axis=0)]
    all_to_all x3 -> x4, waiting for transfers between devices: 27.8 us -> 20.2 us  [gather(): lax.all_to_all(jnp.broadcast_to(block[None], (count,) + block.shape), axe...]
    all_to_all x3 -> x4, starting transfers between devices: 32.9 us -> 40.2 us  [gather(): lax.all_to_all(jnp.broadcast_to(block[None], (count,) + block.shape), axe...]
  transfers between devices with their start and end apart: 20 -> 23, of which waited for: 9 -> 12; matrix products, arithmetic and copies ran while one was open for 2% -> 3% of each run, Pallas kernels for 3% -> 3%
where the time goes in v4:
time: 229 us; the launch traced here: 228 us
  starting transfers between devices  116 us (51%)
  waiting for transfers between devices  69 us (30%)
  local copies, waits for them, and re-layouts  18.4 us (8%)
  Pallas kernels  10.9 us (5%)
  blocking collectives  8.71 us (4%)
  other arithmetic  3.33 us (1%)
    all_to_all x4, starting transfers between devices, gather(): lax.all_to_all(jnp.broadcast_to(block[None], (count,) + block.shape), axe...  40.2 us
    all_to_all x3, starting transfers between devices, scatter_sum(): return jnp.sum(lax.all_to_all(parts, axes, 0, 0).astype(F32), axis=0)  23.4 us
    all_to_all x4, waiting for transfers between devices, gather(): lax.all_to_all(jnp.broadcast_to(block[None], (count,) + block.shape), axe...  20.2 us
    ppermute x6, starting transfers between devices, quad_send(): return lax.ppermute(piece, QUAD, [(i, i ^ step) for i in range(4)])  16.3 us
    all_to_all x3, waiting for transfers between devices, scatter_sum(): return jnp.sum(lax.all_to_all(parts, axes, 0, 0).astype(F32), axis=0)  13.6 us
    ppermute x2, starting transfers between devices, edges(): lax.ppermute(lax.slice_in_dim(block, block.shape[dim] - 1, None, axis=dim...  13.3 us
    pallas_call x7, Pallas kernels, call(): pl.pallas_call(kernel, out_shape=out_shape, in_specs=[smem] + [vmem] * (l...  10.9 us
    ppermute x1, waiting for transfers between devices, ring_outer(): lax.ppermute(high, ('xh', 'zh'), down)  10.4 us
  transfers between devices with their start and end apart: 23, of which 12 were waited for; matrix products, arithmetic and copies ran while one was open for 3% of the time, Pallas kernels for 3%

profile of v4, /device:TPU:1, one launch (start us, length us, event | category | flops | bytes accessed | tf_op | source)
XLA Modules:
  0.0 227.7 jit_solution(12537822463163041283)
XLA Ops:
  0.7 1.3 copy-done.1
  3.9 3.9 %collective-permute-start.4 = (bf16[288,2048]{1,0:T(8,128)(2,1)S(1)}, bf16[288,2048]{1,0:T(8,128)(2,1)S(1)}, u32[]{:S(2)}, u32[]{:S(2)}) collective-permute-start(bf16[288,2048]{1,0:T(8,128)(2,1)S(1)} %get-tuple-element.23), channel_id=1, source_target_pairs={{0,48},{24,72},{48,0},{72,24},{1,49},{25,73},{49,1},{73,25},{2,50}... | collective-permute-start | bytes 3538952 | tf_op jit(solution)/shard_map/ppermute | solution.py:84
  8.6 4.0 %collective-permute-start.3 = (bf16[2,144,1]{2,0,1:T(2,128)(2,1)S(1)}, bf16[2,144,1]{2,0,1:T(2,128)(2,1)S(1)}, u32[]{:S(2)}, u32[]{:S(2)}) collective-permute-start(bf16[2,144,1]{2,0,1:T(2,128)(2,1)S(1)} %get-tuple-element.86), channel_id=1, source_target_pairs={{0,1},{1,2},{2,3},{3,4},{4,5},{5,6},{6,7},{7,8},{8,9},{9,10},{10,1... | collective-permute-start | bytes 1736 | tf_op jit(solution)/shard_map/ppermute | solution.py:32
  12.6 1.3 collective-permute-start.2
  14.1 9.3 %collective-permute-start.1 = (bf16[2,1,128]{2,0,1:T(2,128)(2,1)S(1)}, bf16[2,1,128]{2,0,1:T(2,128)(2,1)S(1)}, u32[]{:S(2)}, u32[]{:S(2)}) collective-permute-start(bf16[2,1,128]{2,0,1:T(2,128)(2,1)S(1)} %get-tuple-element.84), channel_id=1, source_target_pairs={{0,24},{24,48},{48,72},{72,96},{96,120},{120,144},{144,168},{168,1... | collective-permute-start | bytes 1544 | tf_op jit(solution)/shard_map/ppermute | solution.py:32
  23.5 1.9 collective-permute-start
  25.4 1.1 collective-permute-done.1
  26.5 9.4 %collective-permute-done = bf16[2,1,128]{2,0,1:T(2,128)(2,1)S(1)} collective-permute-done((bf16[2,1,128]{2,0,1:T(2,128)(2,1)S(1)}, bf16[2,1,128]{2,0,1:T(2,128)(2,1)S(1)}, u32[]{:S(2)}, u32[]{:S(2)}) %collective-permute-start) | collective-permute-done | bytes 544 | tf_op jit(solution)/shard_map/ppermute | solution.py:33
  37.6 7.2 %all-to-all-start = ((bf16[8,144,256]{2,1,0:T(8,128)(2,1)}), bf16[8,144,256]{2,1,0:T(8,128)(2,1)S(1)}, u32[]{:S(2)}, u32[]{:S(2)}) async-start(bf16[8,144,256]{2,1,0:T(8,128)(2,1)} %broadcast_in_dim.10), calls=%async_computation | async-start | bytes 1179648 | tf_op jit(solution)/shard_map/all_to_all | solution.py:20
  44.8 1.9 collective-permute-start.5
  47.6 2.4 %collective-permute-start.6 = (bf16[144,2048]{1,0:T(8,128)(2,1)}, bf16[144,2048]{1,0:T(8,128)(2,1)}, u32[]{:S(2)}, u32[]{:S(2)}) collective-permute-start(bf16[144,2048]{1,0:T(8,128)(2,1)} %slice.189), channel_id=1, source_target_pairs={{0,24},{24,0},{48,72},{72,48},{1,25},{25,1},{49,73},{73,49},{2,26}... | collective-permute-start | bytes 1769480 | tf_op jit(solution)/shard_map/ppermute | solution.py:84
  50.0 1.1 copy-done.8
  51.1 1.2 shard_map.150
  52.4 2.4 %collective-permute-start.7 = (bf16[256,1024]{1,0:T(8,128)(2,1)}, bf16[256,1024]{1,0:T(8,128)(2,1)S(1)}, u32[]{:S(2)}, u32[]{:S(2)}) collective-permute-start(bf16[256,1024]{1,0:T(8,128)(2,1)} %get-tuple-element.29), channel_id=1, source_target_pairs={{0,1},{1,2},{2,0},{3,4},{4,5},{5,3},{6,7},{7,8},{8,6},{9,10},{10,1... | collective-permute-start | bytes 1572872 | tf_op jit(solution)/shard_map/ppermute | solution.py:100
  54.8 3.8 %collective-permute-start.8 = (bf16[256,1024]{1,0:T(8,128)(2,1)}, bf16[256,1024]{1,0:T(8,128)(2,1)S(1)}, u32[]{:S(2)}, u32[]{:S(2)}) collective-permute-start(bf16[256,1024]{1,0:T(8,128)(2,1)} %get-tuple-element.30), channel_id=1, source_target_pairs={{0,2},{1,0},{2,1},{3,5},{4,3},{5,4},{6,8},{7,6},{8,7},{9,11},{10,9... | collective-permute-start | bytes 1572872 | tf_op jit(solution)/shard_map/ppermute | solution.py:100
  58.6 5.7 %all-to-all-done.held_ref = bf16[8,144,256]{2,1,0:T(8,128)(2,1)S(1)} async-done(((bf16[8,144,256]{2,1,0:T(8,128)(2,1)}), bf16[8,144,256]{2,1,0:T(8,128)(2,1)S(1)}, u32[]{:S(2)}, u32[]{:S(2)}) %all-to-all-start) | async-done | bytes 589856 | tf_op jit(solution)/shard_map/all_to_all | solution.py:20
  64.3 1.1 copy-done.10
  65.3 2.2 shard_map.149
  67.5 8.7 %all_to_all.40 = bf16[4,144,256]{2,1,0:T(8,128)(2,1)S(1)} all-to-all(bf16[4,144,256]{2,1,0:T(8,128)(2,1)S(1)} %shard_map.149), channel_id=1, replica_groups=mesh['y'=8,'xl'=2,'c'=2,'xh'=2,'zh'=4,'zl'=3] {'xl','c'}, dimensions={0} | all-to-all | bytes 589824 | tf_op jit(solution)/shard_map/all_to_all | solution.py:24
  76.3 4.3 %collective-permute-done.8.t2 = bf16[256,1024]{1,0:T(8,128)(2,1)S(1)} collective-permute-done((bf16[256,1024]{1,0:T(8,128)(2,1)}, bf16[256,1024]{1,0:T(8,128)(2,1)S(1)}, u32[]{:S(2)}, u32[]{:S(2)}) %collective-permute-start.8) | collective-permute-done | bytes 524320 | tf_op jit(solution)/shard_map/ppermute | solution.py:100
  81.4 16.3 %all-to-all-start.2 = ((bf16[8,288,128]{2,1,0:T(8,128)(2,1)}), bf16[8,288,128]{2,1,0:T(8,128)(2,1)S(1)}, u32[]{:S(2)}, u32[]{:S(2)}) async-start(bf16[8,288,128]{2,1,0:T(8,128)(2,1)} %broadcast_in_dim.11), calls=%async_computation.2 | async-start | bytes 1179648 | tf_op jit(solution)/shard_map/all_to_all | solution.py:20
  97.7 1.3 copy-done.2
  99.0 1.3 shard_map.152
  102.0 2.0 collective-permute-start.9
  104.0 12.5 %all-to-all-done.2.held_ref = bf16[8,288,128]{2,1,0:T(8,128)(2,1)S(1)} async-done(((bf16[8,288,128]{2,1,0:T(8,128)(2,1)}), bf16[8,288,128]{2,1,0:T(8,128)(2,1)S(1)}, u32[]{:S(2)}, u32[]{:S(2)}) %all-to-all-start.2) | async-done | bytes 589856 | tf_op jit(solution)/shard_map/all_to_all | solution.py:20
  117.9 10.4 %all-to-all-start.3 = ((bf16[3,288,128]{2,1,0:T(8,128)(2,1)}), bf16[3,288,128]{2,1,0:T(8,128)(2,1)S(1)}, u32[]{:S(2)}, u32[]{:S(2)}) async-start(bf16[3,288,128]{2,1,0:T(8,128)(2,1)} %copy-done.4), calls=%async_computation.3 | async-start | bytes 442368 | tf_op jit(solution)/shard_map/all_to_all | solution.py:24
  128.3 4.2 %all-to-all-done.3 = bf16[3,288,128]{2,1,0:T(8,128)(2,1)S(1)} async-done(((bf16[3,288,128]{2,1,0:T(8,128)(2,1)}), bf16[3,288,128]{2,1,0:T(8,128)(2,1)S(1)}, u32[]{:S(2)}, u32[]{:S(2)}) %all-to-all-start.3) | async-done | bytes 221216 | tf_op jit(solution)/shard_map/all_to_all | solution.py:24
  132.6 3.1 %collective-permute-done.9.t2 = bf16[288,2048]{1,0:T(8,128)(2,1)S(1)} collective-permute-done((bf16[288,2048]{1,0:T(8,128)(2,1)}, bf16[288,2048]{1,0:T(8,128)(2,1)S(1)}, u32[]{:S(2)}, u32[]{:S(2)}) %collective-permute-start.9) | collective-permute-done | bytes 1179680 | tf_op jit(solution)/shard_map/ppermute | solution.py:84
  136.7 9.4 %all-to-all-start.4 = ((bf16[8,288,128]{2,1,0:T(8,128)(2,1)}), bf16[8,288,128]{2,1,0:T(8,128)(2,1)S(1)}, u32[]{:S(2)}, u32[]{:S(2)}) async-start(bf16[8,288,128]{2,1,0:T(8,128)(2,1)} %broadcast_in_dim.13), calls=%async_computation.4 | async-start | bytes 1179648 | tf_op jit(solution)/shard_map/all_to_all | solution.py:20
  146.2 5.2 %collective-permute-start.10 = (bf16[16,1024]{1,0:T(8,128)(2,1)S(1)}, bf16[16,1024]{1,0:T(8,128)(2,1)S(1)}, u32[]{:S(2)}, u32[]{:S(2)}) collective-permute-start(bf16[16,1024]{1,0:T(8,128)(2,1)S(1)} %fusion.33), channel_id=1, source_target_pairs={{0,3},{3,6},{6,9},{9,12},{12,15},{15,18},{18,21},{1,4},{4,7},{7,10... | collective-permute-start | bytes 98312 | tf_op jit(solution)/shard_map/ppermute | solution.py:251
  151.4 1.3 collective-permute-start.11
  152.7 4.1 %collective-permute-start.12 = (bf16[144,2048]{1,0:T(8,128)(2,1)}, bf16[144,2048]{1,0:T(8,128)(2,1)}, u32[]{:S(2)}, u32[]{:S(2)}) collective-permute-start(bf16[144,2048]{1,0:T(8,128)(2,1)} %copy-done.11), channel_id=1, source_target_pairs={{0,24},{24,0},{48,72},{72,48},{1,25},{25,1},{49,73},{73,49},{2,26}... | collective-permute-start | bytes 1769480 | tf_op jit(solution)/shard_map/ppermute | solution.py:84
  156.8 0.9 slice.198
  157.7 1.9 collective-permute-start.13
  159.6 10.4 %collective-permute-done.11.hi_ref = bf16[16,1024]{1,0:T(8,128)(2,1)S(1)} collective-permute-done((bf16[16,1024]{1,0:T(8,128)(2,1)S(1)}, bf16[16,1024]{1,0:T(8,128)(2,1)S(1)}, u32[]{:S(2)}, u32[]{:S(2)}) %collective-permute-start.11) | collective-permute-done | bytes 32800 | tf_op jit(solution)/shard_map/ppermute | solution.py:251
  170.0 1.6 shard_map.153
  172.3 5.1 %all-to-all-start.5 = ((bf16[3,320,128]{2,1,0:T(8,128)(2,1)}), bf16[3,320,128]{2,1,0:T(8,128)(2,1)S(1)}, u32[]{:S(2)}, u32[]{:S(2)}) async-start(bf16[3,320,128]{2,1,0:T(8,128)(2,1)} %copy-done.3), calls=%async_computation.5 | async-start | bytes 491520 | tf_op jit(solution)/shard_map/all_to_all | solution.py:24
  178.3 3.5 %all-to-all-done.5 = bf16[3,320,128]{2,1,0:T(8,128)(2,1)S(1)} async-done(((bf16[3,320,128]{2,1,0:T(8,128)(2,1)}), bf16[3,320,128]{2,1,0:T(8,128)(2,1)S(1)}, u32[]{:S(2)}, u32[]{:S(2)}) %all-to-all-start.5) | async-done | bytes 245792 | tf_op jit(solution)/shard_map/all_to_all | solution.py:24
  181.9 0.9 broadcast_in_dim.14
  182.8 7.3 %all-to-all-start.6 = ((bf16[8,160,256]{2,1,0:T(8,128)(2,1)}), bf16[8,160,256]{2,1,0:T(8,128)(2,1)S(1)}, u32[]{:S(2)}, u32[]{:S(2)}) async-start(bf16[8,160,256]{2,1,0:T(8,128)(2,1)} %broadcast_in_dim.14), calls=%async_computation.6 | async-start | bytes 1310720 | tf_op jit(solution)/shard_map/all_to_all | solution.py:20
  192.0 3.4 %collective-permute-start.14 = (bf16[16,2048]{1,0:T(8,128)(2,1)S(1)}, bf16[16,2048]{1,0:T(8,128)(2,1)S(1)}, u32[]{:S(2)}, u32[]{:S(2)}) collective-permute-start(bf16[16,2048]{1,0:T(8,128)(2,1)S(1)} %fusion.27), channel_id=1, source_target_pairs={{0,96},{96,192},{192,288},{288,384},{384,480},{480,576},{576,672},... | collective-permute-start | bytes 196616 | tf_op jit(solution)/shard_map/ppermute | solution.py:259
  195.5 3.1 %collective-permute-start.15 = (bf16[16,2048]{1,0:T(8,128)(2,1)S(1)}, bf16[16,2048]{1,0:T(8,128)(2,1)S(1)}, u32[]{:S(2)}, u32[]{:S(2)}) collective-permute-start(bf16[16,2048]{1,0:T(8,128)(2,1)S(1)} %fusion.23), channel_id=1, source_target_pairs={{96,0},{192,96},{288,192},{384,288},{480,384},{576,480},{672,576},... | collective-permute-start | bytes 196616 | tf_op jit(solution)/shard_map/ppermute | solution.py:259
  198.6 6.9 %collective-permute-done.14.lo_ref = bf16[16,2048]{1,0:T(8,128)(2,1)S(1)} collective-permute-done((bf16[16,2048]{1,0:T(8,128)(2,1)S(1)}, bf16[16,2048]{1,0:T(8,128)(2,1)S(1)}, u32[]{:S(2)}, u32[]{:S(2)}) %collective-permute-start.14) | collective-permute-done | bytes 65568 | tf_op jit(solution)/shard_map/ppermute | solution.py:259
  205.5 2.1 all-to-all-done.6.held_ref
  207.6 3.7 %shard_map.154 = bf16[4,160,256]{2,1,0:T(8,128)(2,1)} custom-call(s32[1]{0:T(128)} %bitcast.1.me_ref, bf16[8,160,256]{2,1,0:T(8,128)(2,1)S(1)} %all-to-all-done.6.held_ref, bf16[144,2048]{1,0:T(8,128)(2,1)S(1)} %copy-done.6, bf16[144,2048]{1,0:T(8,128)(2,1)} %collective-permute-done.12.t1, bf16[288,2048]{1,0:T(8,128)(2,1)S(1)} %collective-permute-done.9.t2, ...), custom_call_target="tpu_custom_call" | custom-call | flops 603979776 | bytes 4063232 | tf_op jit(solution)/shard_map/pallas_call | solution.py:53
  211.3 8.0 %all-to-all-start.7 = ((bf16[4,160,256]{2,1,0:T(8,128)(2,1)}), bf16[4,160,256]{2,1,0:T(8,128)(2,1)S(1)}, u32[]{:S(2)}, u32[]{:S(2)}) async-start(bf16[4,160,256]{2,1,0:T(8,128)(2,1)} %shard_map.154), calls=%async_computation.7 | async-start | bytes 655360 | tf_op jit(solution)/shard_map/all_to_all | solution.py:24
  219.3 5.9 %all-to-all-done.7 = bf16[4,160,256]{2,1,0:T(8,128)(2,1)S(1)} async-done(((bf16[4,160,256]{2,1,0:T(8,128)(2,1)}), bf16[4,160,256]{2,1,0:T(8,128)(2,1)S(1)}, u32[]{:S(2)}, u32[]{:S(2)}) %all-to-all-start.7) | async-done | bytes 327712 | tf_op jit(solution)/shard_map/all_to_all | solution.py:24
  226.1 1.6 fusion.4
  (108 shorter events, 14.9 us)
Async XLA Ops:
  0.6 7.6 %copy-start = (bf16[16,2]{0,1:T(2,128)(2,1)S(1)}, bf16[16,2]{0,1:T(2,128)(2,1)}, u32[]{:S(2)}) copy-start(bf16[16,2]{0,1:T(2,128)(2,1)} %param.17) | copy-start | bytes 196
  0.7 1.3 copy-start.1
  2.0 5.9 %copy-start.13 = (s32[144,128]{1,0:T(8,128)S(1)}, s32[144,128]{1,0:T(8,128)}, u32[]{:S(2)}) copy-start(s32[144,128]{1,0:T(8,128)} %param.15) | copy-start | bytes 221188
  2.0 5.9 %copy-start.14 = (bf16[16,144,128]{2,1,0:T(8,128)(2,1)S(1)}, bf16[16,144,128]{2,1,0:T(8,128)(2,1)}, u32[]{:S(2)}) copy-start(bf16[16,144,128]{2,1,0:T(8,128)(2,1)} %param.13) | copy-start | bytes 1769476
  2.0 5.9 %copy-start.15 = (bf16[16,144,128]{2,1,0:T(8,128)(2,1)S(1)}, bf16[16,144,128]{2,1,0:T(8,128)(2,1)}, u32[]{:S(2)}) copy-start(bf16[16,144,128]{2,1,0:T(8,128)(2,1)} %param.14) | copy-start | bytes 1769476
  2.0 5.9 %copy-start.17 = (s32[144,128]{1,0:T(8,128)S(1)}, s32[144,128]{1,0:T(8,128)}, u32[]{:S(2)}) copy-start(s32[144,128]{1,0:T(8,128)} %param.16) | copy-start | bytes 221188
  2.3 0.8 copy-start.9
  3.1 0.8 copy-start.12
  3.9 32.7 %collective-permute-start.4 = (bf16[288,2048]{1,0:T(8,128)(2,1)S(1)}, bf16[288,2048]{1,0:T(8,128)(2,1)S(1)}, u32[]{:S(2)}, u32[]{:S(2)}) collective-permute-start(bf16[288,2048]{1,0:T(8,128)(2,1)S(1)} %get-tuple-element.23), channel_id=1, source_target_pairs={{0,48},{24,72},{48,0},{72,24},{1,49},{25,73},{49,1},{73,25},{2,50}... | collective-permute-start | bytes 3538952 | tf_op jit(solution)/shard_map/ppermute | solution.py:84
  8.6 27.3 %collective-permute-start.3 = (bf16[2,144,1]{2,0,1:T(2,128)(2,1)S(1)}, bf16[2,144,1]{2,0,1:T(2,128)(2,1)S(1)}, u32[]{:S(2)}, u32[]{:S(2)}) collective-permute-start(bf16[2,144,1]{2,0,1:T(2,128)(2,1)S(1)} %get-tuple-element.86), channel_id=1, source_target_pairs={{0,1},{1,2},{2,3},{3,4},{4,5},{5,6},{6,7},{7,8},{8,9},{9,10},{10,1... | collective-permute-start | bytes 1736 | tf_op jit(solution)/shard_map/ppermute | solution.py:32
  12.6 23.4 %collective-permute-start.2 = (bf16[2,144,1]{2,0,1:T(2,128)(2,1)S(1)}, bf16[2,144,1]{2,0,1:T(2,128)(2,1)S(1)}, u32[]{:S(2)}, u32[]{:S(2)}) collective-permute-start(bf16[2,144,1]{2,0,1:T(2,128)(2,1)S(1)} %get-tuple-element.85), channel_id=1, source_target_pairs={{1,0},{2,1},{3,2},{4,3},{5,4},{6,5},{7,6},{8,7},{9,8},{10,9},{11,1... | collective-permute-start | bytes 1736 | tf_op jit(solution)/shard_map/ppermute | solution.py:33
  14.1 12.4 %collective-permute-start.1 = (bf16[2,1,128]{2,0,1:T(2,128)(2,1)S(1)}, bf16[2,1,128]{2,0,1:T(2,128)(2,1)S(1)}, u32[]{:S(2)}, u32[]{:S(2)}) collective-permute-start(bf16[2,1,128]{2,0,1:T(2,128)(2,1)S(1)} %get-tuple-element.84), channel_id=1, source_target_pairs={{0,24},{24,48},{48,72},{72,96},{96,120},{120,144},{144,168},{168,1... | collective-permute-start | bytes 1544 | tf_op jit(solution)/shard_map/ppermute | solution.py:32
  23.5 12.5 %collective-permute-start = (bf16[2,1,128]{2,0,1:T(2,128)(2,1)S(1)}, bf16[2,1,128]{2,0,1:T(2,128)(2,1)S(1)}, u32[]{:S(2)}, u32[]{:S(2)}) collective-permute-start(bf16[2,1,128]{2,0,1:T(2,128)(2,1)S(1)} %get-tuple-element.83), channel_id=1, source_target_pairs={{24,0},{48,24},{72,48},{96,72},{120,96},{144,120},{168,144},{192,1... | collective-permute-start | bytes 1544 | tf_op jit(solution)/shard_map/ppermute | solution.py:33
  37.6 12.4 %copy-start.7 = (bf16[128,3072]{1,0:T(8,128)(2,1)S(1)}, bf16[128,3072]{1,0:T(8,128)(2,1)}, u32[]{:S(2)}) copy-start(bf16[128,3072]{1,0:T(8,128)(2,1)} %first_ref.1) | copy-start | bytes 2359300
  37.6 26.7 %all-to-all-start = ((bf16[8,144,256]{2,1,0:T(8,128)(2,1)}), bf16[8,144,256]{2,1,0:T(8,128)(2,1)S(1)}, u32[]{:S(2)}, u32[]{:S(2)}) async-start(bf16[8,144,256]{2,1,0:T(8,128)(2,1)} %broadcast_in_dim.10), calls=%async_computation | async-start | bytes 1179648 | tf_op jit(solution)/shard_map/all_to_all | solution.py:20
  44.8 13.8 %collective-permute-start.5 = (bf16[144,2048]{1,0:T(8,128)(2,1)}, bf16[144,2048]{1,0:T(8,128)(2,1)}, u32[]{:S(2)}, u32[]{:S(2)}) collective-permute-start(bf16[144,2048]{1,0:T(8,128)(2,1)} %copy-done.12), channel_id=1, source_target_pairs={{0,24},{24,0},{48,72},{72,48},{1,25},{25,1},{49,73},{73,49},{2,26}... | collective-permute-start | bytes 1769480 | tf_op jit(solution)/shard_map/ppermute | solution.py:84
  47.6 11.0 %collective-permute-start.6 = (bf16[144,2048]{1,0:T(8,128)(2,1)}, bf16[144,2048]{1,0:T(8,128)(2,1)}, u32[]{:S(2)}, u32[]{:S(2)}) collective-permute-start(bf16[144,2048]{1,0:T(8,128)(2,1)} %slice.189), channel_id=1, source_target_pairs={{0,24},{24,0},{48,72},{72,48},{1,25},{25,1},{49,73},{73,49},{2,26}... | collective-permute-start | bytes 1769480 | tf_op jit(solution)/shard_map/ppermute | solution.py:84
  50.0 1.1 copy-start.8
  52.4 23.9 %collective-permute-start.7 = (bf16[256,1024]{1,0:T(8,128)(2,1)}, bf16[256,1024]{1,0:T(8,128)(2,1)S(1)}, u32[]{:S(2)}, u32[]{:S(2)}) collective-permute-start(bf16[256,1024]{1,0:T(8,128)(2,1)} %get-tuple-element.29), channel_id=1, source_target_pairs={{0,1},{1,2},{2,0},{3,4},{4,5},{5,3},{6,7},{7,8},{8,6},{9,10},{10,1... | collective-permute-start | bytes 1572872 | tf_op jit(solution)/shard_map/ppermute | solution.py:100
  54.8 25.7 %collective-permute-start.8 = (bf16[256,1024]{1,0:T(8,128)(2,1)}, bf16[256,1024]{1,0:T(8,128)(2,1)S(1)}, u32[]{:S(2)}, u32[]{:S(2)}) collective-permute-start(bf16[256,1024]{1,0:T(8,128)(2,1)} %get-tuple-element.30), channel_id=1, source_target_pairs={{0,2},{1,0},{2,1},{3,5},{4,3},{5,4},{6,8},{7,6},{8,7},{9,11},{10,9... | collective-permute-start | bytes 1572872 | tf_op jit(solution)/shard_map/ppermute | solution.py:100
  64.3 1.1 copy-start.10
  81.4 35.1 %all-to-all-start.2 = ((bf16[8,288,128]{2,1,0:T(8,128)(2,1)}), bf16[8,288,128]{2,1,0:T(8,128)(2,1)S(1)}, u32[]{:S(2)}, u32[]{:S(2)}) async-start(bf16[8,288,128]{2,1,0:T(8,128)(2,1)} %broadcast_in_dim.11), calls=%async_computation.2 | async-start | bytes 1179648 | tf_op jit(solution)/shard_map/all_to_all | solution.py:20
  97.7 1.3 copy-start.2
  100.4 0.8 copy-start.5
  101.2 0.8 copy-start.11
  102.0 26.3 %copy-start.19 = (f32[144]{0:T(256)S(1)}, f32[144]{0:T(256)}, u32[]{:S(2)}) copy-start(f32[144]{0:T(256)} %param.23) | copy-start | bytes 1732
  102.0 26.3 %copy-start.21 = (f32[128]{0:T(128)S(1)}, f32[128]{0:T(128)}, u32[]{:S(2)}) copy-start(f32[128]{0:T(128)} %param.24) | copy-start | bytes 1540
  102.0 33.7 %copy-start.22 = (f32[2]{0:T(128)S(1)}, f32[2]{0:T(128)}, u32[]{:S(2)}) copy-start(f32[2]{0:T(128)} %param.25) | copy-start | bytes 28
  102.0 33.7 %collective-permute-start.9 = (bf16[288,2048]{1,0:T(8,128)(2,1)}, bf16[288,2048]{1,0:T(8,128)(2,1)S(1)}, u32[]{:S(2)}, u32[]{:S(2)}) collective-permute-start(bf16[288,2048]{1,0:T(8,128)(2,1)} %get-tuple-element.35), channel_id=1, source_target_pairs={{0,48},{24,72},{48,0},{72,24},{1,49},{25,73},{49,1},{73,25},{2,50}... | collective-permute-start | bytes 3538952 | tf_op jit(solution)/shard_map/ppermute | solution.py:84
  117.2 0.7 copy-start.4
  117.9 14.7 %all-to-all-start.3 = ((bf16[3,288,128]{2,1,0:T(8,128)(2,1)}), bf16[3,288,128]{2,1,0:T(8,128)(2,1)S(1)}, u32[]{:S(2)}, u32[]{:S(2)}) async-start(bf16[3,288,128]{2,1,0:T(8,128)(2,1)} %copy-done.4), calls=%async_computation.3 | async-start | bytes 442368 | tf_op jit(solution)/shard_map/all_to_all | solution.py:24
  136.7 33.3 %all-to-all-start.4 = ((bf16[8,288,128]{2,1,0:T(8,128)(2,1)}), bf16[8,288,128]{2,1,0:T(8,128)(2,1)S(1)}, u32[]{:S(2)}, u32[]{:S(2)}) async-start(bf16[8,288,128]{2,1,0:T(8,128)(2,1)} %broadcast_in_dim.13), calls=%async_computation.4 | async-start | bytes 1179648 | tf_op jit(solution)/shard_map/all_to_all | solution.py:20
  146.2 13.5 %collective-permute-start.10 = (bf16[16,1024]{1,0:T(8,128)(2,1)S(1)}, bf16[16,1024]{1,0:T(8,128)(2,1)S(1)}, u32[]{:S(2)}, u32[]{:S(2)}) collective-permute-start(bf16[16,1024]{1,0:T(8,128)(2,1)S(1)} %fusion.33), channel_id=1, source_target_pairs={{0,3},{3,6},{6,9},{9,12},{12,15},{15,18},{18,21},{1,4},{4,7},{7,10... | collective-permute-start | bytes 98312 | tf_op jit(solution)/shard_map/ppermute | solution.py:251
  151.4 18.6 %collective-permute-start.11 = (bf16[16,1024]{1,0:T(8,128)(2,1)S(1)}, bf16[16,1024]{1,0:T(8,128)(2,1)S(1)}, u32[]{:S(2)}, u32[]{:S(2)}) collective-permute-start(bf16[16,1024]{1,0:T(8,128)(2,1)S(1)} %fusion.30), channel_id=1, source_target_pairs={{3,0},{6,3},{9,6},{12,9},{15,12},{18,15},{21,18},{4,1},{7,4},{10,7... | collective-permute-start | bytes 98312 | tf_op jit(solution)/shard_map/ppermute | solution.py:251
  152.7 29.1 %collective-permute-start.12 = (bf16[144,2048]{1,0:T(8,128)(2,1)}, bf16[144,2048]{1,0:T(8,128)(2,1)}, u32[]{:S(2)}, u32[]{:S(2)}) collective-permute-start(bf16[144,2048]{1,0:T(8,128)(2,1)} %copy-done.11), channel_id=1, source_target_pairs={{0,24},{24,0},{48,72},{72,48},{1,25},{25,1},{49,73},{73,49},{2,26}... | collective-permute-start | bytes 1769480 | tf_op jit(solution)/shard_map/ppermute | solution.py:84
  157.7 24.1 %collective-permute-start.13 = (bf16[144,2048]{1,0:T(8,128)(2,1)}, bf16[144,2048]{1,0:T(8,128)(2,1)}, u32[]{:S(2)}, u32[]{:S(2)}) collective-permute-start(bf16[144,2048]{1,0:T(8,128)(2,1)} %slice.198), channel_id=1, source_target_pairs={{0,24},{24,0},{48,72},{72,48},{1,25},{25,1},{49,73},{73,49},{2,26}... | collective-permute-start | bytes 1769480 | tf_op jit(solution)/shard_map/ppermute | solution.py:84
  171.6 0.7 copy-start.3
  172.3 9.4 %all-to-all-start.5 = ((bf16[3,320,128]{2,1,0:T(8,128)(2,1)}), bf16[3,320,128]{2,1,0:T(8,128)(2,1)S(1)}, u32[]{:S(2)}, u32[]{:S(2)}) async-start(bf16[3,320,128]{2,1,0:T(8,128)(2,1)} %copy-done.3), calls=%async_computation.5 | async-start | bytes 491520 | tf_op jit(solution)/shard_map/all_to_all | solution.py:24
  182.8 24.8 %copy-start.6 = (bf16[144,2048]{1,0:T(8,128)(2,1)S(1)}, bf16[144,2048]{1,0:T(8,128)(2,1)}, u32[]{:S(2)}) copy-start(bf16[144,2048]{1,0:T(8,128)(2,1)} %copy-done.5) | copy-start | bytes 1769476
  182.8 24.8 %all-to-all-start.6 = ((bf16[8,160,256]{2,1,0:T(8,128)(2,1)}), bf16[8,160,256]{2,1,0:T(8,128)(2,1)S(1)}, u32[]{:S(2)}, u32[]{:S(2)}) async-start(bf16[8,160,256]{2,1,0:T(8,128)(2,1)} %broadcast_in_dim.14), calls=%async_computation.6 | async-start | bytes 1310720 | tf_op jit(solution)/shard_map/all_to_all | solution.py:20
  192.0 13.5 %collective-permute-start.14 = (bf16[16,2048]{1,0:T(8,128)(2,1)S(1)}, bf16[16,2048]{1,0:T(8,128)(2,1)S(1)}, u32[]{:S(2)}, u32[]{:S(2)}) collective-permute-start(bf16[16,2048]{1,0:T(8,128)(2,1)S(1)} %fusion.27), channel_id=1, source_target_pairs={{0,96},{96,192},{192,288},{288,384},{384,480},{480,576},{576,672},... | collective-permute-start | bytes 196616 | tf_op jit(solution)/shard_map/ppermute | solution.py:259
  195.5 23.9 %copy-start.20 = (f32[16,2]{0,1:T(2,128)S(1)}, f32[16,2]{0,1:T(2,128)}, u32[]{:S(2)}) copy-start(f32[16,2]{0,1:T(2,128)} %param.18) | copy-start | bytes 388
  195.5 10.1 %collective-permute-start.15 = (bf16[16,2048]{1,0:T(8,128)(2,1)S(1)}, bf16[16,2048]{1,0:T(8,128)(2,1)S(1)}, u32[]{:S(2)}, u32[]{:S(2)}) collective-permute-start(bf16[16,2048]{1,0:T(8,128)(2,1)S(1)} %fusion.23), channel_id=1, source_target_pairs={{96,0},{192,96},{288,192},{384,288},{480,384},{576,480},{672,576},... | collective-permute-start | bytes 196616 | tf_op jit(solution)/shard_map/ppermute | solution.py:259
  211.3 13.9 %all-to-all-start.7 = ((bf16[4,160,256]{2,1,0:T(8,128)(2,1)}), bf16[4,160,256]{2,1,0:T(8,128)(2,1)S(1)}, u32[]{:S(2)}, u32[]{:S(2)}) async-start(bf16[4,160,256]{2,1,0:T(8,128)(2,1)} %shard_map.154), calls=%async_computation.7 | async-start | bytes 655360 | tf_op jit(solution)/shard_map/all_to_all | solution.py:24
  225.2 0.9 copy-start.18
  225.6 2.0 copy-start.16

commit v5 on v4

--- a/solution.py
+++ b/solution.py
@@ -65,19 +65,19 @@
     return 9 * (place // 2) + 4 * (place % 2) + half
 
 
-def quad_cut_kernel(me_ref, rows_ref, own_ref, core_ref, chip_ref):
-    me = me_ref[0]
-    places = ((own_ref, 0), (core_ref, 0), (chip_ref, 0), (chip_ref, 144))
-    for step, (out_ref, row) in enumerate(places):
+def quad_cut_kernel(me_ref, rows_ref, *out_refs):
+    me = me_ref[0]
+    for step, out_ref in enumerate(out_refs):
         other = lax.bitwise_xor(me, step)
         for y in range(8):
             start = pl.multiple_of((window(y, 0) + other) * 128, 128)
-            out_ref[row : row + 144, y * 256 : (y + 1) * 256] = rows_ref[:, pl.ds(start, 256)]
+            back = lax.rem(256 - 64 * (y % 2) - 16 * other, 256)
+            packed = pltpu.roll(rows_ref[:, pl.ds(start, 256)].astype(F32), back, 1)
+            out_ref[:, 144 * y : 144 * (y + 1)] = packed[:, :144].astype(BF)
 
 
 def quad_cut(me, rows):
-    shapes = [jax.ShapeDtypeStruct((count, 2048), BF) for count in (144, 144, 288)]
-    return call(quad_cut_kernel, shapes, (me, rows))
+    return call(quad_cut_kernel, [jax.ShapeDtypeStruct((144, 1152), BF)] * 4, (me, rows))
 
 
 def quad_send(piece, step):
@@ -94,33 +94,31 @@
             out_ref[128:, g * 128 : (g + 1) * 128] = second_ref[:, pl.ds(start, 128)]
 
 
-def ring_tables(me, first, second):
-    pieces = call(ring_cut_kernel, [jax.ShapeDtypeStruct((256, 1024), BF)] * 3, (me, first, second))
+def ring_cut(me, first, second):
+    return call(ring_cut_kernel, [jax.ShapeDtypeStruct((256, 1024), BF)] * 3, (me, first, second))
+
+
+def ring_tables(pieces):
     moved = [
         lax.ppermute(pieces[step], "zl", [(i, (i + step) % 3) for i in range(3)]) for step in (1, 2)
     ]
     return [pieces[0]] + moved
 
 
-def x_kernel(me_ref, held_ref, t0, t1, t2, t3, out_ref, placed):
-    me = me_ref[0]
-    placed[...] = jnp.zeros_like(placed)
-    for y in range(8):
-        start = pl.multiple_of(256 * y + 64 * (y % 2) + 16 * me, 16)
-        placed[pl.ds(start, 144), :] = held_ref[y]
+def x_kernel(me_ref, held_ref, t0, t1, t2, t3, out_ref):
+    me = me_ref[0]
     for step, table in enumerate((t0, t1, t2, t3)):
-        part = jnp.dot(table[:144, :], placed[...], preferred_element_type=F32)
+        part = jnp.dot(table[...], held_ref[...], preferred_element_type=F32)
         out_ref[lax.bitwise_xor(me, step)] = part.astype(BF)
 
 
 def transform_x(me, block, table):
-    held = gather(block, "y", 8)
+    held = gather(block, "y", 8).reshape(1152, 256)
     parts = call(
         x_kernel,
         jax.ShapeDtypeStruct((4, 144, 256), BF),
         (me, held, *table),
-        [pltpu.VMEM((2048, 256), BF)],
-        flops=2 * 576 * 2048 * 256,
+        flops=2 * 576 * 1152 * 256,
     )
     return scatter_sum(parts, QUAD)
 
@@ -157,22 +155,19 @@
 
 def x_back_kernel(me_ref, held_ref, t0, t1, t2, t3, lo_ref, hi_ref, out_ref, placed, side, last, first, sums):
     me = me_ref[0]
-    placed[...] = jnp.zeros_like(placed)
     sums[...] = jnp.zeros_like(sums)
     for y in range(8):
-        shift = 64 * (y % 2) + 16 * me
-        placed[pl.ds(pl.multiple_of(256 * y + shift, 16), 144), :] = held_ref[y, :144, :]
-        turned = pltpu.roll(held_ref[y, 144:160, :].astype(F32), shift, 1)
-        side[:, 256 * y : 256 * (y + 1)] = turned.astype(BF)
+        placed[144 * y : 144 * (y + 1), :] = held_ref[y, :144, :]
+        side[:, 144 * y : 144 * (y + 1)] = held_ref[y, 144:160, :144]
     last[0] = jnp.dot(lo_ref[...], placed[...], preferred_element_type=F32)[8:16]
     first[5] = jnp.dot(hi_ref[...], placed[...], preferred_element_type=F32)[:8]
     for step, table in enumerate((t0, t1, t2, t3)):
         target = lax.bitwise_xor(me, step)
-        part = jnp.dot(table[:144, :], placed[...], preferred_element_type=F32)
+        part = jnp.dot(table[...], placed[...], preferred_element_type=F32)
         out_ref[target, :144, :] = part.astype(BF)
         last[target + 1] = part[136:144]
         first[target + 1] = part[:8]
-        sums[target, :, :144] = nt_dot(side[...], table[:144, :])
+        sums[target, :, :144] = nt_dot(side[...], table[...])
     row = lax.broadcasted_iota(jnp.int32, (16, 256), 0)
     for target in range(4):
         low = jnp.broadcast_to(last[target][7:8], (16, 256))
@@ -184,8 +179,8 @@
 def transform_x_back(me, block, table, outer):
     held = gather(block, "y", 8)
     scratch = [
-        pltpu.VMEM((2048, 256), BF),
-        pltpu.VMEM((16, 2048), BF),
+        pltpu.VMEM((1152, 256), BF),
+        pltpu.VMEM((16, 1152), BF),
         pltpu.VMEM((5, 8, 256), F32),
         pltpu.VMEM((6, 8, 256), F32),
         pltpu.VMEM((4, 16, 256), F32),
@@ -195,7 +190,7 @@
         jax.ShapeDtypeStruct((4, 160, 256), BF),
         (me, held, *table, *outer),
         scratch,
-        flops=2 * 576 * 2048 * 256,
+        flops=2 * 576 * 1152 * 256,
     )
     return scatter_sum(parts, QUAD)
 
@@ -301,23 +296,23 @@
     divergence = (mask_f[None] * (centre_x(flux_u) + centre_y(flux_v))).astype(BF)
     quad_me = (lax.axis_index("xl") * 2 + lax.axis_index("c")).astype(jnp.int32).reshape(1)
     ring_me = lax.axis_index("zl").astype(jnp.int32).reshape(1)
-    cut_fx = quad_cut(quad_me, forward_x)
-    divergence, fx_chip = lax.optimization_barrier((divergence, quad_send(cut_fx[2], 2)))
-    table_fx = (cut_fx[0], quad_send(cut_fx[1], 1), fx_chip, quad_send(fx_chip[144:], 1))
-    table_y = ring_tables(ring_me, forward_y, inverse_y)
+    cut_fx, cut_y = quad_cut(quad_me, forward_x), ring_cut(ring_me, forward_y, inverse_y)
+    divergence, cut_fx, cut_y = lax.optimization_barrier((divergence, cut_fx, cut_y))
+    table_fx = [cut_fx[0]] + [quad_send(cut_fx[step], step) for step in (1, 2, 3)]
+    table_y = ring_tables(cut_y)
     spec_x = transform_x(quad_me, to_x(divergence.reshape(288, 128)), table_fx).astype(BF)
     spec_x, table_y = lax.optimization_barrier((spec_x, table_y))
     spec_xy = transform_y(ring_me, to_y(spec_x), table_y, 0).reshape(2, 144, 128)
     cut_ix = quad_cut(quad_me, inverse_x)
-    spec_xy, ix_chip = lax.optimization_barrier((spec_xy, quad_send(cut_ix[2], 2)))
+    spec_xy, ix_two = lax.optimization_barrier((spec_xy, quad_send(cut_ix[2], 2)))
     denom = eigen_x[None, :, None] + eigen_y[None, None, :] + mode_shift[:, None, None]
     scaled = (spec_xy / denom).astype(BF)
     outer_y = ring_outer(ring_me[0], table_y)
     back_y = transform_y_back(ring_me, scaled.reshape(288, 128), table_y, outer_y).astype(BF)
     back_y, ix_one, ix_three = lax.optimization_barrier(
-        (back_y, quad_send(cut_ix[1], 1), quad_send(ix_chip[144:], 1))
-    )
-    table_ix = (cut_ix[0], ix_one, ix_chip, ix_three)
+        (back_y, quad_send(cut_ix[1], 1), quad_send(cut_ix[3], 3))
+    )
+    table_ix = (cut_ix[0], ix_one, ix_two, ix_three)
     outer_x = quad_outer(quad_me[0], table_ix)
     total = transform_x_back(quad_me, with_sides(back_y), table_ix, outer_x)
     pressure = to_y(total[:144]).reshape(2, 144, 128)

time: 229 us -> 226 us (0.987)
  blocking collectives: 8.71 us -> 48.5 us
  waiting for transfers between devices: 69 us -> 40.3 us
  starting transfers between devices: 116 us -> 103 us
  local copies, waits for them, and re-layouts: 18.4 us -> 8.26 us
  Pallas kernels: 10.9 us -> 15.3 us
  other arithmetic: 3.33 us -> 6.18 us
    all_to_all x0 -> x1, blocking collectives: none -> 40.2 us  [gather(): lax.all_to_all(jnp.broadcast_to(block[None], (count,) + block.shape), axe...]
    all_to_all x4 -> x3, starting transfers between devices: 40.2 us -> 14.6 us  [gather(): lax.all_to_all(jnp.broadcast_to(block[None], (count,) + block.shape), axe...]
    all_to_all x4 -> x3, waiting for transfers between devices: 20.2 us -> 3.63 us  [gather(): lax.all_to_all(jnp.broadcast_to(block[None], (count,) + block.shape), axe...]
    ppermute x6, waiting for transfers between devices: 3.12 us -> 15.3 us  [quad_send(): return lax.ppermute(piece, QUAD, [(i, i ^ step) for i in range(4)])]
    ppermute x1, waiting for transfers between devices: 10.4 us -> 0.45 us  [ring_outer(): lax.ppermute(high, ('xh', 'zh'), down)]
    ppermute x2, waiting for transfers between devices: 9.41 us -> 0.01 us  [edges(): high = lax.ppermute(lax.slice_in_dim(block, 0, 1, axis=dim), axes, backward)]
    all_to_all x3, starting transfers between devices: 23.4 us -> 32.3 us  [scatter_sum(): return jnp.sum(lax.all_to_all(parts, axes, 0, 0).astype(F32), axis=0)]
    unnamed x47 -> x41, local copies, waits for them, and re-layouts: 9.79 us -> 3.46 us
  transfers between devices with their start and end apart: 23 -> 22, of which waited for: 12 -> 9; matrix products, arithmetic and copies ran while one was open for 3% -> 2% of each run, Pallas kernels for 3% -> 5%
where the time goes in v5:
time: 226 us; the launch traced here: 225 us
  starting transfers between devices  103 us (46%)
  blocking collectives  48.5 us (21%)
  waiting for transfers between devices  40.3 us (18%)
  Pallas kernels  15.3 us (7%)
  local copies, waits for them, and re-layouts  8.26 us (4%)
  other arithmetic  6.18 us (3%)
    all_to_all x1, blocking collectives, gather(): lax.all_to_all(jnp.broadcast_to(block[None], (count,) + block.shape), axe...  40.2 us
    all_to_all x3, starting transfers between devices, scatter_sum(): return jnp.sum(lax.all_to_all(parts, axes, 0, 0).astype(F32), axis=0)  32.3 us
    ppermute x6, starting transfers between devices, quad_send(): return lax.ppermute(piece, QUAD, [(i, i ^ step) for i in range(4)])  19.5 us
    ppermute x6, waiting for transfers between devices, quad_send(): return lax.ppermute(piece, QUAD, [(i, i ^ step) for i in range(4)])  15.3 us
    pallas_call x7, Pallas kernels, call(): pl.pallas_call(kernel, out_shape=out_shape, in_specs=[smem] + [vmem] * (l...  15.3 us
    all_to_all x3, starting transfers between devices, gather(): lax.all_to_all(jnp.broadcast_to(block[None], (count,) + block.shape), axe...  14.6 us
    all_to_all x3, waiting for transfers between devices, scatter_sum(): return jnp.sum(lax.all_to_all(parts, axes, 0, 0).astype(F32), axis=0)  10.2 us
    ppermute x2, starting transfers between devices, edges(): lax.ppermute(lax.slice_in_dim(block, block.shape[dim] - 1, None, axis=dim...  9.54 us
  transfers between devices with their start and end apart: 22, of which 9 were waited for; matrix products, arithmetic and copies ran while one was open for 2% of the time, Pallas kernels for 5%

profile of v5, /device:TPU:1, one launch (start us, length us, event | category | flops | bytes accessed | tf_op | source)
XLA Modules:
  0.0 224.7 jit_solution(4059335446180149091)
XLA Ops:
  0.6 1.6 fusion.8
  2.3 0.9 fusion.46
  3.2 0.8 fusion.45
  4.0 5.6 %collective-permute-start.3 = (bf16[2,144,1]{2,0,1:T(2,128)(2,1)S(1)}, bf16[2,144,1]{2,0,1:T(2,128)(2,1)}, u32[]{:S(2)}, u32[]{:S(2)}) collective-permute-start(bf16[2,144,1]{2,0,1:T(2,128)(2,1)S(1)} %get-tuple-element.102), channel_id=1, source_target_pairs={{0,1},{1,2},{2,3},{3,4},{4,5},{5,6},{6,7},{7,8},{8,9},{9,10},{10,1... | collective-permute-start | bytes 1736 | tf_op jit(solution)/shard_map/ppermute | solution.py:32
  9.6 1.3 collective-permute-start.2
  10.8 0.9 fusion.47
  11.7 4.0 %collective-permute-start.1 = (bf16[2,1,128]{2,0,1:T(2,128)(2,1)S(1)}, bf16[2,1,128]{2,0,1:T(2,128)(2,1)S(1)}, u32[]{:S(2)}, u32[]{:S(2)}) collective-permute-start(bf16[2,1,128]{2,0,1:T(2,128)(2,1)S(1)} %get-tuple-element.100), channel_id=1, source_target_pairs={{0,24},{24,48},{48,72},{72,96},{96,120},{120,144},{144,168},{168,1... | collective-permute-start | bytes 1544 | tf_op jit(solution)/shard_map/ppermute | solution.py:32
  15.7 6.8 %collective-permute-start = (bf16[2,1,128]{2,0,1:T(2,128)(2,1)S(1)}, bf16[2,1,128]{2,0,1:T(2,128)(2,1)S(1)}, u32[]{:S(2)}, u32[]{:S(2)}) collective-permute-start(bf16[2,1,128]{2,0,1:T(2,128)(2,1)S(1)} %get-tuple-element.99), channel_id=1, source_target_pairs={{24,0},{48,24},{72,48},{96,72},{120,96},{144,120},{168,144},{192,1... | collective-permute-start | bytes 1544 | tf_op jit(solution)/shard_map/ppermute | solution.py:33
  23.2 3.7 %shard_map.148 = (bf16[144,1152]{1,0:T(8,128)(2,1)S(1)}, bf16[144,1152]{1,0:T(8,128)(2,1)}, bf16[144,1152]{1,0:T(8,128)(2,1)}, bf16[144,1152]{1,0:T(8,128)(2,1)}) custom-call(s32[1]{0:T(128)} %bitcast.1.me_ref, bf16[144,4608]{1,0:T(8,128)(2,1)S(1)} %copy-done.1), custom_call_target="tpu_custom_call" | custom-call | bytes 2654208 | tf_op jit(solution)/shard_map/pallas_call | solution.py:53
  26.9 1.1 shard_map.149
  28.0 1.0 convert_element_type.75
  29.8 0.9 broadcast_in_dim.10
  30.7 3.5 %all-to-all-start = ((bf16[8,144,256]{2,1,0:T(8,128)(2,1)}), bf16[8,144,256]{2,1,0:T(8,128)(2,1)S(1)}, u32[]{:S(2)}, u32[]{:S(2)}) async-start(bf16[8,144,256]{2,1,0:T(8,128)(2,1)} %broadcast_in_dim.10), calls=%async_computation | async-start | bytes 1179648 | tf_op jit(solution)/shard_map/all_to_all | solution.py:20
  34.2 5.8 %collective-permute-start.4 = (bf16[144,1152]{1,0:T(8,128)(2,1)}, bf16[144,1152]{1,0:T(8,128)(2,1)S(1)}, u32[]{:S(2)}, u32[]{:S(2)}) collective-permute-start(bf16[144,1152]{1,0:T(8,128)(2,1)} %get-tuple-element.40), channel_id=1, source_target_pairs={{0,24},{24,0},{48,72},{72,48},{1,25},{25,1},{49,73},{73,49},{2,26}... | collective-permute-start | bytes 995336 | tf_op jit(solution)/shard_map/ppermute | solution.py:84
  40.0 1.9 collective-permute-start.5
  41.9 3.5 %collective-permute-start.6 = (bf16[144,1152]{1,0:T(8,128)(2,1)}, bf16[144,1152]{1,0:T(8,128)(2,1)S(1)}, u32[]{:S(2)}, u32[]{:S(2)}) collective-permute-start(bf16[144,1152]{1,0:T(8,128)(2,1)} %get-tuple-element.42), channel_id=1, source_target_pairs={{0,72},{24,48},{48,24},{72,0},{1,73},{25,49},{49,25},{73,1},{2,74}... | collective-permute-start | bytes 995336 | tf_op jit(solution)/shard_map/ppermute | solution.py:84
  45.5 4.3 %collective-permute-start.7 = (bf16[256,1024]{1,0:T(8,128)(2,1)}, bf16[256,1024]{1,0:T(8,128)(2,1)S(1)}, u32[]{:S(2)}, u32[]{:S(2)}) collective-permute-start(bf16[256,1024]{1,0:T(8,128)(2,1)} %get-tuple-element.44), channel_id=1, source_target_pairs={{0,1},{1,2},{2,0},{3,4},{4,5},{5,3},{6,7},{7,8},{8,6},{9,10},{10,1... | collective-permute-start | bytes 1572872 | tf_op jit(solution)/shard_map/ppermute | solution.py:103
  49.8 1.9 collective-permute-start.8
  51.7 7.3 %collective-permute-done.6.t3 = bf16[144,1152]{1,0:T(8,128)(2,1)S(1)} collective-permute-done((bf16[144,1152]{1,0:T(8,128)(2,1)}, bf16[144,1152]{1,0:T(8,128)(2,1)S(1)}, u32[]{:S(2)}, u32[]{:S(2)}) %collective-permute-start.6) | collective-permute-done | bytes 331808 | tf_op jit(solution)/shard_map/ppermute | solution.py:84
  59.7 1.0 copy-done.6
  61.3 8.3 %all_to_all.40 = bf16[4,144,256]{2,1,0:T(8,128)(2,1)S(1)} all-to-all(bf16[4,144,256]{2,1,0:T(8,128)(2,1)S(1)} %shard_map.150), channel_id=1, replica_groups=mesh['y'=8,'xl'=2,'c'=2,'xh'=2,'zh'=4,'zl'=3] {'xl','c'}, dimensions={0} | all-to-all | bytes 589824 | tf_op jit(solution)/shard_map/all_to_all | solution.py:24
  69.6 4.0 %collective-permute-done.8.t2 = bf16[256,1024]{1,0:T(8,128)(2,1)S(1)} collective-permute-done((bf16[256,1024]{1,0:T(8,128)(2,1)}, bf16[256,1024]{1,0:T(8,128)(2,1)S(1)}, u32[]{:S(2)}, u32[]{:S(2)}) %collective-permute-start.8) | collective-permute-done | bytes 524320 | tf_op jit(solution)/shard_map/ppermute | solution.py:103
  73.7 40.2 %all_to_all.41.held_ref = bf16[8,288,128]{2,1,0:T(8,128)(2,1)S(1)} all-to-all(bf16[8,288,128]{2,1,0:T(8,128)(2,1)S(1)} %broadcast_in_dim.11), channel_id=1, replica_groups=mesh['y'=8,'xl'=2,'c'=2,'xh'=2,'zh'=4,'zl'=3] {'xh','zh'}, dimensions={0} | all-to-all | bytes 1179648 | tf_op jit(solution)/shard_map/all_to_all | solution.py:20
  113.9 1.4 shard_map.151
  115.2 6.4 %all-to-all-start.3 = ((bf16[3,288,128]{2,1,0:T(8,128)(2,1)}), bf16[3,288,128]{2,1,0:T(8,128)(2,1)S(1)}, u32[]{:S(2)}, u32[]{:S(2)}) async-start(bf16[3,288,128]{2,1,0:T(8,128)(2,1)} %shard_map.151), calls=%async_computation.3 | async-start | bytes 442368 | tf_op jit(solution)/shard_map/all_to_all | solution.py:24
  121.7 3.5 %shard_map.152 = (bf16[144,1152]{1,0:T(8,128)(2,1)S(1)}, bf16[144,1152]{1,0:T(8,128)(2,1)S(1)}, bf16[144,1152]{1,0:T(8,128)(2,1)}, bf16[144,1152]{1,0:T(8,128)(2,1)S(1)}) custom-call(s32[1]{0:T(128)} %bitcast.1.me_ref, bf16[144,4608]{1,0:T(8,128)(2,1)S(1)} %copy-done.2), custom_call_target="tpu_custom_call" | custom-call | bytes 2654208 | tf_op jit(solution)/shard_map/pallas_call | solution.py:53
  126.6 1.9 collective-permute-start.9
  128.7 8.0 %collective-permute-done.9.t2 = bf16[144,1152]{1,0:T(8,128)(2,1)S(1)} collective-permute-done((bf16[144,1152]{1,0:T(8,128)(2,1)}, bf16[144,1152]{1,0:T(8,128)(2,1)S(1)}, u32[]{:S(2)}, u32[]{:S(2)}) %collective-permute-start.9) | collective-permute-done | bytes 331808 | tf_op jit(solution)/shard_map/ppermute | solution.py:84
  136.8 0.9 broadcast_in_dim.13
  137.6 4.1 %all-to-all-start.4 = ((bf16[8,288,128]{2,1,0:T(8,128)(2,1)}), bf16[8,288,128]{2,1,0:T(8,128)(2,1)S(1)}, u32[]{:S(2)}, u32[]{:S(2)}) async-start(bf16[8,288,128]{2,1,0:T(8,128)(2,1)} %broadcast_in_dim.13), calls=%async_computation.4 | async-start | bytes 1179648 | tf_op jit(solution)/shard_map/all_to_all | solution.py:20
  141.9 5.2 %collective-permute-start.10 = (bf16[16,1024]{1,0:T(8,128)(2,1)S(1)}, bf16[16,1024]{1,0:T(8,128)(2,1)S(1)}, u32[]{:S(2)}, u32[]{:S(2)}) collective-permute-start(bf16[16,1024]{1,0:T(8,128)(2,1)S(1)} %fusion.33), channel_id=1, source_target_pairs={{0,3},{3,6},{6,9},{9,12},{12,15},{15,18},{18,21},{1,4},{4,7},{7,10... | collective-permute-start | bytes 98312 | tf_op jit(solution)/shard_map/ppermute | solution.py:246
  147.1 1.3 collective-permute-start.11
  148.4 4.4 %collective-permute-start.12 = (bf16[144,1152]{1,0:T(8,128)(2,1)}, bf16[144,1152]{1,0:T(8,128)(2,1)S(1)}, u32[]{:S(2)}, u32[]{:S(2)}) collective-permute-start(bf16[144,1152]{1,0:T(8,128)(2,1)} %copy-done.9), channel_id=1, source_target_pairs={{0,24},{24,0},{48,72},{72,48},{1,25},{25,1},{49,73},{73,49},{2,26}... | collective-permute-start | bytes 995336 | tf_op jit(solution)/shard_map/ppermute | solution.py:84
  152.8 1.9 collective-permute-start.13
  155.3 2.3 %shard_map.153 = bf16[3,320,128]{2,1,0:T(8,128)(2,1)} custom-call(s32[1]{0:T(128)} %bitcast.2.me_ref, bf16[8,288,128]{2,1,0:T(8,128)(2,1)S(1)} %all-to-all-done.4.held_ref, bf16[256,1024]{1,0:T(8,128)(2,1)S(1)} %get-tuple-element.47.t0, bf16[256,1024]{1,0:T(8,128)(2,1)S(1)} %collective-permute-done.7.t1, bf16[256,1024]{1,0:T(8,128)(2,1)S(1)} %collective-permute-done.8.t2, ...), custom_call_target="tpu_custom_call" | custom-call | flops 226492416 | bytes 2473984 | tf_op jit(solution)/shard_map/pallas_call | solution.py:53
  157.6 18.5 %all-to-all-start.5 = ((bf16[3,320,128]{2,1,0:T(8,128)(2,1)}), bf16[3,320,128]{2,1,0:T(8,128)(2,1)S(1)}, u32[]{:S(2)}, u32[]{:S(2)}) async-start(bf16[3,320,128]{2,1,0:T(8,128)(2,1)} %shard_map.153), calls=%async_computation.5 | async-start | bytes 491520 | tf_op jit(solution)/shard_map/all_to_all | solution.py:24
  176.1 4.4 %all-to-all-done.5 = bf16[3,320,128]{2,1,0:T(8,128)(2,1)S(1)} async-done(((bf16[3,320,128]{2,1,0:T(8,128)(2,1)}), bf16[3,320,128]{2,1,0:T(8,128)(2,1)S(1)}, u32[]{:S(2)}, u32[]{:S(2)}) %all-to-all-start.5) | async-done | bytes 245792 | tf_op jit(solution)/shard_map/all_to_all | solution.py:24
  180.6 0.9 broadcast_in_dim.14
  181.5 6.9 %all-to-all-start.6 = ((bf16[8,160,256]{2,1,0:T(8,128)(2,1)}), bf16[8,160,256]{2,1,0:T(8,128)(2,1)S(1)}, u32[]{:S(2)}, u32[]{:S(2)}) async-start(bf16[8,160,256]{2,1,0:T(8,128)(2,1)} %broadcast_in_dim.14), calls=%async_computation.6 | async-start | bytes 1310720 | tf_op jit(solution)/shard_map/all_to_all | solution.py:20
  188.4 0.8 slice_bitcast_fusion.4
  189.3 3.4 %collective-permute-start.14 = (bf16[16,1152]{1,0:T(8,128)(2,1)S(1)}, bf16[16,1152]{1,0:T(8,128)(2,1)S(1)}, u32[]{:S(2)}, u32[]{:S(2)}) collective-permute-start(bf16[16,1152]{1,0:T(8,128)(2,1)S(1)} %fusion.27), channel_id=1, source_target_pairs={{0,96},{96,192},{192,288},{288,384},{384,480},{480,576},{576,672},... | collective-permute-start | bytes 110600 | tf_op jit(solution)/shard_map/ppermute | solution.py:254
  192.7 3.1 %collective-permute-start.15 = (bf16[16,1152]{1,0:T(8,128)(2,1)S(1)}, bf16[16,1152]{1,0:T(8,128)(2,1)S(1)}, u32[]{:S(2)}, u32[]{:S(2)}) collective-permute-start(bf16[16,1152]{1,0:T(8,128)(2,1)S(1)} %fusion.23), channel_id=1, source_target_pairs={{96,0},{192,96},{288,192},{384,288},{480,384},{576,480},{672,576},... | collective-permute-start | bytes 110600 | tf_op jit(solution)/shard_map/ppermute | solution.py:254
  195.9 6.7 %collective-permute-done.14.lo_ref = bf16[16,1152]{1,0:T(8,128)(2,1)S(1)} collective-permute-done((bf16[16,1152]{1,0:T(8,128)(2,1)S(1)}, bf16[16,1152]{1,0:T(8,128)(2,1)S(1)}, u32[]{:S(2)}, u32[]{:S(2)}) %collective-permute-start.14) | collective-permute-done | bytes 36896 | tf_op jit(solution)/shard_map/ppermute | solution.py:254
  202.6 3.5 %all-to-all-done.6.held_ref = bf16[8,160,256]{2,1,0:T(8,128)(2,1)S(1)} async-done(((bf16[8,160,256]{2,1,0:T(8,128)(2,1)}), bf16[8,160,256]{2,1,0:T(8,128)(2,1)S(1)}, u32[]{:S(2)}, u32[]{:S(2)}) %all-to-all-start.6) | async-done | bytes 655392 | tf_op jit(solution)/shard_map/all_to_all | solution.py:20
  206.1 2.8 %shard_map.154 = bf16[4,160,256]{2,1,0:T(8,128)(2,1)} custom-call(s32[1]{0:T(128)} %bitcast.1.me_ref, bf16[8,160,256]{2,1,0:T(8,128)(2,1)S(1)} %all-to-all-done.6.held_ref, bf16[144,1152]{1,0:T(8,128)(2,1)S(1)} %get-tuple-element.55.t0, bf16[144,1152]{1,0:T(8,128)(2,1)S(1)} %collective-permute-done.12.t1, bf16[144,1152]{1,0:T(8,128)(2,1)S(1)} %collective-permute-done.9.t2, ...), custom_call_target="tpu_custom_call" | custom-call | flops 339738624 | bytes 2383872 | tf_op jit(solution)/shard_map/pallas_call | solution.py:53
  208.9 7.4 %all-to-all-start.7 = ((bf16[4,160,256]{2,1,0:T(8,128)(2,1)}), bf16[4,160,256]{2,1,0:T(8,128)(2,1)S(1)}, u32[]{:S(2)}, u32[]{:S(2)}) async-start(bf16[4,160,256]{2,1,0:T(8,128)(2,1)} %shard_map.154), calls=%async_computation.7 | async-start | bytes 655360 | tf_op jit(solution)/shard_map/all_to_all | solution.py:24
  216.3 5.9 %all-to-all-done.7 = bf16[4,160,256]{2,1,0:T(8,128)(2,1)S(1)} async-done(((bf16[4,160,256]{2,1,0:T(8,128)(2,1)}), bf16[4,160,256]{2,1,0:T(8,128)(2,1)S(1)}, u32[]{:S(2)}, u32[]{:S(2)}) %all-to-all-start.7) | async-done | bytes 327712 | tf_op jit(solution)/shard_map/all_to_all | solution.py:24
  223.1 1.6 fusion.4
  (99 shorter events, 6.2 us)
Async XLA Ops:
  0.6 1.7 copy-start
  2.3 20.3 %copy-start.10 = (s32[144,128]{1,0:T(8,128)S(1)}, s32[144,128]{1,0:T(8,128)}, u32[]{:S(2)}) copy-start(s32[144,128]{1,0:T(8,128)} %param.15) | copy-start | bytes 221188
  2.3 20.9 %copy-start.1 = (bf16[144,4608]{1,0:T(8,128)(2,1)S(1)}, bf16[144,4608]{1,0:T(8,128)(2,1)}, u32[]{:S(2)}) copy-start(bf16[144,4608]{1,0:T(8,128)(2,1)} %rows_ref.2) | copy-start | bytes 3981316
  4.0 22.9 %copy-start.3 = (bf16[128,3072]{1,0:T(8,128)(2,1)S(1)}, bf16[128,3072]{1,0:T(8,128)(2,1)}, u32[]{:S(2)}) copy-start(bf16[128,3072]{1,0:T(8,128)(2,1)} %first_ref.1) | copy-start | bytes 2359300
  4.0 22.9 %copy-start.4 = (bf16[128,3072]{1,0:T(8,128)(2,1)S(1)}, bf16[128,3072]{1,0:T(8,128)(2,1)}, u32[]{:S(2)}) copy-start(bf16[128,3072]{1,0:T(8,128)(2,1)} %second_ref.1) | copy-start | bytes 2359300
  4.0 24.0 %collective-permute-start.3 = (bf16[2,144,1]{2,0,1:T(2,128)(2,1)S(1)}, bf16[2,144,1]{2,0,1:T(2,128)(2,1)}, u32[]{:S(2)}, u32[]{:S(2)}) collective-permute-start(bf16[2,144,1]{2,0,1:T(2,128)(2,1)S(1)} %get-tuple-element.102), channel_id=1, source_target_pairs={{0,1},{1,2},{2,3},{3,4},{4,5},{5,6},{6,7},{7,8},{8,9},{9,10},{10,1... | collective-permute-start | bytes 1736 | tf_op jit(solution)/shard_map/ppermute | solution.py:32
  9.6 19.5 %collective-permute-start.2 = (bf16[2,144,1]{2,0,1:T(2,128)(2,1)}, bf16[2,144,1]{2,0,1:T(2,128)(2,1)S(1)}, u32[]{:S(2)}, u32[]{:S(2)}) collective-permute-start(bf16[2,144,1]{2,0,1:T(2,128)(2,1)} %get-tuple-element.101), channel_id=1, source_target_pairs={{1,0},{2,1},{3,2},{4,3},{5,4},{6,5},{7,6},{8,7},{9,8},{10,9},{11,1... | collective-permute-start | bytes 1736 | tf_op jit(solution)/shard_map/ppermute | solution.py:33
  11.7 16.3 %collective-permute-start.1 = (bf16[2,1,128]{2,0,1:T(2,128)(2,1)S(1)}, bf16[2,1,128]{2,0,1:T(2,128)(2,1)S(1)}, u32[]{:S(2)}, u32[]{:S(2)}) collective-permute-start(bf16[2,1,128]{2,0,1:T(2,128)(2,1)S(1)} %get-tuple-element.100), channel_id=1, source_target_pairs={{0,24},{24,48},{48,72},{72,96},{96,120},{120,144},{144,168},{168,1... | collective-permute-start | bytes 1544 | tf_op jit(solution)/shard_map/ppermute | solution.py:32
  15.7 12.3 %collective-permute-start = (bf16[2,1,128]{2,0,1:T(2,128)(2,1)S(1)}, bf16[2,1,128]{2,0,1:T(2,128)(2,1)S(1)}, u32[]{:S(2)}, u32[]{:S(2)}) collective-permute-start(bf16[2,1,128]{2,0,1:T(2,128)(2,1)S(1)} %get-tuple-element.99), channel_id=1, source_target_pairs={{24,0},{48,24},{72,48},{96,72},{120,96},{144,120},{168,144},{192,1... | collective-permute-start | bytes 1544 | tf_op jit(solution)/shard_map/ppermute | solution.py:33
  26.9 2.2 copy-start.12
  26.9 2.2 copy-start.13
  26.9 2.2 copy-start.15
  28.0 13.9 %copy-start.7 = (bf16[256,1024]{1,0:T(8,128)(2,1)}, bf16[256,1024]{1,0:T(8,128)(2,1)S(1)}, u32[]{:S(2)}) copy-start(bf16[256,1024]{1,0:T(8,128)(2,1)S(1)} %get-tuple-element.45) | copy-start | bytes 1572868
  30.7 29.1 %all-to-all-start = ((bf16[8,144,256]{2,1,0:T(8,128)(2,1)}), bf16[8,144,256]{2,1,0:T(8,128)(2,1)S(1)}, u32[]{:S(2)}, u32[]{:S(2)}) async-start(bf16[8,144,256]{2,1,0:T(8,128)(2,1)} %broadcast_in_dim.10), calls=%async_computation | async-start | bytes 1179648 | tf_op jit(solution)/shard_map/all_to_all | solution.py:20
  34.2 17.5 %collective-permute-start.4 = (bf16[144,1152]{1,0:T(8,128)(2,1)}, bf16[144,1152]{1,0:T(8,128)(2,1)S(1)}, u32[]{:S(2)}, u32[]{:S(2)}) collective-permute-start(bf16[144,1152]{1,0:T(8,128)(2,1)} %get-tuple-element.40), channel_id=1, source_target_pairs={{0,24},{24,0},{48,72},{72,48},{1,25},{25,1},{49,73},{73,49},{2,26}... | collective-permute-start | bytes 995336 | tf_op jit(solution)/shard_map/ppermute | solution.py:84
  40.0 11.7 %collective-permute-start.5 = (bf16[144,1152]{1,0:T(8,128)(2,1)}, bf16[144,1152]{1,0:T(8,128)(2,1)S(1)}, u32[]{:S(2)}, u32[]{:S(2)}) collective-permute-start(bf16[144,1152]{1,0:T(8,128)(2,1)} %get-tuple-element.41), channel_id=1, source_target_pairs={{0,48},{24,72},{48,0},{72,24},{1,49},{25,73},{49,1},{73,25},{2,50}... | collective-permute-start | bytes 995336 | tf_op jit(solution)/shard_map/ppermute | solution.py:84
  41.9 17.1 %collective-permute-start.6 = (bf16[144,1152]{1,0:T(8,128)(2,1)}, bf16[144,1152]{1,0:T(8,128)(2,1)S(1)}, u32[]{:S(2)}, u32[]{:S(2)}) collective-permute-start(bf16[144,1152]{1,0:T(8,128)(2,1)} %get-tuple-element.42), channel_id=1, source_target_pairs={{0,72},{24,48},{48,24},{72,0},{1,73},{25,49},{49,25},{73,1},{2,74}... | collective-permute-start | bytes 995336 | tf_op jit(solution)/shard_map/ppermute | solution.py:84
  45.5 24.1 %collective-permute-start.7 = (bf16[256,1024]{1,0:T(8,128)(2,1)}, bf16[256,1024]{1,0:T(8,128)(2,1)S(1)}, u32[]{:S(2)}, u32[]{:S(2)}) collective-permute-start(bf16[256,1024]{1,0:T(8,128)(2,1)} %get-tuple-element.44), channel_id=1, source_target_pairs={{0,1},{1,2},{2,0},{3,4},{4,5},{5,3},{6,7},{7,8},{8,6},{9,10},{10,1... | collective-permute-start | bytes 1572872 | tf_op jit(solution)/shard_map/ppermute | solution.py:103
  49.8 23.8 %collective-permute-start.8 = (bf16[256,1024]{1,0:T(8,128)(2,1)}, bf16[256,1024]{1,0:T(8,128)(2,1)S(1)}, u32[]{:S(2)}, u32[]{:S(2)}) collective-permute-start(bf16[256,1024]{1,0:T(8,128)(2,1)} %copy-done.7), channel_id=1, source_target_pairs={{0,2},{1,0},{2,1},{3,5},{4,3},{5,4},{6,8},{7,6},{8,7},{9,11},{10,9... | collective-permute-start | bytes 1572872 | tf_op jit(solution)/shard_map/ppermute | solution.py:103
  59.0 0.7 copy-start.5
  59.7 1.0 copy-start.6
  113.9 7.8 %copy-start.2 = (bf16[144,4608]{1,0:T(8,128)(2,1)S(1)}, bf16[144,4608]{1,0:T(8,128)(2,1)}, u32[]{:S(2)}) copy-start(bf16[144,4608]{1,0:T(8,128)(2,1)} %rows_ref.3) | copy-start | bytes 3981316
  115.2 13.3 %copy-start.16 = (f32[144]{0:T(256)S(1)}, f32[144]{0:T(256)}, u32[]{:S(2)}) copy-start(f32[144]{0:T(256)} %param.23) | copy-start | bytes 1732
  115.2 13.3 %copy-start.18 = (f32[128]{0:T(128)S(1)}, f32[128]{0:T(128)}, u32[]{:S(2)}) copy-start(f32[128]{0:T(128)} %param.24) | copy-start | bytes 1540
  115.2 21.4 %copy-start.19 = (f32[2]{0:T(128)S(1)}, f32[2]{0:T(128)}, u32[]{:S(2)}) copy-start(f32[2]{0:T(128)} %param.25) | copy-start | bytes 28
  115.2 13.4 %all-to-all-start.3 = ((bf16[3,288,128]{2,1,0:T(8,128)(2,1)}), bf16[3,288,128]{2,1,0:T(8,128)(2,1)S(1)}, u32[]{:S(2)}, u32[]{:S(2)}) async-start(bf16[3,288,128]{2,1,0:T(8,128)(2,1)} %shard_map.151), calls=%async_computation.3 | async-start | bytes 442368 | tf_op jit(solution)/shard_map/all_to_all | solution.py:24
  125.2 0.7 copy-start.8
  125.9 0.7 copy-start.9
  126.6 10.0 %collective-permute-start.9 = (bf16[144,1152]{1,0:T(8,128)(2,1)}, bf16[144,1152]{1,0:T(8,128)(2,1)S(1)}, u32[]{:S(2)}, u32[]{:S(2)}) collective-permute-start(bf16[144,1152]{1,0:T(8,128)(2,1)} %get-tuple-element.50), channel_id=1, source_target_pairs={{0,48},{24,72},{48,0},{72,24},{1,49},{25,73},{49,1},{73,25},{2,50}... | collective-permute-start | bytes 995336 | tf_op jit(solution)/shard_map/ppermute | solution.py:84
  137.6 17.6 %all-to-all-start.4 = ((bf16[8,288,128]{2,1,0:T(8,128)(2,1)}), bf16[8,288,128]{2,1,0:T(8,128)(2,1)S(1)}, u32[]{:S(2)}, u32[]{:S(2)}) async-start(bf16[8,288,128]{2,1,0:T(8,128)(2,1)} %broadcast_in_dim.13), calls=%async_computation.4 | async-start | bytes 1179648 | tf_op jit(solution)/shard_map/all_to_all | solution.py:20
  141.9 12.9 %collective-permute-start.10 = (bf16[16,1024]{1,0:T(8,128)(2,1)S(1)}, bf16[16,1024]{1,0:T(8,128)(2,1)S(1)}, u32[]{:S(2)}, u32[]{:S(2)}) collective-permute-start(bf16[16,1024]{1,0:T(8,128)(2,1)S(1)} %fusion.33), channel_id=1, source_target_pairs={{0,3},{3,6},{6,9},{9,12},{12,15},{15,18},{18,21},{1,4},{4,7},{7,10... | collective-permute-start | bytes 98312 | tf_op jit(solution)/shard_map/ppermute | solution.py:246
  147.1 8.1 %collective-permute-start.11 = (bf16[16,1024]{1,0:T(8,128)(2,1)S(1)}, bf16[16,1024]{1,0:T(8,128)(2,1)S(1)}, u32[]{:S(2)}, u32[]{:S(2)}) collective-permute-start(bf16[16,1024]{1,0:T(8,128)(2,1)S(1)} %fusion.30), channel_id=1, source_target_pairs={{3,0},{6,3},{9,6},{12,9},{15,12},{18,15},{21,18},{4,1},{7,4},{10,7... | collective-permute-start | bytes 98312 | tf_op jit(solution)/shard_map/ppermute | solution.py:246
  148.4 32.1 %collective-permute-start.12 = (bf16[144,1152]{1,0:T(8,128)(2,1)}, bf16[144,1152]{1,0:T(8,128)(2,1)S(1)}, u32[]{:S(2)}, u32[]{:S(2)}) collective-permute-start(bf16[144,1152]{1,0:T(8,128)(2,1)} %copy-done.9), channel_id=1, source_target_pairs={{0,24},{24,0},{48,72},{72,48},{1,25},{25,1},{49,73},{73,49},{2,26}... | collective-permute-start | bytes 995336 | tf_op jit(solution)/shard_map/ppermute | solution.py:84
  152.8 27.7 %collective-permute-start.13 = (bf16[144,1152]{1,0:T(8,128)(2,1)}, bf16[144,1152]{1,0:T(8,128)(2,1)}, u32[]{:S(2)}, u32[]{:S(2)}) collective-permute-start(bf16[144,1152]{1,0:T(8,128)(2,1)} %copy-done.8), channel_id=1, source_target_pairs={{0,72},{24,48},{48,24},{72,0},{1,73},{25,49},{49,25},{73,1},{2,74}... | collective-permute-start | bytes 995336 | tf_op jit(solution)/shard_map/ppermute | solution.py:84
  157.6 22.9 %all-to-all-start.5 = ((bf16[3,320,128]{2,1,0:T(8,128)(2,1)}), bf16[3,320,128]{2,1,0:T(8,128)(2,1)S(1)}, u32[]{:S(2)}, u32[]{:S(2)}) async-start(bf16[3,320,128]{2,1,0:T(8,128)(2,1)} %shard_map.153), calls=%async_computation.5 | async-start | bytes 491520 | tf_op jit(solution)/shard_map/all_to_all | solution.py:24
  181.5 24.6 %all-to-all-start.6 = ((bf16[8,160,256]{2,1,0:T(8,128)(2,1)}), bf16[8,160,256]{2,1,0:T(8,128)(2,1)S(1)}, u32[]{:S(2)}, u32[]{:S(2)}) async-start(bf16[8,160,256]{2,1,0:T(8,128)(2,1)} %broadcast_in_dim.14), calls=%async_computation.6 | async-start | bytes 1310720 | tf_op jit(solution)/shard_map/all_to_all | solution.py:20
  189.3 13.3 %collective-permute-start.14 = (bf16[16,1152]{1,0:T(8,128)(2,1)S(1)}, bf16[16,1152]{1,0:T(8,128)(2,1)S(1)}, u32[]{:S(2)}, u32[]{:S(2)}) collective-permute-start(bf16[16,1152]{1,0:T(8,128)(2,1)S(1)} %fusion.27), channel_id=1, source_target_pairs={{0,96},{96,192},{192,288},{288,384},{384,480},{480,576},{576,672},... | collective-permute-start | bytes 110600 | tf_op jit(solution)/shard_map/ppermute | solution.py:254
  192.7 23.6 %copy-start.17 = (f32[16,2]{0,1:T(2,128)S(1)}, f32[16,2]{0,1:T(2,128)}, u32[]{:S(2)}) copy-start(f32[16,2]{0,1:T(2,128)} %param.18) | copy-start | bytes 388
  192.7 9.8 %collective-permute-start.15 = (bf16[16,1152]{1,0:T(8,128)(2,1)S(1)}, bf16[16,1152]{1,0:T(8,128)(2,1)S(1)}, u32[]{:S(2)}, u32[]{:S(2)}) collective-permute-start(bf16[16,1152]{1,0:T(8,128)(2,1)S(1)} %fusion.23), channel_id=1, source_target_pairs={{96,0},{192,96},{288,192},{384,288},{480,384},{576,480},{672,576},... | collective-permute-start | bytes 110600 | tf_op jit(solution)/shard_map/ppermute | solution.py:254
  208.9 13.3 %all-to-all-start.7 = ((bf16[4,160,256]{2,1,0:T(8,128)(2,1)}), bf16[4,160,256]{2,1,0:T(8,128)(2,1)S(1)}, u32[]{:S(2)}, u32[]{:S(2)}) async-start(bf16[4,160,256]{2,1,0:T(8,128)(2,1)} %shard_map.154), calls=%async_computation.7 | async-start | bytes 655360 | tf_op jit(solution)/shard_map/all_to_all | solution.py:24
  222.2 0.9 copy-start.14
  222.7 2.1 copy-start.11

commit v6 on v5

--- a/solution.py
+++ b/solution.py
@@ -16,12 +16,8 @@
 F32 = jnp.float32
 
 
-def gather(block, axes, count):
-    return lax.all_to_all(jnp.broadcast_to(block[None], (count,) + block.shape), axes, 0, 0)
-
-
-def scatter_sum(parts, axes):
-    return jnp.sum(lax.all_to_all(parts, axes, 0, 0).astype(F32), axis=0)
+def exchange(parts, axes):
+    return lax.all_to_all(parts, axes, 0, 0)
 
 
 def edges(block, axes, dim, count, periodic):
@@ -112,15 +108,10 @@
         out_ref[lax.bitwise_xor(me, step)] = part.astype(BF)
 
 
-def transform_x(me, block, table):
-    held = gather(block, "y", 8).reshape(1152, 256)
-    parts = call(
-        x_kernel,
-        jax.ShapeDtypeStruct((4, 144, 256), BF),
-        (me, held, *table),
-        flops=2 * 576 * 1152 * 256,
-    )
-    return scatter_sum(parts, QUAD)
+def x_products(me, held, table):
+    held = held.reshape(1152, 256)
+    out = jax.ShapeDtypeStruct((4, 144, 256), BF)
+    return call(x_kernel, out, (me, held, *table), flops=2 * 576 * 1152 * 256)
 
 
 def y_kernel(offset, me_ref, held_ref, t0, t1, t2, out_ref, placed):
@@ -137,16 +128,50 @@
         out_ref[lax.rem(me + 3 - step, 3)] = part.astype(BF)
 
 
-def transform_y(me, block, table, offset):
-    held = gather(block, ("xh", "zh"), 8)
-    parts = call(
-        functools.partial(y_kernel, offset),
-        jax.ShapeDtypeStruct((3, 288, 128), BF),
-        (me, held, *table),
-        [pltpu.VMEM((288, 1024), BF)],
-        flops=2 * 288 * 1024 * 384,
-    )
-    return scatter_sum(parts, "zl")
+def y_products(me, held, table):
+    out = jax.ShapeDtypeStruct((3, 288, 128), BF)
+    scratch = [pltpu.VMEM((288, 1024), BF)]
+    return call(functools.partial(y_kernel, 0), out, (me, held, *table), scratch, flops=2 * 288 * 1024 * 384)
+
+
+def added(got_ref):
+    total = got_ref[0].astype(F32)
+    for source in range(1, got_ref.shape[0]):
+        total = total + got_ref[source].astype(F32)
+    return total
+
+
+def to_y_kernel(me_ref, got_ref, out_ref):
+    total = added(got_ref).astype(BF)
+    for g in range(8):
+        out_ref[g, :144, :] = total[:, :128]
+        out_ref[g, 144:, :] = total[:, 128:]
+
+
+def scale_kernel(shift_ref, got_ref, x_ref, y_ref, out_ref):
+    total = added(got_ref)
+    denom = x_ref[...] + y_ref[...]
+    for mode in range(2):
+        rows = slice(144 * mode, 144 * (mode + 1))
+        scaled = (total[rows] / (denom + shift_ref[mode])).astype(BF)
+        for g in range(8):
+            out_ref[g, rows, :] = scaled
+
+
+def to_x_kernel(me_ref, got_ref, out_ref):
+    total = added(got_ref)
+    main = total[:288].astype(BF)
+    sides = jnp.concatenate(
+        [
+            jnp.concatenate([total[288:296], total[304:312]], axis=0),
+            jnp.concatenate([total[296:304], total[312:320]], axis=0),
+        ],
+        axis=1,
+    ).astype(BF)
+    for g in range(8):
+        out_ref[g, :144, :128] = main[:144]
+        out_ref[g, :144, 128:] = main[144:]
+        out_ref[g, 144:, :] = sides
 
 
 def nt_dot(left, right):
@@ -176,8 +201,7 @@
         out_ref[target, 144:160, :] = group.astype(BF)
 
 
-def transform_x_back(me, block, table, outer):
-    held = gather(block, "y", 8)
+def x_back_products(me, held, table, outer):
     scratch = [
         pltpu.VMEM((1152, 256), BF),
         pltpu.VMEM((16, 1152), BF),
@@ -185,14 +209,8 @@
         pltpu.VMEM((6, 8, 256), F32),
         pltpu.VMEM((4, 16, 256), F32),
     ]
-    parts = call(
-        x_back_kernel,
-        jax.ShapeDtypeStruct((4, 160, 256), BF),
-        (me, held, *table, *outer),
-        scratch,
-        flops=2 * 576 * 1152 * 256,
-    )
-    return scatter_sum(parts, QUAD)
+    out = jax.ShapeDtypeStruct((4, 160, 256), BF)
+    return call(x_back_kernel, out, (me, held, *table, *outer), scratch, flops=2 * 576 * 1152 * 256)
 
 
 def y_back_kernel(me_ref, held_ref, t0, t1, t2, lo_ref, hi_ref, out_ref, placed, last, first):
@@ -221,21 +239,14 @@
             out_ref[target, 288 + 16 * mode : 304 + 16 * mode, :] = group.astype(BF)
 
 
-def transform_y_back(me, block, table, outer):
-    held = gather(block, ("xh", "zh"), 8)
+def y_back_products(me, held, table, outer):
     scratch = [
         pltpu.VMEM((400, 1024), BF),
         pltpu.VMEM((4, 16, 1024), BF),
         pltpu.VMEM((5, 16, 1024), BF),
     ]
-    parts = call(
-        y_back_kernel,
-        jax.ShapeDtypeStruct((3, 320, 128), BF),
-        (me, held, *table, *outer),
-        scratch,
-        flops=2 * 288 * 1024 * 384,
-    )
-    return scatter_sum(parts, "zl")
+    out = jax.ShapeDtypeStruct((3, 320, 128), BF)
+    return call(y_back_kernel, out, (me, held, *table, *outer), scratch, flops=2 * 288 * 1024 * 384)
 
 
 def ring_outer(me, table):
@@ -252,14 +263,6 @@
     up = [(i, (i + 1) % 8) for i in range(8)]
     down = [((i + 1) % 8, i) for i in range(8)]
     return lax.ppermute(low, "y", up), lax.ppermute(high, "y", down)
-
-
-def with_sides(back):
-    sides = [
-        jnp.concatenate([back[288 + 16 * m : 296 + 16 * m], back[296 + 16 * m : 304 + 16 * m]], axis=1)
-        for m in range(2)
-    ]
-    return jnp.concatenate([to_x(back[:288])] + sides, axis=0)
 
 
 def to_x(block):
@@ -297,24 +300,29 @@
     quad_me = (lax.axis_index("xl") * 2 + lax.axis_index("c")).astype(jnp.int32).reshape(1)
     ring_me = lax.axis_index("zl").astype(jnp.int32).reshape(1)
     cut_fx, cut_y = quad_cut(quad_me, forward_x), ring_cut(ring_me, forward_y, inverse_y)
-    divergence, cut_fx, cut_y = lax.optimization_barrier((divergence, cut_fx, cut_y))
-    table_fx = [cut_fx[0]] + [quad_send(cut_fx[step], step) for step in (1, 2, 3)]
+    divergence, fx_two, cut_y = lax.optimization_barrier((divergence, quad_send(cut_fx[2], 2), cut_y))
+    table_fx = (cut_fx[0], quad_send(cut_fx[1], 1), fx_two, quad_send(cut_fx[3], 3))
     table_y = ring_tables(cut_y)
-    spec_x = transform_x(quad_me, to_x(divergence.reshape(288, 128)), table_fx).astype(BF)
-    spec_x, table_y = lax.optimization_barrier((spec_x, table_y))
-    spec_xy = transform_y(ring_me, to_y(spec_x), table_y, 0).reshape(2, 144, 128)
+    block = to_x(divergence.reshape(288, 128))
+    held = exchange(jnp.broadcast_to(block[None], (8, 144, 256)), "y")
+    got = exchange(x_products(quad_me, held, table_fx), QUAD)
+    got, table_y = lax.optimization_barrier((got, table_y))
+    spread = jax.ShapeDtypeStruct((8, 288, 128), BF)
+    held = exchange(call(to_y_kernel, spread, (quad_me, got)), ("xh", "zh"))
     cut_ix = quad_cut(quad_me, inverse_x)
-    spec_xy, ix_two = lax.optimization_barrier((spec_xy, quad_send(cut_ix[2], 2)))
-    denom = eigen_x[None, :, None] + eigen_y[None, None, :] + mode_shift[:, None, None]
-    scaled = (spec_xy / denom).astype(BF)
-    outer_y = ring_outer(ring_me[0], table_y)
-    back_y = transform_y_back(ring_me, scaled.reshape(288, 128), table_y, outer_y).astype(BF)
-    back_y, ix_one, ix_three = lax.optimization_barrier(
-        (back_y, quad_send(cut_ix[1], 1), quad_send(cut_ix[3], 3))
+    held, table_ix = lax.optimization_barrier(
+        (held, [cut_ix[0]] + [quad_send(cut_ix[step], step) for step in (1, 2, 3)])
     )
-    table_ix = (cut_ix[0], ix_one, ix_two, ix_three)
-    outer_x = quad_outer(quad_me[0], table_ix)
-    total = transform_x_back(quad_me, with_sides(back_y), table_ix, outer_x)
+    got = exchange(y_products(ring_me, held, table_y), "zl")
+    eigen = (eigen_x.reshape(144, 1), eigen_y.reshape(1, 128))
+    held = exchange(call(scale_kernel, spread, (mode_shift, got, *eigen)), ("xh", "zh"))
+    outer_y, outer_x = ring_outer(ring_me[0], table_y), quad_outer(quad_me[0], table_ix)
+    held, outer_x = lax.optimization_barrier((held, outer_x))
+    got = exchange(y_back_products(ring_me, held, table_y, outer_y), "zl")
+    spread = jax.ShapeDtypeStruct((8, 160, 256), BF)
+    held = exchange(call(to_x_kernel, spread, (quad_me, got)), "y")
+    parts = exchange(x_back_products(quad_me, held, table_ix, outer_x), QUAD)
+    total = jnp.sum(parts.astype(F32), axis=0)
     pressure = to_y(total[:144]).reshape(2, 144, 128)
     low, high = total[146].reshape(2, 1, 128), total[147].reshape(2, 1, 128)
     padded = jnp.concatenate([low, pressure, high], axis=1)

time: 226 us -> 226 us (level)
  blocking collectives: 48.5 us -> 35.8 us
  starting transfers between devices: 103 us -> 107 us
  waiting for transfers between devices: 40.3 us -> 44.3 us
  Pallas kernels: 15.3 us -> 17.7 us
    all_to_all x2, blocking collectives: 48.5 us -> 35.8 us  [exchange(): return lax.all_to_all(parts, axes, 0, 0)]
    ppermute x1, waiting for transfers between devices: 0.45 us -> 7.97 us  [ring_outer(): lax.ppermute(high, ('xh', 'zh'), down)]
    ppermute x2, waiting for transfers between devices: 6.7 us -> 0.01 us  [quad_outer(): return (lax.ppermute(low, 'y', up), lax.ppermute(high, 'y', down))]
    ppermute x2, waiting for transfers between devices: 3.96 us -> 9.9 us  [ring_tables(): lax.ppermute(pieces[step], 'zl', [(i, (i + step) % 3) for i in range(3)])]
    all_to_all x6, starting transfers between devices: 46.9 us -> 51.2 us  [exchange(): return lax.all_to_all(parts, axes, 0, 0)]
    pallas_call x7 -> x10, Pallas kernels: 15.3 us -> 17.7 us  [call(): pl.pallas_call(kernel, out_shape=out_shape, in_specs=[smem] + [vmem] * (l...]
  transfers between devices with their start and end apart: 22 -> 22, of which waited for: 9 -> 9; matrix products, arithmetic and copies ran while one was open for 2% -> 4% of each run, Pallas kernels for 5% -> 6%
where the time goes in v6:
time: 226 us; the launch traced here: 224 us
  starting transfers between devices  107 us (47%)
  waiting for transfers between devices  44.3 us (20%)
  blocking collectives  35.8 us (16%)
  Pallas kernels  17.7 us (8%)
  local copies, waits for them, and re-layouts  9.66 us (4%)
  other arithmetic  8.12 us (4%)
    all_to_all x6, starting transfers between devices, exchange(): return lax.all_to_all(parts, axes, 0, 0)  51.2 us
    all_to_all x2, blocking collectives, exchange(): return lax.all_to_all(parts, axes, 0, 0)  35.8 us
    pallas_call x10, Pallas kernels, call(): pl.pallas_call(kernel, out_shape=out_shape, in_specs=[smem] + [vmem] * (l...  17.7 us
    ppermute x6, starting transfers between devices, quad_send(): return lax.ppermute(piece, QUAD, [(i, i ^ step) for i in range(4)])  17.3 us
    ppermute x6, waiting for transfers between devices, quad_send(): return lax.ppermute(piece, QUAD, [(i, i ^ step) for i in range(4)])  13.4 us
    all_to_all x6, waiting for transfers between devices, exchange(): return lax.all_to_all(parts, axes, 0, 0)  13 us
    ppermute x2, waiting for transfers between devices, ring_tables(): lax.ppermute(pieces[step], 'zl', [(i, (i + step) % 3) for i in range(3)])  9.9 us
    ppermute x2, starting transfers between devices, edges(): lax.ppermute(lax.slice_in_dim(block, block.shape[dim] - 1, None, axis=dim...  9.53 us
  transfers between devices with their start and end apart: 22, of which 9 were waited for; matrix products, arithmetic and copies ran while one was open for 4% of the time, Pallas kernels for 6%

profile of v6, /device:TPU:1, one launch (start us, length us, event | category | flops | bytes accessed | tf_op | source)
XLA Modules:
  0.0 224.4 jit_solution(1368231124570972057)
XLA Ops:
  0.6 1.6 fusion.8
  3.3 5.6 %collective-permute-start.3 = (bf16[2,144,1]{2,0,1:T(2,128)(2,1)}, bf16[2,144,1]{2,0,1:T(2,128)(2,1)}, u32[]{:S(2)}, u32[]{:S(2)}) collective-permute-start(bf16[2,144,1]{2,0,1:T(2,128)(2,1)} %get-tuple-element.94), channel_id=1, source_target_pairs={{0,1},{1,2},{2,3},{3,4},{4,5},{5,6},{6,7},{7,8},{8,9},{9,10},{10,1... | collective-permute-start | bytes 1736 | tf_op jit(solution)/shard_map/ppermute | solution.py:28
  8.9 1.3 collective-permute-start.2
  10.2 0.9 fusion.44
  11.1 3.9 %collective-permute-start.1 = (bf16[2,1,128]{2,0,1:T(2,128)(2,1)S(1)}, bf16[2,1,128]{2,0,1:T(2,128)(2,1)S(1)}, u32[]{:S(2)}, u32[]{:S(2)}) collective-permute-start(bf16[2,1,128]{2,0,1:T(2,128)(2,1)S(1)} %get-tuple-element.92), channel_id=1, source_target_pairs={{0,24},{24,48},{48,72},{72,96},{96,120},{120,144},{144,168},{168,1... | collective-permute-start | bytes 1544 | tf_op jit(solution)/shard_map/ppermute | solution.py:28
  15.0 6.9 %collective-permute-start = (bf16[2,1,128]{2,0,1:T(2,128)(2,1)S(1)}, bf16[2,1,128]{2,0,1:T(2,128)(2,1)S(1)}, u32[]{:S(2)}, u32[]{:S(2)}) collective-permute-start(bf16[2,1,128]{2,0,1:T(2,128)(2,1)S(1)} %get-tuple-element.91), channel_id=1, source_target_pairs={{24,0},{48,24},{72,48},{96,72},{120,96},{144,120},{168,144},{192,1... | collective-permute-start | bytes 1544 | tf_op jit(solution)/shard_map/ppermute | solution.py:29
  21.9 3.7 %shard_map.148 = (bf16[144,1152]{1,0:T(8,128)(2,1)S(1)}, bf16[144,1152]{1,0:T(8,128)(2,1)}, bf16[144,1152]{1,0:T(8,128)(2,1)}, bf16[144,1152]{1,0:T(8,128)(2,1)}) custom-call(s32[1]{0:T(128)} %bitcast.1.me_ref, bf16[144,4608]{1,0:T(8,128)(2,1)S(1)} %copy-done.1), custom_call_target="tpu_custom_call" | custom-call | bytes 2654208 | tf_op jit(solution)/shard_map/pallas_call | solution.py:49
  25.6 1.9 collective-permute-start.4
  27.6 1.1 shard_map.149
  29.5 0.9 convert_element_type.65
  30.5 1.5 fusion.19
  32.1 1.6 collective-permute-done.4.t2
  34.7 5.1 %all-to-all-start = ((bf16[8,144,256]{2,1,0:T(8,128)(2,1)}), bf16[8,144,256]{2,1,0:T(8,128)(2,1)S(1)}, u32[]{:S(2)}, u32[]{:S(2)}) async-start(bf16[8,144,256]{2,1,0:T(8,128)(2,1)} %broadcast_in_dim.2), calls=%async_computation | async-start | bytes 1179648 | tf_op jit(solution)/shard_map/all_to_all | solution.py:20
  39.8 5.4 %collective-permute-start.5 = (bf16[144,1152]{1,0:T(8,128)(2,1)}, bf16[144,1152]{1,0:T(8,128)(2,1)S(1)}, u32[]{:S(2)}, u32[]{:S(2)}) collective-permute-start(bf16[144,1152]{1,0:T(8,128)(2,1)} %get-tuple-element.37), channel_id=1, source_target_pairs={{0,24},{24,0},{48,72},{72,48},{1,25},{25,1},{49,73},{73,49},{2,26}... | collective-permute-start | bytes 995336 | tf_op jit(solution)/shard_map/ppermute | solution.py:80
  45.2 1.9 collective-permute-start.6
  47.1 4.3 %collective-permute-start.7 = (bf16[256,1024]{1,0:T(8,128)(2,1)}, bf16[256,1024]{1,0:T(8,128)(2,1)S(1)}, u32[]{:S(2)}, u32[]{:S(2)}) collective-permute-start(bf16[256,1024]{1,0:T(8,128)(2,1)} %get-tuple-element.41), channel_id=1, source_target_pairs={{0,1},{1,2},{2,0},{3,4},{4,5},{5,3},{6,7},{7,8},{8,6},{9,10},{10,1... | collective-permute-start | bytes 1572872 | tf_op jit(solution)/shard_map/ppermute | solution.py:99
  51.4 1.9 collective-permute-start.8
  53.4 3.6 %collective-permute-done.6.t3 = bf16[144,1152]{1,0:T(8,128)(2,1)S(1)} collective-permute-done((bf16[144,1152]{1,0:T(8,128)(2,1)}, bf16[144,1152]{1,0:T(8,128)(2,1)S(1)}, u32[]{:S(2)}, u32[]{:S(2)}) %collective-permute-start.6) | collective-permute-done | bytes 331808 | tf_op jit(solution)/shard_map/ppermute | solution.py:80
  57.0 1.0 copy-done.8
  58.0 1.3 shard_map.150
  59.3 6.1 %all-to-all-start.1 = ((bf16[4,144,256]{2,1,0:T(8,128)(2,1)}), bf16[4,144,256]{2,1,0:T(8,128)(2,1)S(1)}, u32[]{:S(2)}, u32[]{:S(2)}) async-start(bf16[4,144,256]{2,1,0:T(8,128)(2,1)} %shard_map.150), calls=%async_computation.1 | async-start | bytes 589824 | tf_op jit(solution)/shard_map/all_to_all | solution.py:20
  65.3 9.9 %collective-permute-done.8.t2 = bf16[256,1024]{1,0:T(8,128)(2,1)S(1)} collective-permute-done((bf16[256,1024]{1,0:T(8,128)(2,1)}, bf16[256,1024]{1,0:T(8,128)(2,1)S(1)}, u32[]{:S(2)}, u32[]{:S(2)}) %collective-permute-start.8) | collective-permute-done | bytes 524320 | tf_op jit(solution)/shard_map/ppermute | solution.py:99
  76.1 16.1 %all-to-all-start.2 = ((bf16[8,288,128]{2,1,0:T(8,128)(2,1)}), bf16[8,288,128]{2,1,0:T(8,128)(2,1)S(1)}, u32[]{:S(2)}, u32[]{:S(2)}) async-start(bf16[8,288,128]{2,1,0:T(8,128)(2,1)} %shard_map.151), calls=%async_computation.2 | async-start | bytes 1179648 | tf_op jit(solution)/shard_map/all_to_all | solution.py:20
  92.2 3.7 %shard_map.152 = (bf16[144,1152]{1,0:T(8,128)(2,1)S(1)}, bf16[144,1152]{1,0:T(8,128)(2,1)}, bf16[144,1152]{1,0:T(8,128)(2,1)}, bf16[144,1152]{1,0:T(8,128)(2,1)}) custom-call(s32[1]{0:T(128)} %bitcast.1.me_ref, bf16[144,4608]{1,0:T(8,128)(2,1)S(1)} %copy-done.2), custom_call_target="tpu_custom_call" | custom-call | bytes 2654208 | tf_op jit(solution)/shard_map/pallas_call | solution.py:49
  96.6 2.7 %collective-permute-start.9 = (bf16[144,1152]{1,0:T(8,128)(2,1)}, bf16[144,1152]{1,0:T(8,128)(2,1)S(1)}, u32[]{:S(2)}, u32[]{:S(2)}) collective-permute-start(bf16[144,1152]{1,0:T(8,128)(2,1)} %get-tuple-element.45), channel_id=1, source_target_pairs={{0,24},{24,0},{48,72},{72,48},{1,25},{25,1},{49,73},{73,49},{2,26}... | collective-permute-start | bytes 995336 | tf_op jit(solution)/shard_map/ppermute | solution.py:80
  99.3 2.1 collective-permute-start.10
  101.4 3.4 %collective-permute-start.11 = (bf16[144,1152]{1,0:T(8,128)(2,1)}, bf16[144,1152]{1,0:T(8,128)(2,1)S(1)}, u32[]{:S(2)}, u32[]{:S(2)}) collective-permute-start(bf16[144,1152]{1,0:T(8,128)(2,1)} %get-tuple-element.47), channel_id=1, source_target_pairs={{0,72},{24,48},{48,24},{72,0},{1,73},{25,49},{49,25},{73,1},{2,74}... | collective-permute-start | bytes 995336 | tf_op jit(solution)/shard_map/ppermute | solution.py:80
  108.0 6.0 %collective-permute-start.14 = (bf16[16,1024]{1,0:T(8,128)(2,1)}, bf16[16,1024]{1,0:T(8,128)(2,1)}, u32[]{:S(2)}, u32[]{:S(2)}) collective-permute-start(bf16[16,1024]{1,0:T(8,128)(2,1)} %fusion.33), channel_id=1, source_target_pairs={{0,3},{3,6},{6,9},{9,12},{12,15},{15,18},{18,21},{1,4},{4,7},{7,10... | collective-permute-start | bytes 98312 | tf_op jit(solution)/shard_map/ppermute | solution.py:257
  114.2 7.9 %collective-permute-done.11.t3 = bf16[144,1152]{1,0:T(8,128)(2,1)S(1)} collective-permute-done((bf16[144,1152]{1,0:T(8,128)(2,1)}, bf16[144,1152]{1,0:T(8,128)(2,1)S(1)}, u32[]{:S(2)}, u32[]{:S(2)}) %collective-permute-start.11) | collective-permute-done | bytes 331808 | tf_op jit(solution)/shard_map/ppermute | solution.py:80
  122.2 1.4 shard_map.153
  123.5 3.5 %all-to-all-start.3 = ((bf16[3,288,128]{2,1,0:T(8,128)(2,1)}), bf16[3,288,128]{2,1,0:T(8,128)(2,1)S(1)}, u32[]{:S(2)}, u32[]{:S(2)}) async-start(bf16[3,288,128]{2,1,0:T(8,128)(2,1)} %shard_map.153), calls=%async_computation.3 | async-start | bytes 442368 | tf_op jit(solution)/shard_map/all_to_all | solution.py:20
  127.6 4.0 %all-to-all-done.3.got_ref = bf16[3,288,128]{2,1,0:T(8,128)(2,1)S(1)} async-done(((bf16[3,288,128]{2,1,0:T(8,128)(2,1)}), bf16[3,288,128]{2,1,0:T(8,128)(2,1)S(1)}, u32[]{:S(2)}, u32[]{:S(2)}) %all-to-all-start.3) | async-done | bytes 221216 | tf_op jit(solution)/shard_map/all_to_all | solution.py:20
  131.7 0.9 copy-done.9
  132.6 1.5 shard_map.154
  134.0 11.7 %all-to-all-start.4 = ((bf16[8,288,128]{2,1,0:T(8,128)(2,1)}), bf16[8,288,128]{2,1,0:T(8,128)(2,1)S(1)}, u32[]{:S(2)}, u32[]{:S(2)}) async-start(bf16[8,288,128]{2,1,0:T(8,128)(2,1)} %shard_map.154), calls=%async_computation.4 | async-start | bytes 1179648 | tf_op jit(solution)/shard_map/all_to_all | solution.py:20
  145.8 3.6 %collective-permute-start.12 = (bf16[16,1152]{1,0:T(8,128)(2,1)S(1)}, bf16[16,1152]{1,0:T(8,128)(2,1)S(1)}, u32[]{:S(2)}, u32[]{:S(2)}) collective-permute-start(bf16[16,1152]{1,0:T(8,128)(2,1)S(1)} %fusion.27), channel_id=1, source_target_pairs={{0,96},{96,192},{192,288},{288,384},{384,480},{480,576},{576,672},... | collective-permute-start | bytes 110600 | tf_op jit(solution)/shard_map/ppermute | solution.py:265
  149.5 3.1 %collective-permute-start.13 = (bf16[16,1152]{1,0:T(8,128)(2,1)S(1)}, bf16[16,1152]{1,0:T(8,128)(2,1)S(1)}, u32[]{:S(2)}, u32[]{:S(2)}) collective-permute-start(bf16[16,1152]{1,0:T(8,128)(2,1)S(1)} %fusion.23), channel_id=1, source_target_pairs={{96,0},{192,96},{288,192},{384,288},{480,384},{576,480},{672,576},... | collective-permute-start | bytes 110600 | tf_op jit(solution)/shard_map/ppermute | solution.py:265
  152.7 1.4 fusion.30
  154.1 1.3 collective-permute-start.15
  156.0 3.1 %all-to-all-done.4.held_ref = bf16[8,288,128]{2,1,0:T(8,128)(2,1)S(1)} async-done(((bf16[8,288,128]{2,1,0:T(8,128)(2,1)}), bf16[8,288,128]{2,1,0:T(8,128)(2,1)S(1)}, u32[]{:S(2)}, u32[]{:S(2)}) %all-to-all-start.4) | async-done | bytes 589856 | tf_op jit(solution)/shard_map/all_to_all | solution.py:20
  159.1 8.0 %collective-permute-done.15.hi_ref = bf16[16,1024]{1,0:T(8,128)(2,1)} collective-permute-done((bf16[16,1024]{1,0:T(8,128)(2,1)}, bf16[16,1024]{1,0:T(8,128)(2,1)}, u32[]{:S(2)}, u32[]{:S(2)}) %collective-permute-start.15) | collective-permute-done | bytes 32800 | tf_op jit(solution)/shard_map/ppermute | solution.py:257
  167.1 2.4 %shard_map.155 = bf16[3,320,128]{2,1,0:T(8,128)(2,1)S(1)} custom-call(s32[1]{0:T(128)} %bitcast.2.me_ref, bf16[8,288,128]{2,1,0:T(8,128)(2,1)S(1)} %all-to-all-done.4.held_ref, bf16[256,1024]{1,0:T(8,128)(2,1)S(1)} %get-tuple-element.49.t0, bf16[256,1024]{1,0:T(8,128)(2,1)S(1)} %collective-permute-done.7.t1, ...), custom_call_target="tpu_custom_call" | custom-call | flops 226492416 | bytes 2473984 | tf_op jit(solution)/shard_map/pallas_call | solution.py:49
  169.4 13.2 %all_to_all.40.got_ref = bf16[3,320,128]{2,1,0:T(8,128)(2,1)S(1)} all-to-all(bf16[3,320,128]{2,1,0:T(8,128)(2,1)S(1)} %shard_map.155), channel_id=1, replica_groups=mesh['y'=8,'xl'=2,'c'=2,'xh'=2,'zh'=4,'zl'=3] {'zl'}, dimensions={0} | all-to-all | bytes 491520 | tf_op jit(solution)/shard_map/all_to_all | solution.py:20
  182.8 22.6 %all_to_all.41.held_ref = bf16[8,160,256]{2,1,0:T(8,128)(2,1)S(1)} all-to-all(bf16[8,160,256]{2,1,0:T(8,128)(2,1)S(1)} %shard_map.156), channel_id=1, replica_groups=mesh['y'=8,'xl'=2,'c'=2,'xh'=2,'zh'=4,'zl'=3] {'y'}, dimensions={0} | all-to-all | bytes 1310720 | tf_op jit(solution)/shard_map/all_to_all | solution.py:20
  205.4 1.8 shard_map.157
  207.2 8.8 %all-to-all-start.7 = ((bf16[4,160,256]{2,1,0:T(8,128)(2,1)}), bf16[4,160,256]{2,1,0:T(8,128)(2,1)S(1)}, u32[]{:S(2)}, u32[]{:S(2)}) async-start(bf16[4,160,256]{2,1,0:T(8,128)(2,1)} %shard_map.157), calls=%async_computation.7 | async-start | bytes 655360 | tf_op jit(solution)/shard_map/all_to_all | solution.py:20
  216.0 5.9 %all-to-all-done.7 = bf16[4,160,256]{2,1,0:T(8,128)(2,1)S(1)} async-done(((bf16[4,160,256]{2,1,0:T(8,128)(2,1)}), bf16[4,160,256]{2,1,0:T(8,128)(2,1)S(1)}, u32[]{:S(2)}, u32[]{:S(2)}) %all-to-all-start.7) | async-done | bytes 327712 | tf_op jit(solution)/shard_map/all_to_all | solution.py:20
  222.8 1.6 fusion.4
  (92 shorter events, 10.3 us)
Async XLA Ops:
  0.6 1.7 copy-start
  2.3 19.6 %copy-start.1 = (bf16[144,4608]{1,0:T(8,128)(2,1)S(1)}, bf16[144,4608]{1,0:T(8,128)(2,1)}, u32[]{:S(2)}) copy-start(bf16[144,4608]{1,0:T(8,128)(2,1)} %rows_ref.2) | copy-start | bytes 3981316
  2.5 25.0 %copy-start.15 = (s32[144,128]{1,0:T(8,128)S(1)}, s32[144,128]{1,0:T(8,128)}, u32[]{:S(2)}) copy-start(s32[144,128]{1,0:T(8,128)} %param.15) | copy-start | bytes 221188
  3.3 24.3 %copy-start.3 = (bf16[128,3072]{1,0:T(8,128)(2,1)S(1)}, bf16[128,3072]{1,0:T(8,128)(2,1)}, u32[]{:S(2)}) copy-start(bf16[128,3072]{1,0:T(8,128)(2,1)} %first_ref.1) | copy-start | bytes 2359300
  3.3 24.3 %copy-start.4 = (bf16[128,3072]{1,0:T(8,128)(2,1)S(1)}, bf16[128,3072]{1,0:T(8,128)(2,1)}, u32[]{:S(2)}) copy-start(bf16[128,3072]{1,0:T(8,128)(2,1)} %second_ref.1) | copy-start | bytes 2359300
  3.3 26.2 %collective-permute-start.3 = (bf16[2,144,1]{2,0,1:T(2,128)(2,1)}, bf16[2,144,1]{2,0,1:T(2,128)(2,1)}, u32[]{:S(2)}, u32[]{:S(2)}) collective-permute-start(bf16[2,144,1]{2,0,1:T(2,128)(2,1)} %get-tuple-element.94), channel_id=1, source_target_pairs={{0,1},{1,2},{2,3},{3,4},{4,5},{5,6},{6,7},{7,8},{8,9},{9,10},{10,1... | collective-permute-start | bytes 1736 | tf_op jit(solution)/shard_map/ppermute | solution.py:28
  8.9 21.6 %collective-permute-start.2 = (bf16[2,144,1]{2,0,1:T(2,128)(2,1)}, bf16[2,144,1]{2,0,1:T(2,128)(2,1)S(1)}, u32[]{:S(2)}, u32[]{:S(2)}) collective-permute-start(bf16[2,144,1]{2,0,1:T(2,128)(2,1)} %get-tuple-element.93), channel_id=1, source_target_pairs={{1,0},{2,1},{3,2},{4,3},{5,4},{6,5},{7,6},{8,7},{9,8},{10,9},{11,1... | collective-permute-start | bytes 1736 | tf_op jit(solution)/shard_map/ppermute | solution.py:29
  11.1 18.4 %collective-permute-start.1 = (bf16[2,1,128]{2,0,1:T(2,128)(2,1)S(1)}, bf16[2,1,128]{2,0,1:T(2,128)(2,1)S(1)}, u32[]{:S(2)}, u32[]{:S(2)}) collective-permute-start(bf16[2,1,128]{2,0,1:T(2,128)(2,1)S(1)} %get-tuple-element.92), channel_id=1, source_target_pairs={{0,24},{24,48},{48,72},{72,96},{96,120},{120,144},{144,168},{168,1... | collective-permute-start | bytes 1544 | tf_op jit(solution)/shard_map/ppermute | solution.py:28
  15.0 14.5 %collective-permute-start = (bf16[2,1,128]{2,0,1:T(2,128)(2,1)S(1)}, bf16[2,1,128]{2,0,1:T(2,128)(2,1)S(1)}, u32[]{:S(2)}, u32[]{:S(2)}) collective-permute-start(bf16[2,1,128]{2,0,1:T(2,128)(2,1)S(1)} %get-tuple-element.91), channel_id=1, source_target_pairs={{24,0},{48,24},{72,48},{96,72},{120,96},{144,120},{168,144},{192,1... | collective-permute-start | bytes 1544 | tf_op jit(solution)/shard_map/ppermute | solution.py:29
  25.6 8.1 %collective-permute-start.4 = (bf16[144,1152]{1,0:T(8,128)(2,1)}, bf16[144,1152]{1,0:T(8,128)(2,1)S(1)}, u32[]{:S(2)}, u32[]{:S(2)}) collective-permute-start(bf16[144,1152]{1,0:T(8,128)(2,1)} %get-tuple-element.31), channel_id=1, source_target_pairs={{0,48},{24,72},{48,0},{72,24},{1,49},{25,73},{49,1},{73,25},{2,50}... | collective-permute-start | bytes 995336 | tf_op jit(solution)/shard_map/ppermute | solution.py:80
  28.7 0.8 copy-start.14
  33.7 1.0 copy-start.7
  34.7 22.3 %all-to-all-start = ((bf16[8,144,256]{2,1,0:T(8,128)(2,1)}), bf16[8,144,256]{2,1,0:T(8,128)(2,1)S(1)}, u32[]{:S(2)}, u32[]{:S(2)}) async-start(bf16[8,144,256]{2,1,0:T(8,128)(2,1)} %broadcast_in_dim.2), calls=%async_computation | async-start | bytes 1179648 | tf_op jit(solution)/shard_map/all_to_all | solution.py:20
  39.8 13.5 %collective-permute-start.5 = (bf16[144,1152]{1,0:T(8,128)(2,1)}, bf16[144,1152]{1,0:T(8,128)(2,1)S(1)}, u32[]{:S(2)}, u32[]{:S(2)}) collective-permute-start(bf16[144,1152]{1,0:T(8,128)(2,1)} %get-tuple-element.37), channel_id=1, source_target_pairs={{0,24},{24,0},{48,72},{72,48},{1,25},{25,1},{49,73},{73,49},{2,26}... | collective-permute-start | bytes 995336 | tf_op jit(solution)/shard_map/ppermute | solution.py:80
  45.2 11.8 %collective-permute-start.6 = (bf16[144,1152]{1,0:T(8,128)(2,1)}, bf16[144,1152]{1,0:T(8,128)(2,1)S(1)}, u32[]{:S(2)}, u32[]{:S(2)}) collective-permute-start(bf16[144,1152]{1,0:T(8,128)(2,1)} %get-tuple-element.39), channel_id=1, source_target_pairs={{0,72},{24,48},{48,24},{72,0},{1,73},{25,49},{49,25},{73,1},{2,74}... | collective-permute-start | bytes 995336 | tf_op jit(solution)/shard_map/ppermute | solution.py:80
  47.1 18.2 %collective-permute-start.7 = (bf16[256,1024]{1,0:T(8,128)(2,1)}, bf16[256,1024]{1,0:T(8,128)(2,1)S(1)}, u32[]{:S(2)}, u32[]{:S(2)}) collective-permute-start(bf16[256,1024]{1,0:T(8,128)(2,1)} %get-tuple-element.41), channel_id=1, source_target_pairs={{0,1},{1,2},{2,0},{3,4},{4,5},{5,3},{6,7},{7,8},{8,6},{9,10},{10,1... | collective-permute-start | bytes 1572872 | tf_op jit(solution)/shard_map/ppermute | solution.py:99
  51.4 23.8 %collective-permute-start.8 = (bf16[256,1024]{1,0:T(8,128)(2,1)}, bf16[256,1024]{1,0:T(8,128)(2,1)S(1)}, u32[]{:S(2)}, u32[]{:S(2)}) collective-permute-start(bf16[256,1024]{1,0:T(8,128)(2,1)} %copy-done.14), channel_id=1, source_target_pairs={{0,2},{1,0},{2,1},{3,5},{4,3},{5,4},{6,8},{7,6},{8,7},{9,11},{10,9... | collective-permute-start | bytes 1572872 | tf_op jit(solution)/shard_map/ppermute | solution.py:99
  57.0 1.0 copy-start.8
  59.3 16.0 %all-to-all-start.1 = ((bf16[4,144,256]{2,1,0:T(8,128)(2,1)}), bf16[4,144,256]{2,1,0:T(8,128)(2,1)S(1)}, u32[]{:S(2)}, u32[]{:S(2)}) async-start(bf16[4,144,256]{2,1,0:T(8,128)(2,1)} %shard_map.150), calls=%async_computation.1 | async-start | bytes 589824 | tf_op jit(solution)/shard_map/all_to_all | solution.py:20
  65.3 26.9 %copy-start.2 = (bf16[144,4608]{1,0:T(8,128)(2,1)S(1)}, bf16[144,4608]{1,0:T(8,128)(2,1)}, u32[]{:S(2)}) copy-start(bf16[144,4608]{1,0:T(8,128)(2,1)} %rows_ref.3) | copy-start | bytes 3981316
  76.1 28.7 %copy-start.19 = (f32[144]{0:T(256)S(1)}, f32[144]{0:T(256)}, u32[]{:S(2)}) copy-start(f32[144]{0:T(256)} %param.23) | copy-start | bytes 1732
  76.1 46.0 %all-to-all-start.2 = ((bf16[8,288,128]{2,1,0:T(8,128)(2,1)}), bf16[8,288,128]{2,1,0:T(8,128)(2,1)S(1)}, u32[]{:S(2)}, u32[]{:S(2)}) async-start(bf16[8,288,128]{2,1,0:T(8,128)(2,1)} %shard_map.151), calls=%async_computation.2 | async-start | bytes 1179648 | tf_op jit(solution)/shard_map/all_to_all | solution.py:20
  95.9 0.7 copy-start.5
  96.6 17.4 %collective-permute-start.9 = (bf16[144,1152]{1,0:T(8,128)(2,1)}, bf16[144,1152]{1,0:T(8,128)(2,1)S(1)}, u32[]{:S(2)}, u32[]{:S(2)}) collective-permute-start(bf16[144,1152]{1,0:T(8,128)(2,1)} %get-tuple-element.45), channel_id=1, source_target_pairs={{0,24},{24,0},{48,72},{72,48},{1,25},{25,1},{49,73},{73,49},{2,26}... | collective-permute-start | bytes 995336 | tf_op jit(solution)/shard_map/ppermute | solution.py:80
  99.3 14.9 %collective-permute-start.10 = (bf16[144,1152]{1,0:T(8,128)(2,1)}, bf16[144,1152]{1,0:T(8,128)(2,1)S(1)}, u32[]{:S(2)}, u32[]{:S(2)}) collective-permute-start(bf16[144,1152]{1,0:T(8,128)(2,1)} %get-tuple-element.46), channel_id=1, source_target_pairs={{0,48},{24,72},{48,0},{72,24},{1,49},{25,73},{49,1},{73,25},{2,50}... | collective-permute-start | bytes 995336 | tf_op jit(solution)/shard_map/ppermute | solution.py:80
  101.4 20.7 %collective-permute-start.11 = (bf16[144,1152]{1,0:T(8,128)(2,1)}, bf16[144,1152]{1,0:T(8,128)(2,1)S(1)}, u32[]{:S(2)}, u32[]{:S(2)}) collective-permute-start(bf16[144,1152]{1,0:T(8,128)(2,1)} %get-tuple-element.47), channel_id=1, source_target_pairs={{0,72},{24,48},{48,24},{72,0},{1,73},{25,49},{49,25},{73,1},{2,74}... | collective-permute-start | bytes 995336 | tf_op jit(solution)/shard_map/ppermute | solution.py:80
  108.0 51.1 %collective-permute-start.14 = (bf16[16,1024]{1,0:T(8,128)(2,1)}, bf16[16,1024]{1,0:T(8,128)(2,1)}, u32[]{:S(2)}, u32[]{:S(2)}) collective-permute-start(bf16[16,1024]{1,0:T(8,128)(2,1)} %fusion.33), channel_id=1, source_target_pairs={{0,3},{3,6},{6,9},{9,12},{12,15},{15,18},{18,21},{1,4},{4,7},{7,10... | collective-permute-start | bytes 98312 | tf_op jit(solution)/shard_map/ppermute | solution.py:257
  122.2 4.8 %copy-start.6 = (bf16[144,1152]{1,0:T(8,128)(2,1)S(1)}, bf16[144,1152]{1,0:T(8,128)(2,1)}, u32[]{:S(2)}) copy-start(bf16[144,1152]{1,0:T(8,128)(2,1)} %copy-done.5) | copy-start | bytes 995332
  122.2 9.5 %copy-start.12 = (f32[2]{0:T(128)S(1)}, f32[2]{0:T(128)}, u32[]{:S(2)}) copy-start(f32[2]{0:T(128)} %shift_ref.1) | copy-start | bytes 28
  122.2 9.5 %copy-start.13 = (f32[128]{0:T(128)S(1)}, f32[128]{0:T(128)}, u32[]{:S(2)}) copy-start(f32[128]{0:T(128)} %param.24) | copy-start | bytes 1540
  123.5 8.1 %all-to-all-start.3 = ((bf16[3,288,128]{2,1,0:T(8,128)(2,1)}), bf16[3,288,128]{2,1,0:T(8,128)(2,1)S(1)}, u32[]{:S(2)}, u32[]{:S(2)}) async-start(bf16[3,288,128]{2,1,0:T(8,128)(2,1)} %shard_map.153), calls=%async_computation.3 | async-start | bytes 442368 | tf_op jit(solution)/shard_map/all_to_all | solution.py:20
  131.7 0.9 copy-start.9
  134.0 25.1 %all-to-all-start.4 = ((bf16[8,288,128]{2,1,0:T(8,128)(2,1)}), bf16[8,288,128]{2,1,0:T(8,128)(2,1)S(1)}, u32[]{:S(2)}, u32[]{:S(2)}) async-start(bf16[8,288,128]{2,1,0:T(8,128)(2,1)} %shard_map.154), calls=%async_computation.4 | async-start | bytes 1179648 | tf_op jit(solution)/shard_map/all_to_all | solution.py:20
  145.8 9.6 %collective-permute-start.12 = (bf16[16,1152]{1,0:T(8,128)(2,1)S(1)}, bf16[16,1152]{1,0:T(8,128)(2,1)S(1)}, u32[]{:S(2)}, u32[]{:S(2)}) collective-permute-start(bf16[16,1152]{1,0:T(8,128)(2,1)S(1)} %fusion.27), channel_id=1, source_target_pairs={{0,96},{96,192},{192,288},{288,384},{384,480},{480,576},{576,672},... | collective-permute-start | bytes 110600 | tf_op jit(solution)/shard_map/ppermute | solution.py:265
  149.5 5.9 %collective-permute-start.13 = (bf16[16,1152]{1,0:T(8,128)(2,1)S(1)}, bf16[16,1152]{1,0:T(8,128)(2,1)S(1)}, u32[]{:S(2)}, u32[]{:S(2)}) collective-permute-start(bf16[16,1152]{1,0:T(8,128)(2,1)S(1)} %fusion.23), channel_id=1, source_target_pairs={{96,0},{192,96},{288,192},{384,288},{480,384},{576,480},{672,576},... | collective-permute-start | bytes 110600 | tf_op jit(solution)/shard_map/ppermute | solution.py:265
  154.1 13.0 %collective-permute-start.15 = (bf16[16,1024]{1,0:T(8,128)(2,1)}, bf16[16,1024]{1,0:T(8,128)(2,1)}, u32[]{:S(2)}, u32[]{:S(2)}) collective-permute-start(bf16[16,1024]{1,0:T(8,128)(2,1)} %fusion.30), channel_id=1, source_target_pairs={{3,0},{6,3},{9,6},{12,9},{15,12},{18,15},{21,18},{4,1},{7,4},{10,7... | collective-permute-start | bytes 98312 | tf_op jit(solution)/shard_map/ppermute | solution.py:257
  155.4 0.6 copy-start.10
  182.7 22.7 %copy-start.11 = (bf16[16,1152]{1,0:T(8,128)(2,1)S(1)}, bf16[16,1152]{1,0:T(8,128)(2,1)}, u32[]{:S(2)}) copy-start(bf16[16,1152]{1,0:T(8,128)(2,1)} %copy-done.10) | copy-start | bytes 110596
  205.4 10.6 %copy-start.20 = (f32[16,2]{0,1:T(2,128)S(1)}, f32[16,2]{0,1:T(2,128)}, u32[]{:S(2)}) copy-start(f32[16,2]{0,1:T(2,128)} %param.18) | copy-start | bytes 388
  207.2 14.7 %all-to-all-start.7 = ((bf16[4,160,256]{2,1,0:T(8,128)(2,1)}), bf16[4,160,256]{2,1,0:T(8,128)(2,1)S(1)}, u32[]{:S(2)}, u32[]{:S(2)}) async-start(bf16[4,160,256]{2,1,0:T(8,128)(2,1)} %shard_map.157), calls=%async_computation.7 | async-start | bytes 655360 | tf_op jit(solution)/shard_map/all_to_all | solution.py:20
  221.9 0.9 copy-start.16
  221.9 0.9 copy-start.18
  222.3 2.1 copy-start.17

commit v7 on v6

--- a/solution.py
+++ b/solution.py
@@ -94,11 +94,8 @@
     return call(ring_cut_kernel, [jax.ShapeDtypeStruct((256, 1024), BF)] * 3, (me, first, second))
 
 
-def ring_tables(pieces):
-    moved = [
-        lax.ppermute(pieces[step], "zl", [(i, (i + step) % 3) for i in range(3)]) for step in (1, 2)
-    ]
-    return [pieces[0]] + moved
+def ring_send(piece, step):
+    return lax.ppermute(piece, "zl", [(i, (i + step) % 3) for i in range(3)])
 
 
 def x_kernel(me_ref, held_ref, t0, t1, t2, t3, out_ref):
@@ -300,16 +297,18 @@
     quad_me = (lax.axis_index("xl") * 2 + lax.axis_index("c")).astype(jnp.int32).reshape(1)
     ring_me = lax.axis_index("zl").astype(jnp.int32).reshape(1)
     cut_fx, cut_y = quad_cut(quad_me, forward_x), ring_cut(ring_me, forward_y, inverse_y)
-    divergence, fx_two, cut_y = lax.optimization_barrier((divergence, quad_send(cut_fx[2], 2), cut_y))
-    table_fx = (cut_fx[0], quad_send(cut_fx[1], 1), fx_two, quad_send(cut_fx[3], 3))
-    table_y = ring_tables(cut_y)
+    divergence, y_one, fx_two = lax.optimization_barrier((divergence, ring_send(cut_y[1], 1), cut_fx[2]))
+    cut_fx = [cut_fx[0], cut_fx[1], fx_two, cut_fx[3]]
+    table_fx = [cut_fx[0]] + [quad_send(cut_fx[step], step) for step in (1, 2, 3)]
+    y_two = ring_send(cut_y[2], 2)
     block = to_x(divergence.reshape(288, 128))
     held = exchange(jnp.broadcast_to(block[None], (8, 144, 256)), "y")
     got = exchange(x_products(quad_me, held, table_fx), QUAD)
-    got, table_y = lax.optimization_barrier((got, table_y))
+    got, y_two = lax.optimization_barrier((got, y_two))
+    cut_ix = quad_cut(quad_me, inverse_x)
+    table_y = (cut_y[0], y_one, y_two)
     spread = jax.ShapeDtypeStruct((8, 288, 128), BF)
     held = exchange(call(to_y_kernel, spread, (quad_me, got)), ("xh", "zh"))
-    cut_ix = quad_cut(quad_me, inverse_x)
     held, table_ix = lax.optimization_barrier(
         (held, [cut_ix[0]] + [quad_send(cut_ix[step], step) for step in (1, 2, 3)])
     )

time: 226 us -> 227 us (level)
  blocking collectives: 35.8 us -> 41.5 us
  waiting for transfers between devices: 44.3 us -> 40.7 us
    ppermute x2, waiting for transfers between devices: 9.9 us -> 0.01 us  [ring_send(): return lax.ppermute(piece, 'zl', [(i, (i + step) % 3) for i in range(3)])]
    all_to_all x6, waiting for transfers between devices: 13 us -> 20.4 us  [exchange(): return lax.all_to_all(parts, axes, 0, 0)]
    all_to_all x2, blocking collectives: 35.8 us -> 41.5 us  [exchange(): return lax.all_to_all(parts, axes, 0, 0)]
    ppermute x1, waiting for transfers between devices: 7.97 us -> 4.18 us  [ring_outer(): lax.ppermute(high, ('xh', 'zh'), down)]
    all_to_all x6, starting transfers between devices: 51.2 us -> 47.9 us  [exchange(): return lax.all_to_all(parts, axes, 0, 0)]
    ppermute x6, waiting for transfers between devices: 13.4 us -> 16 us  [quad_send(): return lax.ppermute(piece, QUAD, [(i, i ^ step) for i in range(4)])]
  transfers between devices with their start and end apart: 22 -> 22, of which waited for: 9 -> 8; matrix products, arithmetic and copies ran while one was open for 4% -> 3% of each run, Pallas kernels for 6% -> 6%
where the time goes in v7:
time: 227 us; the launch traced here: 226 us
  starting transfers between devices  105 us (46%)
  blocking collectives  41.5 us (18%)
  waiting for transfers between devices  40.7 us (18%)
  Pallas kernels  17.7 us (8%)
  local copies, waits for them, and re-layouts  11.5 us (5%)
  other arithmetic  7.07 us (3%)
    all_to_all x6, starting transfers between devices, exchange(): return lax.all_to_all(parts, axes, 0, 0)  47.9 us
    all_to_all x2, blocking collectives, exchange(): return lax.all_to_all(parts, axes, 0, 0)  41.5 us
    all_to_all x6, waiting for transfers between devices, exchange(): return lax.all_to_all(parts, axes, 0, 0)  20.4 us
    ppermute x6, starting transfers between devices, quad_send(): return lax.ppermute(piece, QUAD, [(i, i ^ step) for i in range(4)])  19.4 us
    pallas_call x10, Pallas kernels, call(): pl.pallas_call(kernel, out_shape=out_shape, in_specs=[smem] + [vmem] * (l...  17.7 us
    ppermute x6, waiting for transfers between devices, quad_send(): return lax.ppermute(piece, QUAD, [(i, i ^ step) for i in range(4)])  16 us
    ppermute x2, starting transfers between devices, edges(): lax.ppermute(lax.slice_in_dim(block, block.shape[dim] - 1, None, axis=dim...  9.06 us
    ppermute x2, starting transfers between devices, edges(): high = lax.ppermute(lax.slice_in_dim(block, 0, 1, axis=dim), axes, backward)  7.79 us
  transfers between devices with their start and end apart: 22, of which 8 were waited for; matrix products, arithmetic and copies ran while one was open for 3% of the time, Pallas kernels for 6%

profile of v7, /device:TPU:1, one launch (start us, length us, event | category | flops | bytes accessed | tf_op | source)
XLA Modules:
  0.0 225.9 jit_solution(6762963738358948129)
XLA Ops:
  0.6 2.4 %fusion.8 = (bf16[16,144,128]{2,1,0:T(8,128)(2,1)}, bf16[16,144,128]{2,1,0:T(8,128)(2,1)S(1)}) fusion(bf16[16,144,128]{2,1,0:T(8,128)(2,1)} %param.13, s32[144,128]{1,0:T(8,128)} %param.15, s32[144,128]{1,0:T(8,128)} %param.16, bf16[16,144,128]{2,1,0:T(8,128)(2,1)} %param.14), kind=kLoop, calls=%fused_computation.13 | loop fusion | flops 2949120 | bytes 2506752 | tf_op jit(solution)/shard_map/mul | solution.py:291
  4.1 4.8 %collective-permute-start.3 = (bf16[2,144,1]{2,0,1:T(2,128)(2,1)}, bf16[2,144,1]{2,0,1:T(2,128)(2,1)S(1)}, u32[]{:S(2)}, u32[]{:S(2)}) collective-permute-start(bf16[2,144,1]{2,0,1:T(2,128)(2,1)} %get-tuple-element.86), channel_id=1, source_target_pairs={{0,1},{1,2},{2,3},{3,4},{4,5},{5,6},{6,7},{7,8},{8,9},{9,10},{10,1... | collective-permute-start | bytes 1736 | tf_op jit(solution)/shard_map/ppermute | solution.py:28
  8.9 1.3 collective-permute-start.2
  10.3 1.1 copy-done.4
  11.4 1.1 shard_map.148
  13.3 4.6 %collective-permute-start.4 = (bf16[256,1024]{1,0:T(8,128)(2,1)}, bf16[256,1024]{1,0:T(8,128)(2,1)S(1)}, u32[]{:S(2)}, u32[]{:S(2)}) collective-permute-start(bf16[256,1024]{1,0:T(8,128)(2,1)} %get-tuple-element.27), channel_id=1, source_target_pairs={{0,1},{1,2},{2,0},{3,4},{4,5},{5,3},{6,7},{7,8},{8,6},{9,10},{10,1... | collective-permute-start | bytes 1572872 | tf_op jit(solution)/shard_map/ppermute | solution.py:98
  17.9 1.3 fusion.44
  19.2 4.2 %collective-permute-start.1 = (bf16[2,1,128]{2,0,1:T(2,128)(2,1)S(1)}, bf16[2,1,128]{2,0,1:T(2,128)(2,1)S(1)}, u32[]{:S(2)}, u32[]{:S(2)}) collective-permute-start(bf16[2,1,128]{2,0,1:T(2,128)(2,1)S(1)} %get-tuple-element.84), channel_id=1, source_target_pairs={{0,24},{24,48},{48,72},{72,96},{96,120},{120,144},{144,168},{168,1... | collective-permute-start | bytes 1544 | tf_op jit(solution)/shard_map/ppermute | solution.py:28
  23.5 6.5 %collective-permute-start = (bf16[2,1,128]{2,0,1:T(2,128)(2,1)S(1)}, bf16[2,1,128]{2,0,1:T(2,128)(2,1)S(1)}, u32[]{:S(2)}, u32[]{:S(2)}) collective-permute-start(bf16[2,1,128]{2,0,1:T(2,128)(2,1)S(1)} %get-tuple-element.83), channel_id=1, source_target_pairs={{24,0},{48,24},{72,48},{96,72},{120,96},{144,120},{168,144},{192,1... | collective-permute-start | bytes 1544 | tf_op jit(solution)/shard_map/ppermute | solution.py:29
  30.0 3.7 %shard_map.149 = (bf16[144,1152]{1,0:T(8,128)(2,1)S(1)}, bf16[144,1152]{1,0:T(8,128)(2,1)}, bf16[144,1152]{1,0:T(8,128)(2,1)}, bf16[144,1152]{1,0:T(8,128)(2,1)}) custom-call(s32[1]{0:T(128)} %bitcast.1.me_ref, bf16[144,4608]{1,0:T(8,128)(2,1)S(1)} %copy-done.1), custom_call_target="tpu_custom_call" | custom-call | bytes 2654208 | tf_op jit(solution)/shard_map/pallas_call | solution.py:49
  35.4 3.6 %all-to-all-start = ((bf16[8,144,256]{2,1,0:T(8,128)(2,1)}), bf16[8,144,256]{2,1,0:T(8,128)(2,1)S(1)}, u32[]{:S(2)}, u32[]{:S(2)}) async-start(bf16[8,144,256]{2,1,0:T(8,128)(2,1)} %broadcast_in_dim.2), calls=%async_computation | async-start | bytes 1179648 | tf_op jit(solution)/shard_map/all_to_all | solution.py:20
  39.1 5.7 %collective-permute-start.5 = (bf16[144,1152]{1,0:T(8,128)(2,1)}, bf16[144,1152]{1,0:T(8,128)(2,1)S(1)}, u32[]{:S(2)}, u32[]{:S(2)}) collective-permute-start(bf16[144,1152]{1,0:T(8,128)(2,1)} %get-tuple-element.31), channel_id=1, source_target_pairs={{0,24},{24,0},{48,72},{72,48},{1,25},{25,1},{49,73},{73,49},{2,26}... | collective-permute-start | bytes 995336 | tf_op jit(solution)/shard_map/ppermute | solution.py:80
  44.7 1.9 collective-permute-start.7
  46.7 3.3 %collective-permute-start.6 = (bf16[144,1152]{1,0:T(8,128)(2,1)}, bf16[144,1152]{1,0:T(8,128)(2,1)S(1)}, u32[]{:S(2)}, u32[]{:S(2)}) collective-permute-start(bf16[144,1152]{1,0:T(8,128)(2,1)} %get-tuple-element.32), channel_id=1, source_target_pairs={{0,48},{24,72},{48,0},{72,24},{1,49},{25,73},{49,1},{73,25},{2,50}... | collective-permute-start | bytes 995336 | tf_op jit(solution)/shard_map/ppermute | solution.py:80
  49.9 1.9 collective-permute-start.8
  51.9 5.3 %collective-permute-done.7.t3 = bf16[144,1152]{1,0:T(8,128)(2,1)S(1)} collective-permute-done((bf16[144,1152]{1,0:T(8,128)(2,1)}, bf16[144,1152]{1,0:T(8,128)(2,1)S(1)}, u32[]{:S(2)}, u32[]{:S(2)}) %collective-permute-start.7) | collective-permute-done | bytes 331808 | tf_op jit(solution)/shard_map/ppermute | solution.py:80
  57.2 5.9 %collective-permute-done.6.t2 = bf16[144,1152]{1,0:T(8,128)(2,1)S(1)} collective-permute-done((bf16[144,1152]{1,0:T(8,128)(2,1)}, bf16[144,1152]{1,0:T(8,128)(2,1)S(1)}, u32[]{:S(2)}, u32[]{:S(2)}) %collective-permute-start.6) | collective-permute-done | bytes 331808 | tf_op jit(solution)/shard_map/ppermute | solution.py:80
  63.8 1.0 copy-done.8
  64.7 1.3 shard_map.150
  66.0 4.4 %all-to-all-start.1 = ((bf16[4,144,256]{2,1,0:T(8,128)(2,1)}), bf16[4,144,256]{2,1,0:T(8,128)(2,1)S(1)}, u32[]{:S(2)}, u32[]{:S(2)}) async-start(bf16[4,144,256]{2,1,0:T(8,128)(2,1)} %shard_map.150), calls=%async_computation.1 | async-start | bytes 589824 | tf_op jit(solution)/shard_map/all_to_all | solution.py:20
  70.5 5.5 %all-to-all-done.1.got_ref = bf16[4,144,256]{2,1,0:T(8,128)(2,1)S(1)} async-done(((bf16[4,144,256]{2,1,0:T(8,128)(2,1)}), bf16[4,144,256]{2,1,0:T(8,128)(2,1)S(1)}, u32[]{:S(2)}, u32[]{:S(2)}) %all-to-all-start.1) | async-done | bytes 294944 | tf_op jit(solution)/shard_map/all_to_all | solution.py:20
  76.0 0.9 shard_map.151
  76.9 14.2 %all-to-all-start.2 = ((bf16[8,288,128]{2,1,0:T(8,128)(2,1)}), bf16[8,288,128]{2,1,0:T(8,128)(2,1)S(1)}, u32[]{:S(2)}, u32[]{:S(2)}) async-start(bf16[8,288,128]{2,1,0:T(8,128)(2,1)} %shard_map.151), calls=%async_computation.2 | async-start | bytes 1179648 | tf_op jit(solution)/shard_map/all_to_all | solution.py:20
  91.1 3.7 %shard_map.152 = (bf16[144,1152]{1,0:T(8,128)(2,1)S(1)}, bf16[144,1152]{1,0:T(8,128)(2,1)}, bf16[144,1152]{1,0:T(8,128)(2,1)}, bf16[144,1152]{1,0:T(8,128)(2,1)}) custom-call(s32[1]{0:T(128)} %bitcast.1.me_ref, bf16[144,4608]{1,0:T(8,128)(2,1)S(1)} %copy-done.2), custom_call_target="tpu_custom_call" | custom-call | bytes 2654208 | tf_op jit(solution)/shard_map/pallas_call | solution.py:49
  95.5 3.0 %collective-permute-start.9 = (bf16[144,1152]{1,0:T(8,128)(2,1)}, bf16[144,1152]{1,0:T(8,128)(2,1)S(1)}, u32[]{:S(2)}, u32[]{:S(2)}) collective-permute-start(bf16[144,1152]{1,0:T(8,128)(2,1)} %get-tuple-element.37), channel_id=1, source_target_pairs={{0,24},{24,0},{48,72},{72,48},{1,25},{25,1},{49,73},{73,49},{2,26}... | collective-permute-start | bytes 995336 | tf_op jit(solution)/shard_map/ppermute | solution.py:80
  98.6 1.9 collective-permute-start.10
  100.5 3.5 %collective-permute-start.11 = (bf16[144,1152]{1,0:T(8,128)(2,1)}, bf16[144,1152]{1,0:T(8,128)(2,1)S(1)}, u32[]{:S(2)}, u32[]{:S(2)}) collective-permute-start(bf16[144,1152]{1,0:T(8,128)(2,1)} %get-tuple-element.39), channel_id=1, source_target_pairs={{0,72},{24,48},{48,24},{72,0},{1,73},{25,49},{49,25},{73,1},{2,74}... | collective-permute-start | bytes 995336 | tf_op jit(solution)/shard_map/ppermute | solution.py:80
  107.3 6.0 %collective-permute-start.14 = (bf16[16,1024]{1,0:T(8,128)(2,1)}, bf16[16,1024]{1,0:T(8,128)(2,1)}, u32[]{:S(2)}, u32[]{:S(2)}) collective-permute-start(bf16[16,1024]{1,0:T(8,128)(2,1)} %fusion.33), channel_id=1, source_target_pairs={{0,3},{3,6},{6,9},{9,12},{12,15},{15,18},{18,21},{1,4},{4,7},{7,10... | collective-permute-start | bytes 98312 | tf_op jit(solution)/shard_map/ppermute | solution.py:254
  113.3 4.9 %collective-permute-done.11.t3 = bf16[144,1152]{1,0:T(8,128)(2,1)S(1)} collective-permute-done((bf16[144,1152]{1,0:T(8,128)(2,1)}, bf16[144,1152]{1,0:T(8,128)(2,1)S(1)}, u32[]{:S(2)}, u32[]{:S(2)}) %collective-permute-start.11) | collective-permute-done | bytes 331808 | tf_op jit(solution)/shard_map/ppermute | solution.py:80
  118.2 1.4 shard_map.153
  119.6 7.4 %all-to-all-start.3 = ((bf16[3,288,128]{2,1,0:T(8,128)(2,1)}), bf16[3,288,128]{2,1,0:T(8,128)(2,1)S(1)}, u32[]{:S(2)}, u32[]{:S(2)}) async-start(bf16[3,288,128]{2,1,0:T(8,128)(2,1)} %shard_map.153), calls=%async_computation.3 | async-start | bytes 442368 | tf_op jit(solution)/shard_map/all_to_all | solution.py:20
  127.6 5.9 %all-to-all-done.3.got_ref = bf16[3,288,128]{2,1,0:T(8,128)(2,1)S(1)} async-done(((bf16[3,288,128]{2,1,0:T(8,128)(2,1)}), bf16[3,288,128]{2,1,0:T(8,128)(2,1)S(1)}, u32[]{:S(2)}, u32[]{:S(2)}) %all-to-all-start.3) | async-done | bytes 221216 | tf_op jit(solution)/shard_map/all_to_all | solution.py:20
  133.5 0.9 copy-done.9
  134.4 1.5 shard_map.154
  135.9 10.7 %all-to-all-start.4 = ((bf16[8,288,128]{2,1,0:T(8,128)(2,1)}), bf16[8,288,128]{2,1,0:T(8,128)(2,1)S(1)}, u32[]{:S(2)}, u32[]{:S(2)}) async-start(bf16[8,288,128]{2,1,0:T(8,128)(2,1)} %shard_map.154), calls=%async_computation.4 | async-start | bytes 1179648 | tf_op jit(solution)/shard_map/all_to_all | solution.py:20
  146.6 3.6 %collective-permute-start.12 = (bf16[16,1152]{1,0:T(8,128)(2,1)S(1)}, bf16[16,1152]{1,0:T(8,128)(2,1)S(1)}, u32[]{:S(2)}, u32[]{:S(2)}) collective-permute-start(bf16[16,1152]{1,0:T(8,128)(2,1)S(1)} %fusion.27), channel_id=1, source_target_pairs={{0,96},{96,192},{192,288},{288,384},{384,480},{480,576},{576,672},... | collective-permute-start | bytes 110600 | tf_op jit(solution)/shard_map/ppermute | solution.py:262
  150.3 3.2 %collective-permute-start.13 = (bf16[16,1152]{1,0:T(8,128)(2,1)S(1)}, bf16[16,1152]{1,0:T(8,128)(2,1)S(1)}, u32[]{:S(2)}, u32[]{:S(2)}) collective-permute-start(bf16[16,1152]{1,0:T(8,128)(2,1)S(1)} %fusion.23), channel_id=1, source_target_pairs={{96,0},{192,96},{288,192},{384,288},{480,384},{576,480},{672,576},... | collective-permute-start | bytes 110600 | tf_op jit(solution)/shard_map/ppermute | solution.py:262
  153.5 1.4 fusion.30
  154.9 1.3 collective-permute-start.15
  156.8 3.2 %all-to-all-done.4.held_ref = bf16[8,288,128]{2,1,0:T(8,128)(2,1)S(1)} async-done(((bf16[8,288,128]{2,1,0:T(8,128)(2,1)}), bf16[8,288,128]{2,1,0:T(8,128)(2,1)S(1)}, u32[]{:S(2)}, u32[]{:S(2)}) %all-to-all-start.4) | async-done | bytes 589856 | tf_op jit(solution)/shard_map/all_to_all | solution.py:20
  160.0 4.2 %collective-permute-done.15.hi_ref = bf16[16,1024]{1,0:T(8,128)(2,1)} collective-permute-done((bf16[16,1024]{1,0:T(8,128)(2,1)}, bf16[16,1024]{1,0:T(8,128)(2,1)}, u32[]{:S(2)}, u32[]{:S(2)}) %collective-permute-start.15) | collective-permute-done | bytes 32800 | tf_op jit(solution)/shard_map/ppermute | solution.py:254
  164.2 2.4 %shard_map.155 = bf16[3,320,128]{2,1,0:T(8,128)(2,1)S(1)} custom-call(s32[1]{0:T(128)} %bitcast.2.me_ref, bf16[8,288,128]{2,1,0:T(8,128)(2,1)S(1)} %all-to-all-done.4.held_ref, bf16[256,1024]{1,0:T(8,128)(2,1)S(1)} %get-tuple-element.41.t0, bf16[256,1024]{1,0:T(8,128)(2,1)S(1)} %collective-permute-done.4.t1, ...), custom_call_target="tpu_custom_call" | custom-call | flops 226492416 | bytes 2473984 | tf_op jit(solution)/shard_map/pallas_call | solution.py:49
  166.6 17.6 %all_to_all.40.got_ref = bf16[3,320,128]{2,1,0:T(8,128)(2,1)S(1)} all-to-all(bf16[3,320,128]{2,1,0:T(8,128)(2,1)S(1)} %shard_map.155), channel_id=1, replica_groups=mesh['y'=8,'xl'=2,'c'=2,'xh'=2,'zh'=4,'zl'=3] {'zl'}, dimensions={0} | all-to-all | bytes 491520 | tf_op jit(solution)/shard_map/all_to_all | solution.py:20
  184.3 23.9 %all_to_all.41.held_ref = bf16[8,160,256]{2,1,0:T(8,128)(2,1)S(1)} all-to-all(bf16[8,160,256]{2,1,0:T(8,128)(2,1)S(1)} %shard_map.156), channel_id=1, replica_groups=mesh['y'=8,'xl'=2,'c'=2,'xh'=2,'zh'=4,'zl'=3] {'y'}, dimensions={0} | all-to-all | bytes 1310720 | tf_op jit(solution)/shard_map/all_to_all | solution.py:20
  208.1 1.8 shard_map.157
  209.9 7.5 %all-to-all-start.7 = ((bf16[4,160,256]{2,1,0:T(8,128)(2,1)}), bf16[4,160,256]{2,1,0:T(8,128)(2,1)S(1)}, u32[]{:S(2)}, u32[]{:S(2)}) async-start(bf16[4,160,256]{2,1,0:T(8,128)(2,1)} %shard_map.157), calls=%async_computation.7 | async-start | bytes 655360 | tf_op jit(solution)/shard_map/all_to_all | solution.py:20
  217.5 5.9 %all-to-all-done.7 = bf16[4,160,256]{2,1,0:T(8,128)(2,1)S(1)} async-done(((bf16[4,160,256]{2,1,0:T(8,128)(2,1)}), bf16[4,160,256]{2,1,0:T(8,128)(2,1)S(1)}, u32[]{:S(2)}, u32[]{:S(2)}) %all-to-all-start.7) | async-done | bytes 327712 | tf_op jit(solution)/shard_map/all_to_all | solution.py:20
  224.3 1.6 fusion.4
  (92 shorter events, 10.5 us)
Async XLA Ops:
  0.6 2.5 %copy-start = (bf16[16,2]{0,1:T(2,128)(2,1)S(1)}, bf16[16,2]{0,1:T(2,128)(2,1)}, u32[]{:S(2)}) copy-start(bf16[16,2]{0,1:T(2,128)(2,1)} %param.17) | copy-start | bytes 196
  3.1 7.2 %copy-start.3 = (bf16[128,3072]{1,0:T(8,128)(2,1)S(1)}, bf16[128,3072]{1,0:T(8,128)(2,1)}, u32[]{:S(2)}) copy-start(bf16[128,3072]{1,0:T(8,128)(2,1)} %first_ref.1) | copy-start | bytes 2359300
  4.1 29.6 %collective-permute-start.3 = (bf16[2,144,1]{2,0,1:T(2,128)(2,1)}, bf16[2,144,1]{2,0,1:T(2,128)(2,1)S(1)}, u32[]{:S(2)}, u32[]{:S(2)}) collective-permute-start(bf16[2,144,1]{2,0,1:T(2,128)(2,1)} %get-tuple-element.86), channel_id=1, source_target_pairs={{0,1},{1,2},{2,3},{3,4},{4,5},{5,6},{6,7},{7,8},{8,9},{9,10},{10,1... | collective-permute-start | bytes 1736 | tf_op jit(solution)/shard_map/ppermute | solution.py:28
  8.9 24.9 %collective-permute-start.2 = (bf16[2,144,1]{2,0,1:T(2,128)(2,1)}, bf16[2,144,1]{2,0,1:T(2,128)(2,1)S(1)}, u32[]{:S(2)}, u32[]{:S(2)}) collective-permute-start(bf16[2,144,1]{2,0,1:T(2,128)(2,1)} %get-tuple-element.85), channel_id=1, source_target_pairs={{1,0},{2,1},{3,2},{4,3},{5,4},{6,5},{7,6},{8,7},{9,8},{10,9},{11,1... | collective-permute-start | bytes 1736 | tf_op jit(solution)/shard_map/ppermute | solution.py:29
  10.3 1.1 copy-start.4
  11.4 18.6 %copy-start.15 = (s32[144,128]{1,0:T(8,128)S(1)}, s32[144,128]{1,0:T(8,128)}, u32[]{:S(2)}) copy-start(s32[144,128]{1,0:T(8,128)} %param.15) | copy-start | bytes 221188
  11.4 18.6 %copy-start.1 = (bf16[144,4608]{1,0:T(8,128)(2,1)S(1)}, bf16[144,4608]{1,0:T(8,128)(2,1)}, u32[]{:S(2)}) copy-start(bf16[144,4608]{1,0:T(8,128)(2,1)} %rows_ref.2) | copy-start | bytes 3981316
  12.5 0.8 copy-start.14
  13.3 21.1 %collective-permute-start.4 = (bf16[256,1024]{1,0:T(8,128)(2,1)}, bf16[256,1024]{1,0:T(8,128)(2,1)S(1)}, u32[]{:S(2)}, u32[]{:S(2)}) collective-permute-start(bf16[256,1024]{1,0:T(8,128)(2,1)} %get-tuple-element.27), channel_id=1, source_target_pairs={{0,1},{1,2},{2,0},{3,4},{4,5},{5,3},{6,7},{7,8},{8,6},{9,10},{10,1... | collective-permute-start | bytes 1572872 | tf_op jit(solution)/shard_map/ppermute | solution.py:98
  19.2 14.5 %collective-permute-start.1 = (bf16[2,1,128]{2,0,1:T(2,128)(2,1)S(1)}, bf16[2,1,128]{2,0,1:T(2,128)(2,1)S(1)}, u32[]{:S(2)}, u32[]{:S(2)}) collective-permute-start(bf16[2,1,128]{2,0,1:T(2,128)(2,1)S(1)} %get-tuple-element.84), channel_id=1, source_target_pairs={{0,24},{24,48},{48,72},{72,96},{96,120},{120,144},{144,168},{168,1... | collective-permute-start | bytes 1544 | tf_op jit(solution)/shard_map/ppermute | solution.py:28
  23.5 10.3 %collective-permute-start = (bf16[2,1,128]{2,0,1:T(2,128)(2,1)S(1)}, bf16[2,1,128]{2,0,1:T(2,128)(2,1)S(1)}, u32[]{:S(2)}, u32[]{:S(2)}) collective-permute-start(bf16[2,1,128]{2,0,1:T(2,128)(2,1)S(1)} %get-tuple-element.83), channel_id=1, source_target_pairs={{24,0},{48,24},{72,48},{96,72},{120,96},{144,120},{168,144},{192,1... | collective-permute-start | bytes 1544 | tf_op jit(solution)/shard_map/ppermute | solution.py:29
  35.4 28.3 %all-to-all-start = ((bf16[8,144,256]{2,1,0:T(8,128)(2,1)}), bf16[8,144,256]{2,1,0:T(8,128)(2,1)S(1)}, u32[]{:S(2)}, u32[]{:S(2)}) async-start(bf16[8,144,256]{2,1,0:T(8,128)(2,1)} %broadcast_in_dim.2), calls=%async_computation | async-start | bytes 1179648 | tf_op jit(solution)/shard_map/all_to_all | solution.py:20
  39.1 12.8 %collective-permute-start.5 = (bf16[144,1152]{1,0:T(8,128)(2,1)}, bf16[144,1152]{1,0:T(8,128)(2,1)S(1)}, u32[]{:S(2)}, u32[]{:S(2)}) collective-permute-start(bf16[144,1152]{1,0:T(8,128)(2,1)} %get-tuple-element.31), channel_id=1, source_target_pairs={{0,24},{24,0},{48,72},{72,48},{1,25},{25,1},{49,73},{73,49},{2,26}... | collective-permute-start | bytes 995336 | tf_op jit(solution)/shard_map/ppermute | solution.py:80
  44.7 12.4 %collective-permute-start.7 = (bf16[144,1152]{1,0:T(8,128)(2,1)}, bf16[144,1152]{1,0:T(8,128)(2,1)S(1)}, u32[]{:S(2)}, u32[]{:S(2)}) collective-permute-start(bf16[144,1152]{1,0:T(8,128)(2,1)} %get-tuple-element.33), channel_id=1, source_target_pairs={{0,72},{24,48},{48,24},{72,0},{1,73},{25,49},{49,25},{73,1},{2,74}... | collective-permute-start | bytes 995336 | tf_op jit(solution)/shard_map/ppermute | solution.py:80
  46.7 16.4 %collective-permute-start.6 = (bf16[144,1152]{1,0:T(8,128)(2,1)}, bf16[144,1152]{1,0:T(8,128)(2,1)S(1)}, u32[]{:S(2)}, u32[]{:S(2)}) collective-permute-start(bf16[144,1152]{1,0:T(8,128)(2,1)} %get-tuple-element.32), channel_id=1, source_target_pairs={{0,48},{24,72},{48,0},{72,24},{1,49},{25,73},{49,1},{73,25},{2,50}... | collective-permute-start | bytes 995336 | tf_op jit(solution)/shard_map/ppermute | solution.py:80
  49.9 20.5 %collective-permute-start.8 = (bf16[256,1024]{1,0:T(8,128)(2,1)}, bf16[256,1024]{1,0:T(8,128)(2,1)S(1)}, u32[]{:S(2)}, u32[]{:S(2)}) collective-permute-start(bf16[256,1024]{1,0:T(8,128)(2,1)} %copy-done.14), channel_id=1, source_target_pairs={{0,2},{1,0},{2,1},{3,5},{4,3},{5,4},{6,8},{7,6},{8,7},{9,11},{10,9... | collective-permute-start | bytes 1572872 | tf_op jit(solution)/shard_map/ppermute | solution.py:98
  63.0 0.7 copy-start.7
  63.8 1.0 copy-start.8
  66.0 10.0 %all-to-all-start.1 = ((bf16[4,144,256]{2,1,0:T(8,128)(2,1)}), bf16[4,144,256]{2,1,0:T(8,128)(2,1)S(1)}, u32[]{:S(2)}, u32[]{:S(2)}) async-start(bf16[4,144,256]{2,1,0:T(8,128)(2,1)} %shard_map.150), calls=%async_computation.1 | async-start | bytes 589824 | tf_op jit(solution)/shard_map/all_to_all | solution.py:20
  70.5 20.6 %copy-start.2 = (bf16[144,4608]{1,0:T(8,128)(2,1)S(1)}, bf16[144,4608]{1,0:T(8,128)(2,1)}, u32[]{:S(2)}) copy-start(bf16[144,4608]{1,0:T(8,128)(2,1)} %rows_ref.3) | copy-start | bytes 3981316
  76.9 27.2 %copy-start.19 = (f32[144]{0:T(256)S(1)}, f32[144]{0:T(256)}, u32[]{:S(2)}) copy-start(f32[144]{0:T(256)} %param.23) | copy-start | bytes 1732
  76.9 41.3 %all-to-all-start.2 = ((bf16[8,288,128]{2,1,0:T(8,128)(2,1)}), bf16[8,288,128]{2,1,0:T(8,128)(2,1)S(1)}, u32[]{:S(2)}, u32[]{:S(2)}) async-start(bf16[8,288,128]{2,1,0:T(8,128)(2,1)} %shard_map.151), calls=%async_computation.2 | async-start | bytes 1179648 | tf_op jit(solution)/shard_map/all_to_all | solution.py:20
  94.8 0.7 copy-start.5
  95.5 17.8 %collective-permute-start.9 = (bf16[144,1152]{1,0:T(8,128)(2,1)}, bf16[144,1152]{1,0:T(8,128)(2,1)S(1)}, u32[]{:S(2)}, u32[]{:S(2)}) collective-permute-start(bf16[144,1152]{1,0:T(8,128)(2,1)} %get-tuple-element.37), channel_id=1, source_target_pairs={{0,24},{24,0},{48,72},{72,48},{1,25},{25,1},{49,73},{73,49},{2,26}... | collective-permute-start | bytes 995336 | tf_op jit(solution)/shard_map/ppermute | solution.py:80
  98.6 14.8 %collective-permute-start.10 = (bf16[144,1152]{1,0:T(8,128)(2,1)}, bf16[144,1152]{1,0:T(8,128)(2,1)S(1)}, u32[]{:S(2)}, u32[]{:S(2)}) collective-permute-start(bf16[144,1152]{1,0:T(8,128)(2,1)} %get-tuple-element.38), channel_id=1, source_target_pairs={{0,48},{24,72},{48,0},{72,24},{1,49},{25,73},{49,1},{73,25},{2,50}... | collective-permute-start | bytes 995336 | tf_op jit(solution)/shard_map/ppermute | solution.py:80
  100.5 17.7 %collective-permute-start.11 = (bf16[144,1152]{1,0:T(8,128)(2,1)}, bf16[144,1152]{1,0:T(8,128)(2,1)S(1)}, u32[]{:S(2)}, u32[]{:S(2)}) collective-permute-start(bf16[144,1152]{1,0:T(8,128)(2,1)} %get-tuple-element.39), channel_id=1, source_target_pairs={{0,72},{24,48},{48,24},{72,0},{1,73},{25,49},{49,25},{73,1},{2,74}... | collective-permute-start | bytes 995336 | tf_op jit(solution)/shard_map/ppermute | solution.py:80
  107.3 52.7 %collective-permute-start.14 = (bf16[16,1024]{1,0:T(8,128)(2,1)}, bf16[16,1024]{1,0:T(8,128)(2,1)}, u32[]{:S(2)}, u32[]{:S(2)}) collective-permute-start(bf16[16,1024]{1,0:T(8,128)(2,1)} %fusion.33), channel_id=1, source_target_pairs={{0,3},{3,6},{6,9},{9,12},{12,15},{15,18},{18,21},{1,4},{4,7},{7,10... | collective-permute-start | bytes 98312 | tf_op jit(solution)/shard_map/ppermute | solution.py:254
  118.2 8.8 %copy-start.6 = (bf16[144,1152]{1,0:T(8,128)(2,1)S(1)}, bf16[144,1152]{1,0:T(8,128)(2,1)}, u32[]{:S(2)}) copy-start(bf16[144,1152]{1,0:T(8,128)(2,1)} %copy-done.5) | copy-start | bytes 995332
  118.2 15.3 %copy-start.12 = (f32[2]{0:T(128)S(1)}, f32[2]{0:T(128)}, u32[]{:S(2)}) copy-start(f32[2]{0:T(128)} %shift_ref.1) | copy-start | bytes 28
  118.2 15.3 %copy-start.13 = (f32[128]{0:T(128)S(1)}, f32[128]{0:T(128)}, u32[]{:S(2)}) copy-start(f32[128]{0:T(128)} %param.24) | copy-start | bytes 1540
  119.6 13.9 %all-to-all-start.3 = ((bf16[3,288,128]{2,1,0:T(8,128)(2,1)}), bf16[3,288,128]{2,1,0:T(8,128)(2,1)S(1)}, u32[]{:S(2)}, u32[]{:S(2)}) async-start(bf16[3,288,128]{2,1,0:T(8,128)(2,1)} %shard_map.153), calls=%async_computation.3 | async-start | bytes 442368 | tf_op jit(solution)/shard_map/all_to_all | solution.py:20
  133.5 0.9 copy-start.9
  135.9 24.1 %all-to-all-start.4 = ((bf16[8,288,128]{2,1,0:T(8,128)(2,1)}), bf16[8,288,128]{2,1,0:T(8,128)(2,1)S(1)}, u32[]{:S(2)}, u32[]{:S(2)}) async-start(bf16[8,288,128]{2,1,0:T(8,128)(2,1)} %shard_map.154), calls=%async_computation.4 | async-start | bytes 1179648 | tf_op jit(solution)/shard_map/all_to_all | solution.py:20
  146.6 9.6 %collective-permute-start.12 = (bf16[16,1152]{1,0:T(8,128)(2,1)S(1)}, bf16[16,1152]{1,0:T(8,128)(2,1)S(1)}, u32[]{:S(2)}, u32[]{:S(2)}) collective-permute-start(bf16[16,1152]{1,0:T(8,128)(2,1)S(1)} %fusion.27), channel_id=1, source_target_pairs={{0,96},{96,192},{192,288},{288,384},{384,480},{480,576},{576,672},... | collective-permute-start | bytes 110600 | tf_op jit(solution)/shard_map/ppermute | solution.py:262
  150.3 5.9 %collective-permute-start.13 = (bf16[16,1152]{1,0:T(8,128)(2,1)S(1)}, bf16[16,1152]{1,0:T(8,128)(2,1)S(1)}, u32[]{:S(2)}, u32[]{:S(2)}) collective-permute-start(bf16[16,1152]{1,0:T(8,128)(2,1)S(1)} %fusion.23), channel_id=1, source_target_pairs={{96,0},{192,96},{288,192},{384,288},{480,384},{576,480},{672,576},... | collective-permute-start | bytes 110600 | tf_op jit(solution)/shard_map/ppermute | solution.py:262
  154.9 9.3 %collective-permute-start.15 = (bf16[16,1024]{1,0:T(8,128)(2,1)}, bf16[16,1024]{1,0:T(8,128)(2,1)}, u32[]{:S(2)}, u32[]{:S(2)}) collective-permute-start(bf16[16,1024]{1,0:T(8,128)(2,1)} %fusion.30), channel_id=1, source_target_pairs={{3,0},{6,3},{9,6},{12,9},{15,12},{18,15},{21,18},{4,1},{7,4},{10,7... | collective-permute-start | bytes 98312 | tf_op jit(solution)/shard_map/ppermute | solution.py:254
  156.2 0.6 copy-start.10
  184.2 24.0 %copy-start.11 = (bf16[16,1152]{1,0:T(8,128)(2,1)S(1)}, bf16[16,1152]{1,0:T(8,128)(2,1)}, u32[]{:S(2)}) copy-start(bf16[16,1152]{1,0:T(8,128)(2,1)} %copy-done.10) | copy-start | bytes 110596
  208.1 9.3 %copy-start.20 = (f32[16,2]{0,1:T(2,128)S(1)}, f32[16,2]{0,1:T(2,128)}, u32[]{:S(2)}) copy-start(f32[16,2]{0,1:T(2,128)} %param.18) | copy-start | bytes 388
  209.9 13.4 %all-to-all-start.7 = ((bf16[4,160,256]{2,1,0:T(8,128)(2,1)}), bf16[4,160,256]{2,1,0:T(8,128)(2,1)S(1)}, u32[]{:S(2)}, u32[]{:S(2)}) async-start(bf16[4,160,256]{2,1,0:T(8,128)(2,1)} %shard_map.157), calls=%async_computation.7 | async-start | bytes 655360 | tf_op jit(solution)/shard_map/all_to_all | solution.py:20
  223.4 0.9 copy-start.16
  223.4 0.9 copy-start.18
  223.8 2.1 copy-start.17

commit v8 on v7

--- a/solution.py
+++ b/solution.py
@@ -145,9 +145,9 @@
         out_ref[g, 144:, :] = total[:, 128:]
 
 
-def scale_kernel(shift_ref, got_ref, x_ref, y_ref, out_ref):
+def scale_kernel(shift_ref, got_ref, denom_ref, out_ref):
     total = added(got_ref)
-    denom = x_ref[...] + y_ref[...]
+    denom = denom_ref[...]
     for mode in range(2):
         rows = slice(144 * mode, 144 * (mode + 1))
         scaled = (total[rows] / (denom + shift_ref[mode])).astype(BF)
@@ -304,18 +304,20 @@
     block = to_x(divergence.reshape(288, 128))
     held = exchange(jnp.broadcast_to(block[None], (8, 144, 256)), "y")
     got = exchange(x_products(quad_me, held, table_fx), QUAD)
-    got, y_two = lax.optimization_barrier((got, y_two))
+    shapes = (mode_shape[:, 0], mode_shape[:, 1])
+    got, y_two, (shape_zero, shape_one) = lax.optimization_barrier((got, y_two, shapes))
     cut_ix = quad_cut(quad_me, inverse_x)
     table_y = (cut_y[0], y_one, y_two)
     spread = jax.ShapeDtypeStruct((8, 288, 128), BF)
     held = exchange(call(to_y_kernel, spread, (quad_me, got)), ("xh", "zh"))
-    held, table_ix = lax.optimization_barrier(
-        (held, [cut_ix[0]] + [quad_send(cut_ix[step], step) for step in (1, 2, 3)])
-    )
+    table_ix = [cut_ix[0]] + [quad_send(cut_ix[step], step) for step in (1, 2, 3)]
+    denom = eigen_x[:, None] + eigen_y[None, :]
+    held, table_ix, denom = lax.optimization_barrier((held, table_ix, denom))
     got = exchange(y_products(ring_me, held, table_y), "zl")
-    eigen = (eigen_x.reshape(144, 1), eigen_y.reshape(1, 128))
-    held = exchange(call(scale_kernel, spread, (mode_shift, got, *eigen)), ("xh", "zh"))
-    outer_y, outer_x = ring_outer(ring_me[0], table_y), quad_outer(quad_me[0], table_ix)
+    got, table_ix, table_y = lax.optimization_barrier((got, table_ix, table_y))
+    outer_y = ring_outer(ring_me[0], table_y)
+    held = exchange(call(scale_kernel, spread, (mode_shift, got, denom)), ("xh", "zh"))
+    outer_x = quad_outer(quad_me[0], table_ix)
     held, outer_x = lax.optimization_barrier((held, outer_x))
     got = exchange(y_back_products(ring_me, held, table_y, outer_y), "zl")
     spread = jax.ShapeDtypeStruct((8, 160, 256), BF)
@@ -330,8 +332,8 @@
     padded = jnp.concatenate([sides[:, 0, :, None], pressure, sides[:, 1, :, None]], axis=2)
     grad_y = 0.5 * (padded[:, :, 2:] - padded[:, :, :-2])
     wet_f = wet_int.astype(F32)
-    shape_zero = mode_shape[:, 0][:, None, None]
-    shape_one = mode_shape[:, 1][:, None, None]
+    shape_zero = shape_zero[:, None, None]
+    shape_one = shape_one[:, None, None]
     u_correct = (-wet_f * (shape_zero * grad_x[0][None] + shape_one * grad_x[1][None])).astype(BF)
     v_correct = (-wet_f * (shape_zero * grad_y[0][None] + shape_one * grad_y[1][None])).astype(BF)
     return (u_correct, v_correct, pressure)

time: 227 us -> 227 us (level)
  starting transfers between devices: 105 us -> 95.4 us
  blocking collectives: 41.5 us -> 50.8 us
  local copies, waits for them, and re-layouts: 11.5 us -> 8.34 us
    all_to_all x6 -> x5, starting transfers between devices: 47.9 us -> 38.1 us  [exchange(): return lax.all_to_all(parts, axes, 0, 0)]
    ppermute x6, waiting for transfers between devices: 16 us -> 25.6 us  [quad_send(): return lax.ppermute(piece, QUAD, [(i, i ^ step) for i in range(4)])]
    all_to_all x2 -> x3, blocking collectives: 41.5 us -> 50.8 us  [exchange(): return lax.all_to_all(parts, axes, 0, 0)]
    all_to_all x6 -> x5, waiting for transfers between devices: 20.4 us -> 12 us  [exchange(): return lax.all_to_all(parts, axes, 0, 0)]
  transfers between devices with their start and end apart: 22 -> 21, of which waited for: 8 -> 7; matrix products, arithmetic and copies ran while one was open for 3% -> 2% of each run, Pallas kernels for 6% -> 4%
where the time goes in v8:
time: 227 us; the launch traced here: 224 us
  starting transfers between devices  95.4 us (42%)
  blocking collectives  50.8 us (22%)
  waiting for transfers between devices  42.8 us (19%)
  Pallas kernels  16 us (7%)
  local copies, waits for them, and re-layouts  8.34 us (4%)
  other arithmetic  7.93 us (3%)
    all_to_all x3, blocking collectives, exchange(): return lax.all_to_all(parts, axes, 0, 0)  50.8 us
    all_to_all x5, starting transfers between devices, exchange(): return lax.all_to_all(parts, axes, 0, 0)  38.1 us
    ppermute x6, waiting for transfers between devices, quad_send(): return lax.ppermute(piece, QUAD, [(i, i ^ step) for i in range(4)])  25.6 us
    ppermute x6, starting transfers between devices, quad_send(): return lax.ppermute(piece, QUAD, [(i, i ^ step) for i in range(4)])  19.4 us
    pallas_call x10, Pallas kernels, call(): pl.pallas_call(kernel, out_shape=out_shape, in_specs=[smem] + [vmem] * (l...  16 us
    all_to_all x5, waiting for transfers between devices, exchange(): return lax.all_to_all(parts, axes, 0, 0)  12 us
    ppermute x2, starting transfers between devices, edges(): lax.ppermute(lax.slice_in_dim(block, block.shape[dim] - 1, None, axis=dim...  9.96 us
    ppermute x2, starting transfers between devices, edges(): high = lax.ppermute(lax.slice_in_dim(block, 0, 1, axis=dim), axes, backward)  8.13 us
  transfers between devices with their start and end apart: 21, of which 7 were waited for; matrix products, arithmetic and copies ran while one was open for 2% of the time, Pallas kernels for 4%

profile of v8, /device:TPU:1, one launch (start us, length us, event | category | flops | bytes accessed | tf_op | source)
XLA Modules:
  0.0 224.0 jit_solution(11723732413623136270)
XLA Ops:
  0.6 2.4 %fusion.8 = (bf16[16,144,128]{2,1,0:T(8,128)(2,1)}, bf16[16,144,128]{2,1,0:T(8,128)(2,1)S(1)}) fusion(bf16[16,144,128]{2,1,0:T(8,128)(2,1)} %param.13, s32[144,128]{1,0:T(8,128)} %param.15, s32[144,128]{1,0:T(8,128)} %param.16, bf16[16,144,128]{2,1,0:T(8,128)(2,1)} %param.14), kind=kLoop, calls=%fused_computation.13 | loop fusion | flops 2949120 | bytes 2506752 | tf_op jit(solution)/shard_map/mul | solution.py:291
  4.1 5.5 %collective-permute-start.3 = (bf16[2,144,1]{2,0,1:T(2,128)(2,1)}, bf16[2,144,1]{2,0,1:T(2,128)(2,1)}, u32[]{:S(2)}, u32[]{:S(2)}) collective-permute-start(bf16[2,144,1]{2,0,1:T(2,128)(2,1)} %get-tuple-element.108), channel_id=1, source_target_pairs={{0,1},{1,2},{2,3},{3,4},{4,5},{5,6},{6,7},{7,8},{8,9},{9,10},{10,1... | collective-permute-start | bytes 1736 | tf_op jit(solution)/shard_map/ppermute | solution.py:28
  9.6 1.3 collective-permute-start.2
  10.9 1.1 copy-done.4
  12.0 1.1 shard_map.148
  13.9 4.0 %collective-permute-start.4 = (bf16[256,1024]{1,0:T(8,128)(2,1)}, bf16[256,1024]{1,0:T(8,128)(2,1)S(1)}, u32[]{:S(2)}, u32[]{:S(2)}) collective-permute-start(bf16[256,1024]{1,0:T(8,128)(2,1)} %get-tuple-element.38), channel_id=1, source_target_pairs={{0,1},{1,2},{2,0},{3,4},{4,5},{5,3},{6,7},{7,8},{8,6},{9,10},{10,1... | collective-permute-start | bytes 1572872 | tf_op jit(solution)/shard_map/ppermute | solution.py:98
  17.9 1.3 fusion.44
  19.2 4.5 %collective-permute-start.1 = (bf16[2,1,128]{2,0,1:T(2,128)(2,1)S(1)}, bf16[2,1,128]{2,0,1:T(2,128)(2,1)S(1)}, u32[]{:S(2)}, u32[]{:S(2)}) collective-permute-start(bf16[2,1,128]{2,0,1:T(2,128)(2,1)S(1)} %get-tuple-element.106), channel_id=1, source_target_pairs={{0,24},{24,48},{48,72},{72,96},{96,120},{120,144},{144,168},{168,1... | collective-permute-start | bytes 1544 | tf_op jit(solution)/shard_map/ppermute | solution.py:28
  23.7 6.8 %collective-permute-start = (bf16[2,1,128]{2,0,1:T(2,128)(2,1)S(1)}, bf16[2,1,128]{2,0,1:T(2,128)(2,1)S(1)}, u32[]{:S(2)}, u32[]{:S(2)}) collective-permute-start(bf16[2,1,128]{2,0,1:T(2,128)(2,1)S(1)} %get-tuple-element.105), channel_id=1, source_target_pairs={{24,0},{48,24},{72,48},{96,72},{120,96},{144,120},{168,144},{192,1... | collective-permute-start | bytes 1544 | tf_op jit(solution)/shard_map/ppermute | solution.py:29
  30.6 3.7 %shard_map.149 = (bf16[144,1152]{1,0:T(8,128)(2,1)S(1)}, bf16[144,1152]{1,0:T(8,128)(2,1)}, bf16[144,1152]{1,0:T(8,128)(2,1)}, bf16[144,1152]{1,0:T(8,128)(2,1)}) custom-call(s32[1]{0:T(128)} %bitcast.me_ref, bf16[144,4608]{1,0:T(8,128)(2,1)S(1)} %copy-done.1), custom_call_target="tpu_custom_call" | custom-call | bytes 2654208 | tf_op jit(solution)/shard_map/pallas_call | solution.py:49
  34.4 0.9 convert_element_type.65
  36.1 0.9 broadcast_in_dim.2
  36.9 3.5 %all-to-all-start = ((bf16[8,144,256]{2,1,0:T(8,128)(2,1)}), bf16[8,144,256]{2,1,0:T(8,128)(2,1)S(1)}, u32[]{:S(2)}, u32[]{:S(2)}) async-start(bf16[8,144,256]{2,1,0:T(8,128)(2,1)} %broadcast_in_dim.2), calls=%async_computation | async-start | bytes 1179648 | tf_op jit(solution)/shard_map/all_to_all | solution.py:20
  40.5 5.8 %collective-permute-start.5 = (bf16[144,1152]{1,0:T(8,128)(2,1)}, bf16[144,1152]{1,0:T(8,128)(2,1)S(1)}, u32[]{:S(2)}, u32[]{:S(2)}) collective-permute-start(bf16[144,1152]{1,0:T(8,128)(2,1)} %get-tuple-element.42), channel_id=1, source_target_pairs={{0,24},{24,0},{48,72},{72,48},{1,25},{25,1},{49,73},{73,49},{2,26}... | collective-permute-start | bytes 995336 | tf_op jit(solution)/shard_map/ppermute | solution.py:80
  46.2 1.9 collective-permute-start.7
  48.2 3.3 %collective-permute-start.6 = (bf16[144,1152]{1,0:T(8,128)(2,1)}, bf16[144,1152]{1,0:T(8,128)(2,1)S(1)}, u32[]{:S(2)}, u32[]{:S(2)}) collective-permute-start(bf16[144,1152]{1,0:T(8,128)(2,1)} %get-tuple-element.43), channel_id=1, source_target_pairs={{0,48},{24,72},{48,0},{72,24},{1,49},{25,73},{49,1},{73,25},{2,50}... | collective-permute-start | bytes 995336 | tf_op jit(solution)/shard_map/ppermute | solution.py:80
  51.4 1.9 collective-permute-start.8
  53.4 5.3 %collective-permute-done.7.t3 = bf16[144,1152]{1,0:T(8,128)(2,1)S(1)} collective-permute-done((bf16[144,1152]{1,0:T(8,128)(2,1)}, bf16[144,1152]{1,0:T(8,128)(2,1)S(1)}, u32[]{:S(2)}, u32[]{:S(2)}) %collective-permute-start.7) | collective-permute-done | bytes 331808 | tf_op jit(solution)/shard_map/ppermute | solution.py:80
  58.7 5.9 %collective-permute-done.6.t2 = bf16[144,1152]{1,0:T(8,128)(2,1)S(1)} collective-permute-done((bf16[144,1152]{1,0:T(8,128)(2,1)}, bf16[144,1152]{1,0:T(8,128)(2,1)S(1)}, u32[]{:S(2)}, u32[]{:S(2)}) %collective-permute-start.6) | collective-permute-done | bytes 331808 | tf_op jit(solution)/shard_map/ppermute | solution.py:80
  65.3 1.0 copy-done.8
  66.2 1.3 shard_map.150
  67.5 4.4 %all-to-all-start.1 = ((bf16[4,144,256]{2,1,0:T(8,128)(2,1)}), bf16[4,144,256]{2,1,0:T(8,128)(2,1)S(1)}, u32[]{:S(2)}, u32[]{:S(2)}) async-start(bf16[4,144,256]{2,1,0:T(8,128)(2,1)} %shard_map.150), calls=%async_computation.1 | async-start | bytes 589824 | tf_op jit(solution)/shard_map/all_to_all | solution.py:20
  72.0 5.5 %all-to-all-done.1.got_ref = bf16[4,144,256]{2,1,0:T(8,128)(2,1)S(1)} async-done(((bf16[4,144,256]{2,1,0:T(8,128)(2,1)}), bf16[4,144,256]{2,1,0:T(8,128)(2,1)S(1)}, u32[]{:S(2)}, u32[]{:S(2)}) %all-to-all-start.1) | async-done | bytes 294944 | tf_op jit(solution)/shard_map/all_to_all | solution.py:20
  77.5 0.9 shard_map.151
  78.4 13.4 %all-to-all-start.2 = ((bf16[8,288,128]{2,1,0:T(8,128)(2,1)}), bf16[8,288,128]{2,1,0:T(8,128)(2,1)S(1)}, u32[]{:S(2)}, u32[]{:S(2)}) async-start(bf16[8,288,128]{2,1,0:T(8,128)(2,1)} %shard_map.151), calls=%async_computation.2 | async-start | bytes 1179648 | tf_op jit(solution)/shard_map/all_to_all | solution.py:20
  91.8 2.8 %shard_map.152 = (bf16[144,1152]{1,0:T(8,128)(2,1)S(1)}, bf16[144,1152]{1,0:T(8,128)(2,1)S(1)}, bf16[144,1152]{1,0:T(8,128)(2,1)S(1)}, bf16[144,1152]{1,0:T(8,128)(2,1)S(1)}) custom-call(s32[1]{0:T(128)} %bitcast.me_ref, bf16[144,4608]{1,0:T(8,128)(2,1)S(1)} %copy-done.2), custom_call_target="tpu_custom_call" | custom-call | bytes 2654208 | tf_op jit(solution)/shard_map/pallas_call | solution.py:49
  95.4 3.0 %collective-permute-start.9 = (bf16[144,1152]{1,0:T(8,128)(2,1)S(1)}, bf16[144,1152]{1,0:T(8,128)(2,1)S(1)}, u32[]{:S(2)}, u32[]{:S(2)}) collective-permute-start(bf16[144,1152]{1,0:T(8,128)(2,1)S(1)} %get-tuple-element.49), channel_id=1, source_target_pairs={{0,24},{24,0},{48,72},{72,48},{1,25},{25,1},{49,73},{73,49},{2,26}... | collective-permute-start | bytes 995336 | tf_op jit(solution)/shard_map/ppermute | solution.py:80
  98.4 1.9 collective-permute-start.10
  100.3 3.5 %collective-permute-start.11 = (bf16[144,1152]{1,0:T(8,128)(2,1)S(1)}, bf16[144,1152]{1,0:T(8,128)(2,1)S(1)}, u32[]{:S(2)}, u32[]{:S(2)}) collective-permute-start(bf16[144,1152]{1,0:T(8,128)(2,1)S(1)} %get-tuple-element.51), channel_id=1, source_target_pairs={{0,72},{24,48},{48,24},{72,0},{1,73},{25,49},{49,25},{73,1},{2,74}... | collective-permute-start | bytes 995336 | tf_op jit(solution)/shard_map/ppermute | solution.py:80
  104.6 7.2 %collective-permute-done.10.t2 = bf16[144,1152]{1,0:T(8,128)(2,1)S(1)} collective-permute-done((bf16[144,1152]{1,0:T(8,128)(2,1)S(1)}, bf16[144,1152]{1,0:T(8,128)(2,1)S(1)}, u32[]{:S(2)}, u32[]{:S(2)}) %collective-permute-start.10) | collective-permute-done | bytes 331808 | tf_op jit(solution)/shard_map/ppermute | solution.py:80
  111.8 7.2 %collective-permute-done.11.t3 = bf16[144,1152]{1,0:T(8,128)(2,1)S(1)} collective-permute-done((bf16[144,1152]{1,0:T(8,128)(2,1)S(1)}, bf16[144,1152]{1,0:T(8,128)(2,1)S(1)}, u32[]{:S(2)}, u32[]{:S(2)}) %collective-permute-start.11) | collective-permute-done | bytes 331808 | tf_op jit(solution)/shard_map/ppermute | solution.py:80
  119.0 1.4 shard_map.153
  120.4 5.9 %all-to-all-start.3 = ((bf16[3,288,128]{2,1,0:T(8,128)(2,1)}), bf16[3,288,128]{2,1,0:T(8,128)(2,1)S(1)}, u32[]{:S(2)}, u32[]{:S(2)}) async-start(bf16[3,288,128]{2,1,0:T(8,128)(2,1)} %shard_map.153), calls=%async_computation.3 | async-start | bytes 442368 | tf_op jit(solution)/shard_map/all_to_all | solution.py:20
  126.2 6.5 %all-to-all-done.3.got_ref = bf16[3,288,128]{2,1,0:T(8,128)(2,1)S(1)} async-done(((bf16[3,288,128]{2,1,0:T(8,128)(2,1)}), bf16[3,288,128]{2,1,0:T(8,128)(2,1)S(1)}, u32[]{:S(2)}, u32[]{:S(2)}) %all-to-all-start.3) | async-done | bytes 221216 | tf_op jit(solution)/shard_map/all_to_all | solution.py:20
  132.7 0.9 copy-done.9
  133.6 1.4 shard_map.154
  135.0 10.9 %all-to-all-start.4 = ((bf16[8,288,128]{2,1,0:T(8,128)(2,1)}), bf16[8,288,128]{2,1,0:T(8,128)(2,1)S(1)}, u32[]{:S(2)}, u32[]{:S(2)}) async-start(bf16[8,288,128]{2,1,0:T(8,128)(2,1)} %shard_map.154), calls=%async_computation.4 | async-start | bytes 1179648 | tf_op jit(solution)/shard_map/all_to_all | solution.py:20
  146.0 3.6 %collective-permute-start.12 = (bf16[16,1152]{1,0:T(8,128)(2,1)S(1)}, bf16[16,1152]{1,0:T(8,128)(2,1)S(1)}, u32[]{:S(2)}, u32[]{:S(2)}) collective-permute-start(bf16[16,1152]{1,0:T(8,128)(2,1)S(1)} %fusion.27), channel_id=1, source_target_pairs={{0,96},{96,192},{192,288},{288,384},{384,480},{480,576},{576,672},... | collective-permute-start | bytes 110600 | tf_op jit(solution)/shard_map/ppermute | solution.py:262
  149.7 3.1 %collective-permute-start.13 = (bf16[16,1152]{1,0:T(8,128)(2,1)S(1)}, bf16[16,1152]{1,0:T(8,128)(2,1)S(1)}, u32[]{:S(2)}, u32[]{:S(2)}) collective-permute-start(bf16[16,1152]{1,0:T(8,128)(2,1)S(1)} %fusion.23), channel_id=1, source_target_pairs={{96,0},{192,96},{288,192},{384,288},{480,384},{576,480},{672,576},... | collective-permute-start | bytes 110600 | tf_op jit(solution)/shard_map/ppermute | solution.py:262
  153.6 5.8 %collective-permute-start.14 = (bf16[16,1024]{1,0:T(8,128)(2,1)}, bf16[16,1024]{1,0:T(8,128)(2,1)}, u32[]{:S(2)}, u32[]{:S(2)}) collective-permute-start(bf16[16,1024]{1,0:T(8,128)(2,1)} %fusion.33), channel_id=1, source_target_pairs={{0,3},{3,6},{6,9},{9,12},{12,15},{15,18},{18,21},{1,4},{4,7},{7,10... | collective-permute-start | bytes 98312 | tf_op jit(solution)/shard_map/ppermute | solution.py:254
  160.0 1.3 collective-permute-start.15
  161.9 5.2 %collective-permute-done.15.hi_ref = bf16[16,1024]{1,0:T(8,128)(2,1)} collective-permute-done((bf16[16,1024]{1,0:T(8,128)(2,1)}, bf16[16,1024]{1,0:T(8,128)(2,1)}, u32[]{:S(2)}, u32[]{:S(2)}) %collective-permute-start.15) | collective-permute-done | bytes 32800 | tf_op jit(solution)/shard_map/ppermute | solution.py:254
  167.1 2.4 %shard_map.155 = bf16[3,320,128]{2,1,0:T(8,128)(2,1)S(1)} custom-call(s32[1]{0:T(128)} %bitcast.4.me_ref, bf16[8,288,128]{2,1,0:T(8,128)(2,1)S(1)} %all-to-all-done.4.held_ref, bf16[256,1024]{1,0:T(8,128)(2,1)S(1)} %get-tuple-element.67.t0, bf16[256,1024]{1,0:T(8,128)(2,1)S(1)} %collective-permute-done.4.t1, ...), custom_call_target="tpu_custom_call" | custom-call | flops 226492416 | bytes 2473984 | tf_op jit(solution)/shard_map/pallas_call | solution.py:49
  169.5 14.4 %all_to_all.40.got_ref = bf16[3,320,128]{2,1,0:T(8,128)(2,1)S(1)} all-to-all(bf16[3,320,128]{2,1,0:T(8,128)(2,1)S(1)} %shard_map.155), channel_id=1, replica_groups=mesh['y'=8,'xl'=2,'c'=2,'xh'=2,'zh'=4,'zl'=3] {'zl'}, dimensions={0} | all-to-all | bytes 491520 | tf_op jit(solution)/shard_map/all_to_all | solution.py:20
  184.0 23.9 %all_to_all.41.held_ref = bf16[8,160,256]{2,1,0:T(8,128)(2,1)S(1)} all-to-all(bf16[8,160,256]{2,1,0:T(8,128)(2,1)S(1)} %shard_map.156), channel_id=1, replica_groups=mesh['y'=8,'xl'=2,'c'=2,'xh'=2,'zh'=4,'zl'=3] {'y'}, dimensions={0} | all-to-all | bytes 1310720 | tf_op jit(solution)/shard_map/all_to_all | solution.py:20
  207.9 1.1 shard_map.157
  209.0 12.5 %all_to_all.42 = bf16[4,160,256]{2,1,0:T(8,128)(2,1)S(1)} all-to-all(bf16[4,160,256]{2,1,0:T(8,128)(2,1)S(1)} %shard_map.157), channel_id=1, replica_groups=mesh['y'=8,'xl'=2,'c'=2,'xh'=2,'zh'=4,'zl'=3] {'xl','c'}, dimensions={0} | all-to-all | bytes 655360 | tf_op jit(solution)/shard_map/all_to_all | solution.py:20
  222.4 1.6 fusion.4
  (91 shorter events, 7.8 us)
Async XLA Ops:
  0.6 2.5 %copy-start = (bf16[16,2]{0,1:T(2,128)(2,1)S(1)}, bf16[16,2]{0,1:T(2,128)(2,1)}, u32[]{:S(2)}) copy-start(bf16[16,2]{0,1:T(2,128)(2,1)} %param.17) | copy-start | bytes 196
  3.1 7.8 %copy-start.3 = (bf16[128,3072]{1,0:T(8,128)(2,1)S(1)}, bf16[128,3072]{1,0:T(8,128)(2,1)}, u32[]{:S(2)}) copy-start(bf16[128,3072]{1,0:T(8,128)(2,1)} %first_ref.1) | copy-start | bytes 2359300
  4.1 30.2 %collective-permute-start.3 = (bf16[2,144,1]{2,0,1:T(2,128)(2,1)}, bf16[2,144,1]{2,0,1:T(2,128)(2,1)}, u32[]{:S(2)}, u32[]{:S(2)}) collective-permute-start(bf16[2,144,1]{2,0,1:T(2,128)(2,1)} %get-tuple-element.108), channel_id=1, source_target_pairs={{0,1},{1,2},{2,3},{3,4},{4,5},{5,6},{6,7},{7,8},{8,9},{9,10},{10,1... | collective-permute-start | bytes 1736 | tf_op jit(solution)/shard_map/ppermute | solution.py:28
  9.6 25.7 %collective-permute-start.2 = (bf16[2,144,1]{2,0,1:T(2,128)(2,1)}, bf16[2,144,1]{2,0,1:T(2,128)(2,1)S(1)}, u32[]{:S(2)}, u32[]{:S(2)}) collective-permute-start(bf16[2,144,1]{2,0,1:T(2,128)(2,1)} %get-tuple-element.107), channel_id=1, source_target_pairs={{1,0},{2,1},{3,2},{4,3},{5,4},{6,5},{7,6},{8,7},{9,8},{10,9},{11,1... | collective-permute-start | bytes 1736 | tf_op jit(solution)/shard_map/ppermute | solution.py:29
  10.9 1.1 copy-start.4
  12.0 18.6 %copy-start.14 = (s32[144,128]{1,0:T(8,128)S(1)}, s32[144,128]{1,0:T(8,128)}, u32[]{:S(2)}) copy-start(s32[144,128]{1,0:T(8,128)} %param.15) | copy-start | bytes 221188
  12.0 18.6 %copy-start.1 = (bf16[144,4608]{1,0:T(8,128)(2,1)S(1)}, bf16[144,4608]{1,0:T(8,128)(2,1)}, u32[]{:S(2)}) copy-start(bf16[144,4608]{1,0:T(8,128)(2,1)} %rows_ref.2) | copy-start | bytes 3981316
  13.1 0.8 copy-start.13
  13.9 22.0 %collective-permute-start.4 = (bf16[256,1024]{1,0:T(8,128)(2,1)}, bf16[256,1024]{1,0:T(8,128)(2,1)S(1)}, u32[]{:S(2)}, u32[]{:S(2)}) collective-permute-start(bf16[256,1024]{1,0:T(8,128)(2,1)} %get-tuple-element.38), channel_id=1, source_target_pairs={{0,1},{1,2},{2,0},{3,4},{4,5},{5,3},{6,7},{7,8},{8,6},{9,10},{10,1... | collective-permute-start | bytes 1572872 | tf_op jit(solution)/shard_map/ppermute | solution.py:98
  19.2 15.1 %collective-permute-start.1 = (bf16[2,1,128]{2,0,1:T(2,128)(2,1)S(1)}, bf16[2,1,128]{2,0,1:T(2,128)(2,1)S(1)}, u32[]{:S(2)}, u32[]{:S(2)}) collective-permute-start(bf16[2,1,128]{2,0,1:T(2,128)(2,1)S(1)} %get-tuple-element.106), channel_id=1, source_target_pairs={{0,24},{24,48},{48,72},{72,96},{96,120},{120,144},{144,168},{168,1... | collective-permute-start | bytes 1544 | tf_op jit(solution)/shard_map/ppermute | solution.py:28
  23.7 10.6 %collective-permute-start = (bf16[2,1,128]{2,0,1:T(2,128)(2,1)S(1)}, bf16[2,1,128]{2,0,1:T(2,128)(2,1)S(1)}, u32[]{:S(2)}, u32[]{:S(2)}) collective-permute-start(bf16[2,1,128]{2,0,1:T(2,128)(2,1)S(1)} %get-tuple-element.105), channel_id=1, source_target_pairs={{24,0},{48,24},{72,48},{96,72},{120,96},{144,120},{168,144},{192,1... | collective-permute-start | bytes 1544 | tf_op jit(solution)/shard_map/ppermute | solution.py:29
  36.9 28.3 %all-to-all-start = ((bf16[8,144,256]{2,1,0:T(8,128)(2,1)}), bf16[8,144,256]{2,1,0:T(8,128)(2,1)S(1)}, u32[]{:S(2)}, u32[]{:S(2)}) async-start(bf16[8,144,256]{2,1,0:T(8,128)(2,1)} %broadcast_in_dim.2), calls=%async_computation | async-start | bytes 1179648 | tf_op jit(solution)/shard_map/all_to_all | solution.py:20
  40.5 12.9 %collective-permute-start.5 = (bf16[144,1152]{1,0:T(8,128)(2,1)}, bf16[144,1152]{1,0:T(8,128)(2,1)S(1)}, u32[]{:S(2)}, u32[]{:S(2)}) collective-permute-start(bf16[144,1152]{1,0:T(8,128)(2,1)} %get-tuple-element.42), channel_id=1, source_target_pairs={{0,24},{24,0},{48,72},{72,48},{1,25},{25,1},{49,73},{73,49},{2,26}... | collective-permute-start | bytes 995336 | tf_op jit(solution)/shard_map/ppermute | solution.py:80
  46.2 12.4 %collective-permute-start.7 = (bf16[144,1152]{1,0:T(8,128)(2,1)}, bf16[144,1152]{1,0:T(8,128)(2,1)S(1)}, u32[]{:S(2)}, u32[]{:S(2)}) collective-permute-start(bf16[144,1152]{1,0:T(8,128)(2,1)} %get-tuple-element.44), channel_id=1, source_target_pairs={{0,72},{24,48},{48,24},{72,0},{1,73},{25,49},{49,25},{73,1},{2,74}... | collective-permute-start | bytes 995336 | tf_op jit(solution)/shard_map/ppermute | solution.py:80
  48.2 16.4 %collective-permute-start.6 = (bf16[144,1152]{1,0:T(8,128)(2,1)}, bf16[144,1152]{1,0:T(8,128)(2,1)S(1)}, u32[]{:S(2)}, u32[]{:S(2)}) collective-permute-start(bf16[144,1152]{1,0:T(8,128)(2,1)} %get-tuple-element.43), channel_id=1, source_target_pairs={{0,48},{24,72},{48,0},{72,24},{1,49},{25,73},{49,1},{73,25},{2,50}... | collective-permute-start | bytes 995336 | tf_op jit(solution)/shard_map/ppermute | solution.py:80
  51.4 20.6 %collective-permute-start.8 = (bf16[256,1024]{1,0:T(8,128)(2,1)}, bf16[256,1024]{1,0:T(8,128)(2,1)S(1)}, u32[]{:S(2)}, u32[]{:S(2)}) collective-permute-start(bf16[256,1024]{1,0:T(8,128)(2,1)} %copy-done.13), channel_id=1, source_target_pairs={{0,2},{1,0},{2,1},{3,5},{4,3},{5,4},{6,8},{7,6},{8,7},{9,11},{10,9... | collective-permute-start | bytes 1572872 | tf_op jit(solution)/shard_map/ppermute | solution.py:98
  64.5 0.7 copy-start.7
  65.3 1.0 copy-start.8
  66.2 5.7 %copy-start.19 = (f32[16,2]{0,1:T(2,128)S(1)}, f32[16,2]{0,1:T(2,128)}, u32[]{:S(2)}) copy-start(f32[16,2]{0,1:T(2,128)} %param.18) | copy-start | bytes 388
  67.5 10.0 %all-to-all-start.1 = ((bf16[4,144,256]{2,1,0:T(8,128)(2,1)}), bf16[4,144,256]{2,1,0:T(8,128)(2,1)S(1)}, u32[]{:S(2)}, u32[]{:S(2)}) async-start(bf16[4,144,256]{2,1,0:T(8,128)(2,1)} %shard_map.150), calls=%async_computation.1 | async-start | bytes 589824 | tf_op jit(solution)/shard_map/all_to_all | solution.py:20
  72.0 19.8 %copy-start.2 = (bf16[144,4608]{1,0:T(8,128)(2,1)S(1)}, bf16[144,4608]{1,0:T(8,128)(2,1)}, u32[]{:S(2)}) copy-start(bf16[144,4608]{1,0:T(8,128)(2,1)} %rows_ref.3) | copy-start | bytes 3981316
  78.4 25.5 %copy-start.18 = (f32[144]{0:T(256)S(1)}, f32[144]{0:T(256)}, u32[]{:S(2)}) copy-start(f32[144]{0:T(256)} %param.23) | copy-start | bytes 1732
  78.4 25.5 %copy-start.20 = (f32[128]{0:T(128)S(1)}, f32[128]{0:T(128)}, u32[]{:S(2)}) copy-start(f32[128]{0:T(128)} %param.24) | copy-start | bytes 1540
  78.4 40.6 %all-to-all-start.2 = ((bf16[8,288,128]{2,1,0:T(8,128)(2,1)}), bf16[8,288,128]{2,1,0:T(8,128)(2,1)S(1)}, u32[]{:S(2)}, u32[]{:S(2)}) async-start(bf16[8,288,128]{2,1,0:T(8,128)(2,1)} %shard_map.151), calls=%async_computation.2 | async-start | bytes 1179648 | tf_op jit(solution)/shard_map/all_to_all | solution.py:20
  94.6 0.7 copy-start.5
  95.4 9.3 %collective-permute-start.9 = (bf16[144,1152]{1,0:T(8,128)(2,1)S(1)}, bf16[144,1152]{1,0:T(8,128)(2,1)S(1)}, u32[]{:S(2)}, u32[]{:S(2)}) collective-permute-start(bf16[144,1152]{1,0:T(8,128)(2,1)S(1)} %get-tuple-element.49), channel_id=1, source_target_pairs={{0,24},{24,0},{48,72},{72,48},{1,25},{25,1},{49,73},{73,49},{2,26}... | collective-permute-start | bytes 995336 | tf_op jit(solution)/shard_map/ppermute | solution.py:80
  98.4 13.4 %collective-permute-start.10 = (bf16[144,1152]{1,0:T(8,128)(2,1)S(1)}, bf16[144,1152]{1,0:T(8,128)(2,1)S(1)}, u32[]{:S(2)}, u32[]{:S(2)}) collective-permute-start(bf16[144,1152]{1,0:T(8,128)(2,1)S(1)} %get-tuple-element.50), channel_id=1, source_target_pairs={{0,48},{24,72},{48,0},{72,24},{1,49},{25,73},{49,1},{73,25},{2,50}... | collective-permute-start | bytes 995336 | tf_op jit(solution)/shard_map/ppermute | solution.py:80
  100.3 18.7 %collective-permute-start.11 = (bf16[144,1152]{1,0:T(8,128)(2,1)S(1)}, bf16[144,1152]{1,0:T(8,128)(2,1)S(1)}, u32[]{:S(2)}, u32[]{:S(2)}) collective-permute-start(bf16[144,1152]{1,0:T(8,128)(2,1)S(1)} %get-tuple-element.51), channel_id=1, source_target_pairs={{0,72},{24,48},{48,24},{72,0},{1,73},{25,49},{49,25},{73,1},{2,74}... | collective-permute-start | bytes 995336 | tf_op jit(solution)/shard_map/ppermute | solution.py:80
  119.0 13.7 %copy-start.12 = (f32[2]{0:T(128)S(1)}, f32[2]{0:T(128)}, u32[]{:S(2)}) copy-start(f32[2]{0:T(128)} %shift_ref.1) | copy-start | bytes 28
  120.4 25.5 %copy-start.6 = (bf16[144,1152]{1,0:T(8,128)(2,1)S(1)}, bf16[144,1152]{1,0:T(8,128)(2,1)}, u32[]{:S(2)}) copy-start(bf16[144,1152]{1,0:T(8,128)(2,1)} %copy-done.5) | copy-start | bytes 995332
  120.4 12.4 %all-to-all-start.3 = ((bf16[3,288,128]{2,1,0:T(8,128)(2,1)}), bf16[3,288,128]{2,1,0:T(8,128)(2,1)S(1)}, u32[]{:S(2)}, u32[]{:S(2)}) async-start(bf16[3,288,128]{2,1,0:T(8,128)(2,1)} %shard_map.153), calls=%async_computation.3 | async-start | bytes 442368 | tf_op jit(solution)/shard_map/all_to_all | solution.py:20
  132.7 0.9 copy-start.9
  135.0 26.9 %all-to-all-start.4 = ((bf16[8,288,128]{2,1,0:T(8,128)(2,1)}), bf16[8,288,128]{2,1,0:T(8,128)(2,1)S(1)}, u32[]{:S(2)}, u32[]{:S(2)}) async-start(bf16[8,288,128]{2,1,0:T(8,128)(2,1)} %shard_map.154), calls=%async_computation.4 | async-start | bytes 1179648 | tf_op jit(solution)/shard_map/all_to_all | solution.py:20
  146.0 15.2 %collective-permute-start.12 = (bf16[16,1152]{1,0:T(8,128)(2,1)S(1)}, bf16[16,1152]{1,0:T(8,128)(2,1)S(1)}, u32[]{:S(2)}, u32[]{:S(2)}) collective-permute-start(bf16[16,1152]{1,0:T(8,128)(2,1)S(1)} %fusion.27), channel_id=1, source_target_pairs={{0,96},{96,192},{192,288},{288,384},{384,480},{480,576},{576,672},... | collective-permute-start | bytes 110600 | tf_op jit(solution)/shard_map/ppermute | solution.py:262
  149.7 11.5 %collective-permute-start.13 = (bf16[16,1152]{1,0:T(8,128)(2,1)S(1)}, bf16[16,1152]{1,0:T(8,128)(2,1)S(1)}, u32[]{:S(2)}, u32[]{:S(2)}) collective-permute-start(bf16[16,1152]{1,0:T(8,128)(2,1)S(1)} %fusion.23), channel_id=1, source_target_pairs={{96,0},{192,96},{288,192},{384,288},{480,384},{576,480},{672,576},... | collective-permute-start | bytes 110600 | tf_op jit(solution)/shard_map/ppermute | solution.py:262
  153.6 8.3 %collective-permute-start.14 = (bf16[16,1024]{1,0:T(8,128)(2,1)}, bf16[16,1024]{1,0:T(8,128)(2,1)}, u32[]{:S(2)}, u32[]{:S(2)}) collective-permute-start(bf16[16,1024]{1,0:T(8,128)(2,1)} %fusion.33), channel_id=1, source_target_pairs={{0,3},{3,6},{6,9},{9,12},{12,15},{15,18},{18,21},{1,4},{4,7},{7,10... | collective-permute-start | bytes 98312 | tf_op jit(solution)/shard_map/ppermute | solution.py:254
  160.0 7.2 %collective-permute-start.15 = (bf16[16,1024]{1,0:T(8,128)(2,1)}, bf16[16,1024]{1,0:T(8,128)(2,1)}, u32[]{:S(2)}, u32[]{:S(2)}) collective-permute-start(bf16[16,1024]{1,0:T(8,128)(2,1)} %fusion.30), channel_id=1, source_target_pairs={{3,0},{6,3},{9,6},{12,9},{15,12},{18,15},{21,18},{4,1},{7,4},{10,7... | collective-permute-start | bytes 98312 | tf_op jit(solution)/shard_map/ppermute | solution.py:254
  161.3 0.6 copy-start.10
  183.9 24.0 %copy-start.11 = (bf16[16,1152]{1,0:T(8,128)(2,1)S(1)}, bf16[16,1152]{1,0:T(8,128)(2,1)}, u32[]{:S(2)}) copy-start(bf16[16,1152]{1,0:T(8,128)(2,1)} %copy-done.10) | copy-start | bytes 110596
  221.5 0.9 copy-start.15
  221.5 0.9 copy-start.17
  221.9 2.1 copy-start.16

commit v9 on v8

--- a/solution.py
+++ b/solution.py
@@ -299,7 +299,9 @@
     cut_fx, cut_y = quad_cut(quad_me, forward_x), ring_cut(ring_me, forward_y, inverse_y)
     divergence, y_one, fx_two = lax.optimization_barrier((divergence, ring_send(cut_y[1], 1), cut_fx[2]))
     cut_fx = [cut_fx[0], cut_fx[1], fx_two, cut_fx[3]]
-    table_fx = [cut_fx[0]] + [quad_send(cut_fx[step], step) for step in (1, 2, 3)]
+    fx_two, fx_three = quad_send(cut_fx[2], 2), quad_send(cut_fx[3], 3)
+    core, fx_two = lax.optimization_barrier((cut_fx[1], fx_two))
+    table_fx = (cut_fx[0], quad_send(core, 1), fx_two, fx_three)
     y_two = ring_send(cut_y[2], 2)
     block = to_x(divergence.reshape(288, 128))
     held = exchange(jnp.broadcast_to(block[None], (8, 144, 256)), "y")
@@ -310,7 +312,9 @@
     table_y = (cut_y[0], y_one, y_two)
     spread = jax.ShapeDtypeStruct((8, 288, 128), BF)
     held = exchange(call(to_y_kernel, spread, (quad_me, got)), ("xh", "zh"))
-    table_ix = [cut_ix[0]] + [quad_send(cut_ix[step], step) for step in (1, 2, 3)]
+    ix_two, ix_three = quad_send(cut_ix[2], 2), quad_send(cut_ix[3], 3)
+    core, ix_two = lax.optimization_barrier((cut_ix[1], ix_two))
+    table_ix = (cut_ix[0], quad_send(core, 1), ix_two, ix_three)
     denom = eigen_x[:, None] + eigen_y[None, :]
     held, table_ix, denom = lax.optimization_barrier((held, table_ix, denom))
     got = exchange(y_products(ring_me, held, table_y), "zl")

time: 227 us -> 222 us (0.978)
  waiting for transfers between devices: 42.8 us -> 31.6 us
  starting transfers between devices: 95.4 us -> 101 us
    ppermute x6, waiting for transfers between devices: 25.6 us -> 12.9 us  [quad_send(): return lax.ppermute(piece, QUAD, [(i, i ^ step) for i in range(4)])]
    ppermute x2, waiting for transfers between devices: 0.01 us -> 6.99 us  [ring_send(): return lax.ppermute(piece, 'zl', [(i, (i + step) % 3) for i in range(3)])]
    ppermute x6, starting transfers between devices: 19.4 us -> 26 us  [quad_send(): return lax.ppermute(piece, QUAD, [(i, i ^ step) for i in range(4)])]
    all_to_all x5, waiting for transfers between devices: 12 us -> 6.51 us  [exchange(): return lax.all_to_all(parts, axes, 0, 0)]
    unnamed x43 -> x45, local copies, waits for them, and re-layouts: 6.18 us -> 6.2 us
  transfers between devices with their start and end apart: 21 -> 21, of which waited for: 7 -> 7; matrix products, arithmetic and copies ran while one was open for 2% -> 3% of each run, Pallas kernels for 4% -> 4%
where the time goes in v9:
time: 222 us; the launch traced here: 221 us
  starting transfers between devices  101 us (45%)
  blocking collectives  52.1 us (23%)
  waiting for transfers between devices  31.6 us (14%)
  Pallas kernels  15.9 us (7%)
  local copies, waits for them, and re-layouts  8.36 us (4%)
  other arithmetic  7.91 us (4%)
    all_to_all x3, blocking collectives, exchange(): return lax.all_to_all(parts, axes, 0, 0)  52.1 us
    all_to_all x5, starting transfers between devices, exchange(): return lax.all_to_all(parts, axes, 0, 0)  37.8 us
    ppermute x6, starting transfers between devices, quad_send(): return lax.ppermute(piece, QUAD, [(i, i ^ step) for i in range(4)])  26 us
    pallas_call x10, Pallas kernels, call(): pl.pallas_call(kernel, out_shape=out_shape, in_specs=[smem] + [vmem] * (l...  15.9 us
    ppermute x6, waiting for transfers between devices, quad_send(): return lax.ppermute(piece, QUAD, [(i, i ^ step) for i in range(4)])  12.9 us
    ppermute x2, starting transfers between devices, edges(): lax.ppermute(lax.slice_in_dim(block, block.shape[dim] - 1, None, axis=dim...  9.94 us
    ppermute x2, starting transfers between devices, edges(): high = lax.ppermute(lax.slice_in_dim(block, 0, 1, axis=dim), axes, backward)  8.13 us
    ppermute x2, waiting for transfers between devices, ring_send(): return lax.ppermute(piece, 'zl', [(i, (i + step) % 3) for i in range(3)])  6.99 us
  transfers between devices with their start and end apart: 21, of which 7 were waited for; matrix products, arithmetic and copies ran while one was open for 3% of the time, Pallas kernels for 4%

profile of v9, /device:TPU:1, one launch (start us, length us, event | category | flops | bytes accessed | tf_op | source)
XLA Modules:
  0.0 220.5 jit_solution(5424050037315660642)
XLA Ops:
  0.6 2.4 %fusion.8 = (bf16[16,144,128]{2,1,0:T(8,128)(2,1)}, bf16[16,144,128]{2,1,0:T(8,128)(2,1)S(1)}) fusion(bf16[16,144,128]{2,1,0:T(8,128)(2,1)} %param.13, s32[144,128]{1,0:T(8,128)} %param.15, s32[144,128]{1,0:T(8,128)} %param.16, bf16[16,144,128]{2,1,0:T(8,128)(2,1)} %param.14), kind=kLoop, calls=%fused_computation.13 | loop fusion | flops 2949120 | bytes 2506752 | tf_op jit(solution)/shard_map/mul | solution.py:291
  3.3 0.8 fusion.42
  4.1 5.5 %collective-permute-start.3 = (bf16[2,144,1]{2,0,1:T(2,128)(2,1)}, bf16[2,144,1]{2,0,1:T(2,128)(2,1)}, u32[]{:S(2)}, u32[]{:S(2)}) collective-permute-start(bf16[2,144,1]{2,0,1:T(2,128)(2,1)} %get-tuple-element.116), channel_id=1, source_target_pairs={{0,1},{1,2},{2,3},{3,4},{4,5},{5,6},{6,7},{7,8},{8,9},{9,10},{10,1... | collective-permute-start | bytes 1736 | tf_op jit(solution)/shard_map/ppermute | solution.py:28
  9.6 1.3 collective-permute-start.2
  10.9 1.1 copy-done.4
  12.0 1.1 shard_map.148
  13.9 4.0 %collective-permute-start.4 = (bf16[256,1024]{1,0:T(8,128)(2,1)}, bf16[256,1024]{1,0:T(8,128)(2,1)S(1)}, u32[]{:S(2)}, u32[]{:S(2)}) collective-permute-start(bf16[256,1024]{1,0:T(8,128)(2,1)} %get-tuple-element.42), channel_id=1, source_target_pairs={{0,1},{1,2},{2,0},{3,4},{4,5},{5,3},{6,7},{7,8},{8,6},{9,10},{10,1... | collective-permute-start | bytes 1572872 | tf_op jit(solution)/shard_map/ppermute | solution.py:98
  17.9 1.9 fusion.44
  19.9 4.5 %collective-permute-start.1 = (bf16[2,1,128]{2,0,1:T(2,128)(2,1)S(1)}, bf16[2,1,128]{2,0,1:T(2,128)(2,1)S(1)}, u32[]{:S(2)}, u32[]{:S(2)}) collective-permute-start(bf16[2,1,128]{2,0,1:T(2,128)(2,1)S(1)} %get-tuple-element.114), channel_id=1, source_target_pairs={{0,24},{24,48},{48,72},{72,96},{96,120},{120,144},{144,168},{168,1... | collective-permute-start | bytes 1544 | tf_op jit(solution)/shard_map/ppermute | solution.py:28
  24.4 6.9 %collective-permute-start = (bf16[2,1,128]{2,0,1:T(2,128)(2,1)S(1)}, bf16[2,1,128]{2,0,1:T(2,128)(2,1)S(1)}, u32[]{:S(2)}, u32[]{:S(2)}) collective-permute-start(bf16[2,1,128]{2,0,1:T(2,128)(2,1)S(1)} %get-tuple-element.113), channel_id=1, source_target_pairs={{24,0},{48,24},{72,48},{96,72},{120,96},{144,120},{168,144},{192,1... | collective-permute-start | bytes 1544 | tf_op jit(solution)/shard_map/ppermute | solution.py:29
  31.3 3.6 %shard_map.149 = (bf16[144,1152]{1,0:T(8,128)(2,1)S(1)}, bf16[144,1152]{1,0:T(8,128)(2,1)}, bf16[144,1152]{1,0:T(8,128)(2,1)S(1)}, bf16[144,1152]{1,0:T(8,128)(2,1)}) custom-call(s32[1]{0:T(128)} %bitcast.me_ref, bf16[144,4608]{1,0:T(8,128)(2,1)S(1)} %copy-done.1), custom_call_target="tpu_custom_call" | custom-call | bytes 2654208 | tf_op jit(solution)/shard_map/pallas_call | solution.py:49
  34.9 0.9 convert_element_type.65
  36.6 0.9 broadcast_in_dim.2
  37.5 3.5 %all-to-all-start = ((bf16[8,144,256]{2,1,0:T(8,128)(2,1)}), bf16[8,144,256]{2,1,0:T(8,128)(2,1)S(1)}, u32[]{:S(2)}, u32[]{:S(2)}) async-start(bf16[8,144,256]{2,1,0:T(8,128)(2,1)} %broadcast_in_dim.2), calls=%async_computation | async-start | bytes 1179648 | tf_op jit(solution)/shard_map/all_to_all | solution.py:20
  41.0 4.7 %collective-permute-start.5 = (bf16[144,1152]{1,0:T(8,128)(2,1)S(1)}, bf16[144,1152]{1,0:T(8,128)(2,1)S(1)}, u32[]{:S(2)}, u32[]{:S(2)}) collective-permute-start(bf16[144,1152]{1,0:T(8,128)(2,1)S(1)} %get-tuple-element.47), channel_id=1, source_target_pairs={{0,48},{24,72},{48,0},{72,24},{1,49},{25,73},{49,1},{73,25},{2,50}... | collective-permute-start | bytes 995336 | tf_op jit(solution)/shard_map/ppermute | solution.py:80
  45.8 4.6 %collective-permute-start.7 = (bf16[144,1152]{1,0:T(8,128)(2,1)}, bf16[144,1152]{1,0:T(8,128)(2,1)S(1)}, u32[]{:S(2)}, u32[]{:S(2)}) collective-permute-start(bf16[144,1152]{1,0:T(8,128)(2,1)} %get-tuple-element.50), channel_id=1, source_target_pairs={{0,72},{24,48},{48,24},{72,0},{1,73},{25,49},{49,25},{73,1},{2,74}... | collective-permute-start | bytes 995336 | tf_op jit(solution)/shard_map/ppermute | solution.py:80
  50.3 1.7 collective-permute-done.5.t2
  52.1 6.8 %collective-permute-start.6 = (bf16[144,1152]{1,0:T(8,128)(2,1)}, bf16[144,1152]{1,0:T(8,128)(2,1)S(1)}, u32[]{:S(2)}, u32[]{:S(2)}) collective-permute-start(bf16[144,1152]{1,0:T(8,128)(2,1)} %get-tuple-element.48), channel_id=1, source_target_pairs={{0,24},{24,0},{48,72},{72,48},{1,25},{25,1},{49,73},{73,49},{2,26}... | collective-permute-start | bytes 995336 | tf_op jit(solution)/shard_map/ppermute | solution.py:80
  58.9 1.9 collective-permute-start.8
  61.7 1.0 copy-done.8
  62.6 1.3 shard_map.150
  63.9 3.7 %all-to-all-start.1 = ((bf16[4,144,256]{2,1,0:T(8,128)(2,1)}), bf16[4,144,256]{2,1,0:T(8,128)(2,1)S(1)}, u32[]{:S(2)}, u32[]{:S(2)}) async-start(bf16[4,144,256]{2,1,0:T(8,128)(2,1)} %shard_map.150), calls=%async_computation.1 | async-start | bytes 589824 | tf_op jit(solution)/shard_map/all_to_all | solution.py:20
  67.6 7.0 %collective-permute-done.8.t2 = bf16[256,1024]{1,0:T(8,128)(2,1)S(1)} collective-permute-done((bf16[256,1024]{1,0:T(8,128)(2,1)}, bf16[256,1024]{1,0:T(8,128)(2,1)S(1)}, u32[]{:S(2)}, u32[]{:S(2)}) %collective-permute-start.8) | collective-permute-done | bytes 524320 | tf_op jit(solution)/shard_map/ppermute | solution.py:98
  74.6 0.9 shard_map.151
  75.5 13.8 %all-to-all-start.2 = ((bf16[8,288,128]{2,1,0:T(8,128)(2,1)}), bf16[8,288,128]{2,1,0:T(8,128)(2,1)S(1)}, u32[]{:S(2)}, u32[]{:S(2)}) async-start(bf16[8,288,128]{2,1,0:T(8,128)(2,1)} %shard_map.151), calls=%async_computation.2 | async-start | bytes 1179648 | tf_op jit(solution)/shard_map/all_to_all | solution.py:20
  89.3 2.8 %shard_map.152 = (bf16[144,1152]{1,0:T(8,128)(2,1)S(1)}, bf16[144,1152]{1,0:T(8,128)(2,1)S(1)}, bf16[144,1152]{1,0:T(8,128)(2,1)S(1)}, bf16[144,1152]{1,0:T(8,128)(2,1)S(1)}) custom-call(s32[1]{0:T(128)} %bitcast.me_ref, bf16[144,4608]{1,0:T(8,128)(2,1)S(1)} %copy-done.2), custom_call_target="tpu_custom_call" | custom-call | bytes 2654208 | tf_op jit(solution)/shard_map/pallas_call | solution.py:49
  92.8 2.3 %collective-permute-start.9 = (bf16[144,1152]{1,0:T(8,128)(2,1)S(1)}, bf16[144,1152]{1,0:T(8,128)(2,1)S(1)}, u32[]{:S(2)}, u32[]{:S(2)}) collective-permute-start(bf16[144,1152]{1,0:T(8,128)(2,1)S(1)} %get-tuple-element.56), channel_id=1, source_target_pairs={{0,48},{24,72},{48,0},{72,24},{1,49},{25,73},{49,1},{73,25},{2,50}... | collective-permute-start | bytes 995336 | tf_op jit(solution)/shard_map/ppermute | solution.py:80
  95.1 4.0 %collective-permute-start.11 = (bf16[144,1152]{1,0:T(8,128)(2,1)S(1)}, bf16[144,1152]{1,0:T(8,128)(2,1)S(1)}, u32[]{:S(2)}, u32[]{:S(2)}) collective-permute-start(bf16[144,1152]{1,0:T(8,128)(2,1)S(1)} %get-tuple-element.59), channel_id=1, source_target_pairs={{0,72},{24,48},{48,24},{72,0},{1,73},{25,49},{49,25},{73,1},{2,74}... | collective-permute-start | bytes 995336 | tf_op jit(solution)/shard_map/ppermute | solution.py:80
  99.1 7.9 %collective-permute-done.9.t2 = bf16[144,1152]{1,0:T(8,128)(2,1)S(1)} collective-permute-done((bf16[144,1152]{1,0:T(8,128)(2,1)S(1)}, bf16[144,1152]{1,0:T(8,128)(2,1)S(1)}, u32[]{:S(2)}, u32[]{:S(2)}) %collective-permute-start.9) | collective-permute-done | bytes 331808 | tf_op jit(solution)/shard_map/ppermute | solution.py:80
  107.0 3.5 %collective-permute-start.10 = (bf16[144,1152]{1,0:T(8,128)(2,1)S(1)}, bf16[144,1152]{1,0:T(8,128)(2,1)S(1)}, u32[]{:S(2)}, u32[]{:S(2)}) collective-permute-start(bf16[144,1152]{1,0:T(8,128)(2,1)S(1)} %get-tuple-element.57), channel_id=1, source_target_pairs={{0,24},{24,0},{48,72},{72,48},{1,25},{25,1},{49,73},{73,49},{2,26}... | collective-permute-start | bytes 995336 | tf_op jit(solution)/shard_map/ppermute | solution.py:80
  111.3 3.2 %collective-permute-done.11.t3 = bf16[144,1152]{1,0:T(8,128)(2,1)S(1)} collective-permute-done((bf16[144,1152]{1,0:T(8,128)(2,1)S(1)}, bf16[144,1152]{1,0:T(8,128)(2,1)S(1)}, u32[]{:S(2)}, u32[]{:S(2)}) %collective-permute-start.11) | collective-permute-done | bytes 331808 | tf_op jit(solution)/shard_map/ppermute | solution.py:80
  114.5 1.4 shard_map.153
  115.8 7.4 %all-to-all-start.3 = ((bf16[3,288,128]{2,1,0:T(8,128)(2,1)}), bf16[3,288,128]{2,1,0:T(8,128)(2,1)S(1)}, u32[]{:S(2)}, u32[]{:S(2)}) async-start(bf16[3,288,128]{2,1,0:T(8,128)(2,1)} %shard_map.153), calls=%async_computation.3 | async-start | bytes 442368 | tf_op jit(solution)/shard_map/all_to_all | solution.py:20
  123.3 6.5 %all-to-all-done.3.got_ref = bf16[3,288,128]{2,1,0:T(8,128)(2,1)S(1)} async-done(((bf16[3,288,128]{2,1,0:T(8,128)(2,1)}), bf16[3,288,128]{2,1,0:T(8,128)(2,1)S(1)}, u32[]{:S(2)}, u32[]{:S(2)}) %all-to-all-start.3) | async-done | bytes 221216 | tf_op jit(solution)/shard_map/all_to_all | solution.py:20
  129.8 0.9 copy-done.9
  130.7 1.4 shard_map.154
  132.1 9.3 %all-to-all-start.4 = ((bf16[8,288,128]{2,1,0:T(8,128)(2,1)}), bf16[8,288,128]{2,1,0:T(8,128)(2,1)S(1)}, u32[]{:S(2)}, u32[]{:S(2)}) async-start(bf16[8,288,128]{2,1,0:T(8,128)(2,1)} %shard_map.154), calls=%async_computation.4 | async-start | bytes 1179648 | tf_op jit(solution)/shard_map/all_to_all | solution.py:20
  141.5 3.2 %collective-permute-start.12 = (bf16[16,1152]{1,0:T(8,128)(2,1)S(1)}, bf16[16,1152]{1,0:T(8,128)(2,1)S(1)}, u32[]{:S(2)}, u32[]{:S(2)}) collective-permute-start(bf16[16,1152]{1,0:T(8,128)(2,1)S(1)} %fusion.27), channel_id=1, source_target_pairs={{0,96},{96,192},{192,288},{288,384},{384,480},{480,576},{576,672},... | collective-permute-start | bytes 110600 | tf_op jit(solution)/shard_map/ppermute | solution.py:262
  144.8 3.3 %collective-permute-start.13 = (bf16[16,1152]{1,0:T(8,128)(2,1)S(1)}, bf16[16,1152]{1,0:T(8,128)(2,1)S(1)}, u32[]{:S(2)}, u32[]{:S(2)}) collective-permute-start(bf16[16,1152]{1,0:T(8,128)(2,1)S(1)} %fusion.23), channel_id=1, source_target_pairs={{96,0},{192,96},{288,192},{384,288},{480,384},{576,480},{672,576},... | collective-permute-start | bytes 110600 | tf_op jit(solution)/shard_map/ppermute | solution.py:262
  148.8 5.7 %collective-permute-start.14 = (bf16[16,1024]{1,0:T(8,128)(2,1)}, bf16[16,1024]{1,0:T(8,128)(2,1)}, u32[]{:S(2)}, u32[]{:S(2)}) collective-permute-start(bf16[16,1024]{1,0:T(8,128)(2,1)} %fusion.33), channel_id=1, source_target_pairs={{0,3},{3,6},{6,9},{9,12},{12,15},{15,18},{18,21},{1,4},{4,7},{7,10... | collective-permute-start | bytes 98312 | tf_op jit(solution)/shard_map/ppermute | solution.py:254
  155.2 1.3 collective-permute-start.15
  157.1 5.2 %collective-permute-done.15.hi_ref = bf16[16,1024]{1,0:T(8,128)(2,1)} collective-permute-done((bf16[16,1024]{1,0:T(8,128)(2,1)}, bf16[16,1024]{1,0:T(8,128)(2,1)}, u32[]{:S(2)}, u32[]{:S(2)}) %collective-permute-start.15) | collective-permute-done | bytes 32800 | tf_op jit(solution)/shard_map/ppermute | solution.py:254
  162.3 2.4 %shard_map.155 = bf16[3,320,128]{2,1,0:T(8,128)(2,1)S(1)} custom-call(s32[1]{0:T(128)} %bitcast.4.me_ref, bf16[8,288,128]{2,1,0:T(8,128)(2,1)S(1)} %all-to-all-done.4.held_ref, bf16[256,1024]{1,0:T(8,128)(2,1)S(1)} %get-tuple-element.75.t0, bf16[256,1024]{1,0:T(8,128)(2,1)S(1)} %collective-permute-done.4.t1, ...), custom_call_target="tpu_custom_call" | custom-call | flops 226492416 | bytes 2473984 | tf_op jit(solution)/shard_map/pallas_call | solution.py:49
  164.7 15.8 %all_to_all.40.got_ref = bf16[3,320,128]{2,1,0:T(8,128)(2,1)S(1)} all-to-all(bf16[3,320,128]{2,1,0:T(8,128)(2,1)S(1)} %shard_map.155), channel_id=1, replica_groups=mesh['y'=8,'xl'=2,'c'=2,'xh'=2,'zh'=4,'zl'=3] {'zl'}, dimensions={0} | all-to-all | bytes 491520 | tf_op jit(solution)/shard_map/all_to_all | solution.py:20
  180.6 22.4 %all_to_all.41.held_ref = bf16[8,160,256]{2,1,0:T(8,128)(2,1)S(1)} all-to-all(bf16[8,160,256]{2,1,0:T(8,128)(2,1)S(1)} %shard_map.156), channel_id=1, replica_groups=mesh['y'=8,'xl'=2,'c'=2,'xh'=2,'zh'=4,'zl'=3] {'y'}, dimensions={0} | all-to-all | bytes 1310720 | tf_op jit(solution)/shard_map/all_to_all | solution.py:20
  203.0 1.1 shard_map.157
  204.1 13.9 %all_to_all.42 = bf16[4,160,256]{2,1,0:T(8,128)(2,1)S(1)} all-to-all(bf16[4,160,256]{2,1,0:T(8,128)(2,1)S(1)} %shard_map.157), channel_id=1, replica_groups=mesh['y'=8,'xl'=2,'c'=2,'xh'=2,'zh'=4,'zl'=3] {'xl','c'}, dimensions={0} | all-to-all | bytes 655360 | tf_op jit(solution)/shard_map/all_to_all | solution.py:20
  218.9 1.6 fusion.4
  (93 shorter events, 7.1 us)
Async XLA Ops:
  0.6 2.5 %copy-start = (bf16[16,2]{0,1:T(2,128)(2,1)S(1)}, bf16[16,2]{0,1:T(2,128)(2,1)}, u32[]{:S(2)}) copy-start(bf16[16,2]{0,1:T(2,128)(2,1)} %param.17) | copy-start | bytes 196
  3.1 7.8 %copy-start.3 = (bf16[128,3072]{1,0:T(8,128)(2,1)S(1)}, bf16[128,3072]{1,0:T(8,128)(2,1)}, u32[]{:S(2)}) copy-start(bf16[128,3072]{1,0:T(8,128)(2,1)} %first_ref.1) | copy-start | bytes 2359300
  4.1 30.8 %collective-permute-start.3 = (bf16[2,144,1]{2,0,1:T(2,128)(2,1)}, bf16[2,144,1]{2,0,1:T(2,128)(2,1)}, u32[]{:S(2)}, u32[]{:S(2)}) collective-permute-start(bf16[2,144,1]{2,0,1:T(2,128)(2,1)} %get-tuple-element.116), channel_id=1, source_target_pairs={{0,1},{1,2},{2,3},{3,4},{4,5},{5,6},{6,7},{7,8},{8,9},{9,10},{10,1... | collective-permute-start | bytes 1736 | tf_op jit(solution)/shard_map/ppermute | solution.py:28
  9.6 26.3 %collective-permute-start.2 = (bf16[2,144,1]{2,0,1:T(2,128)(2,1)}, bf16[2,144,1]{2,0,1:T(2,128)(2,1)S(1)}, u32[]{:S(2)}, u32[]{:S(2)}) collective-permute-start(bf16[2,144,1]{2,0,1:T(2,128)(2,1)} %get-tuple-element.115), channel_id=1, source_target_pairs={{1,0},{2,1},{3,2},{4,3},{5,4},{6,5},{7,6},{8,7},{9,8},{10,9},{11,1... | collective-permute-start | bytes 1736 | tf_op jit(solution)/shard_map/ppermute | solution.py:29
  10.9 1.1 copy-start.4
  12.0 19.2 %copy-start.14 = (s32[144,128]{1,0:T(8,128)S(1)}, s32[144,128]{1,0:T(8,128)}, u32[]{:S(2)}) copy-start(s32[144,128]{1,0:T(8,128)} %param.15) | copy-start | bytes 221188
  12.0 19.2 %copy-start.1 = (bf16[144,4608]{1,0:T(8,128)(2,1)S(1)}, bf16[144,4608]{1,0:T(8,128)(2,1)}, u32[]{:S(2)}) copy-start(bf16[144,4608]{1,0:T(8,128)(2,1)} %rows_ref.2) | copy-start | bytes 3981316
  13.1 0.8 copy-start.13
  13.9 22.6 %collective-permute-start.4 = (bf16[256,1024]{1,0:T(8,128)(2,1)}, bf16[256,1024]{1,0:T(8,128)(2,1)S(1)}, u32[]{:S(2)}, u32[]{:S(2)}) collective-permute-start(bf16[256,1024]{1,0:T(8,128)(2,1)} %get-tuple-element.42), channel_id=1, source_target_pairs={{0,1},{1,2},{2,0},{3,4},{4,5},{5,3},{6,7},{7,8},{8,6},{9,10},{10,1... | collective-permute-start | bytes 1572872 | tf_op jit(solution)/shard_map/ppermute | solution.py:98
  19.9 15.0 %collective-permute-start.1 = (bf16[2,1,128]{2,0,1:T(2,128)(2,1)S(1)}, bf16[2,1,128]{2,0,1:T(2,128)(2,1)S(1)}, u32[]{:S(2)}, u32[]{:S(2)}) collective-permute-start(bf16[2,1,128]{2,0,1:T(2,128)(2,1)S(1)} %get-tuple-element.114), channel_id=1, source_target_pairs={{0,24},{24,48},{48,72},{72,96},{96,120},{120,144},{144,168},{168,1... | collective-permute-start | bytes 1544 | tf_op jit(solution)/shard_map/ppermute | solution.py:28
  24.4 10.5 %collective-permute-start = (bf16[2,1,128]{2,0,1:T(2,128)(2,1)S(1)}, bf16[2,1,128]{2,0,1:T(2,128)(2,1)S(1)}, u32[]{:S(2)}, u32[]{:S(2)}) collective-permute-start(bf16[2,1,128]{2,0,1:T(2,128)(2,1)S(1)} %get-tuple-element.113), channel_id=1, source_target_pairs={{24,0},{48,24},{72,48},{96,72},{120,96},{144,120},{168,144},{192,1... | collective-permute-start | bytes 1544 | tf_op jit(solution)/shard_map/ppermute | solution.py:29
  31.3 4.7 %copy-start.17 = (f32[2,144,128]{2,0,1:T(2,128)S(1)}, f32[2,144,128]{2,0,1:T(2,128)}, u32[]{:S(2)}) copy-start(f32[2,144,128]{2,0,1:T(2,128)} %get-tuple-element.123) | copy-start | bytes 442372
  37.5 24.2 %all-to-all-start = ((bf16[8,144,256]{2,1,0:T(8,128)(2,1)}), bf16[8,144,256]{2,1,0:T(8,128)(2,1)S(1)}, u32[]{:S(2)}, u32[]{:S(2)}) async-start(bf16[8,144,256]{2,1,0:T(8,128)(2,1)} %broadcast_in_dim.2), calls=%async_computation | async-start | bytes 1179648 | tf_op jit(solution)/shard_map/all_to_all | solution.py:20
  41.0 11.0 %collective-permute-start.5 = (bf16[144,1152]{1,0:T(8,128)(2,1)S(1)}, bf16[144,1152]{1,0:T(8,128)(2,1)S(1)}, u32[]{:S(2)}, u32[]{:S(2)}) collective-permute-start(bf16[144,1152]{1,0:T(8,128)(2,1)S(1)} %get-tuple-element.47), channel_id=1, source_target_pairs={{0,48},{24,72},{48,0},{72,24},{1,49},{25,73},{49,1},{73,25},{2,50}... | collective-permute-start | bytes 995336 | tf_op jit(solution)/shard_map/ppermute | solution.py:80
  45.8 15.2 %collective-permute-start.7 = (bf16[144,1152]{1,0:T(8,128)(2,1)}, bf16[144,1152]{1,0:T(8,128)(2,1)S(1)}, u32[]{:S(2)}, u32[]{:S(2)}) collective-permute-start(bf16[144,1152]{1,0:T(8,128)(2,1)} %get-tuple-element.50), channel_id=1, source_target_pairs={{0,72},{24,48},{48,24},{72,0},{1,73},{25,49},{49,25},{73,1},{2,74}... | collective-permute-start | bytes 995336 | tf_op jit(solution)/shard_map/ppermute | solution.py:80
  52.1 8.8 %collective-permute-start.6 = (bf16[144,1152]{1,0:T(8,128)(2,1)}, bf16[144,1152]{1,0:T(8,128)(2,1)S(1)}, u32[]{:S(2)}, u32[]{:S(2)}) collective-permute-start(bf16[144,1152]{1,0:T(8,128)(2,1)} %get-tuple-element.48), channel_id=1, source_target_pairs={{0,24},{24,0},{48,72},{72,48},{1,25},{25,1},{49,73},{73,49},{2,26}... | collective-permute-start | bytes 995336 | tf_op jit(solution)/shard_map/ppermute | solution.py:80
  58.9 15.6 %collective-permute-start.8 = (bf16[256,1024]{1,0:T(8,128)(2,1)}, bf16[256,1024]{1,0:T(8,128)(2,1)S(1)}, u32[]{:S(2)}, u32[]{:S(2)}) collective-permute-start(bf16[256,1024]{1,0:T(8,128)(2,1)} %copy-done.13), channel_id=1, source_target_pairs={{0,2},{1,0},{2,1},{3,5},{4,3},{5,4},{6,8},{7,6},{8,7},{9,11},{10,9... | collective-permute-start | bytes 1572872 | tf_op jit(solution)/shard_map/ppermute | solution.py:98
  60.9 0.7 copy-start.7
  61.7 1.0 copy-start.8
  62.6 4.9 %copy-start.20 = (f32[16,2]{0,1:T(2,128)S(1)}, f32[16,2]{0,1:T(2,128)}, u32[]{:S(2)}) copy-start(f32[16,2]{0,1:T(2,128)} %param.18) | copy-start | bytes 388
  63.9 10.7 %all-to-all-start.1 = ((bf16[4,144,256]{2,1,0:T(8,128)(2,1)}), bf16[4,144,256]{2,1,0:T(8,128)(2,1)S(1)}, u32[]{:S(2)}, u32[]{:S(2)}) async-start(bf16[4,144,256]{2,1,0:T(8,128)(2,1)} %shard_map.150), calls=%async_computation.1 | async-start | bytes 589824 | tf_op jit(solution)/shard_map/all_to_all | solution.py:20
  67.6 21.7 %copy-start.2 = (bf16[144,4608]{1,0:T(8,128)(2,1)S(1)}, bf16[144,4608]{1,0:T(8,128)(2,1)}, u32[]{:S(2)}) copy-start(bf16[144,4608]{1,0:T(8,128)(2,1)} %rows_ref.3) | copy-start | bytes 3981316
  75.4 35.1 %copy-start.19 = (f32[144]{0:T(256)S(1)}, f32[144]{0:T(256)}, u32[]{:S(2)}) copy-start(f32[144]{0:T(256)} %param.23) | copy-start | bytes 1732
  75.4 35.1 %copy-start.21 = (f32[128]{0:T(128)S(1)}, f32[128]{0:T(128)}, u32[]{:S(2)}) copy-start(f32[128]{0:T(128)} %param.24) | copy-start | bytes 1540
  75.5 39.0 %all-to-all-start.2 = ((bf16[8,288,128]{2,1,0:T(8,128)(2,1)}), bf16[8,288,128]{2,1,0:T(8,128)(2,1)S(1)}, u32[]{:S(2)}, u32[]{:S(2)}) async-start(bf16[8,288,128]{2,1,0:T(8,128)(2,1)} %shard_map.151), calls=%async_computation.2 | async-start | bytes 1179648 | tf_op jit(solution)/shard_map/all_to_all | solution.py:20
  92.1 0.7 copy-start.5
  92.8 14.2 %collective-permute-start.9 = (bf16[144,1152]{1,0:T(8,128)(2,1)S(1)}, bf16[144,1152]{1,0:T(8,128)(2,1)S(1)}, u32[]{:S(2)}, u32[]{:S(2)}) collective-permute-start(bf16[144,1152]{1,0:T(8,128)(2,1)S(1)} %get-tuple-element.56), channel_id=1, source_target_pairs={{0,48},{24,72},{48,0},{72,24},{1,49},{25,73},{49,1},{73,25},{2,50}... | collective-permute-start | bytes 995336 | tf_op jit(solution)/shard_map/ppermute | solution.py:80
  95.1 19.4 %collective-permute-start.11 = (bf16[144,1152]{1,0:T(8,128)(2,1)S(1)}, bf16[144,1152]{1,0:T(8,128)(2,1)S(1)}, u32[]{:S(2)}, u32[]{:S(2)}) collective-permute-start(bf16[144,1152]{1,0:T(8,128)(2,1)S(1)} %get-tuple-element.59), channel_id=1, source_target_pairs={{0,72},{24,48},{48,24},{72,0},{1,73},{25,49},{49,25},{73,1},{2,74}... | collective-permute-start | bytes 995336 | tf_op jit(solution)/shard_map/ppermute | solution.py:80
  107.0 7.4 %collective-permute-start.10 = (bf16[144,1152]{1,0:T(8,128)(2,1)S(1)}, bf16[144,1152]{1,0:T(8,128)(2,1)S(1)}, u32[]{:S(2)}, u32[]{:S(2)}) collective-permute-start(bf16[144,1152]{1,0:T(8,128)(2,1)S(1)} %get-tuple-element.57), channel_id=1, source_target_pairs={{0,24},{24,0},{48,72},{72,48},{1,25},{25,1},{49,73},{73,49},{2,26}... | collective-permute-start | bytes 995336 | tf_op jit(solution)/shard_map/ppermute | solution.py:80
  114.5 15.3 %copy-start.12 = (f32[2]{0:T(128)S(1)}, f32[2]{0:T(128)}, u32[]{:S(2)}) copy-start(f32[2]{0:T(128)} %shift_ref.1) | copy-start | bytes 28
  115.8 25.6 %copy-start.6 = (bf16[144,1152]{1,0:T(8,128)(2,1)S(1)}, bf16[144,1152]{1,0:T(8,128)(2,1)}, u32[]{:S(2)}) copy-start(bf16[144,1152]{1,0:T(8,128)(2,1)} %copy-done.5) | copy-start | bytes 995332
  115.8 13.9 %all-to-all-start.3 = ((bf16[3,288,128]{2,1,0:T(8,128)(2,1)}), bf16[3,288,128]{2,1,0:T(8,128)(2,1)S(1)}, u32[]{:S(2)}, u32[]{:S(2)}) async-start(bf16[3,288,128]{2,1,0:T(8,128)(2,1)} %shard_map.153), calls=%async_computation.3 | async-start | bytes 442368 | tf_op jit(solution)/shard_map/all_to_all | solution.py:20
  129.8 0.9 copy-start.9
  132.1 25.0 %all-to-all-start.4 = ((bf16[8,288,128]{2,1,0:T(8,128)(2,1)}), bf16[8,288,128]{2,1,0:T(8,128)(2,1)S(1)}, u32[]{:S(2)}, u32[]{:S(2)}) async-start(bf16[8,288,128]{2,1,0:T(8,128)(2,1)} %shard_map.154), calls=%async_computation.4 | async-start | bytes 1179648 | tf_op jit(solution)/shard_map/all_to_all | solution.py:20
  141.5 14.9 %collective-permute-start.12 = (bf16[16,1152]{1,0:T(8,128)(2,1)S(1)}, bf16[16,1152]{1,0:T(8,128)(2,1)S(1)}, u32[]{:S(2)}, u32[]{:S(2)}) collective-permute-start(bf16[16,1152]{1,0:T(8,128)(2,1)S(1)} %fusion.27), channel_id=1, source_target_pairs={{0,96},{96,192},{192,288},{288,384},{384,480},{480,576},{576,672},... | collective-permute-start | bytes 110600 | tf_op jit(solution)/shard_map/ppermute | solution.py:262
  144.8 11.7 %collective-permute-start.13 = (bf16[16,1152]{1,0:T(8,128)(2,1)S(1)}, bf16[16,1152]{1,0:T(8,128)(2,1)S(1)}, u32[]{:S(2)}, u32[]{:S(2)}) collective-permute-start(bf16[16,1152]{1,0:T(8,128)(2,1)S(1)} %fusion.23), channel_id=1, source_target_pairs={{96,0},{192,96},{288,192},{384,288},{480,384},{576,480},{672,576},... | collective-permute-start | bytes 110600 | tf_op jit(solution)/shard_map/ppermute | solution.py:262
  148.8 8.3 %collective-permute-start.14 = (bf16[16,1024]{1,0:T(8,128)(2,1)}, bf16[16,1024]{1,0:T(8,128)(2,1)}, u32[]{:S(2)}, u32[]{:S(2)}) collective-permute-start(bf16[16,1024]{1,0:T(8,128)(2,1)} %fusion.33), channel_id=1, source_target_pairs={{0,3},{3,6},{6,9},{9,12},{12,15},{15,18},{18,21},{1,4},{4,7},{7,10... | collective-permute-start | bytes 98312 | tf_op jit(solution)/shard_map/ppermute | solution.py:254
  155.2 7.2 %collective-permute-start.15 = (bf16[16,1024]{1,0:T(8,128)(2,1)}, bf16[16,1024]{1,0:T(8,128)(2,1)}, u32[]{:S(2)}, u32[]{:S(2)}) collective-permute-start(bf16[16,1024]{1,0:T(8,128)(2,1)} %fusion.30), channel_id=1, source_target_pairs={{3,0},{6,3},{9,6},{12,9},{15,12},{18,15},{21,18},{4,1},{7,4},{10,7... | collective-permute-start | bytes 98312 | tf_op jit(solution)/shard_map/ppermute | solution.py:254
  156.5 0.6 copy-start.10
  180.5 22.5 %copy-start.11 = (bf16[16,1152]{1,0:T(8,128)(2,1)S(1)}, bf16[16,1152]{1,0:T(8,128)(2,1)}, u32[]{:S(2)}) copy-start(bf16[16,1152]{1,0:T(8,128)(2,1)} %copy-done.10) | copy-start | bytes 110596
  218.0 0.9 copy-start.15
  218.0 0.9 copy-start.18
  218.4 2.1 copy-start.16

commit v10 on v9

--- a/solution.py
+++ b/solution.py
@@ -305,9 +305,10 @@
     y_two = ring_send(cut_y[2], 2)
     block = to_x(divergence.reshape(288, 128))
     held = exchange(jnp.broadcast_to(block[None], (8, 144, 256)), "y")
+    held, y_two = lax.optimization_barrier((held, y_two))
     got = exchange(x_products(quad_me, held, table_fx), QUAD)
     shapes = (mode_shape[:, 0], mode_shape[:, 1])
-    got, y_two, (shape_zero, shape_one) = lax.optimization_barrier((got, y_two, shapes))
+    got, (shape_zero, shape_one) = lax.optimization_barrier((got, shapes))
     cut_ix = quad_cut(quad_me, inverse_x)
     table_y = (cut_y[0], y_one, y_two)
     spread = jax.ShapeDtypeStruct((8, 288, 128), BF)

time: 222 us -> 222 us (level)
  waiting for transfers between devices: 31.6 us -> 28.8 us
    ppermute x2, waiting for transfers between devices: 6.99 us -> 1.53 us  [ring_send(): return lax.ppermute(piece, 'zl', [(i, (i + step) % 3) for i in range(3)])]
    all_to_all x5, waiting for transfers between devices: 6.51 us -> 10.8 us  [exchange(): return lax.all_to_all(parts, axes, 0, 0)]
    all_to_all x5, starting transfers between devices: 37.8 us -> 40.5 us  [exchange(): return lax.all_to_all(parts, axes, 0, 0)]
    unnamed x45 -> x43, local copies, waits for them, and re-layouts: 6.2 us -> 5.13 us
  transfers between devices with their start and end apart: 21 -> 21, of which waited for: 7 -> 8; matrix products, arithmetic and copies ran while one was open for 3% -> 2% of each run, Pallas kernels for 4% -> 3%
where the time goes in v10:
time: 222 us; the launch traced here: 220 us
  starting transfers between devices  103 us (46%)
  blocking collectives  53.6 us (24%)
  waiting for transfers between devices  28.8 us (13%)
  Pallas kernels  17 us (8%)
  other arithmetic  7.93 us (4%)
  local copies, waits for them, and re-layouts  7.29 us (3%)
    all_to_all x3, blocking collectives, exchange(): return lax.all_to_all(parts, axes, 0, 0)  53.6 us
    all_to_all x5, starting transfers between devices, exchange(): return lax.all_to_all(parts, axes, 0, 0)  40.5 us
    ppermute x6, starting transfers between devices, quad_send(): return lax.ppermute(piece, QUAD, [(i, i ^ step) for i in range(4)])  24.6 us
    pallas_call x10, Pallas kernels, call(): pl.pallas_call(kernel, out_shape=out_shape, in_specs=[smem] + [vmem] * (l...  17 us
    ppermute x6, waiting for transfers between devices, quad_send(): return lax.ppermute(piece, QUAD, [(i, i ^ step) for i in range(4)])  12.1 us
    all_to_all x5, waiting for transfers between devices, exchange(): return lax.all_to_all(parts, axes, 0, 0)  10.8 us
    ppermute x2, starting transfers between devices, edges(): lax.ppermute(lax.slice_in_dim(block, block.shape[dim] - 1, None, axis=dim...  9.95 us
    ppermute x2, starting transfers between devices, edges(): high = lax.ppermute(lax.slice_in_dim(block, 0, 1, axis=dim), axes, backward)  8.14 us
  transfers between devices with their start and end apart: 21, of which 8 were waited for; matrix products, arithmetic and copies ran while one was open for 2% of the time, Pallas kernels for 3%

profile of v10, /device:TPU:1, one launch (start us, length us, event | category | flops | bytes accessed | tf_op | source)
XLA Modules:
  0.0 220.4 jit_solution(15016476696501570189)
XLA Ops:
  0.6 2.4 %fusion.8 = (bf16[16,144,128]{2,1,0:T(8,128)(2,1)}, bf16[16,144,128]{2,1,0:T(8,128)(2,1)S(1)}) fusion(bf16[16,144,128]{2,1,0:T(8,128)(2,1)} %param.13, s32[144,128]{1,0:T(8,128)} %param.15, s32[144,128]{1,0:T(8,128)} %param.16, bf16[16,144,128]{2,1,0:T(8,128)(2,1)} %param.14), kind=kLoop, calls=%fused_computation.13 | loop fusion | flops 2949120 | bytes 2506752 | tf_op jit(solution)/shard_map/mul | solution.py:291
  4.1 5.5 %collective-permute-start.3 = (bf16[2,144,1]{2,0,1:T(2,128)(2,1)}, bf16[2,144,1]{2,0,1:T(2,128)(2,1)}, u32[]{:S(2)}, u32[]{:S(2)}) collective-permute-start(bf16[2,144,1]{2,0,1:T(2,128)(2,1)} %get-tuple-element.118), channel_id=1, source_target_pairs={{0,1},{1,2},{2,3},{3,4},{4,5},{5,6},{6,7},{7,8},{8,9},{9,10},{10,1... | collective-permute-start | bytes 1736 | tf_op jit(solution)/shard_map/ppermute | solution.py:28
  9.6 1.3 collective-permute-start.2
  10.9 1.1 copy-done.4
  12.0 1.2 shard_map.148
  13.3 4.0 %collective-permute-start.4 = (bf16[256,1024]{1,0:T(8,128)(2,1)}, bf16[256,1024]{1,0:T(8,128)(2,1)S(1)}, u32[]{:S(2)}, u32[]{:S(2)}) collective-permute-start(bf16[256,1024]{1,0:T(8,128)(2,1)} %get-tuple-element.43), channel_id=1, source_target_pairs={{0,1},{1,2},{2,0},{3,4},{4,5},{5,3},{6,7},{7,8},{8,6},{9,10},{10,1... | collective-permute-start | bytes 1572872 | tf_op jit(solution)/shard_map/ppermute | solution.py:98
  17.3 1.3 fusion.44
  18.6 4.5 %collective-permute-start.1 = (bf16[2,1,128]{2,0,1:T(2,128)(2,1)S(1)}, bf16[2,1,128]{2,0,1:T(2,128)(2,1)S(1)}, u32[]{:S(2)}, u32[]{:S(2)}) collective-permute-start(bf16[2,1,128]{2,0,1:T(2,128)(2,1)S(1)} %get-tuple-element.116), channel_id=1, source_target_pairs={{0,24},{24,48},{48,72},{72,96},{96,120},{120,144},{144,168},{168,1... | collective-permute-start | bytes 1544 | tf_op jit(solution)/shard_map/ppermute | solution.py:28
  23.1 6.9 %collective-permute-start = (bf16[2,1,128]{2,0,1:T(2,128)(2,1)S(1)}, bf16[2,1,128]{2,0,1:T(2,128)(2,1)S(1)}, u32[]{:S(2)}, u32[]{:S(2)}) collective-permute-start(bf16[2,1,128]{2,0,1:T(2,128)(2,1)S(1)} %get-tuple-element.115), channel_id=1, source_target_pairs={{24,0},{48,24},{72,48},{96,72},{120,96},{144,120},{168,144},{192,1... | collective-permute-start | bytes 1544 | tf_op jit(solution)/shard_map/ppermute | solution.py:29
  30.0 3.5 %shard_map.149 = (bf16[144,1152]{1,0:T(8,128)(2,1)S(1)}, bf16[144,1152]{1,0:T(8,128)(2,1)S(1)}, bf16[144,1152]{1,0:T(8,128)(2,1)}, bf16[144,1152]{1,0:T(8,128)(2,1)S(1)}) custom-call(s32[1]{0:T(128)} %bitcast.me_ref, bf16[144,4608]{1,0:T(8,128)(2,1)S(1)} %copy-done.1), custom_call_target="tpu_custom_call" | custom-call | bytes 2654208 | tf_op jit(solution)/shard_map/pallas_call | solution.py:49
  35.0 0.9 convert_element_type.65
  36.7 0.9 broadcast_in_dim.2
  37.6 3.5 %all-to-all-start = ((bf16[8,144,256]{2,1,0:T(8,128)(2,1)}), bf16[8,144,256]{2,1,0:T(8,128)(2,1)S(1)}, u32[]{:S(2)}, u32[]{:S(2)}) async-start(bf16[8,144,256]{2,1,0:T(8,128)(2,1)} %broadcast_in_dim.2), calls=%async_computation | async-start | bytes 1179648 | tf_op jit(solution)/shard_map/all_to_all | solution.py:20
  41.1 3.4 %collective-permute-start.6 = (bf16[144,1152]{1,0:T(8,128)(2,1)}, bf16[144,1152]{1,0:T(8,128)(2,1)S(1)}, u32[]{:S(2)}, u32[]{:S(2)}) collective-permute-start(bf16[144,1152]{1,0:T(8,128)(2,1)} %get-tuple-element.50), channel_id=1, source_target_pairs={{0,48},{24,72},{48,0},{72,24},{1,49},{25,73},{49,1},{73,25},{2,50}... | collective-permute-start | bytes 995336 | tf_op jit(solution)/shard_map/ppermute | solution.py:80
  44.5 1.9 collective-permute-start.5
  46.4 6.2 %collective-permute-start.8 = (bf16[144,1152]{1,0:T(8,128)(2,1)}, bf16[144,1152]{1,0:T(8,128)(2,1)S(1)}, u32[]{:S(2)}, u32[]{:S(2)}) collective-permute-start(bf16[144,1152]{1,0:T(8,128)(2,1)} %copy-done.13), channel_id=1, source_target_pairs={{0,72},{24,48},{48,24},{72,0},{1,73},{25,49},{49,25},{73,1},{2,74}... | collective-permute-start | bytes 995336 | tf_op jit(solution)/shard_map/ppermute | solution.py:80
  52.6 3.4 %collective-permute-start.7 = (bf16[144,1152]{1,0:T(8,128)(2,1)S(1)}, bf16[144,1152]{1,0:T(8,128)(2,1)}, u32[]{:S(2)}, u32[]{:S(2)}) collective-permute-start(bf16[144,1152]{1,0:T(8,128)(2,1)S(1)} %copy-done.12), channel_id=1, source_target_pairs={{0,24},{24,0},{48,72},{72,48},{1,25},{25,1},{49,73},{73,49},{2,26}... | collective-permute-start | bytes 995336 | tf_op jit(solution)/shard_map/ppermute | solution.py:80
  56.1 1.5 collective-permute-done.5.t2
  57.6 3.0 %collective-permute-done.8.t3 = bf16[144,1152]{1,0:T(8,128)(2,1)S(1)} collective-permute-done((bf16[144,1152]{1,0:T(8,128)(2,1)}, bf16[144,1152]{1,0:T(8,128)(2,1)S(1)}, u32[]{:S(2)}, u32[]{:S(2)}) %collective-permute-start.8) | collective-permute-done | bytes 331808 | tf_op jit(solution)/shard_map/ppermute | solution.py:80
  60.6 2.3 %shard_map.150 = bf16[4,144,256]{2,1,0:T(8,128)(2,1)} custom-call(s32[1]{0:T(128)} %bitcast.me_ref, bf16[1152,256]{1,0:T(8,128)(2,1)S(1)} %bitcast.79, bf16[144,1152]{1,0:T(8,128)(2,1)S(1)} %get-tuple-element.48.t0, bf16[144,1152]{1,0:T(8,128)(2,1)} %collective-permute-done.7.t1, bf16[144,1152]{1,0:T(8,128)(2,1)S(1)} %collective-permute-done.6.t2, ...), custom_call_target="tpu_custom_call" | custom-call | flops 339738624 | bytes 2211840 | tf_op jit(solution)/shard_map/pallas_call | solution.py:49
  62.9 3.8 %all-to-all-start.1 = ((bf16[4,144,256]{2,1,0:T(8,128)(2,1)}), bf16[4,144,256]{2,1,0:T(8,128)(2,1)S(1)}, u32[]{:S(2)}, u32[]{:S(2)}) async-start(bf16[4,144,256]{2,1,0:T(8,128)(2,1)} %shard_map.150), calls=%async_computation.1 | async-start | bytes 589824 | tf_op jit(solution)/shard_map/all_to_all | solution.py:20
  66.7 5.5 %all-to-all-done.1.got_ref = bf16[4,144,256]{2,1,0:T(8,128)(2,1)S(1)} async-done(((bf16[4,144,256]{2,1,0:T(8,128)(2,1)}), bf16[4,144,256]{2,1,0:T(8,128)(2,1)S(1)}, u32[]{:S(2)}, u32[]{:S(2)}) %all-to-all-start.1) | async-done | bytes 294944 | tf_op jit(solution)/shard_map/all_to_all | solution.py:20
  72.2 0.9 shard_map.151
  73.0 15.2 %all-to-all-start.2 = ((bf16[8,288,128]{2,1,0:T(8,128)(2,1)}), bf16[8,288,128]{2,1,0:T(8,128)(2,1)S(1)}, u32[]{:S(2)}, u32[]{:S(2)}) async-start(bf16[8,288,128]{2,1,0:T(8,128)(2,1)} %shard_map.151), calls=%async_computation.2 | async-start | bytes 1179648 | tf_op jit(solution)/shard_map/all_to_all | solution.py:20
  88.3 2.8 %shard_map.152 = (bf16[144,1152]{1,0:T(8,128)(2,1)S(1)}, bf16[144,1152]{1,0:T(8,128)(2,1)S(1)}, bf16[144,1152]{1,0:T(8,128)(2,1)S(1)}, bf16[144,1152]{1,0:T(8,128)(2,1)S(1)}) custom-call(s32[1]{0:T(128)} %bitcast.me_ref, bf16[144,4608]{1,0:T(8,128)(2,1)S(1)} %copy-done.2), custom_call_target="tpu_custom_call" | custom-call | bytes 2654208 | tf_op jit(solution)/shard_map/pallas_call | solution.py:49
  91.8 1.9 collective-permute-start.9
  93.8 4.7 %collective-permute-start.11 = (bf16[144,1152]{1,0:T(8,128)(2,1)S(1)}, bf16[144,1152]{1,0:T(8,128)(2,1)S(1)}, u32[]{:S(2)}, u32[]{:S(2)}) collective-permute-start(bf16[144,1152]{1,0:T(8,128)(2,1)S(1)} %get-tuple-element.61), channel_id=1, source_target_pairs={{0,72},{24,48},{48,24},{72,0},{1,73},{25,49},{49,25},{73,1},{2,74}... | collective-permute-start | bytes 995336 | tf_op jit(solution)/shard_map/ppermute | solution.py:80
  98.4 6.7 %collective-permute-done.9.t2 = bf16[144,1152]{1,0:T(8,128)(2,1)S(1)} collective-permute-done((bf16[144,1152]{1,0:T(8,128)(2,1)S(1)}, bf16[144,1152]{1,0:T(8,128)(2,1)S(1)}, u32[]{:S(2)}, u32[]{:S(2)}) %collective-permute-start.9) | collective-permute-done | bytes 331808 | tf_op jit(solution)/shard_map/ppermute | solution.py:80
  105.2 5.0 %collective-permute-start.10 = (bf16[144,1152]{1,0:T(8,128)(2,1)S(1)}, bf16[144,1152]{1,0:T(8,128)(2,1)S(1)}, u32[]{:S(2)}, u32[]{:S(2)}) collective-permute-start(bf16[144,1152]{1,0:T(8,128)(2,1)S(1)} %get-tuple-element.59), channel_id=1, source_target_pairs={{0,24},{24,0},{48,72},{72,48},{1,25},{25,1},{49,73},{73,49},{2,26}... | collective-permute-start | bytes 995336 | tf_op jit(solution)/shard_map/ppermute | solution.py:80
  110.9 2.4 %collective-permute-done.11.t3 = bf16[144,1152]{1,0:T(8,128)(2,1)S(1)} collective-permute-done((bf16[144,1152]{1,0:T(8,128)(2,1)S(1)}, bf16[144,1152]{1,0:T(8,128)(2,1)S(1)}, u32[]{:S(2)}, u32[]{:S(2)}) %collective-permute-start.11) | collective-permute-done | bytes 331808 | tf_op jit(solution)/shard_map/ppermute | solution.py:80
  113.3 1.4 shard_map.153
  114.7 4.9 %all-to-all-start.3 = ((bf16[3,288,128]{2,1,0:T(8,128)(2,1)}), bf16[3,288,128]{2,1,0:T(8,128)(2,1)S(1)}, u32[]{:S(2)}, u32[]{:S(2)}) async-start(bf16[3,288,128]{2,1,0:T(8,128)(2,1)} %shard_map.153), calls=%async_computation.3 | async-start | bytes 442368 | tf_op jit(solution)/shard_map/all_to_all | solution.py:20
  119.6 4.4 %all-to-all-done.3.got_ref = bf16[3,288,128]{2,1,0:T(8,128)(2,1)S(1)} async-done(((bf16[3,288,128]{2,1,0:T(8,128)(2,1)}), bf16[3,288,128]{2,1,0:T(8,128)(2,1)S(1)}, u32[]{:S(2)}, u32[]{:S(2)}) %all-to-all-start.3) | async-done | bytes 221216 | tf_op jit(solution)/shard_map/all_to_all | solution.py:20
  124.0 0.9 copy-done.7
  124.9 1.4 shard_map.154
  126.3 13.1 %all-to-all-start.4 = ((bf16[8,288,128]{2,1,0:T(8,128)(2,1)}), bf16[8,288,128]{2,1,0:T(8,128)(2,1)S(1)}, u32[]{:S(2)}, u32[]{:S(2)}) async-start(bf16[8,288,128]{2,1,0:T(8,128)(2,1)} %shard_map.154), calls=%async_computation.4 | async-start | bytes 1179648 | tf_op jit(solution)/shard_map/all_to_all | solution.py:20
  139.5 3.8 %collective-permute-start.12 = (bf16[16,1152]{1,0:T(8,128)(2,1)S(1)}, bf16[16,1152]{1,0:T(8,128)(2,1)S(1)}, u32[]{:S(2)}, u32[]{:S(2)}) collective-permute-start(bf16[16,1152]{1,0:T(8,128)(2,1)S(1)} %fusion.27), channel_id=1, source_target_pairs={{0,96},{96,192},{192,288},{288,384},{384,480},{480,576},{576,672},... | collective-permute-start | bytes 110600 | tf_op jit(solution)/shard_map/ppermute | solution.py:262
  143.4 3.1 %collective-permute-start.13 = (bf16[16,1152]{1,0:T(8,128)(2,1)S(1)}, bf16[16,1152]{1,0:T(8,128)(2,1)S(1)}, u32[]{:S(2)}, u32[]{:S(2)}) collective-permute-start(bf16[16,1152]{1,0:T(8,128)(2,1)S(1)} %fusion.23), channel_id=1, source_target_pairs={{96,0},{192,96},{288,192},{384,288},{480,384},{576,480},{672,576},... | collective-permute-start | bytes 110600 | tf_op jit(solution)/shard_map/ppermute | solution.py:262
  147.2 5.8 %collective-permute-start.14 = (bf16[16,1024]{1,0:T(8,128)(2,1)}, bf16[16,1024]{1,0:T(8,128)(2,1)}, u32[]{:S(2)}, u32[]{:S(2)}) collective-permute-start(bf16[16,1024]{1,0:T(8,128)(2,1)} %fusion.33), channel_id=1, source_target_pairs={{0,3},{3,6},{6,9},{9,12},{12,15},{15,18},{18,21},{1,4},{4,7},{7,10... | collective-permute-start | bytes 98312 | tf_op jit(solution)/shard_map/ppermute | solution.py:254
  153.6 1.3 collective-permute-start.15
  155.6 0.9 all-to-all-done.4.held_ref
  156.4 4.3 %collective-permute-done.15.hi_ref = bf16[16,1024]{1,0:T(8,128)(2,1)} collective-permute-done((bf16[16,1024]{1,0:T(8,128)(2,1)}, bf16[16,1024]{1,0:T(8,128)(2,1)}, u32[]{:S(2)}, u32[]{:S(2)}) %collective-permute-start.15) | collective-permute-done | bytes 32800 | tf_op jit(solution)/shard_map/ppermute | solution.py:254
  160.8 2.4 %shard_map.155 = bf16[3,320,128]{2,1,0:T(8,128)(2,1)S(1)} custom-call(s32[1]{0:T(128)} %bitcast.4.me_ref, bf16[8,288,128]{2,1,0:T(8,128)(2,1)S(1)} %all-to-all-done.4.held_ref, bf16[256,1024]{1,0:T(8,128)(2,1)S(1)} %get-tuple-element.77.t0, bf16[256,1024]{1,0:T(8,128)(2,1)S(1)} %collective-permute-done.4.t1, ...), custom_call_target="tpu_custom_call" | custom-call | flops 226492416 | bytes 2473984 | tf_op jit(solution)/shard_map/pallas_call | solution.py:49
  163.1 16.1 %all_to_all.40.got_ref = bf16[3,320,128]{2,1,0:T(8,128)(2,1)S(1)} all-to-all(bf16[3,320,128]{2,1,0:T(8,128)(2,1)S(1)} %shard_map.155), channel_id=1, replica_groups=mesh['y'=8,'xl'=2,'c'=2,'xh'=2,'zh'=4,'zl'=3] {'zl'}, dimensions={0} | all-to-all | bytes 491520 | tf_op jit(solution)/shard_map/all_to_all | solution.py:20
  179.3 25.2 %all_to_all.41.held_ref = bf16[8,160,256]{2,1,0:T(8,128)(2,1)S(1)} all-to-all(bf16[8,160,256]{2,1,0:T(8,128)(2,1)S(1)} %shard_map.156), channel_id=1, replica_groups=mesh['y'=8,'xl'=2,'c'=2,'xh'=2,'zh'=4,'zl'=3] {'y'}, dimensions={0} | all-to-all | bytes 1310720 | tf_op jit(solution)/shard_map/all_to_all | solution.py:20
  204.4 1.1 shard_map.157
  205.5 12.4 %all_to_all.42 = bf16[4,160,256]{2,1,0:T(8,128)(2,1)S(1)} all-to-all(bf16[4,160,256]{2,1,0:T(8,128)(2,1)S(1)} %shard_map.157), channel_id=1, replica_groups=mesh['y'=8,'xl'=2,'c'=2,'xh'=2,'zh'=4,'zl'=3] {'xl','c'}, dimensions={0} | all-to-all | bytes 655360 | tf_op jit(solution)/shard_map/all_to_all | solution.py:20
  218.8 1.6 fusion.4
  (91 shorter events, 7.7 us)
Async XLA Ops:
  0.6 2.5 %copy-start = (bf16[16,2]{0,1:T(2,128)(2,1)S(1)}, bf16[16,2]{0,1:T(2,128)(2,1)}, u32[]{:S(2)}) copy-start(bf16[16,2]{0,1:T(2,128)(2,1)} %param.17) | copy-start | bytes 196
  3.1 7.8 %copy-start.3 = (bf16[128,3072]{1,0:T(8,128)(2,1)S(1)}, bf16[128,3072]{1,0:T(8,128)(2,1)}, u32[]{:S(2)}) copy-start(bf16[128,3072]{1,0:T(8,128)(2,1)} %first_ref.1) | copy-start | bytes 2359300
  4.1 30.9 %collective-permute-start.3 = (bf16[2,144,1]{2,0,1:T(2,128)(2,1)}, bf16[2,144,1]{2,0,1:T(2,128)(2,1)}, u32[]{:S(2)}, u32[]{:S(2)}) collective-permute-start(bf16[2,144,1]{2,0,1:T(2,128)(2,1)} %get-tuple-element.118), channel_id=1, source_target_pairs={{0,1},{1,2},{2,3},{3,4},{4,5},{5,6},{6,7},{7,8},{8,9},{9,10},{10,1... | collective-permute-start | bytes 1736 | tf_op jit(solution)/shard_map/ppermute | solution.py:28
  9.6 26.4 %collective-permute-start.2 = (bf16[2,144,1]{2,0,1:T(2,128)(2,1)}, bf16[2,144,1]{2,0,1:T(2,128)(2,1)S(1)}, u32[]{:S(2)}, u32[]{:S(2)}) collective-permute-start(bf16[2,144,1]{2,0,1:T(2,128)(2,1)} %get-tuple-element.117), channel_id=1, source_target_pairs={{1,0},{2,1},{3,2},{4,3},{5,4},{6,5},{7,6},{8,7},{9,8},{10,9},{11,1... | collective-permute-start | bytes 1736 | tf_op jit(solution)/shard_map/ppermute | solution.py:29
  10.9 1.1 copy-start.4
  12.0 17.9 %copy-start.14 = (s32[144,128]{1,0:T(8,128)S(1)}, s32[144,128]{1,0:T(8,128)}, u32[]{:S(2)}) copy-start(s32[144,128]{1,0:T(8,128)} %param.15) | copy-start | bytes 221188
  12.0 18.0 %copy-start.1 = (bf16[144,4608]{1,0:T(8,128)(2,1)S(1)}, bf16[144,4608]{1,0:T(8,128)(2,1)}, u32[]{:S(2)}) copy-start(bf16[144,4608]{1,0:T(8,128)(2,1)} %rows_ref.2) | copy-start | bytes 3981316
  13.3 23.3 %collective-permute-start.4 = (bf16[256,1024]{1,0:T(8,128)(2,1)}, bf16[256,1024]{1,0:T(8,128)(2,1)S(1)}, u32[]{:S(2)}, u32[]{:S(2)}) collective-permute-start(bf16[256,1024]{1,0:T(8,128)(2,1)} %get-tuple-element.43), channel_id=1, source_target_pairs={{0,1},{1,2},{2,0},{3,4},{4,5},{5,3},{6,7},{7,8},{8,6},{9,10},{10,1... | collective-permute-start | bytes 1572872 | tf_op jit(solution)/shard_map/ppermute | solution.py:98
  18.6 16.4 %collective-permute-start.1 = (bf16[2,1,128]{2,0,1:T(2,128)(2,1)S(1)}, bf16[2,1,128]{2,0,1:T(2,128)(2,1)S(1)}, u32[]{:S(2)}, u32[]{:S(2)}) collective-permute-start(bf16[2,1,128]{2,0,1:T(2,128)(2,1)S(1)} %get-tuple-element.116), channel_id=1, source_target_pairs={{0,24},{24,48},{48,72},{72,96},{96,120},{120,144},{144,168},{168,1... | collective-permute-start | bytes 1544 | tf_op jit(solution)/shard_map/ppermute | solution.py:28
  23.1 11.9 %collective-permute-start = (bf16[2,1,128]{2,0,1:T(2,128)(2,1)S(1)}, bf16[2,1,128]{2,0,1:T(2,128)(2,1)S(1)}, u32[]{:S(2)}, u32[]{:S(2)}) collective-permute-start(bf16[2,1,128]{2,0,1:T(2,128)(2,1)S(1)} %get-tuple-element.115), channel_id=1, source_target_pairs={{24,0},{48,24},{72,48},{96,72},{120,96},{144,120},{168,144},{192,1... | collective-permute-start | bytes 1544 | tf_op jit(solution)/shard_map/ppermute | solution.py:29
  33.5 0.7 copy-start.11
  34.2 0.7 copy-start.13
  36.7 16.0 %copy-start.12 = (bf16[144,1152]{1,0:T(8,128)(2,1)S(1)}, bf16[144,1152]{1,0:T(8,128)(2,1)}, u32[]{:S(2)}) copy-start(bf16[144,1152]{1,0:T(8,128)(2,1)} %copy-done.11) | copy-start | bytes 995332
  37.6 20.1 %all-to-all-start = ((bf16[8,144,256]{2,1,0:T(8,128)(2,1)}), bf16[8,144,256]{2,1,0:T(8,128)(2,1)S(1)}, u32[]{:S(2)}, u32[]{:S(2)}) async-start(bf16[8,144,256]{2,1,0:T(8,128)(2,1)} %broadcast_in_dim.2), calls=%async_computation | async-start | bytes 1179648 | tf_op jit(solution)/shard_map/all_to_all | solution.py:20
  41.1 11.5 %collective-permute-start.6 = (bf16[144,1152]{1,0:T(8,128)(2,1)}, bf16[144,1152]{1,0:T(8,128)(2,1)S(1)}, u32[]{:S(2)}, u32[]{:S(2)}) collective-permute-start(bf16[144,1152]{1,0:T(8,128)(2,1)} %get-tuple-element.50), channel_id=1, source_target_pairs={{0,48},{24,72},{48,0},{72,24},{1,49},{25,73},{49,1},{73,25},{2,50}... | collective-permute-start | bytes 995336 | tf_op jit(solution)/shard_map/ppermute | solution.py:80
  44.5 13.1 %collective-permute-start.5 = (bf16[256,1024]{1,0:T(8,128)(2,1)}, bf16[256,1024]{1,0:T(8,128)(2,1)S(1)}, u32[]{:S(2)}, u32[]{:S(2)}) collective-permute-start(bf16[256,1024]{1,0:T(8,128)(2,1)} %get-tuple-element.46), channel_id=1, source_target_pairs={{0,2},{1,0},{2,1},{3,5},{4,3},{5,4},{6,8},{7,6},{8,7},{9,11},{10,9... | collective-permute-start | bytes 1572872 | tf_op jit(solution)/shard_map/ppermute | solution.py:98
  46.4 14.2 %collective-permute-start.8 = (bf16[144,1152]{1,0:T(8,128)(2,1)}, bf16[144,1152]{1,0:T(8,128)(2,1)S(1)}, u32[]{:S(2)}, u32[]{:S(2)}) collective-permute-start(bf16[144,1152]{1,0:T(8,128)(2,1)} %copy-done.13), channel_id=1, source_target_pairs={{0,72},{24,48},{48,24},{72,0},{1,73},{25,49},{49,25},{73,1},{2,74}... | collective-permute-start | bytes 995336 | tf_op jit(solution)/shard_map/ppermute | solution.py:80
  52.6 8.0 %collective-permute-start.7 = (bf16[144,1152]{1,0:T(8,128)(2,1)S(1)}, bf16[144,1152]{1,0:T(8,128)(2,1)}, u32[]{:S(2)}, u32[]{:S(2)}) collective-permute-start(bf16[144,1152]{1,0:T(8,128)(2,1)S(1)} %copy-done.12), channel_id=1, source_target_pairs={{0,24},{24,0},{48,72},{72,48},{1,25},{25,1},{49,73},{73,49},{2,26}... | collective-permute-start | bytes 995336 | tf_op jit(solution)/shard_map/ppermute | solution.py:80
  60.6 6.0 %copy-start.19 = (f32[16,2]{0,1:T(2,128)S(1)}, f32[16,2]{0,1:T(2,128)}, u32[]{:S(2)}) copy-start(f32[16,2]{0,1:T(2,128)} %param.18) | copy-start | bytes 388
  62.9 9.3 %all-to-all-start.1 = ((bf16[4,144,256]{2,1,0:T(8,128)(2,1)}), bf16[4,144,256]{2,1,0:T(8,128)(2,1)S(1)}, u32[]{:S(2)}, u32[]{:S(2)}) async-start(bf16[4,144,256]{2,1,0:T(8,128)(2,1)} %shard_map.150), calls=%async_computation.1 | async-start | bytes 589824 | tf_op jit(solution)/shard_map/all_to_all | solution.py:20
  66.7 21.6 %copy-start.2 = (bf16[144,4608]{1,0:T(8,128)(2,1)S(1)}, bf16[144,4608]{1,0:T(8,128)(2,1)}, u32[]{:S(2)}) copy-start(bf16[144,4608]{1,0:T(8,128)(2,1)} %rows_ref.3) | copy-start | bytes 3981316
  73.0 37.1 %copy-start.18 = (f32[144]{0:T(256)S(1)}, f32[144]{0:T(256)}, u32[]{:S(2)}) copy-start(f32[144]{0:T(256)} %param.23) | copy-start | bytes 1732
  73.0 37.1 %copy-start.20 = (f32[128]{0:T(128)S(1)}, f32[128]{0:T(128)}, u32[]{:S(2)}) copy-start(f32[128]{0:T(128)} %param.24) | copy-start | bytes 1540
  73.0 40.3 %all-to-all-start.2 = ((bf16[8,288,128]{2,1,0:T(8,128)(2,1)}), bf16[8,288,128]{2,1,0:T(8,128)(2,1)S(1)}, u32[]{:S(2)}, u32[]{:S(2)}) async-start(bf16[8,288,128]{2,1,0:T(8,128)(2,1)} %shard_map.151), calls=%async_computation.2 | async-start | bytes 1179648 | tf_op jit(solution)/shard_map/all_to_all | solution.py:20
  91.1 0.7 copy-start.5
  91.8 13.3 %collective-permute-start.9 = (bf16[144,1152]{1,0:T(8,128)(2,1)S(1)}, bf16[144,1152]{1,0:T(8,128)(2,1)S(1)}, u32[]{:S(2)}, u32[]{:S(2)}) collective-permute-start(bf16[144,1152]{1,0:T(8,128)(2,1)S(1)} %get-tuple-element.58), channel_id=1, source_target_pairs={{0,48},{24,72},{48,0},{72,24},{1,49},{25,73},{49,1},{73,25},{2,50}... | collective-permute-start | bytes 995336 | tf_op jit(solution)/shard_map/ppermute | solution.py:80
  93.8 19.6 %collective-permute-start.11 = (bf16[144,1152]{1,0:T(8,128)(2,1)S(1)}, bf16[144,1152]{1,0:T(8,128)(2,1)S(1)}, u32[]{:S(2)}, u32[]{:S(2)}) collective-permute-start(bf16[144,1152]{1,0:T(8,128)(2,1)S(1)} %get-tuple-element.61), channel_id=1, source_target_pairs={{0,72},{24,48},{48,24},{72,0},{1,73},{25,49},{49,25},{73,1},{2,74}... | collective-permute-start | bytes 995336 | tf_op jit(solution)/shard_map/ppermute | solution.py:80
  105.2 8.2 %collective-permute-start.10 = (bf16[144,1152]{1,0:T(8,128)(2,1)S(1)}, bf16[144,1152]{1,0:T(8,128)(2,1)S(1)}, u32[]{:S(2)}, u32[]{:S(2)}) collective-permute-start(bf16[144,1152]{1,0:T(8,128)(2,1)S(1)} %get-tuple-element.59), channel_id=1, source_target_pairs={{0,24},{24,0},{48,72},{72,48},{1,25},{25,1},{49,73},{73,49},{2,26}... | collective-permute-start | bytes 995336 | tf_op jit(solution)/shard_map/ppermute | solution.py:80
  113.3 10.6 %copy-start.10 = (f32[2]{0:T(128)S(1)}, f32[2]{0:T(128)}, u32[]{:S(2)}) copy-start(f32[2]{0:T(128)} %shift_ref.1) | copy-start | bytes 28
  114.7 24.7 %copy-start.6 = (bf16[144,1152]{1,0:T(8,128)(2,1)S(1)}, bf16[144,1152]{1,0:T(8,128)(2,1)}, u32[]{:S(2)}) copy-start(bf16[144,1152]{1,0:T(8,128)(2,1)} %copy-done.5) | copy-start | bytes 995332
  114.7 9.3 %all-to-all-start.3 = ((bf16[3,288,128]{2,1,0:T(8,128)(2,1)}), bf16[3,288,128]{2,1,0:T(8,128)(2,1)S(1)}, u32[]{:S(2)}, u32[]{:S(2)}) async-start(bf16[3,288,128]{2,1,0:T(8,128)(2,1)} %shard_map.153), calls=%async_computation.3 | async-start | bytes 442368 | tf_op jit(solution)/shard_map/all_to_all | solution.py:20
  124.0 0.9 copy-start.7
  126.3 30.1 %all-to-all-start.4 = ((bf16[8,288,128]{2,1,0:T(8,128)(2,1)}), bf16[8,288,128]{2,1,0:T(8,128)(2,1)S(1)}, u32[]{:S(2)}, u32[]{:S(2)}) async-start(bf16[8,288,128]{2,1,0:T(8,128)(2,1)} %shard_map.154), calls=%async_computation.4 | async-start | bytes 1179648 | tf_op jit(solution)/shard_map/all_to_all | solution.py:20
  139.5 15.4 %collective-permute-start.12 = (bf16[16,1152]{1,0:T(8,128)(2,1)S(1)}, bf16[16,1152]{1,0:T(8,128)(2,1)S(1)}, u32[]{:S(2)}, u32[]{:S(2)}) collective-permute-start(bf16[16,1152]{1,0:T(8,128)(2,1)S(1)} %fusion.27), channel_id=1, source_target_pairs={{0,96},{96,192},{192,288},{288,384},{384,480},{480,576},{576,672},... | collective-permute-start | bytes 110600 | tf_op jit(solution)/shard_map/ppermute | solution.py:262
  143.4 11.5 %collective-permute-start.13 = (bf16[16,1152]{1,0:T(8,128)(2,1)S(1)}, bf16[16,1152]{1,0:T(8,128)(2,1)S(1)}, u32[]{:S(2)}, u32[]{:S(2)}) collective-permute-start(bf16[16,1152]{1,0:T(8,128)(2,1)S(1)} %fusion.23), channel_id=1, source_target_pairs={{96,0},{192,96},{288,192},{384,288},{480,384},{576,480},{672,576},... | collective-permute-start | bytes 110600 | tf_op jit(solution)/shard_map/ppermute | solution.py:262
  147.2 9.2 %collective-permute-start.14 = (bf16[16,1024]{1,0:T(8,128)(2,1)}, bf16[16,1024]{1,0:T(8,128)(2,1)}, u32[]{:S(2)}, u32[]{:S(2)}) collective-permute-start(bf16[16,1024]{1,0:T(8,128)(2,1)} %fusion.33), channel_id=1, source_target_pairs={{0,3},{3,6},{6,9},{9,12},{12,15},{15,18},{18,21},{1,4},{4,7},{7,10... | collective-permute-start | bytes 98312 | tf_op jit(solution)/shard_map/ppermute | solution.py:254
  153.6 7.1 %collective-permute-start.15 = (bf16[16,1024]{1,0:T(8,128)(2,1)}, bf16[16,1024]{1,0:T(8,128)(2,1)}, u32[]{:S(2)}, u32[]{:S(2)}) collective-permute-start(bf16[16,1024]{1,0:T(8,128)(2,1)} %fusion.30), channel_id=1, source_target_pairs={{3,0},{6,3},{9,6},{12,9},{15,12},{18,15},{21,18},{4,1},{7,4},{10,7... | collective-permute-start | bytes 98312 | tf_op jit(solution)/shard_map/ppermute | solution.py:254
  154.9 0.6 copy-start.8
  179.2 25.2 %copy-start.9 = (bf16[16,1152]{1,0:T(8,128)(2,1)S(1)}, bf16[16,1152]{1,0:T(8,128)(2,1)}, u32[]{:S(2)}) copy-start(bf16[16,1152]{1,0:T(8,128)(2,1)} %copy-done.8) | copy-start | bytes 110596
  217.9 0.9 copy-start.15
  217.9 0.9 copy-start.17
  218.3 2.1 copy-start.16

commit v11 on v10

--- a/solution.py
+++ b/solution.py
@@ -136,6 +136,12 @@
     for source in range(1, got_ref.shape[0]):
         total = total + got_ref[source].astype(F32)
     return total
+
+
+def spread_kernel(me_ref, block_ref, out_ref):
+    for y in range(8):
+        out_ref[y, :, :128] = block_ref[0]
+        out_ref[y, :, 128:] = block_ref[1]
 
 
 def to_y_kernel(me_ref, got_ref, out_ref):
@@ -260,10 +266,6 @@
     up = [(i, (i + 1) % 8) for i in range(8)]
     down = [((i + 1) % 8, i) for i in range(8)]
     return lax.ppermute(low, "y", up), lax.ppermute(high, "y", down)
-
-
-def to_x(block):
-    return jnp.concatenate([block[:144], block[144:]], axis=1)
 
 
 def to_y(block):
@@ -303,8 +305,8 @@
     core, fx_two = lax.optimization_barrier((cut_fx[1], fx_two))
     table_fx = (cut_fx[0], quad_send(core, 1), fx_two, fx_three)
     y_two = ring_send(cut_y[2], 2)
-    block = to_x(divergence.reshape(288, 128))
-    held = exchange(jnp.broadcast_to(block[None], (8, 144, 256)), "y")
+    spread = jax.ShapeDtypeStruct((8, 144, 256), BF)
+    held = exchange(call(spread_kernel, spread, (quad_me, divergence)), "y")
     held, y_two = lax.optimization_barrier((held, y_two))
     got = exchange(x_products(quad_me, held, table_fx), QUAD)
     shapes = (mode_shape[:, 0], mode_shape[:, 1])

time: 222 us -> 219 us (0.986)
  local copies, waits for them, and re-layouts: 7.29 us -> 4.79 us
    unnamed x43 -> x42, local copies, waits for them, and re-layouts: 5.13 us -> 3.68 us
    pallas_call x10 -> x11, Pallas kernels: 17 us -> 17.9 us  [call(): pl.pallas_call(kernel, out_shape=out_shape, in_specs=[smem] + [vmem] * (l...]
where the time goes in v11:
time: 219 us; the launch traced here: 218 us
  starting transfers between devices  104 us (47%)
  blocking collectives  52 us (24%)
  waiting for transfers between devices  28.9 us (13%)
  Pallas kernels  17.9 us (8%)
  other arithmetic  7.62 us (3%)
  local copies, waits for them, and re-layouts  4.79 us (2%)
    all_to_all x3, blocking collectives, exchange(): return lax.all_to_all(parts, axes, 0, 0)  52 us
    all_to_all x5, starting transfers between devices, exchange(): return lax.all_to_all(parts, axes, 0, 0)  40.1 us
    ppermute x6, starting transfers between devices, quad_send(): return lax.ppermute(piece, QUAD, [(i, i ^ step) for i in range(4)])  26.3 us
    pallas_call x11, Pallas kernels, call(): pl.pallas_call(kernel, out_shape=out_shape, in_specs=[smem] + [vmem] * (l...  17.9 us
    all_to_all x5, waiting for transfers between devices, exchange(): return lax.all_to_all(parts, axes, 0, 0)  11.9 us
    ppermute x6, waiting for transfers between devices, quad_send(): return lax.ppermute(piece, QUAD, [(i, i ^ step) for i in range(4)])  10.1 us
    ppermute x2, starting transfers between devices, edges(): lax.ppermute(lax.slice_in_dim(block, block.shape[dim] - 1, None, axis=dim...  9.93 us
    ppermute x2, starting transfers between devices, edges(): high = lax.ppermute(lax.slice_in_dim(block, 0, 1, axis=dim), axes, backward)  8.13 us
  transfers between devices with their start and end apart: 21, of which 8 were waited for; matrix products, arithmetic and copies ran while one was open for 2% of the time, Pallas kernels for 3%

profile of v11, /device:TPU:1, one launch (start us, length us, event | category | flops | bytes accessed | tf_op | source)
XLA Modules:
  0.0 217.7 jit_solution(8598030463153857631)
XLA Ops:
  0.6 2.4 %fusion.6 = (bf16[16,144,128]{2,1,0:T(8,128)(2,1)}, bf16[16,144,128]{2,1,0:T(8,128)(2,1)S(1)}) fusion(bf16[16,144,128]{2,1,0:T(8,128)(2,1)} %param.13, s32[144,128]{1,0:T(8,128)} %param.15, s32[144,128]{1,0:T(8,128)} %param.16, bf16[16,144,128]{2,1,0:T(8,128)(2,1)} %param.14), kind=kLoop, calls=%fused_computation.9 | loop fusion | flops 2949120 | bytes 2506752 | tf_op jit(solution)/shard_map/mul | solution.py:293
  4.1 5.4 %collective-permute-start.3 = (bf16[2,144,1]{2,1,0:T(8,128)(2,1)}, bf16[2,144,1]{2,1,0:T(8,128)(2,1)}, u32[]{:S(2)}, u32[]{:S(2)}) collective-permute-start(bf16[2,144,1]{2,1,0:T(8,128)(2,1)} %get-tuple-element.120), channel_id=1, source_target_pairs={{0,1},{1,2},{2,3},{3,4},{4,5},{5,6},{6,7},{7,8},{8,9},{9,10},{10,1... | collective-permute-start | bytes 1736 | tf_op jit(solution)/shard_map/ppermute | solution.py:28
  9.5 1.3 collective-permute-start.2
  10.8 1.1 copy-done.4
  12.0 1.2 shard_map.148
  13.2 4.0 %collective-permute-start.4 = (bf16[256,1024]{1,0:T(8,128)(2,1)}, bf16[256,1024]{1,0:T(8,128)(2,1)S(1)}, u32[]{:S(2)}, u32[]{:S(2)}) collective-permute-start(bf16[256,1024]{1,0:T(8,128)(2,1)} %get-tuple-element.43), channel_id=1, source_target_pairs={{0,1},{1,2},{2,0},{3,4},{4,5},{5,3},{6,7},{7,8},{8,6},{9,10},{10,1... | collective-permute-start | bytes 1572872 | tf_op jit(solution)/shard_map/ppermute | solution.py:98
  17.2 1.3 fusion.9
  18.6 4.5 %collective-permute-start.1 = (bf16[2,1,128]{2,1,0:T(2,128)(2,1)S(1)}, bf16[2,1,128]{2,1,0:T(2,128)(2,1)S(1)}, u32[]{:S(2)}, u32[]{:S(2)}) collective-permute-start(bf16[2,1,128]{2,1,0:T(2,128)(2,1)S(1)} %get-tuple-element.118), channel_id=1, source_target_pairs={{0,24},{24,48},{48,72},{72,96},{96,120},{120,144},{144,168},{168,1... | collective-permute-start | bytes 1544 | tf_op jit(solution)/shard_map/ppermute | solution.py:28
  23.1 6.9 %collective-permute-start = (bf16[2,1,128]{2,1,0:T(2,128)(2,1)S(1)}, bf16[2,1,128]{2,1,0:T(2,128)(2,1)S(1)}, u32[]{:S(2)}, u32[]{:S(2)}) collective-permute-start(bf16[2,1,128]{2,1,0:T(2,128)(2,1)S(1)} %get-tuple-element.117), channel_id=1, source_target_pairs={{24,0},{48,24},{72,48},{96,72},{120,96},{144,120},{168,144},{192,1... | collective-permute-start | bytes 1544 | tf_op jit(solution)/shard_map/ppermute | solution.py:29
  30.0 3.5 %shard_map.149 = (bf16[144,1152]{1,0:T(8,128)(2,1)S(1)}, bf16[144,1152]{1,0:T(8,128)(2,1)S(1)}, bf16[144,1152]{1,0:T(8,128)(2,1)}, bf16[144,1152]{1,0:T(8,128)(2,1)S(1)}) custom-call(s32[1]{0:T(128)} %bitcast.me_ref, bf16[144,4608]{1,0:T(8,128)(2,1)S(1)} %copy-done.1), custom_call_target="tpu_custom_call" | custom-call | bytes 2654208 | tf_op jit(solution)/shard_map/pallas_call | solution.py:49
  33.5 1.0 convert_element_type.65
  34.8 0.9 shard_map.150
  35.7 3.5 %all-to-all-start = ((bf16[8,144,256]{2,1,0:T(8,128)(2,1)}), bf16[8,144,256]{2,1,0:T(8,128)(2,1)S(1)}, u32[]{:S(2)}, u32[]{:S(2)}) async-start(bf16[8,144,256]{2,1,0:T(8,128)(2,1)} %shard_map.150), calls=%async_computation | async-start | bytes 1179648 | tf_op jit(solution)/shard_map/all_to_all | solution.py:20
  39.2 4.8 %collective-permute-start.6 = (bf16[144,1152]{1,0:T(8,128)(2,1)}, bf16[144,1152]{1,0:T(8,128)(2,1)S(1)}, u32[]{:S(2)}, u32[]{:S(2)}) collective-permute-start(bf16[144,1152]{1,0:T(8,128)(2,1)} %get-tuple-element.50), channel_id=1, source_target_pairs={{0,48},{24,72},{48,0},{72,24},{1,49},{25,73},{49,1},{73,25},{2,50}... | collective-permute-start | bytes 995336 | tf_op jit(solution)/shard_map/ppermute | solution.py:80
  44.0 1.9 collective-permute-start.5
  45.9 4.8 %collective-permute-start.8 = (bf16[144,1152]{1,0:T(8,128)(2,1)}, bf16[144,1152]{1,0:T(8,128)(2,1)S(1)}, u32[]{:S(2)}, u32[]{:S(2)}) collective-permute-start(bf16[144,1152]{1,0:T(8,128)(2,1)} %copy-done.13), channel_id=1, source_target_pairs={{0,72},{24,48},{48,24},{72,0},{1,73},{25,49},{49,25},{73,1},{2,74}... | collective-permute-start | bytes 995336 | tf_op jit(solution)/shard_map/ppermute | solution.py:80
  50.7 4.7 %collective-permute-start.7 = (bf16[144,1152]{1,0:T(8,128)(2,1)S(1)}, bf16[144,1152]{1,0:T(8,128)(2,1)}, u32[]{:S(2)}, u32[]{:S(2)}) collective-permute-start(bf16[144,1152]{1,0:T(8,128)(2,1)S(1)} %copy-done.12), channel_id=1, source_target_pairs={{0,24},{24,0},{48,72},{72,48},{1,25},{25,1},{49,73},{73,49},{2,26}... | collective-permute-start | bytes 995336 | tf_op jit(solution)/shard_map/ppermute | solution.py:80
  55.4 3.1 %collective-permute-done.5.t2 = bf16[256,1024]{1,0:T(8,128)(2,1)S(1)} collective-permute-done((bf16[256,1024]{1,0:T(8,128)(2,1)}, bf16[256,1024]{1,0:T(8,128)(2,1)S(1)}, u32[]{:S(2)}, u32[]{:S(2)}) %collective-permute-start.5) | collective-permute-done | bytes 524320 | tf_op jit(solution)/shard_map/ppermute | solution.py:98
  58.5 1.1 collective-permute-done.8.t3
  59.6 2.3 %shard_map.151 = bf16[4,144,256]{2,1,0:T(8,128)(2,1)} custom-call(s32[1]{0:T(128)} %bitcast.me_ref, bf16[1152,256]{1,0:T(8,128)(2,1)S(1)} %bitcast.73, bf16[144,1152]{1,0:T(8,128)(2,1)S(1)} %get-tuple-element.48.t0, bf16[144,1152]{1,0:T(8,128)(2,1)} %collective-permute-done.7.t1, bf16[144,1152]{1,0:T(8,128)(2,1)S(1)} %collective-permute-done.6.t2, ...), custom_call_target="tpu_custom_call" | custom-call | flops 339738624 | bytes 2211840 | tf_op jit(solution)/shard_map/pallas_call | solution.py:49
  61.9 4.2 %all-to-all-start.1 = ((bf16[4,144,256]{2,1,0:T(8,128)(2,1)}), bf16[4,144,256]{2,1,0:T(8,128)(2,1)S(1)}, u32[]{:S(2)}, u32[]{:S(2)}) async-start(bf16[4,144,256]{2,1,0:T(8,128)(2,1)} %shard_map.151), calls=%async_computation.1 | async-start | bytes 589824 | tf_op jit(solution)/shard_map/all_to_all | solution.py:20
  66.1 5.5 %all-to-all-done.1.got_ref = bf16[4,144,256]{2,1,0:T(8,128)(2,1)S(1)} async-done(((bf16[4,144,256]{2,1,0:T(8,128)(2,1)}), bf16[4,144,256]{2,1,0:T(8,128)(2,1)S(1)}, u32[]{:S(2)}, u32[]{:S(2)}) %all-to-all-start.1) | async-done | bytes 294944 | tf_op jit(solution)/shard_map/all_to_all | solution.py:20
  71.7 0.9 shard_map.152
  72.5 15.4 %all-to-all-start.2 = ((bf16[8,288,128]{2,1,0:T(8,128)(2,1)}), bf16[8,288,128]{2,1,0:T(8,128)(2,1)S(1)}, u32[]{:S(2)}, u32[]{:S(2)}) async-start(bf16[8,288,128]{2,1,0:T(8,128)(2,1)} %shard_map.152), calls=%async_computation.2 | async-start | bytes 1179648 | tf_op jit(solution)/shard_map/all_to_all | solution.py:20
  88.0 2.8 %shard_map.153 = (bf16[144,1152]{1,0:T(8,128)(2,1)S(1)}, bf16[144,1152]{1,0:T(8,128)(2,1)S(1)}, bf16[144,1152]{1,0:T(8,128)(2,1)S(1)}, bf16[144,1152]{1,0:T(8,128)(2,1)S(1)}) custom-call(s32[1]{0:T(128)} %bitcast.me_ref, bf16[144,4608]{1,0:T(8,128)(2,1)S(1)} %copy-done.2), custom_call_target="tpu_custom_call" | custom-call | bytes 2654208 | tf_op jit(solution)/shard_map/pallas_call | solution.py:49
  91.5 1.9 collective-permute-start.9
  93.4 4.7 %collective-permute-start.11 = (bf16[144,1152]{1,0:T(8,128)(2,1)S(1)}, bf16[144,1152]{1,0:T(8,128)(2,1)S(1)}, u32[]{:S(2)}, u32[]{:S(2)}) collective-permute-start(bf16[144,1152]{1,0:T(8,128)(2,1)S(1)} %get-tuple-element.61), channel_id=1, source_target_pairs={{0,72},{24,48},{48,24},{72,0},{1,73},{25,49},{49,25},{73,1},{2,74}... | collective-permute-start | bytes 995336 | tf_op jit(solution)/shard_map/ppermute | solution.py:80
  98.1 6.8 %collective-permute-done.9.t2 = bf16[144,1152]{1,0:T(8,128)(2,1)S(1)} collective-permute-done((bf16[144,1152]{1,0:T(8,128)(2,1)S(1)}, bf16[144,1152]{1,0:T(8,128)(2,1)S(1)}, u32[]{:S(2)}, u32[]{:S(2)}) %collective-permute-start.9) | collective-permute-done | bytes 331808 | tf_op jit(solution)/shard_map/ppermute | solution.py:80
  104.9 5.4 %collective-permute-start.10 = (bf16[144,1152]{1,0:T(8,128)(2,1)S(1)}, bf16[144,1152]{1,0:T(8,128)(2,1)S(1)}, u32[]{:S(2)}, u32[]{:S(2)}) collective-permute-start(bf16[144,1152]{1,0:T(8,128)(2,1)S(1)} %get-tuple-element.59), channel_id=1, source_target_pairs={{0,24},{24,0},{48,72},{72,48},{1,25},{25,1},{49,73},{73,49},{2,26}... | collective-permute-start | bytes 995336 | tf_op jit(solution)/shard_map/ppermute | solution.py:80
  111.1 2.2 %collective-permute-done.11.t3 = bf16[144,1152]{1,0:T(8,128)(2,1)S(1)} collective-permute-done((bf16[144,1152]{1,0:T(8,128)(2,1)S(1)}, bf16[144,1152]{1,0:T(8,128)(2,1)S(1)}, u32[]{:S(2)}, u32[]{:S(2)}) %collective-permute-start.11) | collective-permute-done | bytes 331808 | tf_op jit(solution)/shard_map/ppermute | solution.py:80
  113.3 1.4 shard_map.154
  114.7 3.8 %all-to-all-start.3 = ((bf16[3,288,128]{2,1,0:T(8,128)(2,1)}), bf16[3,288,128]{2,1,0:T(8,128)(2,1)S(1)}, u32[]{:S(2)}, u32[]{:S(2)}) async-start(bf16[3,288,128]{2,1,0:T(8,128)(2,1)} %shard_map.154), calls=%async_computation.3 | async-start | bytes 442368 | tf_op jit(solution)/shard_map/all_to_all | solution.py:20
  118.5 4.9 %all-to-all-done.3.got_ref = bf16[3,288,128]{2,1,0:T(8,128)(2,1)S(1)} async-done(((bf16[3,288,128]{2,1,0:T(8,128)(2,1)}), bf16[3,288,128]{2,1,0:T(8,128)(2,1)S(1)}, u32[]{:S(2)}, u32[]{:S(2)}) %all-to-all-start.3) | async-done | bytes 221216 | tf_op jit(solution)/shard_map/all_to_all | solution.py:20
  123.4 0.9 copy-done.7
  124.3 1.4 shard_map.155
  125.7 13.1 %all-to-all-start.4 = ((bf16[8,288,128]{2,1,0:T(8,128)(2,1)}), bf16[8,288,128]{2,1,0:T(8,128)(2,1)S(1)}, u32[]{:S(2)}, u32[]{:S(2)}) async-start(bf16[8,288,128]{2,1,0:T(8,128)(2,1)} %shard_map.155), calls=%async_computation.4 | async-start | bytes 1179648 | tf_op jit(solution)/shard_map/all_to_all | solution.py:20
  138.9 3.2 %collective-permute-start.12 = (bf16[16,1152]{1,0:T(8,128)(2,1)S(1)}, bf16[16,1152]{1,0:T(8,128)(2,1)S(1)}, u32[]{:S(2)}, u32[]{:S(2)}) collective-permute-start(bf16[16,1152]{1,0:T(8,128)(2,1)S(1)} %fusion.29), channel_id=1, source_target_pairs={{0,96},{96,192},{192,288},{288,384},{384,480},{480,576},{576,672},... | collective-permute-start | bytes 110600 | tf_op jit(solution)/shard_map/ppermute | solution.py:268
  142.2 3.3 %collective-permute-start.13 = (bf16[16,1152]{1,0:T(8,128)(2,1)S(1)}, bf16[16,1152]{1,0:T(8,128)(2,1)S(1)}, u32[]{:S(2)}, u32[]{:S(2)}) collective-permute-start(bf16[16,1152]{1,0:T(8,128)(2,1)S(1)} %fusion.25), channel_id=1, source_target_pairs={{96,0},{192,96},{288,192},{384,288},{480,384},{576,480},{672,576},... | collective-permute-start | bytes 110600 | tf_op jit(solution)/shard_map/ppermute | solution.py:268
  146.2 5.8 %collective-permute-start.14 = (bf16[16,1024]{1,0:T(8,128)(2,1)}, bf16[16,1024]{1,0:T(8,128)(2,1)}, u32[]{:S(2)}, u32[]{:S(2)}) collective-permute-start(bf16[16,1024]{1,0:T(8,128)(2,1)} %fusion.35), channel_id=1, source_target_pairs={{0,3},{3,6},{6,9},{9,12},{12,15},{15,18},{18,21},{1,4},{4,7},{7,10... | collective-permute-start | bytes 98312 | tf_op jit(solution)/shard_map/ppermute | solution.py:260
  152.5 1.3 collective-permute-start.15
  154.5 1.4 all-to-all-done.4.held_ref
  155.9 3.8 %collective-permute-done.15.hi_ref = bf16[16,1024]{1,0:T(8,128)(2,1)} collective-permute-done((bf16[16,1024]{1,0:T(8,128)(2,1)}, bf16[16,1024]{1,0:T(8,128)(2,1)}, u32[]{:S(2)}, u32[]{:S(2)}) %collective-permute-start.15) | collective-permute-done | bytes 32800 | tf_op jit(solution)/shard_map/ppermute | solution.py:260
  159.7 2.4 %shard_map.156 = bf16[3,320,128]{2,1,0:T(8,128)(2,1)S(1)} custom-call(s32[1]{0:T(128)} %bitcast.4.me_ref, bf16[8,288,128]{2,1,0:T(8,128)(2,1)S(1)} %all-to-all-done.4.held_ref, bf16[256,1024]{1,0:T(8,128)(2,1)S(1)} %get-tuple-element.77.t0, bf16[256,1024]{1,0:T(8,128)(2,1)S(1)} %collective-permute-done.4.t1, ...), custom_call_target="tpu_custom_call" | custom-call | flops 226492416 | bytes 2473984 | tf_op jit(solution)/shard_map/pallas_call | solution.py:49
  162.0 16.7 %all_to_all.40.got_ref = bf16[3,320,128]{2,1,0:T(8,128)(2,1)S(1)} all-to-all(bf16[3,320,128]{2,1,0:T(8,128)(2,1)S(1)} %shard_map.156), channel_id=1, replica_groups=mesh['y'=8,'xl'=2,'c'=2,'xh'=2,'zh'=4,'zl'=3] {'zl'}, dimensions={0} | all-to-all | bytes 491520 | tf_op jit(solution)/shard_map/all_to_all | solution.py:20
  178.9 21.5 %all_to_all.41.held_ref = bf16[8,160,256]{2,1,0:T(8,128)(2,1)S(1)} all-to-all(bf16[8,160,256]{2,1,0:T(8,128)(2,1)S(1)} %shard_map.157), channel_id=1, replica_groups=mesh['y'=8,'xl'=2,'c'=2,'xh'=2,'zh'=4,'zl'=3] {'y'}, dimensions={0} | all-to-all | bytes 1310720 | tf_op jit(solution)/shard_map/all_to_all | solution.py:20
  200.3 1.1 shard_map.158
  201.4 13.8 %all_to_all.42 = bf16[4,160,256]{2,1,0:T(8,128)(2,1)S(1)} all-to-all(bf16[4,160,256]{2,1,0:T(8,128)(2,1)S(1)} %shard_map.158), channel_id=1, replica_groups=mesh['y'=8,'xl'=2,'c'=2,'xh'=2,'zh'=4,'zl'=3] {'xl','c'}, dimensions={0} | all-to-all | bytes 655360 | tf_op jit(solution)/shard_map/all_to_all | solution.py:20
  216.1 1.6 fusion.4
  (87 shorter events, 5.7 us)
Async XLA Ops:
  0.6 2.5 %copy-start = (bf16[16,2]{0,1:T(2,128)(2,1)S(1)}, bf16[16,2]{0,1:T(2,128)(2,1)}, u32[]{:S(2)}) copy-start(bf16[16,2]{0,1:T(2,128)(2,1)} %param.17) | copy-start | bytes 196
  3.1 7.7 %copy-start.3 = (bf16[128,3072]{1,0:T(8,128)(2,1)S(1)}, bf16[128,3072]{1,0:T(8,128)(2,1)}, u32[]{:S(2)}) copy-start(bf16[128,3072]{1,0:T(8,128)(2,1)} %first_ref.1) | copy-start | bytes 2359300
  4.1 29.4 %collective-permute-start.3 = (bf16[2,144,1]{2,1,0:T(8,128)(2,1)}, bf16[2,144,1]{2,1,0:T(8,128)(2,1)}, u32[]{:S(2)}, u32[]{:S(2)}) collective-permute-start(bf16[2,144,1]{2,1,0:T(8,128)(2,1)} %get-tuple-element.120), channel_id=1, source_target_pairs={{0,1},{1,2},{2,3},{3,4},{4,5},{5,6},{6,7},{7,8},{8,9},{9,10},{10,1... | collective-permute-start | bytes 1736 | tf_op jit(solution)/shard_map/ppermute | solution.py:28
  9.5 25.0 %collective-permute-start.2 = (bf16[2,144,1]{2,1,0:T(8,128)(2,1)}, bf16[2,144,1]{2,1,0:T(8,128)(2,1)S(1)}, u32[]{:S(2)}, u32[]{:S(2)}) collective-permute-start(bf16[2,144,1]{2,1,0:T(8,128)(2,1)} %get-tuple-element.119), channel_id=1, source_target_pairs={{1,0},{2,1},{3,2},{4,3},{5,4},{6,5},{7,6},{8,7},{9,8},{10,9},{11,1... | collective-permute-start | bytes 1736 | tf_op jit(solution)/shard_map/ppermute | solution.py:29
  10.8 1.1 copy-start.4
  12.0 18.0 %copy-start.14 = (s32[144,128]{1,0:T(8,128)S(1)}, s32[144,128]{1,0:T(8,128)}, u32[]{:S(2)}) copy-start(s32[144,128]{1,0:T(8,128)} %param.15) | copy-start | bytes 221188
  12.0 18.0 %copy-start.1 = (bf16[144,4608]{1,0:T(8,128)(2,1)S(1)}, bf16[144,4608]{1,0:T(8,128)(2,1)}, u32[]{:S(2)}) copy-start(bf16[144,4608]{1,0:T(8,128)(2,1)} %rows_ref.2) | copy-start | bytes 3981316
  13.2 21.5 %collective-permute-start.4 = (bf16[256,1024]{1,0:T(8,128)(2,1)}, bf16[256,1024]{1,0:T(8,128)(2,1)S(1)}, u32[]{:S(2)}, u32[]{:S(2)}) collective-permute-start(bf16[256,1024]{1,0:T(8,128)(2,1)} %get-tuple-element.43), channel_id=1, source_target_pairs={{0,1},{1,2},{2,0},{3,4},{4,5},{5,3},{6,7},{7,8},{8,6},{9,10},{10,1... | collective-permute-start | bytes 1572872 | tf_op jit(solution)/shard_map/ppermute | solution.py:98
  18.6 14.9 %collective-permute-start.1 = (bf16[2,1,128]{2,1,0:T(2,128)(2,1)S(1)}, bf16[2,1,128]{2,1,0:T(2,128)(2,1)S(1)}, u32[]{:S(2)}, u32[]{:S(2)}) collective-permute-start(bf16[2,1,128]{2,1,0:T(2,128)(2,1)S(1)} %get-tuple-element.118), channel_id=1, source_target_pairs={{0,24},{24,48},{48,72},{72,96},{96,120},{120,144},{144,168},{168,1... | collective-permute-start | bytes 1544 | tf_op jit(solution)/shard_map/ppermute | solution.py:28
  23.1 10.4 %collective-permute-start = (bf16[2,1,128]{2,1,0:T(2,128)(2,1)S(1)}, bf16[2,1,128]{2,1,0:T(2,128)(2,1)S(1)}, u32[]{:S(2)}, u32[]{:S(2)}) collective-permute-start(bf16[2,1,128]{2,1,0:T(2,128)(2,1)S(1)} %get-tuple-element.117), channel_id=1, source_target_pairs={{24,0},{48,24},{72,48},{96,72},{120,96},{144,120},{168,144},{192,1... | collective-permute-start | bytes 1544 | tf_op jit(solution)/shard_map/ppermute | solution.py:29
  33.5 1.1 copy-start.11
  33.5 1.3 copy-start.13
  34.5 16.2 %copy-start.12 = (bf16[144,1152]{1,0:T(8,128)(2,1)S(1)}, bf16[144,1152]{1,0:T(8,128)(2,1)}, u32[]{:S(2)}) copy-start(bf16[144,1152]{1,0:T(8,128)(2,1)} %copy-done.11) | copy-start | bytes 995332
  35.7 22.9 %all-to-all-start = ((bf16[8,144,256]{2,1,0:T(8,128)(2,1)}), bf16[8,144,256]{2,1,0:T(8,128)(2,1)S(1)}, u32[]{:S(2)}, u32[]{:S(2)}) async-start(bf16[8,144,256]{2,1,0:T(8,128)(2,1)} %shard_map.150), calls=%async_computation | async-start | bytes 1179648 | tf_op jit(solution)/shard_map/all_to_all | solution.py:20
  39.2 11.5 %collective-permute-start.6 = (bf16[144,1152]{1,0:T(8,128)(2,1)}, bf16[144,1152]{1,0:T(8,128)(2,1)S(1)}, u32[]{:S(2)}, u32[]{:S(2)}) collective-permute-start(bf16[144,1152]{1,0:T(8,128)(2,1)} %get-tuple-element.50), channel_id=1, source_target_pairs={{0,48},{24,72},{48,0},{72,24},{1,49},{25,73},{49,1},{73,25},{2,50}... | collective-permute-start | bytes 995336 | tf_op jit(solution)/shard_map/ppermute | solution.py:80
  44.0 14.5 %collective-permute-start.5 = (bf16[256,1024]{1,0:T(8,128)(2,1)}, bf16[256,1024]{1,0:T(8,128)(2,1)S(1)}, u32[]{:S(2)}, u32[]{:S(2)}) collective-permute-start(bf16[256,1024]{1,0:T(8,128)(2,1)} %get-tuple-element.46), channel_id=1, source_target_pairs={{0,2},{1,0},{2,1},{3,5},{4,3},{5,4},{6,8},{7,6},{8,7},{9,11},{10,9... | collective-permute-start | bytes 1572872 | tf_op jit(solution)/shard_map/ppermute | solution.py:98
  45.9 13.7 %collective-permute-start.8 = (bf16[144,1152]{1,0:T(8,128)(2,1)}, bf16[144,1152]{1,0:T(8,128)(2,1)S(1)}, u32[]{:S(2)}, u32[]{:S(2)}) collective-permute-start(bf16[144,1152]{1,0:T(8,128)(2,1)} %copy-done.13), channel_id=1, source_target_pairs={{0,72},{24,48},{48,24},{72,0},{1,73},{25,49},{49,25},{73,1},{2,74}... | collective-permute-start | bytes 995336 | tf_op jit(solution)/shard_map/ppermute | solution.py:80
  50.7 8.9 %collective-permute-start.7 = (bf16[144,1152]{1,0:T(8,128)(2,1)S(1)}, bf16[144,1152]{1,0:T(8,128)(2,1)}, u32[]{:S(2)}, u32[]{:S(2)}) collective-permute-start(bf16[144,1152]{1,0:T(8,128)(2,1)S(1)} %copy-done.12), channel_id=1, source_target_pairs={{0,24},{24,0},{48,72},{72,48},{1,25},{25,1},{49,73},{73,49},{2,26}... | collective-permute-start | bytes 995336 | tf_op jit(solution)/shard_map/ppermute | solution.py:80
  59.6 6.5 %copy-start.19 = (f32[16,2]{0,1:T(2,128)S(1)}, f32[16,2]{0,1:T(2,128)}, u32[]{:S(2)}) copy-start(f32[16,2]{0,1:T(2,128)} %param.18) | copy-start | bytes 388
  61.9 9.7 %all-to-all-start.1 = ((bf16[4,144,256]{2,1,0:T(8,128)(2,1)}), bf16[4,144,256]{2,1,0:T(8,128)(2,1)S(1)}, u32[]{:S(2)}, u32[]{:S(2)}) async-start(bf16[4,144,256]{2,1,0:T(8,128)(2,1)} %shard_map.151), calls=%async_computation.1 | async-start | bytes 589824 | tf_op jit(solution)/shard_map/all_to_all | solution.py:20
  66.1 21.8 %copy-start.2 = (bf16[144,4608]{1,0:T(8,128)(2,1)S(1)}, bf16[144,4608]{1,0:T(8,128)(2,1)}, u32[]{:S(2)}) copy-start(bf16[144,4608]{1,0:T(8,128)(2,1)} %rows_ref.3) | copy-start | bytes 3981316
  72.5 37.8 %copy-start.18 = (f32[144]{0:T(256)S(1)}, f32[144]{0:T(256)}, u32[]{:S(2)}) copy-start(f32[144]{0:T(256)} %param.23) | copy-start | bytes 1732
  72.5 37.8 %copy-start.20 = (f32[128]{0:T(128)S(1)}, f32[128]{0:T(128)}, u32[]{:S(2)}) copy-start(f32[128]{0:T(128)} %param.24) | copy-start | bytes 1540
  72.5 40.8 %all-to-all-start.2 = ((bf16[8,288,128]{2,1,0:T(8,128)(2,1)}), bf16[8,288,128]{2,1,0:T(8,128)(2,1)S(1)}, u32[]{:S(2)}, u32[]{:S(2)}) async-start(bf16[8,288,128]{2,1,0:T(8,128)(2,1)} %shard_map.152), calls=%async_computation.2 | async-start | bytes 1179648 | tf_op jit(solution)/shard_map/all_to_all | solution.py:20
  90.8 0.7 copy-start.5
  91.5 13.4 %collective-permute-start.9 = (bf16[144,1152]{1,0:T(8,128)(2,1)S(1)}, bf16[144,1152]{1,0:T(8,128)(2,1)S(1)}, u32[]{:S(2)}, u32[]{:S(2)}) collective-permute-start(bf16[144,1152]{1,0:T(8,128)(2,1)S(1)} %get-tuple-element.58), channel_id=1, source_target_pairs={{0,48},{24,72},{48,0},{72,24},{1,49},{25,73},{49,1},{73,25},{2,50}... | collective-permute-start | bytes 995336 | tf_op jit(solution)/shard_map/ppermute | solution.py:80
  93.4 19.9 %collective-permute-start.11 = (bf16[144,1152]{1,0:T(8,128)(2,1)S(1)}, bf16[144,1152]{1,0:T(8,128)(2,1)S(1)}, u32[]{:S(2)}, u32[]{:S(2)}) collective-permute-start(bf16[144,1152]{1,0:T(8,128)(2,1)S(1)} %get-tuple-element.61), channel_id=1, source_target_pairs={{0,72},{24,48},{48,24},{72,0},{1,73},{25,49},{49,25},{73,1},{2,74}... | collective-permute-start | bytes 995336 | tf_op jit(solution)/shard_map/ppermute | solution.py:80
  104.9 8.4 %collective-permute-start.10 = (bf16[144,1152]{1,0:T(8,128)(2,1)S(1)}, bf16[144,1152]{1,0:T(8,128)(2,1)S(1)}, u32[]{:S(2)}, u32[]{:S(2)}) collective-permute-start(bf16[144,1152]{1,0:T(8,128)(2,1)S(1)} %get-tuple-element.59), channel_id=1, source_target_pairs={{0,24},{24,0},{48,72},{72,48},{1,25},{25,1},{49,73},{73,49},{2,26}... | collective-permute-start | bytes 995336 | tf_op jit(solution)/shard_map/ppermute | solution.py:80
  113.3 10.1 %copy-start.10 = (f32[2]{0:T(128)S(1)}, f32[2]{0:T(128)}, u32[]{:S(2)}) copy-start(f32[2]{0:T(128)} %shift_ref.1) | copy-start | bytes 28
  114.7 24.1 %copy-start.6 = (bf16[144,1152]{1,0:T(8,128)(2,1)S(1)}, bf16[144,1152]{1,0:T(8,128)(2,1)}, u32[]{:S(2)}) copy-start(bf16[144,1152]{1,0:T(8,128)(2,1)} %copy-done.5) | copy-start | bytes 995332
  114.7 8.7 %all-to-all-start.3 = ((bf16[3,288,128]{2,1,0:T(8,128)(2,1)}), bf16[3,288,128]{2,1,0:T(8,128)(2,1)S(1)}, u32[]{:S(2)}, u32[]{:S(2)}) async-start(bf16[3,288,128]{2,1,0:T(8,128)(2,1)} %shard_map.154), calls=%async_computation.3 | async-start | bytes 442368 | tf_op jit(solution)/shard_map/all_to_all | solution.py:20
  123.4 0.9 copy-start.7
  125.7 30.2 %all-to-all-start.4 = ((bf16[8,288,128]{2,1,0:T(8,128)(2,1)}), bf16[8,288,128]{2,1,0:T(8,128)(2,1)S(1)}, u32[]{:S(2)}, u32[]{:S(2)}) async-start(bf16[8,288,128]{2,1,0:T(8,128)(2,1)} %shard_map.155), calls=%async_computation.4 | async-start | bytes 1179648 | tf_op jit(solution)/shard_map/all_to_all | solution.py:20
  138.9 14.9 %collective-permute-start.12 = (bf16[16,1152]{1,0:T(8,128)(2,1)S(1)}, bf16[16,1152]{1,0:T(8,128)(2,1)S(1)}, u32[]{:S(2)}, u32[]{:S(2)}) collective-permute-start(bf16[16,1152]{1,0:T(8,128)(2,1)S(1)} %fusion.29), channel_id=1, source_target_pairs={{0,96},{96,192},{192,288},{288,384},{384,480},{480,576},{576,672},... | collective-permute-start | bytes 110600 | tf_op jit(solution)/shard_map/ppermute | solution.py:268
  142.2 11.7 %collective-permute-start.13 = (bf16[16,1152]{1,0:T(8,128)(2,1)S(1)}, bf16[16,1152]{1,0:T(8,128)(2,1)S(1)}, u32[]{:S(2)}, u32[]{:S(2)}) collective-permute-start(bf16[16,1152]{1,0:T(8,128)(2,1)S(1)} %fusion.25), channel_id=1, source_target_pairs={{96,0},{192,96},{288,192},{384,288},{480,384},{576,480},{672,576},... | collective-permute-start | bytes 110600 | tf_op jit(solution)/shard_map/ppermute | solution.py:268
  146.2 9.8 %collective-permute-start.14 = (bf16[16,1024]{1,0:T(8,128)(2,1)}, bf16[16,1024]{1,0:T(8,128)(2,1)}, u32[]{:S(2)}, u32[]{:S(2)}) collective-permute-start(bf16[16,1024]{1,0:T(8,128)(2,1)} %fusion.35), channel_id=1, source_target_pairs={{0,3},{3,6},{6,9},{9,12},{12,15},{15,18},{18,21},{1,4},{4,7},{7,10... | collective-permute-start | bytes 98312 | tf_op jit(solution)/shard_map/ppermute | solution.py:260
  152.5 7.1 %collective-permute-start.15 = (bf16[16,1024]{1,0:T(8,128)(2,1)}, bf16[16,1024]{1,0:T(8,128)(2,1)}, u32[]{:S(2)}, u32[]{:S(2)}) collective-permute-start(bf16[16,1024]{1,0:T(8,128)(2,1)} %fusion.32), channel_id=1, source_target_pairs={{3,0},{6,3},{9,6},{12,9},{15,12},{18,15},{21,18},{4,1},{7,4},{10,7... | collective-permute-start | bytes 98312 | tf_op jit(solution)/shard_map/ppermute | solution.py:260
  153.9 0.6 copy-start.8
  178.8 21.6 %copy-start.9 = (bf16[16,1152]{1,0:T(8,128)(2,1)S(1)}, bf16[16,1152]{1,0:T(8,128)(2,1)}, u32[]{:S(2)}) copy-start(bf16[16,1152]{1,0:T(8,128)(2,1)} %copy-done.8) | copy-start | bytes 110596
  215.2 0.9 copy-start.15
  215.2 0.9 copy-start.17
  215.6 2.1 copy-start.16
